TPU v7x, 256 devices: a whole 4x4x8 slice. The times are simulated.
256 devices in a mesh: tm: 8 (over y, core), space: 32 (over x, z).
Axes of the slice: x: 4, y: 4, z: 8, core: 2. Of those that a mesh axis runs over, the one named last changes fastest.
Arguments:
- state_guess: float32 [16, 64, 96, 128], P('tm', 'space'), may hold values from -6 to 6
- adjoint_guess: float32 [16, 64, 96, 128], P('tm', 'space'), may hold values from -6 to 6
- target: float32 [16, 64, 96, 128], P('tm', 'space'), may hold values from -6 to 6
- initial_state: float32 [64, 96, 128], P('space'), may hold values from -6 to 6
- diffusivity: float32 [64, 96, 128], P('space'), may hold values from 0.3 to 3
Outputs:
- state_field: float32 [16, 64, 96, 128], P('tm', 'space')
- adjoint_field: float32 [16, 64, 96, 128], P('tm', 'space')
All inputs are finite; a program needn't handle non-finite values.
Results may differ from a plain program's by a relative error of at most 0.00025.
Values sent between devices are 32-bit elements; how exact they have to be, the bound alone decides.
No kernel may reach another device: no remote copies, remote signals or barrier semaphores. Data moves between devices by JAX's collectives and lax.ppermute only.
A program may use at most 64 MiB of HBM per device.

v0:
```python
import math

import jax
import jax.numpy as jnp
from jax import lax
from jax.sharding import PartitionSpec as P

SWEEPS = 4
OUTER = 2


step_size = 0.25
control_cost = 0.05


def swapped(block, axis, distance):
    count = lax.axis_size(axis)
    route = []
    for low in range(count):
        high = low | 1 << distance
        if high != low and high < count:
            route += [(low, high), (high, low)]
    return lax.ppermute(block, axis, route)


def extended(cells, sides, width):
    for axis, dim in sides:
        count = lax.axis_size(axis)
        ends = count - 1
        head = lax.slice_in_dim(cells, 0, width, axis=dim)
        tail = lax.slice_in_dim(cells, cells.shape[dim] - width, cells.shape[dim], axis=dim)
        cells = jnp.concatenate(
            [
                lax.ppermute(tail, axis, [(i, (i + 1) % count) for i in range(ends)]),
                cells,
                lax.ppermute(head, axis, [((i + 1) % count, i) for i in range(ends)]),
            ],
            axis=dim,
        )
    return cells


def rim_slices(padded):
    return [
        padded[..., 2:, 1:-1, 1:-1],
        padded[..., :-2, 1:-1, 1:-1],
        padded[..., 1:-1, 2:, 1:-1],
        padded[..., 1:-1, :-2, 1:-1],
        padded[..., 1:-1, 1:-1, 2:],
        padded[..., 1:-1, 1:-1, :-2],
    ]


def pad_inner(values):
    widths = [(0, 0)] * (values.ndim - 2) + [(1, 1)] * 2
    return jnp.pad(values, widths)


def neighbour_sum(rimmed, weights):
    pieces = rim_slices(pad_inner(rimmed))
    summed = weights[0] * pieces[0]
    for weight_one, piece_one in zip(weights[1:], pieces[1:]):
        summed = summed + weight_one * piece_one
    return summed


def block_solve(right_side, shift_real, shift_imag, determinant):
    coupling = step_size / control_cost
    state_real = right_side[0]
    state_imag = right_side[1]
    adjoint_real = right_side[2]
    adjoint_imag = right_side[3]
    return jnp.stack(
        [
            (shift_real * state_real + shift_imag * state_imag - coupling * adjoint_real)
            / determinant,
            (shift_real * state_imag - shift_imag * state_real - coupling * adjoint_imag)
            / determinant,
            (step_size * state_real + shift_real * adjoint_real - shift_imag * adjoint_imag)
            / determinant,
            (step_size * state_imag + shift_real * adjoint_imag + shift_imag * adjoint_real)
            / determinant,
        ]
    )


def twiddle(packed, cos_part, sin_part):
    return jnp.stack(
        [
            packed[0] * cos_part - packed[1] * sin_part,
            packed[0] * sin_part + packed[1] * cos_part,
            packed[2] * cos_part - packed[3] * sin_part,
            packed[2] * sin_part + packed[3] * cos_part,
        ]
    )


def butterfly_segment(packed, bit_number, position, device, local_steps, horizon, inverse):
    half_span = local_steps << bit_number
    partner = swapped(packed, "tm", bit_number)
    upper_half = jnp.bitwise_and(jnp.right_shift(device, bit_number), 1) == 0
    offset = jnp.remainder(position, half_span) * (horizon // (2 * half_span))
    angles = (2.0 * math.pi / horizon * offset.astype(jnp.float32)).reshape(-1, 1, 1, 1)
    cos_part = jnp.cos(angles)
    sin_part = jnp.sin(angles)
    if inverse:
        return jnp.where(
            upper_half,
            0.5 * (packed + twiddle(partner, cos_part, sin_part)),
            0.5 * (partner - twiddle(packed, cos_part, sin_part)),
        )
    return jnp.where(upper_half, packed + partner, twiddle(partner - packed, cos_part, -sin_part))


def on_device(state_guess, adjoint_guess, target, initial_state, diffusivity):
    local_steps = state_guess.shape[0]
    section_count = lax.axis_size("tm")
    horizon = local_steps * section_count
    bit_count = horizon.bit_length() - 1
    device = lax.axis_index("tm")
    position = device * local_steps + jnp.arange(local_steps, dtype=jnp.int32)
    kappa_rim = extended(diffusivity, (("space", 0),), 1)
    weights = [0.5 * (diffusivity + beside) for beside in rim_slices(pad_inner(kappa_rim))]
    diagonal = weights[0] + weights[1] + weights[2] + weights[3] + weights[4] + weights[5]
    mode_index = jnp.zeros_like(position)
    for bit_number in range(bit_count):
        picked = jnp.bitwise_and(jnp.right_shift(position, bit_number), 1)
        mode_index = mode_index + jnp.left_shift(picked, bit_count - 1 - bit_number)
    angles = (2.0 * math.pi / horizon * mode_index.astype(jnp.float32)).reshape(-1, 1, 1, 1)
    shift_real = 1.0 - jnp.cos(angles) + step_size * diagonal
    shift_imag = jnp.sin(angles)
    determinant = (
        shift_real * shift_real + shift_imag * shift_imag + step_size * step_size / control_cost
    )
    first_step = jnp.where(device == 0, initial_state, jnp.zeros_like(initial_state))
    source = jnp.concatenate([first_step[None], jnp.zeros_like(state_guess[1:])], 0)
    state_now = state_guess
    adjoint_now = adjoint_guess
    for outer_step in range(OUTER):
        coupled = jnp.stack([state_now, adjoint_now])
        rimmed = extended(coupled, (("tm", 1), ("space", 2)), 1)
        spread_sum = neighbour_sum(rimmed[:, 1:-1], weights)
        before = rimmed[0, :-2, 1:-1]
        later_adjoint = rimmed[1, 2:, 1:-1]
        diffuse_state = diagonal * state_now - spread_sum[0]
        diffuse_adjoint = diagonal * adjoint_now - spread_sum[1]
        res_state = source - (
            state_now - before + step_size * diffuse_state + step_size / control_cost * adjoint_now
        )
        res_adjoint = -step_size * target - (
            adjoint_now - later_adjoint + step_size * diffuse_adjoint - step_size * state_now
        )
        zeros_field = jnp.zeros_like(res_state)
        packed = jnp.stack([res_state, zeros_field, res_adjoint, zeros_field])
        for bit_number in reversed(range(bit_count - 1)):
            packed = butterfly_segment(
                packed, bit_number, position, device, local_steps, horizon, False
            )
        right_side = jnp.stack([packed[:, 0] + packed[:, 1], packed[:, 0] - packed[:, 1]], 1)
        iterate = block_solve(right_side, shift_real, shift_imag, determinant)
        for sweep_index in range(1, SWEEPS):
            sweep_rimmed = extended(iterate, (("space", 2),), 1)
            pushed = right_side + step_size * neighbour_sum(sweep_rimmed, weights)
            iterate = block_solve(pushed, shift_real, shift_imag, determinant)
        packed = jnp.stack(
            [0.5 * (iterate[:, 0] + iterate[:, 1]), 0.5 * (iterate[:, 0] - iterate[:, 1])], 1
        )
        for bit_number in range(bit_count - 1):
            packed = butterfly_segment(
                packed, bit_number, position, device, local_steps, horizon, True
            )
        state_delta = packed[0]
        adjoint_delta = packed[2]
        state_now = state_now + state_delta
        adjoint_now = adjoint_now + adjoint_delta
    return (state_now, adjoint_now)


def solution(mesh):
    in_specs = (
        P("tm", "space", None, None),
        P("tm", "space", None, None),
        P("tm", "space", None, None),
        P("space", None, None),
        P("space", None, None),
    )
    out_specs = (P("tm", "space", None, None), P("tm", "space", None, None))
    return jax.shard_map(
        on_device, mesh=mesh, in_specs=in_specs, out_specs=out_specs, check_vma=False
    )
```

profile of v0, /device:TPU:6, one launch (start us, length us, event | category | flops | bytes accessed | tf_op | source)
XLA Modules:
  0.0 367.4 jit_solution(11780245378815476311)
XLA Ops:
  5.7 8.0 %collective-permute-start = (f32[1,96,128]{2,1,0:T(8,128)S(1)}, f32[1,96,128]{2,1,0:T(8,128)S(1)}, u32[]{:S(2)}, u32[]{:S(2)}) collective-permute-start(f32[1,96,128]{2,1,0:T(8,128)S(1)} %get-tuple-element.150), channel_id=1, source_target_pairs={{1,0},{2,1},{3,2},{4,3},{5,4},{6,5},{7,6},{8,7},{9,8},{10,9},{11,1... | collective-permute-start | bytes 147464 | tf_op jit(solution)/shard_map/ppermute | solution.py:36
  16.9 6.0 %collective-permute-start.4 = (f32[2,4,1,96,128]{4,3,2,1,0:T(8,128)S(1)}, f32[2,4,1,96,128]{4,3,2,1,0:T(8,128)S(1)}, u32[]{:S(2)}, u32[]{:S(2)}) collective-permute-start(f32[2,4,1,96,128]{4,3,2,1,0:T(8,128)S(1)} %get-tuple-element.145), channel_id=1, source_target_pairs={{1,0},{2,1},{3,2},{4,3},{5,4},{6,5},{7,6},{8,7},{9,8},{10,9},{11,1... | collective-permute-start | bytes 1179656 | tf_op jit(solution)/shard_map/ppermute | solution.py:36
  22.9 1.9 collective-permute-start.5
  25.3 6.2 %collective-permute-done.4 = f32[2,4,1,96,128]{4,3,2,1,0:T(8,128)S(1)} collective-permute-done((f32[2,4,1,96,128]{4,3,2,1,0:T(8,128)S(1)}, f32[2,4,1,96,128]{4,3,2,1,0:T(8,128)S(1)}, u32[]{:S(2)}, u32[]{:S(2)}) %collective-permute-start.4) | collective-permute-done | bytes 393248 | tf_op jit(solution)/shard_map/ppermute | solution.py:36
  31.4 6.8 %collective-permute-done.5 = f32[2,4,1,96,128]{4,3,2,1,0:T(8,128)S(1)} collective-permute-done((f32[2,4,1,96,128]{4,3,2,1,0:T(8,128)S(1)}, f32[2,4,1,96,128]{4,3,2,1,0:T(8,128)S(1)}, u32[]{:S(2)}, u32[]{:S(2)}) %collective-permute-start.5) | collective-permute-done | bytes 393248 | tf_op jit(solution)/shard_map/ppermute | solution.py:34
  39.5 4.3 %collective-permute-start.6 = (f32[4,2,2,96,128]{4,3,2,1,0:T(8,128)S(1)}, f32[4,2,2,96,128]{4,3,2,1,0:T(8,128)S(1)}, u32[]{:S(2)}, u32[]{:S(2)}) collective-permute-start(f32[4,2,2,96,128]{4,3,2,1,0:T(8,128)S(1)} %pad_maximum_fusion.5), channel_id=1, source_target_pairs={{0,128},{128,0},{32,160},{160,32},{64,192},{192,64},{96,224},{224,... | collective-permute-start | bytes 2359304 | tf_op jit(solution)/shard_map/ppermute | solution.py:23
  43.8 17.2 %collective-permute-done.6 = f32[4,2,2,96,128]{4,3,2,1,0:T(8,128)S(1)} collective-permute-done((f32[4,2,2,96,128]{4,3,2,1,0:T(8,128)S(1)}, f32[4,2,2,96,128]{4,3,2,1,0:T(8,128)S(1)}, u32[]{:S(2)}, u32[]{:S(2)}) %collective-permute-start.6) | collective-permute-done | bytes 786464 | tf_op jit(solution)/shard_map/ppermute | solution.py:23
  63.0 18.0 %collective-permute-done.7 = f32[4,2,2,96,128]{4,3,2,1,0:T(8,128)} collective-permute-done((f32[4,2,2,96,128]{4,3,2,1,0:T(8,128)}, f32[4,2,2,96,128]{4,3,2,1,0:T(8,128)}, u32[]{:S(2)}, u32[]{:S(2)}) %collective-permute-start.7) | collective-permute-done | bytes 786464 | tf_op jit(solution)/shard_map/ppermute | solution.py:23
  84.4 2.1 collective-permute-done.8
  89.4 6.0 %collective-permute-start.9 = (f32[4,2,1,96,128]{4,3,2,1,0:T(8,128)S(1)}, f32[4,2,1,96,128]{4,3,2,1,0:T(8,128)S(1)}, u32[]{:S(2)}, u32[]{:S(2)}) collective-permute-start(f32[4,2,1,96,128]{4,3,2,1,0:T(8,128)S(1)} %get-tuple-element.141), channel_id=1, source_target_pairs={{1,0},{2,1},{3,2},{4,3},{5,4},{6,5},{7,6},{8,7},{9,8},{10,9},{11,1... | collective-permute-start | bytes 1179656 | tf_op jit(solution)/shard_map/ppermute | solution.py:36
  95.4 7.2 %collective-permute-done.10 = f32[4,2,1,96,128]{4,3,2,1,0:T(8,128)S(1)} collective-permute-done((f32[4,2,1,96,128]{4,3,2,1,0:T(8,128)S(1)}, f32[4,2,1,96,128]{4,3,2,1,0:T(8,128)S(1)}, u32[]{:S(2)}, u32[]{:S(2)}) %collective-permute-start.10) | collective-permute-done | bytes 393248 | tf_op jit(solution)/shard_map/ppermute | solution.py:34
  103.8 2.2 select_maximum_fusion.25
  107.2 6.5 %collective-permute-start.11 = (f32[4,2,1,96,128]{4,3,2,1,0:T(8,128)S(1)}, f32[4,2,1,96,128]{4,3,2,1,0:T(8,128)S(1)}, u32[]{:S(2)}, u32[]{:S(2)}) collective-permute-start(f32[4,2,1,96,128]{4,3,2,1,0:T(8,128)S(1)} %get-tuple-element.139), channel_id=1, source_target_pairs={{1,0},{2,1},{3,2},{4,3},{5,4},{6,5},{7,6},{8,7},{9,8},{10,9},{11,1... | collective-permute-start | bytes 1179656 | tf_op jit(solution)/shard_map/ppermute | solution.py:36
  115.6 5.6 %collective-permute-done.11 = f32[4,2,1,96,128]{4,3,2,1,0:T(8,128)S(1)} collective-permute-done((f32[4,2,1,96,128]{4,3,2,1,0:T(8,128)S(1)}, f32[4,2,1,96,128]{4,3,2,1,0:T(8,128)S(1)}, u32[]{:S(2)}, u32[]{:S(2)}) %collective-permute-start.11) | collective-permute-done | bytes 393248 | tf_op jit(solution)/shard_map/ppermute | solution.py:36
  121.2 6.2 %collective-permute-done.12 = f32[4,2,1,96,128]{4,3,2,1,0:T(8,128)S(1)} collective-permute-done((f32[4,2,1,96,128]{4,3,2,1,0:T(8,128)S(1)}, f32[4,2,1,96,128]{4,3,2,1,0:T(8,128)S(1)}, u32[]{:S(2)}, u32[]{:S(2)}) %collective-permute-start.12) | collective-permute-done | bytes 393248 | tf_op jit(solution)/shard_map/ppermute | solution.py:34
  127.4 2.2 select_maximum_fusion.20
  132.7 4.1 %collective-permute-start.14 = (f32[4,2,1,96,128]{4,3,2,1,0:T(8,128)S(1)}, f32[4,2,1,96,128]{4,3,2,1,0:T(8,128)S(1)}, u32[]{:S(2)}, u32[]{:S(2)}) collective-permute-start(f32[4,2,1,96,128]{4,3,2,1,0:T(8,128)S(1)} %get-tuple-element.136), channel_id=1, source_target_pairs={{0,1},{1,2},{2,3},{3,4},{4,5},{5,6},{6,7},{7,8},{8,9},{9,10},{10,1... | collective-permute-start | bytes 1179656 | tf_op jit(solution)/shard_map/ppermute | solution.py:34
  136.8 4.7 %collective-permute-done.13 = f32[4,2,1,96,128]{4,3,2,1,0:T(8,128)S(1)} collective-permute-done((f32[4,2,1,96,128]{4,3,2,1,0:T(8,128)S(1)}, f32[4,2,1,96,128]{4,3,2,1,0:T(8,128)S(1)}, u32[]{:S(2)}, u32[]{:S(2)}) %collective-permute-start.13) | collective-permute-done | bytes 393248 | tf_op jit(solution)/shard_map/ppermute | solution.py:36
  141.5 4.0 %collective-permute-done.14 = f32[4,2,1,96,128]{4,3,2,1,0:T(8,128)S(1)} collective-permute-done((f32[4,2,1,96,128]{4,3,2,1,0:T(8,128)S(1)}, f32[4,2,1,96,128]{4,3,2,1,0:T(8,128)S(1)}, u32[]{:S(2)}, u32[]{:S(2)}) %collective-permute-start.14) | collective-permute-done | bytes 393248 | tf_op jit(solution)/shard_map/ppermute | solution.py:34
  145.5 2.2 select_maximum_fusion.15
  149.2 2.2 collective-permute-done.15
  152.4 19.2 %collective-permute-done.16 = f32[4,2,2,96,128]{4,3,2,1,0:T(8,128)S(1)} collective-permute-done((f32[4,2,2,96,128]{4,3,2,1,0:T(8,128)S(1)}, f32[4,2,2,96,128]{4,3,2,1,0:T(8,128)S(1)}, u32[]{:S(2)}, u32[]{:S(2)}) %collective-permute-start.16) | collective-permute-done | bytes 786464 | tf_op jit(solution)/shard_map/ppermute | solution.py:23
  172.6 20.2 %collective-permute-done.17 = f32[4,2,2,96,128]{4,3,2,1,0:T(8,128)S(1)} collective-permute-done((f32[4,2,2,96,128]{4,3,2,1,0:T(8,128)S(1)}, f32[4,2,2,96,128]{4,3,2,1,0:T(8,128)S(1)}, u32[]{:S(2)}, u32[]{:S(2)}) %collective-permute-start.17) | collective-permute-done | bytes 786464 | tf_op jit(solution)/shard_map/ppermute | solution.py:23
  196.1 2.5 collective-permute-done.19
  200.7 4.1 %collective-permute-start.21 = (f32[2,4,1,96,128]{4,3,2,1,0:T(8,128)S(1)}, f32[2,4,1,96,128]{4,3,2,1,0:T(8,128)S(1)}, u32[]{:S(2)}, u32[]{:S(2)}) collective-permute-start(f32[2,4,1,96,128]{4,3,2,1,0:T(8,128)S(1)} %get-tuple-element.130), channel_id=1, source_target_pairs={{0,1},{1,2},{2,3},{3,4},{4,5},{5,6},{6,7},{7,8},{8,9},{9,10},{10,1... | collective-permute-start | bytes 1179656 | tf_op jit(solution)/shard_map/ppermute | solution.py:34
  204.8 4.6 %collective-permute-done.20 = f32[2,4,1,96,128]{4,3,2,1,0:T(8,128)S(1)} collective-permute-done((f32[2,4,1,96,128]{4,3,2,1,0:T(8,128)S(1)}, f32[2,4,1,96,128]{4,3,2,1,0:T(8,128)S(1)}, u32[]{:S(2)}, u32[]{:S(2)}) %collective-permute-start.20) | collective-permute-done | bytes 393248 | tf_op jit(solution)/shard_map/ppermute | solution.py:36
  209.4 4.2 %collective-permute-done.21 = f32[2,4,1,96,128]{4,3,2,1,0:T(8,128)S(1)} collective-permute-done((f32[2,4,1,96,128]{4,3,2,1,0:T(8,128)S(1)}, f32[2,4,1,96,128]{4,3,2,1,0:T(8,128)S(1)}, u32[]{:S(2)}, u32[]{:S(2)}) %collective-permute-start.21) | collective-permute-done | bytes 393248 | tf_op jit(solution)/shard_map/ppermute | solution.py:34
  214.8 7.0 %collective-permute-start.22 = (f32[4,2,2,96,128]{4,3,2,1,0:T(8,128)S(1)}, f32[4,2,2,96,128]{4,3,2,1,0:T(8,128)S(1)}, u32[]{:S(2)}, u32[]{:S(2)}) collective-permute-start(f32[4,2,2,96,128]{4,3,2,1,0:T(8,128)S(1)} %pad_maximum_fusion.4), channel_id=1, source_target_pairs={{0,128},{128,0},{32,160},{160,32},{64,192},{192,64},{96,224},{224,... | collective-permute-start | bytes 2359304 | tf_op jit(solution)/shard_map/ppermute | solution.py:23
  221.8 17.8 %collective-permute-done.22 = f32[4,2,2,96,128]{4,3,2,1,0:T(8,128)S(1)} collective-permute-done((f32[4,2,2,96,128]{4,3,2,1,0:T(8,128)S(1)}, f32[4,2,2,96,128]{4,3,2,1,0:T(8,128)S(1)}, u32[]{:S(2)}, u32[]{:S(2)}) %collective-permute-start.22) | collective-permute-done | bytes 786464 | tf_op jit(solution)/shard_map/ppermute | solution.py:23
  240.1 2.1 collective-permute-start.23
  242.2 17.0 %collective-permute-done.23 = f32[4,2,2,96,128]{4,3,2,1,0:T(8,128)S(1)} collective-permute-done((f32[4,2,2,96,128]{4,3,2,1,0:T(8,128)S(1)}, f32[4,2,2,96,128]{4,3,2,1,0:T(8,128)S(1)}, u32[]{:S(2)}, u32[]{:S(2)}) %collective-permute-start.23) | collective-permute-done | bytes 786464 | tf_op jit(solution)/shard_map/ppermute | solution.py:23
  260.1 2.3 collective-permute-done.24
  265.2 4.1 %collective-permute-start.26 = (f32[4,2,1,96,128]{4,3,2,1,0:T(8,128)S(1)}, f32[4,2,1,96,128]{4,3,2,1,0:T(8,128)S(1)}, u32[]{:S(2)}, u32[]{:S(2)}) collective-permute-start(f32[4,2,1,96,128]{4,3,2,1,0:T(8,128)S(1)} %get-tuple-element.126), channel_id=1, source_target_pairs={{0,1},{1,2},{2,3},{3,4},{4,5},{5,6},{6,7},{7,8},{8,9},{9,10},{10,1... | collective-permute-start | bytes 1179656 | tf_op jit(solution)/shard_map/ppermute | solution.py:34
  269.3 7.0 %collective-permute-done.25 = f32[4,2,1,96,128]{4,3,2,1,0:T(8,128)S(1)} collective-permute-done((f32[4,2,1,96,128]{4,3,2,1,0:T(8,128)S(1)}, f32[4,2,1,96,128]{4,3,2,1,0:T(8,128)S(1)}, u32[]{:S(2)}, u32[]{:S(2)}) %collective-permute-start.25) | collective-permute-done | bytes 393248 | tf_op jit(solution)/shard_map/ppermute | solution.py:36
  276.3 4.0 %collective-permute-done.26 = f32[4,2,1,96,128]{4,3,2,1,0:T(8,128)S(1)} collective-permute-done((f32[4,2,1,96,128]{4,3,2,1,0:T(8,128)S(1)}, f32[4,2,1,96,128]{4,3,2,1,0:T(8,128)S(1)}, u32[]{:S(2)}, u32[]{:S(2)}) %collective-permute-start.26) | collective-permute-done | bytes 393248 | tf_op jit(solution)/shard_map/ppermute | solution.py:34
  280.3 2.2 select_maximum_fusion.10
  285.7 3.9 %collective-permute-start.28 = (f32[4,2,1,96,128]{4,3,2,1,0:T(8,128)S(1)}, f32[4,2,1,96,128]{4,3,2,1,0:T(8,128)S(1)}, u32[]{:S(2)}, u32[]{:S(2)}) collective-permute-start(f32[4,2,1,96,128]{4,3,2,1,0:T(8,128)S(1)} %get-tuple-element.124), channel_id=1, source_target_pairs={{0,1},{1,2},{2,3},{3,4},{4,5},{5,6},{6,7},{7,8},{8,9},{9,10},{10,1... | collective-permute-start | bytes 1179656 | tf_op jit(solution)/shard_map/ppermute | solution.py:34
  289.6 6.4 %collective-permute-done.27 = f32[4,2,1,96,128]{4,3,2,1,0:T(8,128)S(1)} collective-permute-done((f32[4,2,1,96,128]{4,3,2,1,0:T(8,128)S(1)}, f32[4,2,1,96,128]{4,3,2,1,0:T(8,128)S(1)}, u32[]{:S(2)}, u32[]{:S(2)}) %collective-permute-start.27) | collective-permute-done | bytes 393248 | tf_op jit(solution)/shard_map/ppermute | solution.py:36
  296.0 4.0 %collective-permute-done.28 = f32[4,2,1,96,128]{4,3,2,1,0:T(8,128)S(1)} collective-permute-done((f32[4,2,1,96,128]{4,3,2,1,0:T(8,128)S(1)}, f32[4,2,1,96,128]{4,3,2,1,0:T(8,128)S(1)}, u32[]{:S(2)}, u32[]{:S(2)}) %collective-permute-start.28) | collective-permute-done | bytes 393248 | tf_op jit(solution)/shard_map/ppermute | solution.py:34
  300.0 2.2 select_maximum_fusion.5
  305.3 3.9 %collective-permute-start.30 = (f32[4,2,1,96,128]{4,3,2,1,0:T(8,128)S(1)}, f32[4,2,1,96,128]{4,3,2,1,0:T(8,128)S(1)}, u32[]{:S(2)}, u32[]{:S(2)}) collective-permute-start(f32[4,2,1,96,128]{4,3,2,1,0:T(8,128)S(1)} %get-tuple-element.122), channel_id=1, source_target_pairs={{0,1},{1,2},{2,3},{3,4},{4,5},{5,6},{6,7},{7,8},{8,9},{9,10},{10,1... | collective-permute-start | bytes 1179656 | tf_op jit(solution)/shard_map/ppermute | solution.py:34
  309.3 5.4 %collective-permute-done.29 = f32[4,2,1,96,128]{4,3,2,1,0:T(8,128)S(1)} collective-permute-done((f32[4,2,1,96,128]{4,3,2,1,0:T(8,128)S(1)}, f32[4,2,1,96,128]{4,3,2,1,0:T(8,128)S(1)}, u32[]{:S(2)}, u32[]{:S(2)}) %collective-permute-start.29) | collective-permute-done | bytes 393248 | tf_op jit(solution)/shard_map/ppermute | solution.py:36
  314.7 4.0 %collective-permute-done.30 = f32[4,2,1,96,128]{4,3,2,1,0:T(8,128)S(1)} collective-permute-done((f32[4,2,1,96,128]{4,3,2,1,0:T(8,128)S(1)}, f32[4,2,1,96,128]{4,3,2,1,0:T(8,128)S(1)}, u32[]{:S(2)}, u32[]{:S(2)}) %collective-permute-start.30) | collective-permute-done | bytes 393248 | tf_op jit(solution)/shard_map/ppermute | solution.py:34
  318.7 2.2 select_maximum_fusion
  322.3 2.3 collective-permute-done.31
  326.1 18.7 %collective-permute-done.32 = f32[4,2,2,96,128]{4,3,2,1,0:T(8,128)S(1)} collective-permute-done((f32[4,2,2,96,128]{4,3,2,1,0:T(8,128)S(1)}, f32[4,2,2,96,128]{4,3,2,1,0:T(8,128)S(1)}, u32[]{:S(2)}, u32[]{:S(2)}) %collective-permute-start.32) | collective-permute-done | bytes 786464 | tf_op jit(solution)/shard_map/ppermute | solution.py:23
  345.7 3.0 collective-permute-start.33
  348.7 17.3 %collective-permute-done.33 = f32[4,2,2,96,128]{4,3,2,1,0:T(8,128)S(1)} collective-permute-done((f32[4,2,2,96,128]{4,3,2,1,0:T(8,128)S(1)}, f32[4,2,2,96,128]{4,3,2,1,0:T(8,128)S(1)}, u32[]{:S(2)}, u32[]{:S(2)}) %collective-permute-start.33) | collective-permute-done | bytes 786464 | tf_op jit(solution)/shard_map/ppermute | solution.py:23
  (141 shorter events, 50.1 us)
Async XLA Ops:
  0.6 37.6 %copy-start.1 = (f32[2,2,96,128]{3,2,1,0:T(8,128)S(1)}, f32[2,2,96,128]{3,2,1,0:T(8,128)}, u32[]{:S(2)}) copy-start(f32[2,2,96,128]{3,2,1,0:T(8,128)} %param.5) | copy-start | bytes 589828
  0.6 37.6 %copy-start = (f32[2,2,96,128]{3,2,1,0:T(8,128)S(1)}, f32[2,2,96,128]{3,2,1,0:T(8,128)}, u32[]{:S(2)}) copy-start(f32[2,2,96,128]{3,2,1,0:T(8,128)} %param.6) | copy-start | bytes 589828
  0.7 24.2 %copy-start.7 = (f32[2,96,128]{2,1,0:T(8,128)S(1)}, f32[2,96,128]{2,1,0:T(8,128)}, u32[]{:S(2)}) copy-start(f32[2,96,128]{2,1,0:T(8,128)} %param.9) | copy-start | bytes 294916
  0.7 24.2 %copy-start.10 = (f32[2,96,128]{2,1,0:T(8,128)S(1)}, f32[2,96,128]{2,1,0:T(8,128)}, u32[]{:S(2)}) copy-start(f32[2,96,128]{2,1,0:T(8,128)} %param.8) | copy-start | bytes 294916
  1.8 13.9 %collective-permute-start.2 = (f32[2,1,2,96,128]{4,3,2,1,0:T(8,128)S(1)}, f32[2,1,2,96,128]{4,3,2,1,0:T(8,128)S(1)}, u32[]{:S(2)}, u32[]{:S(2)}) collective-permute-start(f32[2,1,2,96,128]{4,3,2,1,0:T(8,128)S(1)} %get-tuple-element.148), channel_id=1, source_target_pairs={{0,32},{32,64},{64,96},{96,128},{128,160},{160,192},{192,224},{1,3... | collective-permute-start | bytes 589832 | tf_op jit(solution)/shard_map/ppermute | solution.py:34
  3.6 12.1 %collective-permute-start.3 = (f32[2,1,2,96,128]{4,3,2,1,0:T(8,128)S(1)}, f32[2,1,2,96,128]{4,3,2,1,0:T(8,128)S(1)}, u32[]{:S(2)}, u32[]{:S(2)}) collective-permute-start(f32[2,1,2,96,128]{4,3,2,1,0:T(8,128)S(1)} %get-tuple-element.149), channel_id=1, source_target_pairs={{32,0},{64,32},{96,64},{128,96},{160,128},{192,160},{224,192},{33,... | collective-permute-start | bytes 589832 | tf_op jit(solution)/shard_map/ppermute | solution.py:36
  5.7 19.1 %collective-permute-start = (f32[1,96,128]{2,1,0:T(8,128)S(1)}, f32[1,96,128]{2,1,0:T(8,128)S(1)}, u32[]{:S(2)}, u32[]{:S(2)}) collective-permute-start(f32[1,96,128]{2,1,0:T(8,128)S(1)} %get-tuple-element.150), channel_id=1, source_target_pairs={{1,0},{2,1},{3,2},{4,3},{5,4},{6,5},{7,6},{8,7},{9,8},{10,9},{11,1... | collective-permute-start | bytes 147464 | tf_op jit(solution)/shard_map/ppermute | solution.py:36
  13.8 11.1 %collective-permute-start.1 = (f32[1,96,128]{2,1,0:T(8,128)S(1)}, f32[1,96,128]{2,1,0:T(8,128)S(1)}, u32[]{:S(2)}, u32[]{:S(2)}) collective-permute-start(f32[1,96,128]{2,1,0:T(8,128)S(1)} %get-tuple-element.151), channel_id=1, source_target_pairs={{0,1},{1,2},{2,3},{3,4},{4,5},{5,6},{6,7},{7,8},{8,9},{9,10},{10,1... | collective-permute-start | bytes 147464 | tf_op jit(solution)/shard_map/ppermute | solution.py:34
  16.9 14.6 %collective-permute-start.4 = (f32[2,4,1,96,128]{4,3,2,1,0:T(8,128)S(1)}, f32[2,4,1,96,128]{4,3,2,1,0:T(8,128)S(1)}, u32[]{:S(2)}, u32[]{:S(2)}) collective-permute-start(f32[2,4,1,96,128]{4,3,2,1,0:T(8,128)S(1)} %get-tuple-element.145), channel_id=1, source_target_pairs={{1,0},{2,1},{3,2},{4,3},{5,4},{6,5},{7,6},{8,7},{9,8},{10,9},{11,1... | collective-permute-start | bytes 1179656 | tf_op jit(solution)/shard_map/ppermute | solution.py:36
  22.9 15.4 %collective-permute-start.5 = (f32[2,4,1,96,128]{4,3,2,1,0:T(8,128)S(1)}, f32[2,4,1,96,128]{4,3,2,1,0:T(8,128)S(1)}, u32[]{:S(2)}, u32[]{:S(2)}) collective-permute-start(f32[2,4,1,96,128]{4,3,2,1,0:T(8,128)S(1)} %get-tuple-element.144), channel_id=1, source_target_pairs={{0,1},{1,2},{2,3},{3,4},{4,5},{5,6},{6,7},{7,8},{8,9},{9,10},{10,1... | collective-permute-start | bytes 1179656 | tf_op jit(solution)/shard_map/ppermute | solution.py:34
  25.2 14.0 %copy-start.5 = (f32[2,96,128]{2,1,0:T(8,128)}, f32[2,96,128]{2,1,0:T(8,128)S(1)}, u32[]{:S(2)}) copy-start(f32[2,96,128]{2,1,0:T(8,128)S(1)} %get-tuple-element.3) | copy-start | bytes 294916
  25.2 14.0 %copy-start.8 = (f32[2,2,96,128]{3,2,1,0:T(8,128)S(1)}, f32[2,2,96,128]{3,2,1,0:T(8,128)}, u32[]{:S(2)}) copy-start(f32[2,2,96,128]{3,2,1,0:T(8,128)} %param.7) | copy-start | bytes 589828
  39.5 21.5 %collective-permute-start.6 = (f32[4,2,2,96,128]{4,3,2,1,0:T(8,128)S(1)}, f32[4,2,2,96,128]{4,3,2,1,0:T(8,128)S(1)}, u32[]{:S(2)}, u32[]{:S(2)}) collective-permute-start(f32[4,2,2,96,128]{4,3,2,1,0:T(8,128)S(1)} %pad_maximum_fusion.5), channel_id=1, source_target_pairs={{0,128},{128,0},{32,160},{160,32},{64,192},{192,64},{96,224},{224,... | collective-permute-start | bytes 2359304 | tf_op jit(solution)/shard_map/ppermute | solution.py:23
  61.2 21.3 %copy-start.2 = (f32[1,2,2,96,128]{4,3,2,1,0:T(8,128)}, f32[1,2,2,96,128]{4,3,2,1,0:T(8,128)S(1)}, u32[]{:S(2)}) copy-start(f32[1,2,2,96,128]{4,3,2,1,0:T(8,128)S(1)} %get-tuple-element.115) | copy-start | bytes 589828
  61.2 21.3 %copy-start.3 = (f32[1,2,2,96,128]{4,3,2,1,0:T(8,128)}, f32[1,2,2,96,128]{4,3,2,1,0:T(8,128)S(1)}, u32[]{:S(2)}) copy-start(f32[1,2,2,96,128]{4,3,2,1,0:T(8,128)S(1)} %get-tuple-element.116) | copy-start | bytes 589828
  61.3 21.2 %copy-start.4 = (f32[1,2,2,96,128]{4,3,2,1,0:T(8,128)}, f32[1,2,2,96,128]{4,3,2,1,0:T(8,128)S(1)}, u32[]{:S(2)}) copy-start(f32[1,2,2,96,128]{4,3,2,1,0:T(8,128)S(1)} %get-tuple-element.117) | copy-start | bytes 589828
  62.3 18.7 %collective-permute-start.7 = (f32[4,2,2,96,128]{4,3,2,1,0:T(8,128)}, f32[4,2,2,96,128]{4,3,2,1,0:T(8,128)}, u32[]{:S(2)}, u32[]{:S(2)}) collective-permute-start(f32[4,2,2,96,128]{4,3,2,1,0:T(8,128)} %maximum_select_fusion), channel_id=1, source_target_pairs={{0,64},{64,0},{32,96},{96,32},{128,192},{192,128},{160,224},{224,1... | collective-permute-start | bytes 2359304 | tf_op jit(solution)/shard_map/ppermute | solution.py:23
  84.2 2.4 collective-permute-start.8
  87.4 15.2 %collective-permute-start.10 = (f32[4,2,1,96,128]{4,3,2,1,0:T(8,128)S(1)}, f32[4,2,1,96,128]{4,3,2,1,0:T(8,128)S(1)}, u32[]{:S(2)}, u32[]{:S(2)}) collective-permute-start(f32[4,2,1,96,128]{4,3,2,1,0:T(8,128)S(1)} %get-tuple-element.140), channel_id=1, source_target_pairs={{0,1},{1,2},{2,3},{3,4},{4,5},{5,6},{6,7},{7,8},{8,9},{9,10},{10,1... | collective-permute-start | bytes 1179656 | tf_op jit(solution)/shard_map/ppermute | solution.py:34
  89.4 14.4 %collective-permute-start.9 = (f32[4,2,1,96,128]{4,3,2,1,0:T(8,128)S(1)}, f32[4,2,1,96,128]{4,3,2,1,0:T(8,128)S(1)}, u32[]{:S(2)}, u32[]{:S(2)}) collective-permute-start(f32[4,2,1,96,128]{4,3,2,1,0:T(8,128)S(1)} %get-tuple-element.141), channel_id=1, source_target_pairs={{1,0},{2,1},{3,2},{4,3},{5,4},{6,5},{7,6},{8,7},{9,8},{10,9},{11,1... | collective-permute-start | bytes 1179656 | tf_op jit(solution)/shard_map/ppermute | solution.py:36
  107.2 14.0 %collective-permute-start.11 = (f32[4,2,1,96,128]{4,3,2,1,0:T(8,128)S(1)}, f32[4,2,1,96,128]{4,3,2,1,0:T(8,128)S(1)}, u32[]{:S(2)}, u32[]{:S(2)}) collective-permute-start(f32[4,2,1,96,128]{4,3,2,1,0:T(8,128)S(1)} %get-tuple-element.139), channel_id=1, source_target_pairs={{1,0},{2,1},{3,2},{4,3},{5,4},{6,5},{7,6},{8,7},{9,8},{10,9},{11,1... | collective-permute-start | bytes 1179656 | tf_op jit(solution)/shard_map/ppermute | solution.py:36
  113.7 13.7 %collective-permute-start.12 = (f32[4,2,1,96,128]{4,3,2,1,0:T(8,128)S(1)}, f32[4,2,1,96,128]{4,3,2,1,0:T(8,128)S(1)}, u32[]{:S(2)}, u32[]{:S(2)}) collective-permute-start(f32[4,2,1,96,128]{4,3,2,1,0:T(8,128)S(1)} %get-tuple-element.138), channel_id=1, source_target_pairs={{0,1},{1,2},{2,3},{3,4},{4,5},{5,6},{6,7},{7,8},{8,9},{9,10},{10,1... | collective-permute-start | bytes 1179656 | tf_op jit(solution)/shard_map/ppermute | solution.py:34
  130.8 10.7 %collective-permute-start.13 = (f32[4,2,1,96,128]{4,3,2,1,0:T(8,128)S(1)}, f32[4,2,1,96,128]{4,3,2,1,0:T(8,128)S(1)}, u32[]{:S(2)}, u32[]{:S(2)}) collective-permute-start(f32[4,2,1,96,128]{4,3,2,1,0:T(8,128)S(1)} %get-tuple-element.137), channel_id=1, source_target_pairs={{1,0},{2,1},{3,2},{4,3},{5,4},{6,5},{7,6},{8,7},{9,8},{10,9},{11,1... | collective-permute-start | bytes 1179656 | tf_op jit(solution)/shard_map/ppermute | solution.py:36
  132.7 12.8 %collective-permute-start.14 = (f32[4,2,1,96,128]{4,3,2,1,0:T(8,128)S(1)}, f32[4,2,1,96,128]{4,3,2,1,0:T(8,128)S(1)}, u32[]{:S(2)}, u32[]{:S(2)}) collective-permute-start(f32[4,2,1,96,128]{4,3,2,1,0:T(8,128)S(1)} %get-tuple-element.136), channel_id=1, source_target_pairs={{0,1},{1,2},{2,3},{3,4},{4,5},{5,6},{6,7},{7,8},{8,9},{9,10},{10,1... | collective-permute-start | bytes 1179656 | tf_op jit(solution)/shard_map/ppermute | solution.py:34
  149.0 2.4 collective-permute-start.15
  152.0 19.7 %collective-permute-start.16 = (f32[4,2,2,96,128]{4,3,2,1,0:T(8,128)S(1)}, f32[4,2,2,96,128]{4,3,2,1,0:T(8,128)S(1)}, u32[]{:S(2)}, u32[]{:S(2)}) collective-permute-start(f32[4,2,2,96,128]{4,3,2,1,0:T(8,128)S(1)} %fusion.63), channel_id=1, source_target_pairs={{0,64},{64,0},{32,96},{96,32},{128,192},{192,128},{160,224},{224,1... | collective-permute-start | bytes 2359304 | tf_op jit(solution)/shard_map/ppermute | solution.py:23
  172.5 20.3 %collective-permute-start.17 = (f32[4,2,2,96,128]{4,3,2,1,0:T(8,128)S(1)}, f32[4,2,2,96,128]{4,3,2,1,0:T(8,128)S(1)}, u32[]{:S(2)}, u32[]{:S(2)}) collective-permute-start(f32[4,2,2,96,128]{4,3,2,1,0:T(8,128)S(1)} %fusion.66), channel_id=1, source_target_pairs={{0,128},{128,0},{32,160},{160,32},{64,192},{192,64},{96,224},{224,... | collective-permute-start | bytes 2359304 | tf_op jit(solution)/shard_map/ppermute | solution.py:23
  193.5 2.6 collective-permute-start.18
  194.8 3.8 %collective-permute-start.19 = (f32[2,1,2,96,128]{4,3,2,1,0:T(8,128)S(1)}, f32[2,1,2,96,128]{4,3,2,1,0:T(8,128)S(1)}, u32[]{:S(2)}, u32[]{:S(2)}) collective-permute-start(f32[2,1,2,96,128]{4,3,2,1,0:T(8,128)S(1)} %get-tuple-element.147), channel_id=1, source_target_pairs={{32,0},{64,32},{96,64},{128,96},{160,128},{192,160},{224,192},{33,... | collective-permute-start | bytes 589832 | tf_op jit(solution)/shard_map/ppermute | solution.py:36
  198.8 10.6 %collective-permute-start.20 = (f32[2,4,1,96,128]{4,3,2,1,0:T(8,128)S(1)}, f32[2,4,1,96,128]{4,3,2,1,0:T(8,128)S(1)}, u32[]{:S(2)}, u32[]{:S(2)}) collective-permute-start(f32[2,4,1,96,128]{4,3,2,1,0:T(8,128)S(1)} %get-tuple-element.131), channel_id=1, source_target_pairs={{1,0},{2,1},{3,2},{4,3},{5,4},{6,5},{7,6},{8,7},{9,8},{10,9},{11,1... | collective-permute-start | bytes 1179656 | tf_op jit(solution)/shard_map/ppermute | solution.py:36
  200.7 13.9 %copy-start.6 = (f32[2,96,128]{2,1,0:T(8,128)S(1)}, f32[2,96,128]{2,1,0:T(8,128)}, u32[]{:S(2)}) copy-start(f32[2,96,128]{2,1,0:T(8,128)} %copy-done.5) | copy-start | bytes 294916
  200.7 13.9 %copy-start.9 = (f32[2,2,96,128]{3,2,1,0:T(8,128)S(1)}, f32[2,2,96,128]{3,2,1,0:T(8,128)}, u32[]{:S(2)}) copy-start(f32[2,2,96,128]{3,2,1,0:T(8,128)} %param.7) | copy-start | bytes 589828
  200.7 12.9 %collective-permute-start.21 = (f32[2,4,1,96,128]{4,3,2,1,0:T(8,128)S(1)}, f32[2,4,1,96,128]{4,3,2,1,0:T(8,128)S(1)}, u32[]{:S(2)}, u32[]{:S(2)}) collective-permute-start(f32[2,4,1,96,128]{4,3,2,1,0:T(8,128)S(1)} %get-tuple-element.130), channel_id=1, source_target_pairs={{0,1},{1,2},{2,3},{3,4},{4,5},{5,6},{6,7},{7,8},{8,9},{9,10},{10,1... | collective-permute-start | bytes 1179656 | tf_op jit(solution)/shard_map/ppermute | solution.py:34
  214.8 24.8 %collective-permute-start.22 = (f32[4,2,2,96,128]{4,3,2,1,0:T(8,128)S(1)}, f32[4,2,2,96,128]{4,3,2,1,0:T(8,128)S(1)}, u32[]{:S(2)}, u32[]{:S(2)}) collective-permute-start(f32[4,2,2,96,128]{4,3,2,1,0:T(8,128)S(1)} %pad_maximum_fusion.4), channel_id=1, source_target_pairs={{0,128},{128,0},{32,160},{160,32},{64,192},{192,64},{96,224},{224,... | collective-permute-start | bytes 2359304 | tf_op jit(solution)/shard_map/ppermute | solution.py:23
  240.1 19.1 %collective-permute-start.23 = (f32[4,2,2,96,128]{4,3,2,1,0:T(8,128)S(1)}, f32[4,2,2,96,128]{4,3,2,1,0:T(8,128)S(1)}, u32[]{:S(2)}, u32[]{:S(2)}) collective-permute-start(f32[4,2,2,96,128]{4,3,2,1,0:T(8,128)S(1)} %maximum_select_fusion.3), channel_id=1, source_target_pairs={{0,64},{64,0},{32,96},{96,32},{128,192},{192,128},{160,224},{224,1... | collective-permute-start | bytes 2359304 | tf_op jit(solution)/shard_map/ppermute | solution.py:23
  260.0 2.4 collective-permute-start.24
  263.2 13.1 %collective-permute-start.25 = (f32[4,2,1,96,128]{4,3,2,1,0:T(8,128)S(1)}, f32[4,2,1,96,128]{4,3,2,1,0:T(8,128)S(1)}, u32[]{:S(2)}, u32[]{:S(2)}) collective-permute-start(f32[4,2,1,96,128]{4,3,2,1,0:T(8,128)S(1)} %get-tuple-element.127), channel_id=1, source_target_pairs={{1,0},{2,1},{3,2},{4,3},{5,4},{6,5},{7,6},{8,7},{9,8},{10,9},{11,1... | collective-permute-start | bytes 1179656 | tf_op jit(solution)/shard_map/ppermute | solution.py:36
  265.2 15.2 %collective-permute-start.26 = (f32[4,2,1,96,128]{4,3,2,1,0:T(8,128)S(1)}, f32[4,2,1,96,128]{4,3,2,1,0:T(8,128)S(1)}, u32[]{:S(2)}, u32[]{:S(2)}) collective-permute-start(f32[4,2,1,96,128]{4,3,2,1,0:T(8,128)S(1)} %get-tuple-element.126), channel_id=1, source_target_pairs={{0,1},{1,2},{2,3},{3,4},{4,5},{5,6},{6,7},{7,8},{8,9},{9,10},{10,1... | collective-permute-start | bytes 1179656 | tf_op jit(solution)/shard_map/ppermute | solution.py:34
  283.7 12.2 %collective-permute-start.27 = (f32[4,2,1,96,128]{4,3,2,1,0:T(8,128)S(1)}, f32[4,2,1,96,128]{4,3,2,1,0:T(8,128)S(1)}, u32[]{:S(2)}, u32[]{:S(2)}) collective-permute-start(f32[4,2,1,96,128]{4,3,2,1,0:T(8,128)S(1)} %get-tuple-element.125), channel_id=1, source_target_pairs={{1,0},{2,1},{3,2},{4,3},{5,4},{6,5},{7,6},{8,7},{9,8},{10,9},{11,1... | collective-permute-start | bytes 1179656 | tf_op jit(solution)/shard_map/ppermute | solution.py:36
  285.7 14.3 %collective-permute-start.28 = (f32[4,2,1,96,128]{4,3,2,1,0:T(8,128)S(1)}, f32[4,2,1,96,128]{4,3,2,1,0:T(8,128)S(1)}, u32[]{:S(2)}, u32[]{:S(2)}) collective-permute-start(f32[4,2,1,96,128]{4,3,2,1,0:T(8,128)S(1)} %get-tuple-element.124), channel_id=1, source_target_pairs={{0,1},{1,2},{2,3},{3,4},{4,5},{5,6},{6,7},{7,8},{8,9},{9,10},{10,1... | collective-permute-start | bytes 1179656 | tf_op jit(solution)/shard_map/ppermute | solution.py:34
  303.4 11.3 %collective-permute-start.29 = (f32[4,2,1,96,128]{4,3,2,1,0:T(8,128)S(1)}, f32[4,2,1,96,128]{4,3,2,1,0:T(8,128)S(1)}, u32[]{:S(2)}, u32[]{:S(2)}) collective-permute-start(f32[4,2,1,96,128]{4,3,2,1,0:T(8,128)S(1)} %get-tuple-element.123), channel_id=1, source_target_pairs={{1,0},{2,1},{3,2},{4,3},{5,4},{6,5},{7,6},{8,7},{9,8},{10,9},{11,1... | collective-permute-start | bytes 1179656 | tf_op jit(solution)/shard_map/ppermute | solution.py:36
  305.3 13.4 %collective-permute-start.30 = (f32[4,2,1,96,128]{4,3,2,1,0:T(8,128)S(1)}, f32[4,2,1,96,128]{4,3,2,1,0:T(8,128)S(1)}, u32[]{:S(2)}, u32[]{:S(2)}) collective-permute-start(f32[4,2,1,96,128]{4,3,2,1,0:T(8,128)S(1)} %get-tuple-element.122), channel_id=1, source_target_pairs={{0,1},{1,2},{2,3},{3,4},{4,5},{5,6},{6,7},{7,8},{8,9},{9,10},{10,1... | collective-permute-start | bytes 1179656 | tf_op jit(solution)/shard_map/ppermute | solution.py:34
  322.2 2.4 collective-permute-start.31
  325.2 19.7 %collective-permute-start.32 = (f32[4,2,2,96,128]{4,3,2,1,0:T(8,128)S(1)}, f32[4,2,2,96,128]{4,3,2,1,0:T(8,128)S(1)}, u32[]{:S(2)}, u32[]{:S(2)}) collective-permute-start(f32[4,2,2,96,128]{4,3,2,1,0:T(8,128)S(1)} %fusion.72), channel_id=1, source_target_pairs={{0,64},{64,0},{32,96},{96,32},{128,192},{192,128},{160,224},{224,1... | collective-permute-start | bytes 2359304 | tf_op jit(solution)/shard_map/ppermute | solution.py:23
  345.7 20.3 %collective-permute-start.33 = (f32[4,2,2,96,128]{4,3,2,1,0:T(8,128)S(1)}, f32[4,2,2,96,128]{4,3,2,1,0:T(8,128)S(1)}, u32[]{:S(2)}, u32[]{:S(2)}) collective-permute-start(f32[4,2,2,96,128]{4,3,2,1,0:T(8,128)S(1)} %fusion.75), channel_id=1, source_target_pairs={{0,128},{128,0},{32,160},{160,32},{64,192},{192,64},{96,224},{224,... | collective-permute-start | bytes 2359304 | tf_op jit(solution)/shard_map/ppermute | solution.py:23
where the time goes:
time: 368 us; the launch traced here: 367 us
  waiting for transfers between devices  238 us (65%)
  starting transfers between devices  88.5 us (24%)
  other arithmetic  37.5 us (10%)
    ppermute x12, waiting for transfers between devices, swapped(): return lax.ppermute(block, axis, route)  154 us
    ppermute x11, waiting for transfers between devices, extended(): lax.ppermute(head, axis, [((i + 1) % count, i) for i in range(ends)])  43.5 us
    ppermute x11, waiting for transfers between devices, extended(): lax.ppermute(tail, axis, [(i, (i + 1) % count) for i in range(ends)])  40.6 us
    ppermute x11, starting transfers between devices, extended(): lax.ppermute(head, axis, [((i + 1) % count, i) for i in range(ends)])  38.8 us
    ppermute x11, starting transfers between devices, extended(): lax.ppermute(tail, axis, [(i, (i + 1) % count) for i in range(ends)])  30.9 us
    ppermute x12, starting transfers between devices, swapped(): return lax.ppermute(block, axis, route)  18.8 us
    concatenate x11, other arithmetic, extended(): jnp.concatenate([lax.ppermute(tail, axis, [(i, (i + 1) % count) for i in...  15.7 us
  transfers between devices with their start and end apart: 34, of which 29 were waited for; matrix products, arithmetic and copies ran while one was open for 1% of the time, Pallas kernels for 0%

commit v1 on v0

v1 whole, which is shorter than its diff:
```python
import math

import jax
import jax.numpy as jnp
import numpy as np
from jax import lax
from jax.experimental import pallas as pl
from jax.experimental.pallas import tpu as pltpu
from jax.sharding import PartitionSpec as P

TAU = 0.25
COUPLING = 5.0
DET_SHIFT = 1.25
OUTER = 2

OWN = 12
HALO = 4
WIN = OWN + 2 * HALO


def transform_matrices():
    modes = np.arange(8)[:, None]
    steps = np.concatenate([np.arange(0, 16, 2), np.arange(1, 16, 2)])[None, :]
    angle = 2.0 * np.pi * ((modes * steps) % 16) / 16.0
    real, imag = np.cos(angle), -np.sin(angle)
    imag[0] = np.where(steps[0] % 2 == 0, 1.0, -1.0)
    forward = np.concatenate([real, imag], 0)
    back = forward.T.copy() / 8.0
    back[:, 0] /= 2.0
    back[:, 8] /= 2.0
    eye = np.eye(8)
    return np.kron(eye, forward).astype(np.float32), np.kron(eye, back).astype(np.float32)


def mode_constants():
    theta = 2.0 * np.pi * np.arange(8) / 16.0
    shift_a = 1.0 - np.cos(theta)
    shift_b = shift_a.copy()
    shift_b[0] = 2.0
    lag = np.sin(theta)
    out = np.stack([shift_a, shift_b, lag])[:, :, None] * np.ones((1, 1, 128))
    return out.astype(np.float32)


def whole(*shape):
    return jax.ShapeDtypeStruct(shape, jnp.float32)


def call(body, name, outs, n_in, scratch=(), scalars=1):
    vmem = pl.BlockSpec(memory_space=pltpu.VMEM)
    smem = pl.BlockSpec(memory_space=pltpu.SMEM)
    return pl.pallas_call(
        body,
        name=name,
        out_shape=outs,
        in_specs=[smem] * scalars + [vmem] * n_in,
        out_specs=[vmem] * len(outs),
        scratch_shapes=list(scratch),
        compiler_params=pltpu.CompilerParams(vmem_limit_bytes=48 * 1024 * 1024),
    )


def pack_body(pos, state, adjoint, target, *rest):
    outs, stage = rest[:8], rest[8]
    t = pos[0]
    flip = pos[1]
    for f, ref in enumerate((state, adjoint, target)):
        for n in range(2):
            for x in range(2):
                base = ((f * 2 + n) * 2 + x) * WIN
                for d in range(8):
                    low = OWN * d - HALO
                    first, last = max(low, 0), min(low + WIN, 96)
                    stage[d, base + first - low : base + last - low, :] = ref[n, x ^ flip, first:last, :]
                    if first > low:
                        stage[d, base : base + first - low, :] = jnp.zeros((first - low, 128), jnp.float32)
                    if last < low + WIN:
                        stage[d, base + last - low : base + WIN, :] = jnp.zeros((low + WIN - last, 128), jnp.float32)
    for k in range(8):
        outs[k][...] = stage[t ^ k]


def spread_body(pos, *rest):
    pieces, (own, wish, near, far), stage = rest[:8], rest[8:12], rest[12]
    t = pos[0]
    rows = 12 * WIN
    for k in range(8):
        stage[pl.ds(pl.multiple_of((t ^ k) * rows, 8), rows), :] = pieces[k][...]
    for x in range(2):
        for j in range(WIN):
            for f in range(3):
                for n in range(2):
                    v = stage[pl.ds(((f * 2 + n) * 2 + x) * WIN + j, 8, stride=rows), :]
                    if f < 2:
                        c = f * 2 + n
                        own[x, j, c] = v
                        put_field(near, far, x, j, c, v)
                    else:
                        if 1 <= j <= 18:
                            wish[x, j - 1, n] = v
                        if 2 <= j <= 17:
                            out = far if x == 1 else near
                            out[136 + (j - 2) * 2 + n] = v


def put_field(near, far, x, j, c, v):
    first, second = (near, far) if x == 0 else (far, near)
    if 1 <= j <= 18:
        first[(j - 1) * 4 + c] = v
    if 2 <= j <= 17:
        second[72 + (j - 2) * 4 + c] = v


def region(p, j):
    if p == 2 or p == 3:
        return (p - 2) * 18 + j - 1
    return (36 if p == 1 else 52) + j - 2


def spread_sum(v, around, w):
    px, mx, py, my = around
    up = pltpu.roll(v, 127, 1)
    down = pltpu.roll(v, 1, 1)
    return ((w[0] * px + w[1] * mx) + (w[2] * py + w[3] * my)) + (w[4] * up + w[5] * down)


def row_weights(weights, p, j, count):
    tile = weights[(p - 1) * WIN + j]
    return [jnp.broadcast_to(tile[k : k + 1, :], (8, 128)) for k in range(count)]


def solve(right, td, inv, consts):
    ur, ui, pr, pi = right
    shift_a, shift_b, lag = consts
    inv_a, inv_b = inv
    a = shift_a + td
    b = shift_b + td
    return (
        (a * ur + lag * ui - COUPLING * pr) * inv_a,
        (b * ui - lag * ur - COUPLING * pi) * inv_b,
        (TAU * ur + a * pr - lag * pi) * inv_a,
        (TAU * ui + b * pi + lag * pr) * inv_b,
    )


def inverse_body(weights, consts, inv):
    ca, cb, lag = consts[0], consts[1], consts[2]
    base = lag * lag + DET_SHIFT
    for p, lo, hi in ((2, 1, 19), (3, 1, 19), (1, 2, 18), (4, 2, 18)):
        def row(j, carry, p=p):
            tile = weights[(p - 1) * WIN + j]
            td = jnp.broadcast_to(tile[6:7, :], (8, 128))
            a = ca + td
            b = cb + td
            at = region(p, j)
            inv[at, 0] = 1.0 / (a * a + base)
            inv[at, 1] = 1.0 / (b * b + base)
            return carry
        lax.fori_loop(lo, hi, row, 0)


def residual_body(own, wish, near, far, tnear, tfar, weights, consts, inv, forward, rhs, it, out_near, out_far, res, zed):
    def field(p, j, c):
        if p == 2 or p == 3:
            return own[p - 2, j, c]
        side = near if p < 2 else far
        if p == 1 or p == 4:
            return side[(j - 1) * 4 + c]
        return side[72 + (j - 2) * 4 + c]

    def wanted(p, j, n):
        if p == 2 or p == 3:
            return wish[p - 2, j - 1, n]
        return (tnear if p == 1 else tfar)[136 + (j - 2) * 2 + n]

    sub = lax.broadcasted_iota(jnp.int32, (8, 128), 0)
    first = jnp.where(sub == 0, 1.0, 0.0)
    not_first = jnp.where(sub == 0, 0.0, 1.0)
    not_last = jnp.where(sub == 7, 0.0, 1.0)
    for p, lo, hi in ((2, 1, 19), (3, 1, 19), (1, 2, 18), (4, 2, 18)):
        def row(j, carry, p=p):
            w = row_weights(weights, p, j, 8)
            td = w[6]
            v = [field(p, j, c) for c in range(4)]
            n = [
                spread_sum(v[c], (field(p + 1, j, c), field(p - 1, j, c), field(p, j + 1, c), field(p, j - 1, c)), w)
                for c in range(4)
            ]
            at = region(p, j)
            ue, uo, pe, po = v
            before = pltpu.roll(uo, 1, 0) * not_first
            after = pltpu.roll(pe, 7, 0) * not_last
            res[at, 0] = w[7] * first - (ue - before + (td * ue - n[0]) + COUPLING * pe)
            res[at, 1] = -(uo - ue + (td * uo - n[1]) + COUPLING * po)
            res[at, 2] = -TAU * wanted(p, j, 0) - (pe - po + (td * pe - n[2]) - TAU * ue)
            res[at, 3] = -TAU * wanted(p, j, 1) - (po - after + (td * po - n[3]) - TAU * uo)
            return carry
        lax.fori_loop(lo, hi, row, 0)

    def group(g, carry):
        block = res[pl.ds(g * 4, 4)].reshape(128, 128)
        done = jnp.dot(forward[...], block, precision=lax.Precision.HIGHEST, preferred_element_type=jnp.float32)
        rhs[pl.ds(g * 4, 4)] = done.reshape(4, 4, 8, 128)
        return carry
    lax.fori_loop(0, 17, group, 0)

    cs = (consts[0], consts[1], consts[2])
    for p, lo, hi in ((2, 1, 19), (3, 1, 19), (1, 2, 18), (4, 2, 18)):
        def row(j, carry, p=p):
            td = row_weights(weights, p, j, 8)[6]
            at = region(p, j)
            z = solve([rhs[at, c] for c in range(4)], td, (inv[at, 0], inv[at, 1]), cs)
            for c in range(4):
                zed[at, c] = z[c]
            return carry
        lax.fori_loop(lo, hi, row, 0)

    for p in (2, 3):
        def row(j, carry, p=p):
            w = row_weights(weights, p, j, 8)
            at = region(p, j)
            pushed = []
            for c in range(4):
                around = (zed[region(p + 1, j), c], zed[region(p - 1, j), c], zed[at + 1, c], zed[at - 1, c])
                pushed.append(rhs[at, c] + spread_sum(zed[at, c], around, w))
            z = solve(pushed, w[6], (inv[at, 0], inv[at, 1]), cs)
            for c in range(4):
                it[p - 2, j - 2, c] = z[c]
            return carry
        lax.fori_loop(2, 18, row, 0)
    out_near[0:14] = it[0, 1:15]
    out_near[14:26] = it[1, 2:14]
    out_far[0:14] = it[1, 1:15]
    out_far[14:26] = it[0, 2:14]


def sweep_body(it, near, far, rhs, weights, consts, inv, back, zed, fin):
    def guess(p, j, c):
        if p == 2 or p == 3:
            return it[p - 2, j - 2, c]
        side = near if p < 2 else far
        if p == 1 or p == 4:
            return side[j - 3, c]
        return side[14 + j - 4, c]

    def at2(p, j):
        if p == 2 or p == 3:
            return (p - 2) * 14 + j - 3
        return (28 if p == 1 else 40) + j - 4

    cs = (consts[0], consts[1], consts[2])
    for p, lo, hi in ((2, 3, 17), (3, 3, 17), (1, 4, 16), (4, 4, 16)):
        def row(j, carry, p=p):
            w = row_weights(weights, p, j, 8)
            at = region(p, j)
            pushed = []
            for c in range(4):
                around = (guess(p + 1, j, c), guess(p - 1, j, c), guess(p, j + 1, c), guess(p, j - 1, c))
                pushed.append(rhs[at, c] + spread_sum(guess(p, j, c), around, w))
            z = solve(pushed, w[6], (inv[at, 0], inv[at, 1]), cs)
            for c in range(4):
                zed[at2(p, j), c] = z[c]
            return carry
        lax.fori_loop(lo, hi, row, 0)
    for p in (2, 3):
        def row(j, carry, p=p):
            w = row_weights(weights, p, j, 8)
            at = region(p, j)
            here = at2(p, j)
            pushed = []
            for c in range(4):
                around = (zed[at2(p + 1, j), c], zed[at2(p - 1, j), c], zed[here + 1, c], zed[here - 1, c])
                pushed.append(rhs[at, c] + spread_sum(zed[here, c], around, w))
            z = solve(pushed, w[6], (inv[at, 0], inv[at, 1]), cs)
            for c in range(4):
                fin[(p - 2) * OWN + j - 4, c] = z[c]
            return carry
        lax.fori_loop(4, 16, row, 0)

    def group(g, carry):
        block = fin[pl.ds(g * 4, 4)].reshape(128, 128)
        done = jnp.dot(back[...], block, precision=lax.Precision.HIGHEST, preferred_element_type=jnp.float32)
        fin[pl.ds(g * 4, 4)] = done.reshape(4, 4, 8, 128)
        return carry
    lax.fori_loop(0, 6, group, 0)


def middle_body(pos, it, near, far, rhs, weights, consts, inv, back, own, new, send0, send1, zed, fin):
    sweep_body(it, near, far, rhs, weights, consts, inv, back, zed, fin)
    odd = pos[0] & 1
    for x in range(2):
        for j in range(OWN):
            for c in range(4):
                new[x, j, c] = own[x, j + HALO, c] + fin[x * OWN + j, c]
    top = pl.multiple_of(8 * (1 - odd), 4)
    bottom = 8 * odd
    for x in range(2):
        for j in range(HALO):
            send0[x, j] = new[x, top + j]
            send1[x, j] = new[x, bottom + j]


def widen_body(pos, new, got0, got1, own, near, far):
    odd = pos[0] & 1
    for x in range(2):
        own[x, HALO : HALO + OWN] = new[x]
        own[x, pl.ds(16 * (1 - odd), HALO)] = got0[x]
        own[x, pl.ds(16 * odd, HALO)] = got1[x]
    for x in range(2):
        first, second = (near, far) if x == 0 else (far, near)
        first[0:72] = own[x, 1:19].reshape(72, 8, 128)
        second[72:136] = own[x, 2:18].reshape(64, 8, 128)


def last_body(pos, it, near, far, rhs, weights, consts, inv, back, own, *rest):
    outs, (zed, fin, stage) = rest[:8], rest[8:]
    sweep_body(it, near, far, rhs, weights, consts, inv, back, zed, fin)
    t = pos[0]
    for x in range(2):
        for j in range(OWN):
            for c in range(4):
                stage[pl.ds((c * 2 + x) * OWN + j, 8, stride=8 * OWN), :] = own[x, j + HALO, c] + fin[x * OWN + j, c]
    for k in range(8):
        outs[k][...] = stage[pl.ds(pl.multiple_of((t ^ k) * 8 * OWN, 8), 8 * OWN), :]


def unpack_body(pos, *rest):
    pieces, (state, adjoint), stage = rest[:8], rest[8:10], rest[10]
    t = pos[0]
    flip = pos[1]
    for k in range(8):
        stage[t ^ k] = pieces[k][...]
    for f, ref in enumerate((state, adjoint)):
        for n in range(2):
            for x in range(2):
                base = ((f * 2 + n) * 2 + x) * OWN
                for d in range(8):
                    ref[n, x ^ flip, OWN * d : OWN * (d + 1), :] = stage[d, base : base + OWN, :]


def exchange(pieces):
    count = lax.axis_size("tm")
    return [pieces[0]] + [
        lax.ppermute(pieces[k], "tm", [(i, i ^ k) for i in range(count)]) for k in range(1, count)
    ]


def swap(block, axis, start):
    count = lax.axis_size(axis)
    route = []
    for i in range(start, count - 1, 2):
        route += [(i, i + 1), (i + 1, i)]
    return lax.ppermute(block, axis, route)


def face_weights(kappa, first_state, t, s, flip):
    mid = kappa[1:5, 1:-1]
    lane = lax.broadcasted_iota(jnp.int32, mid.shape, 2)
    row = lax.broadcasted_iota(jnp.int32, mid.shape, 1) + OWN * t - HALO
    local = lax.broadcasted_iota(jnp.int32, mid.shape, 0)
    plane = jnp.where(flip == 1, 2 * s + 2 - local, 2 * s - 1 + local)
    ahead = jnp.where(flip == 1, -1, 1)
    half = 0.5 * TAU
    xp = half * (mid + kappa[2:6, 1:-1])
    xm = half * (mid + kappa[0:4, 1:-1])
    yp = half * (mid + kappa[1:5, 2:])
    ym = half * (mid + kappa[1:5, :-2])
    zp = half * (mid + jnp.pad(mid[..., 1:], ((0, 0), (0, 0), (0, 1))))
    zm = half * (mid + jnp.pad(mid[..., :-1], ((0, 0), (0, 0), (1, 0))))
    td = xp + xm + yp + ym + zp + zm
    inside = lambda q, n: (q >= 0) & (q < n)
    here = inside(plane, 64) & inside(row, 96)
    keep = lambda w, ok: jnp.where(here & ok, w, 0.0)
    kinds = [
        keep(xp, inside(plane + ahead, 64)),
        keep(xm, inside(plane - ahead, 64)),
        keep(yp, row + 1 < 96),
        keep(ym, row > 0),
        keep(zp, lane < 127),
        keep(zm, lane > 0),
        td,
        first_state,
    ]
    return jnp.stack(kinds, 2).reshape(4 * WIN, 8, 128)


def on_device(state_guess, adjoint_guess, target, initial_state, diffusivity):
    t = lax.axis_index("tm").astype(jnp.int32)
    s = lax.axis_index("space").astype(jnp.int32)
    flip = s & 1
    pos = jnp.stack([t, flip])
    forward, back = (jnp.asarray(m) for m in transform_matrices())
    consts = jnp.asarray(mode_constants())

    pieces = call(
        pack_body, "pack", [whole(12 * WIN, 128)] * 8, 3, [pltpu.VMEM((8, 12 * WIN, 128), jnp.float32)]
    )(pos, state_guess, adjoint_guess, target)

    both = jnp.concatenate([diffusivity, initial_state], 0)
    both = jnp.where(flip == 1, both[jnp.array([1, 0, 3, 2])], both)
    both = jnp.pad(both, ((0, 0), (HALO + 2, HALO + 2), (0, 0)))
    both = lax.dynamic_slice_in_dim(both, OWN * t, 24, 1)
    far_c = swap(jnp.stack([both[1], both[0], both[3]]), "space", 0)
    near_c = swap(jnp.stack([both[0], both[1], both[2]]), "space", 1)

    got = exchange(pieces)

    kappa = jnp.stack([near_c[1], near_c[0], both[0], both[1], far_c[0], far_c[1]])[:, 1:23]
    begin = jnp.stack([near_c[2], both[2], both[3], far_c[2]])[:, 2:22]
    weights = face_weights(kappa, begin, t, s, flip)
    inv = call(inverse_body, "inverse", [whole(68, 2, 8, 128)], 2, scalars=0)(weights, consts)[0]

    own, wish, near, far = call(
        spread_body,
        "spread",
        [whole(2, WIN, 4, 8, 128), whole(2, 18, 2, 8, 128), whole(168, 8, 128), whole(168, 8, 128)],
        8,
        [pltpu.VMEM((8 * 12 * WIN, 128), jnp.float32)],
    )(pos, *got)

    sweep_scratch = [pltpu.VMEM((52, 4, 8, 128), jnp.float32), pltpu.VMEM((24, 4, 8, 128), jnp.float32)]
    for outer in range(OUTER):
        far_f = swap(far, "space", 0)
        near_f = swap(near, "space", 1)
        if outer == 0:
            wish_near, wish_far = near_f, far_f
        rhs, it, near_z, far_z = call(
            residual_body,
            "residual",
            [whole(68, 4, 8, 128), whole(2, 16, 4, 8, 128), whole(26, 4, 8, 128), whole(26, 4, 8, 128)],
            10,
            [pltpu.VMEM((68, 4, 8, 128), jnp.float32)] * 2,
            scalars=0,
        )(own, wish, near_f, far_f, wish_near, wish_far, weights, consts, inv, forward)
        far_z = swap(far_z, "space", 0)
        near_z = swap(near_z, "space", 1)
        if outer < OUTER - 1:
            new, send0, send1 = call(
                middle_body,
                "middle",
                [whole(2, OWN, 4, 8, 128), whole(2, HALO, 4, 8, 128), whole(2, HALO, 4, 8, 128)],
                9,
                sweep_scratch,
            )(pos, it, near_z, far_z, rhs, weights, consts, inv, back, own)
            got0 = swap(send0, "tm", 0)
            got1 = swap(send1, "tm", 1)
            own, near, far = call(
                widen_body, "widen", [whole(2, WIN, 4, 8, 128), whole(136, 8, 128), whole(136, 8, 128)], 3
            )(pos, new, got0, got1)
    pieces = call(
        last_body,
        "last",
        [whole(8 * OWN, 128)] * 8,
        9,
        sweep_scratch + [pltpu.VMEM((64 * OWN, 128), jnp.float32)],
    )(pos, it, near_z, far_z, rhs, weights, consts, inv, back, own)
    got = exchange(pieces)
    return tuple(
        call(
            unpack_body,
            "unpack",
            [whole(2, 2, 96, 128)] * 2,
            8,
            [pltpu.VMEM((8, 8 * OWN, 128), jnp.float32)],
        )(pos, *got)
    )


def solution(mesh):
    in_specs = (
        P("tm", "space", None, None),
        P("tm", "space", None, None),
        P("tm", "space", None, None),
        P("space", None, None),
        P("space", None, None),
    )
    out_specs = (P("tm", "space", None, None), P("tm", "space", None, None))
    return jax.shard_map(
        on_device, mesh=mesh, in_specs=in_specs, out_specs=out_specs, check_vma=False
    )
```

time: 368 us -> 171 us (0.46)
  waiting for transfers between devices: 238 us -> 57.5 us
  Pallas kernels: 0 us -> 48 us
  starting transfers between devices: 88.5 us -> 50.7 us
  other arithmetic: 37.5 us -> 3.89 us
  local copies, waits for them, and re-layouts: 1.33 us -> 8.81 us
    ppermute x34 -> x26, waiting for transfers between devices: 238 us -> 57.5 us  [the longest x12 43.4 us: swap(): return lax.ppermute(block, axis, route)]
    pallas_call x0 -> x9, Pallas kernels: none -> 48 us  [the longest x2 26.1 us: on_device(): call(residual_body, 'residual', [whole(68, 4, 8, 128), whole(2, 16, 4, 8,...]
    ppermute x34 -> x26, starting transfers between devices: 88.5 us -> 50.7 us  [the longest x12 25.7 us: swap(): return lax.ppermute(block, axis, route)]
    concatenate x11 -> x0, other arithmetic: 15.7 us -> none  [extended(): jnp.concatenate([lax.ppermute(tail, axis, [(i, (i + 1) % count) for i in...]
    add x12 -> x1, other arithmetic: 6.53 us -> 0.1 us  [face_weights(): td = xp + xm + yp + ym + zp + zm]
    another operation x1 -> x9, local copies, waits for them, and re-layouts: 0.01 us -> 5.03 us  [face_weights(): return jnp.stack(kinds, 2).reshape(4 * WIN, 8, 128)]
    select_n x12 -> x2, other arithmetic: 5.69 us -> 0.84 us  [the longest x1 0.81 us: face_weights(): keep = lambda w, ok: jnp.where(here & ok, w, 0.0)]
    sub x19 -> x0, other arithmetic: 4.63 us -> none  [the longest x12 2.63 us: twiddle(): packed[0] * cos_part - packed[1] * sin_part]
  transfers between devices with their start and end apart: 34 -> 26, of which waited for: 29 -> 14; matrix products, arithmetic and copies ran while one was open for 1% -> 5% of each run, Pallas kernels for 0% -> 1%
where the time goes in v1:
time: 171 us; the launch traced here: 170 us
  waiting for transfers between devices  57.5 us (34%)
  starting transfers between devices  50.7 us (30%)
  Pallas kernels  48 us (28%)
  local copies, waits for them, and re-layouts  8.81 us (5%)
  other arithmetic  3.89 us (2%)
    ppermute x12, waiting for transfers between devices, swap(): return lax.ppermute(block, axis, route)  43.4 us
    pallas_call x2, Pallas kernels, on_device(): call(residual_body, 'residual', [whole(68, 4, 8, 128), whole(2, 16, 4, 8,...  26.1 us
    ppermute x12, starting transfers between devices, swap(): return lax.ppermute(block, axis, route)  25.7 us
    ppermute x14, starting transfers between devices, exchange(): lax.ppermute(pieces[k], 'tm', [(i, i ^ k) for i in range(count)])  25 us
    ppermute x14, waiting for transfers between devices, exchange(): lax.ppermute(pieces[k], 'tm', [(i, i ^ k) for i in range(count)])  14 us
    pallas_call x1, Pallas kernels, on_device(): call(last_body, 'last', [whole(8 * OWN, 128)] * 8, 9, sweep_scratch + [pl...  8.51 us
    pallas_call x1, Pallas kernels, on_device(): call(middle_body, 'middle', [whole(2, OWN, 4, 8, 128), whole(2, HALO, 4,...  8.27 us
    another operation x9, local copies, waits for them, and re-layouts, face_weights(): return jnp.stack(kinds, 2).reshape(4 * WIN, 8, 128)  5.03 us
  transfers between devices with their start and end apart: 26, of which 14 were waited for; matrix products, arithmetic and copies ran while one was open for 5% of the time, Pallas kernels for 1%

profile of v1, /device:TPU:6, one launch (start us, length us, event | category | flops | bytes accessed | tf_op | source)
XLA Modules:
  0.0 169.9 jit_solution(4879616136641777694)
XLA Ops:
  0.7 0.7 pad_clamp_fusion
  1.4 0.9 constant_dynamic-update-slice_fusion.1
  2.3 0.9 constant_dynamic-update-slice_fusion
  3.8 8.0 %collective-permute-start.9 = (f32[3,24,128]{2,1,0:T(8,128)S(1)}, f32[3,24,128]{2,1,0:T(8,128)S(1)}, u32[]{:S(2)}, u32[]{:S(2)}) collective-permute-start(f32[3,24,128]{2,1,0:T(8,128)S(1)} %pad_dynamic-slice_fusion.4), channel_id=1, source_target_pairs={{1,2},{2,1},{3,4},{4,3},{5,6},{6,5},{7,8},{8,7},{9,10},{10,9},{11,... | collective-permute-start | bytes 110600 | tf_op jit(solution)/shard_map/ppermute | solution.py:353
  12.1 0.7 pack.1
  12.9 1.7 collective-permute-start.1
  16.9 3.2 %collective-permute-start.3 = (f32[240,128]{1,0:T(8,128)S(1)}, f32[240,128]{1,0:T(8,128)S(1)}, u32[]{:S(2)}, u32[]{:S(2)}) collective-permute-start(f32[240,128]{1,0:T(8,128)S(1)} %get-tuple-element.40), channel_id=1, source_target_pairs={{0,128},{32,160},{64,192},{96,224},{128,0},{160,32},{192,64},{224,... | collective-permute-start | bytes 368648 | tf_op jit(solution)/shard_map/ppermute | solution.py:344
  20.2 3.0 %collective-permute-start.5 = (f32[240,128]{1,0:T(8,128)S(1)}, f32[240,128]{1,0:T(8,128)S(1)}, u32[]{:S(2)}, u32[]{:S(2)}) collective-permute-start(f32[240,128]{1,0:T(8,128)S(1)} %get-tuple-element.42), channel_id=1, source_target_pairs={{0,192},{32,224},{64,128},{96,160},{128,64},{160,96},{192,0},{224,... | collective-permute-start | bytes 368648 | tf_op jit(solution)/shard_map/ppermute | solution.py:344
  23.3 0.6 stack.68
  24.0 3.0 %collective-permute-done.3.rest_4_ = f32[240,128]{1,0:T(8,128)S(1)} collective-permute-done((f32[240,128]{1,0:T(8,128)S(1)}, f32[240,128]{1,0:T(8,128)S(1)}, u32[]{:S(2)}, u32[]{:S(2)}) %collective-permute-start.3) | collective-permute-done | bytes 122912 | tf_op jit(solution)/shard_map/ppermute | solution.py:344
  26.9 1.7 collective-permute-done.4.rest_5_
  28.6 3.1 %collective-permute-done.5.rest_6_ = f32[240,128]{1,0:T(8,128)S(1)} collective-permute-done((f32[240,128]{1,0:T(8,128)S(1)}, f32[240,128]{1,0:T(8,128)S(1)}, u32[]{:S(2)}, u32[]{:S(2)}) %collective-permute-start.5) | collective-permute-done | bytes 122912 | tf_op jit(solution)/shard_map/ppermute | solution.py:344
  31.7 2.5 %collective-permute-done.6.rest_7_ = f32[240,128]{1,0:T(8,128)S(1)} collective-permute-done((f32[240,128]{1,0:T(8,128)S(1)}, f32[240,128]{1,0:T(8,128)S(1)}, u32[]{:S(2)}, u32[]{:S(2)}) %collective-permute-start.6) | collective-permute-done | bytes 122912 | tf_op jit(solution)/shard_map/ppermute | solution.py:344
  34.2 1.8 %spread.1 = (f32[2,20,4,8,128]{4,3,2,1,0:T(8,128)S(1)}, f32[2,18,2,8,128]{4,3,2,1,0:T(8,128)S(1)}, f32[168,8,128]{2,1,0:T(8,128)}, f32[168,8,128]{2,1,0:T(8,128)S(1)}) custom-call(s32[2]{0:T(128)S(1)} %pad_add_fusion.pos, f32[240,128]{1,0:T(8,128)S(1)} %get-tuple-element.36.rest_0_, f32[240,128]{1,0:T(8,128)S(1)} %collective-permute-done.rest_1_, ...), custom_call_target="tpu_custom_call" | custom-call | tf_op jit(solution)/shard_map/spread/pallas_call | solution.py:413
  36.0 3.9 %collective-permute-start.7 = (f32[168,8,128]{2,1,0:T(8,128)}, f32[168,8,128]{2,1,0:T(8,128)S(1)}, u32[]{:S(2)}, u32[]{:S(2)}) collective-permute-start(f32[168,8,128]{2,1,0:T(8,128)} %get-tuple-element.46), channel_id=1, source_target_pairs={{1,2},{2,1},{3,4},{4,3},{5,6},{6,5},{7,8},{8,7},{9,10},{10,9},{11,... | collective-permute-start | bytes 2064392 | tf_op jit(solution)/shard_map/ppermute | solution.py:353
  39.9 0.8 collective-permute-start.8
  40.9 0.6 stack.66
  41.5 0.8 fusion.11
  42.4 0.6 stack.65
  43.0 0.6 stack.62
  43.6 0.6 stack.59
  44.2 0.6 stack.61
  44.9 1.3 stack.69.weights
  46.2 0.7 inverse.1.inv
  46.9 10.8 %collective-permute-done.7.near.tnear = f32[168,8,128]{2,1,0:T(8,128)S(1)} collective-permute-done((f32[168,8,128]{2,1,0:T(8,128)}, f32[168,8,128]{2,1,0:T(8,128)S(1)}, u32[]{:S(2)}, u32[]{:S(2)}) %collective-permute-start.7) | collective-permute-done | bytes 688160 | tf_op jit(solution)/shard_map/ppermute | solution.py:353
  57.7 12.6 %residual.2 = (f32[68,4,8,128]{3,2,1,0:T(8,128)S(1)}, f32[2,16,4,8,128]{4,3,2,1,0:T(8,128)S(1)}, f32[26,4,8,128]{3,2,1,0:T(8,128)S(1)}, f32[26,4,8,128]{3,2,1,0:T(8,128)S(1)}) custom-call(f32[2,20,4,8,128]{4,3,2,1,0:T(8,128)S(1)} %get-tuple-element.44.own, f32[2,18,2,8,128]{4,3,2,1,0:T(8,128)S(1)} %get-tuple-element.45.wish, ...), custom_call_target="tpu_custom_call" | custom-call | tf_op jit(solution)/shard_map/residual/pallas_call | solution.py:427
  70.2 3.9 %collective-permute-start.11 = (f32[26,4,8,128]{3,2,1,0:T(8,128)S(1)}, f32[26,4,8,128]{3,2,1,0:T(8,128)S(1)}, u32[]{:S(2)}, u32[]{:S(2)}) collective-permute-start(f32[26,4,8,128]{3,2,1,0:T(8,128)S(1)} %get-tuple-element.49), channel_id=1, source_target_pairs={{1,2},{2,1},{3,4},{4,3},{5,6},{6,5},{7,8},{8,7},{9,10},{10,9},{11,... | collective-permute-start | bytes 1277960 | tf_op jit(solution)/shard_map/ppermute | solution.py:353
  74.2 11.0 %collective-permute-done.11.near = f32[26,4,8,128]{3,2,1,0:T(8,128)S(1)} collective-permute-done((f32[26,4,8,128]{3,2,1,0:T(8,128)S(1)}, f32[26,4,8,128]{3,2,1,0:T(8,128)S(1)}, u32[]{:S(2)}, u32[]{:S(2)}) %collective-permute-start.11) | collective-permute-done | bytes 426016 | tf_op jit(solution)/shard_map/ppermute | solution.py:353
  85.2 8.3 %middle.1 = (f32[2,12,4,8,128]{4,3,2,1,0:T(8,128)S(1)}, f32[2,4,4,8,128]{4,3,2,1,0:T(8,128)S(1)}, f32[2,4,4,8,128]{4,3,2,1,0:T(8,128)S(1)}) custom-call(s32[2]{0:T(128)S(1)} %pad_add_fusion.pos, f32[2,16,4,8,128]{4,3,2,1,0:T(8,128)S(1)} %get-tuple-element.48.it, f32[26,4,8,128]{3,2,1,0:T(8,128)S(1)} %collective-permute-done.11.near, ...), custom_call_target="tpu_custom_call" | custom-call | tf_op jit(solution)/shard_map/middle/pallas_call | solution.py:438
  93.6 0.7 collective-permute-start.14
  94.3 0.7 collective-permute-done.13.got0
  94.9 0.7 widen.1
  95.6 3.9 %collective-permute-start.15 = (f32[136,8,128]{2,1,0:T(8,128)S(1)}, f32[136,8,128]{2,1,0:T(8,128)S(1)}, u32[]{:S(2)}, u32[]{:S(2)}) collective-permute-start(f32[136,8,128]{2,1,0:T(8,128)S(1)} %get-tuple-element.56), channel_id=1, source_target_pairs={{1,2},{2,1},{3,4},{4,3},{5,6},{6,5},{7,8},{8,7},{9,10},{10,9},{11,... | collective-permute-start | bytes 1671176 | tf_op jit(solution)/shard_map/ppermute | solution.py:353
  99.6 11.0 %collective-permute-done.15.near = f32[136,8,128]{2,1,0:T(8,128)S(1)} collective-permute-done((f32[136,8,128]{2,1,0:T(8,128)S(1)}, f32[136,8,128]{2,1,0:T(8,128)S(1)}, u32[]{:S(2)}, u32[]{:S(2)}) %collective-permute-start.15) | collective-permute-done | bytes 557088 | tf_op jit(solution)/shard_map/ppermute | solution.py:353
  110.9 13.5 %residual.3 = (f32[68,4,8,128]{3,2,1,0:T(8,128)}, f32[2,16,4,8,128]{4,3,2,1,0:T(8,128)S(1)}, f32[26,4,8,128]{3,2,1,0:T(8,128)S(1)}, f32[26,4,8,128]{3,2,1,0:T(8,128)S(1)}) custom-call(f32[2,20,4,8,128]{4,3,2,1,0:T(8,128)S(1)} %get-tuple-element.55.own, f32[2,18,2,8,128]{4,3,2,1,0:T(8,128)S(1)} %get-tuple-element.45.wish, ...), custom_call_target="tpu_custom_call" | custom-call | tf_op jit(solution)/shard_map/residual/pallas_call | solution.py:427
  124.4 4.0 %collective-permute-start.17 = (f32[26,4,8,128]{3,2,1,0:T(8,128)S(1)}, f32[26,4,8,128]{3,2,1,0:T(8,128)S(1)}, u32[]{:S(2)}, u32[]{:S(2)}) collective-permute-start(f32[26,4,8,128]{3,2,1,0:T(8,128)S(1)} %get-tuple-element.59), channel_id=1, source_target_pairs={{1,2},{2,1},{3,4},{4,3},{5,6},{6,5},{7,8},{8,7},{9,10},{10,9},{11,... | collective-permute-start | bytes 1277960 | tf_op jit(solution)/shard_map/ppermute | solution.py:353
  128.5 9.4 %collective-permute-done.17.near = f32[26,4,8,128]{3,2,1,0:T(8,128)S(1)} collective-permute-done((f32[26,4,8,128]{3,2,1,0:T(8,128)S(1)}, f32[26,4,8,128]{3,2,1,0:T(8,128)S(1)}, u32[]{:S(2)}, u32[]{:S(2)}) %collective-permute-start.17) | collective-permute-done | bytes 426016 | tf_op jit(solution)/shard_map/ppermute | solution.py:353
  138.3 1.2 copy-done
  139.5 8.5 %last.1 = (f32[96,128]{1,0:T(8,128)S(1)}, f32[96,128]{1,0:T(8,128)S(1)}, f32[96,128]{1,0:T(8,128)S(1)}, f32[96,128]{1,0:T(8,128)S(1)}, f32[96,128]{1,0:T(8,128)S...) custom-call(s32[2]{0:T(128)S(1)} %pad_add_fusion.pos, ...), custom_call_target="tpu_custom_call" | custom-call | tf_op jit(solution)/shard_map/last/pallas_call | solution.py:450
  148.1 2.8 %collective-permute-start.19 = (f32[96,128]{1,0:T(8,128)S(1)}, f32[96,128]{1,0:T(8,128)S(1)}, u32[]{:S(2)}, u32[]{:S(2)}) collective-permute-start(f32[96,128]{1,0:T(8,128)S(1)} %get-tuple-element.63), channel_id=1, source_target_pairs={{0,32},{32,0},{64,96},{96,64},{128,160},{160,128},{192,224},{224,1... | collective-permute-start | bytes 147464 | tf_op jit(solution)/shard_map/ppermute | solution.py:344
  150.9 7.7 %collective-permute-start.20 = (f32[96,128]{1,0:T(8,128)S(1)}, f32[96,128]{1,0:T(8,128)S(1)}, u32[]{:S(2)}, u32[]{:S(2)}) collective-permute-start(f32[96,128]{1,0:T(8,128)S(1)} %get-tuple-element.64), channel_id=1, source_target_pairs={{0,64},{32,96},{64,0},{96,32},{128,192},{160,224},{192,128},{224,1... | collective-permute-start | bytes 147464 | tf_op jit(solution)/shard_map/ppermute | solution.py:344
  158.5 2.6 %collective-permute-start.22 = (f32[96,128]{1,0:T(8,128)S(1)}, f32[96,128]{1,0:T(8,128)S(1)}, u32[]{:S(2)}, u32[]{:S(2)}) collective-permute-start(f32[96,128]{1,0:T(8,128)S(1)} %get-tuple-element.66), channel_id=1, source_target_pairs={{0,128},{32,160},{64,192},{96,224},{128,0},{160,32},{192,64},{224,... | collective-permute-start | bytes 147464 | tf_op jit(solution)/shard_map/ppermute | solution.py:344
  161.6 1.6 collective-permute-start.24
  163.1 1.6 collective-permute-start.25
  164.7 1.5 collective-permute-done.23.rest_5_
  166.3 1.4 collective-permute-done.24.rest_6_
  167.7 0.8 collective-permute-done.25.rest_7_
  168.5 1.3 unpack.1
  (59 shorter events, 5.3 us)
Async XLA Ops:
  0.6 11.5 %copy-start.6 = (f32[2,2,96,128]{3,2,1,0:T(8,128)S(1)}, f32[2,2,96,128]{3,2,1,0:T(8,128)}, u32[]{:S(2)}) copy-start(f32[2,2,96,128]{3,2,1,0:T(8,128)} %target.1) | copy-start | bytes 589828
  0.6 11.4 %copy-start.5 = (f32[2,2,96,128]{3,2,1,0:T(8,128)S(1)}, f32[2,2,96,128]{3,2,1,0:T(8,128)}, u32[]{:S(2)}) copy-start(f32[2,2,96,128]{3,2,1,0:T(8,128)} %adjoint.1) | copy-start | bytes 589828
  0.6 11.4 %copy-start.4 = (f32[2,2,96,128]{3,2,1,0:T(8,128)S(1)}, f32[2,2,96,128]{3,2,1,0:T(8,128)}, u32[]{:S(2)}) copy-start(f32[2,2,96,128]{3,2,1,0:T(8,128)} %state.1) | copy-start | bytes 589828
  3.8 16.3 %collective-permute-start.9 = (f32[3,24,128]{2,1,0:T(8,128)S(1)}, f32[3,24,128]{2,1,0:T(8,128)S(1)}, u32[]{:S(2)}, u32[]{:S(2)}) collective-permute-start(f32[3,24,128]{2,1,0:T(8,128)S(1)} %pad_dynamic-slice_fusion.4), channel_id=1, source_target_pairs={{1,2},{2,1},{3,4},{4,3},{5,6},{6,5},{7,8},{8,7},{9,10},{10,9},{11,... | collective-permute-start | bytes 110600 | tf_op jit(solution)/shard_map/ppermute | solution.py:353
  11.9 5.0 %collective-permute-start.10 = (f32[3,24,128]{2,1,0:T(8,128)S(1)}, f32[3,24,128]{2,1,0:T(8,128)S(1)}, u32[]{:S(2)}, u32[]{:S(2)}) collective-permute-start(f32[3,24,128]{2,1,0:T(8,128)S(1)} %pad_maximum_fusion.6), channel_id=1, source_target_pairs={{0,1},{1,0},{2,3},{3,2},{4,5},{5,4},{6,7},{7,6},{8,9},{9,8},{10,11... | collective-permute-start | bytes 110600 | tf_op jit(solution)/shard_map/ppermute | solution.py:353
  12.8 7.4 %collective-permute-start = (f32[240,128]{1,0:T(8,128)S(1)}, f32[240,128]{1,0:T(8,128)S(1)}, u32[]{:S(2)}, u32[]{:S(2)}) collective-permute-start(f32[240,128]{1,0:T(8,128)S(1)} %get-tuple-element.37), channel_id=1, source_target_pairs={{0,32},{32,0},{64,96},{96,64},{128,160},{160,128},{192,224},{224,1... | collective-permute-start | bytes 368648 | tf_op jit(solution)/shard_map/ppermute | solution.py:344
  12.9 10.3 %collective-permute-start.1 = (f32[240,128]{1,0:T(8,128)S(1)}, f32[240,128]{1,0:T(8,128)S(1)}, u32[]{:S(2)}, u32[]{:S(2)}) collective-permute-start(f32[240,128]{1,0:T(8,128)S(1)} %get-tuple-element.38), channel_id=1, source_target_pairs={{0,64},{32,96},{64,0},{96,32},{128,192},{160,224},{192,128},{224,1... | collective-permute-start | bytes 368648 | tf_op jit(solution)/shard_map/ppermute | solution.py:344
  14.5 9.4 %collective-permute-start.2 = (f32[240,128]{1,0:T(8,128)S(1)}, f32[240,128]{1,0:T(8,128)S(1)}, u32[]{:S(2)}, u32[]{:S(2)}) collective-permute-start(f32[240,128]{1,0:T(8,128)S(1)} %get-tuple-element.39), channel_id=1, source_target_pairs={{0,96},{32,64},{64,32},{96,0},{128,224},{160,192},{192,160},{224,1... | collective-permute-start | bytes 368648 | tf_op jit(solution)/shard_map/ppermute | solution.py:344
  16.9 10.0 %collective-permute-start.3 = (f32[240,128]{1,0:T(8,128)S(1)}, f32[240,128]{1,0:T(8,128)S(1)}, u32[]{:S(2)}, u32[]{:S(2)}) collective-permute-start(f32[240,128]{1,0:T(8,128)S(1)} %get-tuple-element.40), channel_id=1, source_target_pairs={{0,128},{32,160},{64,192},{96,224},{128,0},{160,32},{192,64},{224,... | collective-permute-start | bytes 368648 | tf_op jit(solution)/shard_map/ppermute | solution.py:344
  20.1 8.5 %collective-permute-start.4 = (f32[240,128]{1,0:T(8,128)S(1)}, f32[240,128]{1,0:T(8,128)S(1)}, u32[]{:S(2)}, u32[]{:S(2)}) collective-permute-start(f32[240,128]{1,0:T(8,128)S(1)} %get-tuple-element.41), channel_id=1, source_target_pairs={{0,160},{32,128},{64,224},{96,192},{128,32},{160,0},{192,96},{224,... | collective-permute-start | bytes 368648 | tf_op jit(solution)/shard_map/ppermute | solution.py:344
  20.2 11.5 %collective-permute-start.5 = (f32[240,128]{1,0:T(8,128)S(1)}, f32[240,128]{1,0:T(8,128)S(1)}, u32[]{:S(2)}, u32[]{:S(2)}) collective-permute-start(f32[240,128]{1,0:T(8,128)S(1)} %get-tuple-element.42), channel_id=1, source_target_pairs={{0,192},{32,224},{64,128},{96,160},{128,64},{160,96},{192,0},{224,... | collective-permute-start | bytes 368648 | tf_op jit(solution)/shard_map/ppermute | solution.py:344
  23.2 11.0 %collective-permute-start.6 = (f32[240,128]{1,0:T(8,128)S(1)}, f32[240,128]{1,0:T(8,128)S(1)}, u32[]{:S(2)}, u32[]{:S(2)}) collective-permute-start(f32[240,128]{1,0:T(8,128)S(1)} %get-tuple-element.43), channel_id=1, source_target_pairs={{0,224},{32,192},{64,160},{96,128},{128,96},{160,64},{192,32},{224... | collective-permute-start | bytes 368648 | tf_op jit(solution)/shard_map/ppermute | solution.py:344
  36.0 21.7 %collective-permute-start.7 = (f32[168,8,128]{2,1,0:T(8,128)}, f32[168,8,128]{2,1,0:T(8,128)S(1)}, u32[]{:S(2)}, u32[]{:S(2)}) collective-permute-start(f32[168,8,128]{2,1,0:T(8,128)} %get-tuple-element.46), channel_id=1, source_target_pairs={{1,2},{2,1},{3,4},{4,3},{5,6},{6,5},{7,8},{8,7},{9,10},{10,9},{11,... | collective-permute-start | bytes 2064392 | tf_op jit(solution)/shard_map/ppermute | solution.py:353
  39.9 17.8 %collective-permute-start.8 = (f32[168,8,128]{2,1,0:T(8,128)S(1)}, f32[168,8,128]{2,1,0:T(8,128)S(1)}, u32[]{:S(2)}, u32[]{:S(2)}) collective-permute-start(f32[168,8,128]{2,1,0:T(8,128)S(1)} %get-tuple-element.47), channel_id=1, source_target_pairs={{0,1},{1,0},{2,3},{3,2},{4,5},{5,4},{6,7},{7,6},{8,9},{9,8},{10,11... | collective-permute-start | bytes 2064392 | tf_op jit(solution)/shard_map/ppermute | solution.py:353
  40.8 5.4 %copy-start.1 = (f32[3,8,128]{2,1,0:T(8,128)S(1)}, f32[3,8,128]{2,1,0:T(8,128)}, u32[]{:S(2)}) copy-start(f32[3,8,128]{2,1,0:T(8,128)} %constant.53.clone.consts) | copy-start | bytes 36868
  42.3 15.3 %copy-start.3 = (f32[128,128]{1,0:T(8,128)S(1)}, f32[128,128]{1,0:T(8,128)}, u32[]{:S(2)}) copy-start(f32[128,128]{1,0:T(8,128)} %constant.51.clone.forward) | copy-start | bytes 196612
  57.7 27.6 %copy-start.2 = (f32[128,128]{1,0:T(8,128)S(1)}, f32[128,128]{1,0:T(8,128)}, u32[]{:S(2)}) copy-start(f32[128,128]{1,0:T(8,128)} %constant.52.clone.back) | copy-start | bytes 196612
  70.2 15.0 %collective-permute-start.11 = (f32[26,4,8,128]{3,2,1,0:T(8,128)S(1)}, f32[26,4,8,128]{3,2,1,0:T(8,128)S(1)}, u32[]{:S(2)}, u32[]{:S(2)}) collective-permute-start(f32[26,4,8,128]{3,2,1,0:T(8,128)S(1)} %get-tuple-element.49), channel_id=1, source_target_pairs={{1,2},{2,1},{3,4},{4,3},{5,6},{6,5},{7,8},{8,7},{9,10},{10,9},{11,... | collective-permute-start | bytes 1277960 | tf_op jit(solution)/shard_map/ppermute | solution.py:353
  74.1 11.1 %collective-permute-start.12 = (f32[26,4,8,128]{3,2,1,0:T(8,128)S(1)}, f32[26,4,8,128]{3,2,1,0:T(8,128)S(1)}, u32[]{:S(2)}, u32[]{:S(2)}) collective-permute-start(f32[26,4,8,128]{3,2,1,0:T(8,128)S(1)} %get-tuple-element.50), channel_id=1, source_target_pairs={{0,1},{1,0},{2,3},{3,2},{4,5},{5,4},{6,7},{7,6},{8,9},{9,8},{10,11... | collective-permute-start | bytes 1277960 | tf_op jit(solution)/shard_map/ppermute | solution.py:353
  93.5 1.4 collective-permute-start.13
  93.6 1.3 collective-permute-start.14
  95.6 15.0 %collective-permute-start.15 = (f32[136,8,128]{2,1,0:T(8,128)S(1)}, f32[136,8,128]{2,1,0:T(8,128)S(1)}, u32[]{:S(2)}, u32[]{:S(2)}) collective-permute-start(f32[136,8,128]{2,1,0:T(8,128)S(1)} %get-tuple-element.56), channel_id=1, source_target_pairs={{1,2},{2,1},{3,4},{4,3},{5,6},{6,5},{7,8},{8,7},{9,10},{10,9},{11,... | collective-permute-start | bytes 1671176 | tf_op jit(solution)/shard_map/ppermute | solution.py:353
  99.5 11.3 %collective-permute-start.16 = (f32[136,8,128]{2,1,0:T(8,128)S(1)}, f32[136,8,128]{2,1,0:T(8,128)S(1)}, u32[]{:S(2)}, u32[]{:S(2)}) collective-permute-start(f32[136,8,128]{2,1,0:T(8,128)S(1)} %get-tuple-element.57), channel_id=1, source_target_pairs={{0,1},{1,0},{2,3},{3,2},{4,5},{5,4},{6,7},{7,6},{8,9},{9,8},{10,11... | collective-permute-start | bytes 1671176 | tf_op jit(solution)/shard_map/ppermute | solution.py:353
  124.4 13.5 %collective-permute-start.17 = (f32[26,4,8,128]{3,2,1,0:T(8,128)S(1)}, f32[26,4,8,128]{3,2,1,0:T(8,128)S(1)}, u32[]{:S(2)}, u32[]{:S(2)}) collective-permute-start(f32[26,4,8,128]{3,2,1,0:T(8,128)S(1)} %get-tuple-element.59), channel_id=1, source_target_pairs={{1,2},{2,1},{3,4},{4,3},{5,6},{6,5},{7,8},{8,7},{9,10},{10,9},{11,... | collective-permute-start | bytes 1277960 | tf_op jit(solution)/shard_map/ppermute | solution.py:353
  128.4 9.9 %collective-permute-start.18 = (f32[26,4,8,128]{3,2,1,0:T(8,128)S(1)}, f32[26,4,8,128]{3,2,1,0:T(8,128)S(1)}, u32[]{:S(2)}, u32[]{:S(2)}) collective-permute-start(f32[26,4,8,128]{3,2,1,0:T(8,128)S(1)} %get-tuple-element.60), channel_id=1, source_target_pairs={{0,1},{1,0},{2,3},{3,2},{4,5},{5,4},{6,7},{7,6},{8,9},{9,8},{10,11... | collective-permute-start | bytes 1277960 | tf_op jit(solution)/shard_map/ppermute | solution.py:353
  138.3 1.2 copy-start
  148.1 13.5 %collective-permute-start.19 = (f32[96,128]{1,0:T(8,128)S(1)}, f32[96,128]{1,0:T(8,128)S(1)}, u32[]{:S(2)}, u32[]{:S(2)}) collective-permute-start(f32[96,128]{1,0:T(8,128)S(1)} %get-tuple-element.63), channel_id=1, source_target_pairs={{0,32},{32,0},{64,96},{96,64},{128,160},{160,128},{192,224},{224,1... | collective-permute-start | bytes 147464 | tf_op jit(solution)/shard_map/ppermute | solution.py:344
  150.9 12.3 %collective-permute-start.20 = (f32[96,128]{1,0:T(8,128)S(1)}, f32[96,128]{1,0:T(8,128)S(1)}, u32[]{:S(2)}, u32[]{:S(2)}) collective-permute-start(f32[96,128]{1,0:T(8,128)S(1)} %get-tuple-element.64), channel_id=1, source_target_pairs={{0,64},{32,96},{64,0},{96,32},{128,192},{160,224},{192,128},{224,1... | collective-permute-start | bytes 147464 | tf_op jit(solution)/shard_map/ppermute | solution.py:344
  158.5 6.2 %collective-permute-start.21 = (f32[96,128]{1,0:T(8,128)S(1)}, f32[96,128]{1,0:T(8,128)S(1)}, u32[]{:S(2)}, u32[]{:S(2)}) collective-permute-start(f32[96,128]{1,0:T(8,128)S(1)} %get-tuple-element.65), channel_id=1, source_target_pairs={{0,96},{32,64},{64,32},{96,0},{128,224},{160,192},{192,160},{224,1... | collective-permute-start | bytes 147464 | tf_op jit(solution)/shard_map/ppermute | solution.py:344
  158.5 6.2 %collective-permute-start.22 = (f32[96,128]{1,0:T(8,128)S(1)}, f32[96,128]{1,0:T(8,128)S(1)}, u32[]{:S(2)}, u32[]{:S(2)}) collective-permute-start(f32[96,128]{1,0:T(8,128)S(1)} %get-tuple-element.66), channel_id=1, source_target_pairs={{0,128},{32,160},{64,192},{96,224},{128,0},{160,32},{192,64},{224,... | collective-permute-start | bytes 147464 | tf_op jit(solution)/shard_map/ppermute | solution.py:344
  161.1 5.2 %collective-permute-start.23 = (f32[96,128]{1,0:T(8,128)S(1)}, f32[96,128]{1,0:T(8,128)S(1)}, u32[]{:S(2)}, u32[]{:S(2)}) collective-permute-start(f32[96,128]{1,0:T(8,128)S(1)} %get-tuple-element.67), channel_id=1, source_target_pairs={{0,160},{32,128},{64,224},{96,192},{128,32},{160,0},{192,96},{224,... | collective-permute-start | bytes 147464 | tf_op jit(solution)/shard_map/ppermute | solution.py:344
  161.6 6.1 %collective-permute-start.24 = (f32[96,128]{1,0:T(8,128)S(1)}, f32[96,128]{1,0:T(8,128)S(1)}, u32[]{:S(2)}, u32[]{:S(2)}) collective-permute-start(f32[96,128]{1,0:T(8,128)S(1)} %get-tuple-element.68), channel_id=1, source_target_pairs={{0,192},{32,224},{64,128},{96,160},{128,64},{160,96},{192,0},{224,... | collective-permute-start | bytes 147464 | tf_op jit(solution)/shard_map/ppermute | solution.py:344
  163.1 5.4 %collective-permute-start.25 = (f32[96,128]{1,0:T(8,128)S(1)}, f32[96,128]{1,0:T(8,128)S(1)}, u32[]{:S(2)}, u32[]{:S(2)}) collective-permute-start(f32[96,128]{1,0:T(8,128)S(1)} %get-tuple-element.69), channel_id=1, source_target_pairs={{0,224},{32,192},{64,160},{96,128},{128,96},{160,64},{192,32},{224... | collective-permute-start | bytes 147464 | tf_op jit(solution)/shard_map/ppermute | solution.py:344

commit v2 on v1

--- a/solution.py
+++ b/solution.py
@@ -16,6 +16,7 @@
 OWN = 12
 HALO = 4
 WIN = OWN + 2 * HALO
+TALL = 24
 
 
 def transform_matrices():
@@ -56,12 +57,16 @@
         in_specs=[smem] * scalars + [vmem] * n_in,
         out_specs=[vmem] * len(outs),
         scratch_shapes=list(scratch),
-        compiler_params=pltpu.CompilerParams(vmem_limit_bytes=48 * 1024 * 1024),
+        compiler_params=pltpu.CompilerParams(vmem_limit_bytes=16 * 1024 * 1024),
     )
 
 
-def pack_body(pos, state, adjoint, target, *rest):
-    outs, stage = rest[:8], rest[8]
+def rows(lo, hi, body):
+    lax.fori_loop(lo, hi, body, 0, unroll=True)
+
+
+def pack_body(pos, state, adjoint, target, kappa, begin, *rest):
+    outs, (near, far, here, stage) = rest[:8], rest[8:]
     t = pos[0]
     flip = pos[1]
     for f, ref in enumerate((state, adjoint, target)):
@@ -78,6 +83,71 @@
                         stage[d, base + last - low : base + WIN, :] = jnp.zeros((low + WIN - last, 128), jnp.float32)
     for k in range(8):
         outs[k][...] = stage[t ^ k]
+    for d in range(8):
+        @pl.when(t == d)
+        def window(d=d):
+            low = OWN * d - HALO
+            first, last = max(low, 0), min(low + TALL, 96)
+            parts = []
+            for ref, x in ((kappa, 0), (kappa, 1), (begin, 0), (begin, 1)):
+                v = ref[x ^ flip, first:last, :]
+                if first > low:
+                    v = jnp.concatenate([jnp.zeros((first - low, 128), jnp.float32), v], 0)
+                if last < low + TALL:
+                    v = jnp.concatenate([v, jnp.zeros((low + TALL - last, 128), jnp.float32)], 0)
+                parts.append(v)
+            for i, v in enumerate(parts):
+                here[i] = v
+            for i, q in enumerate((0, 1, 2)):
+                near[i] = parts[q]
+            for i, q in enumerate((1, 0, 3)):
+                far[i] = parts[q]
+
+
+def coefficient_body(pos, here, near, far, consts, weights, inv):
+    t, flip, s = pos[0], pos[1], pos[2]
+    kappa = [near[1], near[0], here[0], here[1], far[0], far[1]]
+    begin = [near[2], here[2], here[3], far[2]]
+    lane = lax.broadcasted_iota(jnp.int32, (TALL, 128), 1)
+    row = lax.broadcasted_iota(jnp.int32, (TALL, 128), 0) + (OWN * t - HALO)
+    half = 0.5 * TAU
+    for p in range(1, 5):
+        plane = jnp.where(flip == 1, 2 * s + 3 - p, 2 * s - 2 + p)
+        ahead = jnp.where(flip == 1, plane - 1, plane + 1)
+        behind = jnp.where(flip == 1, plane + 1, plane - 1)
+        real = jnp.where((plane >= 0) & (plane < 64), half, 0.0)
+        to_ahead = jnp.where((ahead >= 0) & (ahead < 64), real, 0.0)
+        to_behind = jnp.where((behind >= 0) & (behind < 64), real, 0.0)
+        k = kappa[p]
+        row_ok = (row >= 0) & (row < 96)
+        xp = k + kappa[p + 1]
+        xm = k + kappa[p - 1]
+        yp = k + pltpu.roll(k, TALL - 1, 0)
+        ym = k + pltpu.roll(k, 1, 0)
+        zp = k + jnp.where(lane < 127, pltpu.roll(k, 127, 1), 0.0)
+        zm = k + jnp.where(lane > 0, pltpu.roll(k, 1, 1), 0.0)
+        kinds = [
+            jnp.where(row_ok, xp * to_ahead, 0.0),
+            jnp.where(row_ok, xm * to_behind, 0.0),
+            jnp.where(row_ok & (row < 95), yp * real, 0.0),
+            jnp.where(row_ok & (row > 0), ym * real, 0.0),
+            jnp.where(row_ok & (lane < 127), zp * real, 0.0),
+            jnp.where(row_ok & (lane > 0), zm * real, 0.0),
+            half * (((xp + xm) + (yp + ym)) + (zp + zm)),
+            begin[p - 1],
+        ]
+        for i, v in enumerate(kinds):
+            weights[pl.ds((p - 1) * TALL * 8 + i, TALL, stride=8), :] = v
+    ca, cb, lag = consts[0], consts[1], consts[2]
+    base = lag * lag + DET_SHIFT
+    for p, lo, hi in ((2, 1, 19), (3, 1, 19), (1, 2, 18), (4, 2, 18)):
+        for j in range(lo, hi):
+            td = jnp.broadcast_to(weights[pl.ds(((p - 1) * TALL + j) * 8 + 6, 1), :], (8, 128))
+            a = ca + td
+            b = cb + td
+            at = region(p, j)
+            inv[at, 0] = 1.0 / (a * a + base)
+            inv[at, 1] = 1.0 / (b * b + base)
 
 
 def spread_body(pos, *rest):
@@ -125,7 +195,7 @@
 
 
 def row_weights(weights, p, j, count):
-    tile = weights[(p - 1) * WIN + j]
+    tile = weights[(p - 1) * TALL + j]
     return [jnp.broadcast_to(tile[k : k + 1, :], (8, 128)) for k in range(count)]
 
 
@@ -141,22 +211,6 @@
         (TAU * ur + a * pr - lag * pi) * inv_a,
         (TAU * ui + b * pi + lag * pr) * inv_b,
     )
-
-
-def inverse_body(weights, consts, inv):
-    ca, cb, lag = consts[0], consts[1], consts[2]
-    base = lag * lag + DET_SHIFT
-    for p, lo, hi in ((2, 1, 19), (3, 1, 19), (1, 2, 18), (4, 2, 18)):
-        def row(j, carry, p=p):
-            tile = weights[(p - 1) * WIN + j]
-            td = jnp.broadcast_to(tile[6:7, :], (8, 128))
-            a = ca + td
-            b = cb + td
-            at = region(p, j)
-            inv[at, 0] = 1.0 / (a * a + base)
-            inv[at, 1] = 1.0 / (b * b + base)
-            return carry
-        lax.fori_loop(lo, hi, row, 0)
 
 
 def residual_body(own, wish, near, far, tnear, tfar, weights, consts, inv, forward, rhs, it, out_near, out_far, res, zed):
@@ -195,14 +249,14 @@
             res[at, 2] = -TAU * wanted(p, j, 0) - (pe - po + (td * pe - n[2]) - TAU * ue)
             res[at, 3] = -TAU * wanted(p, j, 1) - (po - after + (td * po - n[3]) - TAU * uo)
             return carry
-        lax.fori_loop(lo, hi, row, 0)
+        rows(lo, hi, row)
 
     def group(g, carry):
         block = res[pl.ds(g * 4, 4)].reshape(128, 128)
         done = jnp.dot(forward[...], block, precision=lax.Precision.HIGHEST, preferred_element_type=jnp.float32)
         rhs[pl.ds(g * 4, 4)] = done.reshape(4, 4, 8, 128)
         return carry
-    lax.fori_loop(0, 17, group, 0)
+    rows(0, 17, group)
 
     cs = (consts[0], consts[1], consts[2])
     for p, lo, hi in ((2, 1, 19), (3, 1, 19), (1, 2, 18), (4, 2, 18)):
@@ -213,7 +267,7 @@
             for c in range(4):
                 zed[at, c] = z[c]
             return carry
-        lax.fori_loop(lo, hi, row, 0)
+        rows(lo, hi, row)
 
     for p in (2, 3):
         def row(j, carry, p=p):
@@ -227,7 +281,7 @@
             for c in range(4):
                 it[p - 2, j - 2, c] = z[c]
             return carry
-        lax.fori_loop(2, 18, row, 0)
+        rows(2, 18, row)
     out_near[0:14] = it[0, 1:15]
     out_near[14:26] = it[1, 2:14]
     out_far[0:14] = it[1, 1:15]
@@ -261,7 +315,7 @@
             for c in range(4):
                 zed[at2(p, j), c] = z[c]
             return carry
-        lax.fori_loop(lo, hi, row, 0)
+        rows(lo, hi, row)
     for p in (2, 3):
         def row(j, carry, p=p):
             w = row_weights(weights, p, j, 8)
@@ -275,14 +329,14 @@
             for c in range(4):
                 fin[(p - 2) * OWN + j - 4, c] = z[c]
             return carry
-        lax.fori_loop(4, 16, row, 0)
+        rows(4, 16, row)
 
     def group(g, carry):
         block = fin[pl.ds(g * 4, 4)].reshape(128, 128)
         done = jnp.dot(back[...], block, precision=lax.Precision.HIGHEST, preferred_element_type=jnp.float32)
         fin[pl.ds(g * 4, 4)] = done.reshape(4, 4, 8, 128)
         return carry
-    lax.fori_loop(0, 6, group, 0)
+    rows(0, 6, group)
 
 
 def middle_body(pos, it, near, far, rhs, weights, consts, inv, back, own, new, send0, send1, zed, fin):
@@ -353,62 +407,28 @@
     return lax.ppermute(block, axis, route)
 
 
-def face_weights(kappa, first_state, t, s, flip):
-    mid = kappa[1:5, 1:-1]
-    lane = lax.broadcasted_iota(jnp.int32, mid.shape, 2)
-    row = lax.broadcasted_iota(jnp.int32, mid.shape, 1) + OWN * t - HALO
-    local = lax.broadcasted_iota(jnp.int32, mid.shape, 0)
-    plane = jnp.where(flip == 1, 2 * s + 2 - local, 2 * s - 1 + local)
-    ahead = jnp.where(flip == 1, -1, 1)
-    half = 0.5 * TAU
-    xp = half * (mid + kappa[2:6, 1:-1])
-    xm = half * (mid + kappa[0:4, 1:-1])
-    yp = half * (mid + kappa[1:5, 2:])
-    ym = half * (mid + kappa[1:5, :-2])
-    zp = half * (mid + jnp.pad(mid[..., 1:], ((0, 0), (0, 0), (0, 1))))
-    zm = half * (mid + jnp.pad(mid[..., :-1], ((0, 0), (0, 0), (1, 0))))
-    td = xp + xm + yp + ym + zp + zm
-    inside = lambda q, n: (q >= 0) & (q < n)
-    here = inside(plane, 64) & inside(row, 96)
-    keep = lambda w, ok: jnp.where(here & ok, w, 0.0)
-    kinds = [
-        keep(xp, inside(plane + ahead, 64)),
-        keep(xm, inside(plane - ahead, 64)),
-        keep(yp, row + 1 < 96),
-        keep(ym, row > 0),
-        keep(zp, lane < 127),
-        keep(zm, lane > 0),
-        td,
-        first_state,
-    ]
-    return jnp.stack(kinds, 2).reshape(4 * WIN, 8, 128)
-
-
 def on_device(state_guess, adjoint_guess, target, initial_state, diffusivity):
     t = lax.axis_index("tm").astype(jnp.int32)
     s = lax.axis_index("space").astype(jnp.int32)
     flip = s & 1
-    pos = jnp.stack([t, flip])
+    pos = jnp.stack([t, flip, s])
     forward, back = (jnp.asarray(m) for m in transform_matrices())
     consts = jnp.asarray(mode_constants())
 
-    pieces = call(
-        pack_body, "pack", [whole(12 * WIN, 128)] * 8, 3, [pltpu.VMEM((8, 12 * WIN, 128), jnp.float32)]
-    )(pos, state_guess, adjoint_guess, target)
-
-    both = jnp.concatenate([diffusivity, initial_state], 0)
-    both = jnp.where(flip == 1, both[jnp.array([1, 0, 3, 2])], both)
-    both = jnp.pad(both, ((0, 0), (HALO + 2, HALO + 2), (0, 0)))
-    both = lax.dynamic_slice_in_dim(both, OWN * t, 24, 1)
-    far_c = swap(jnp.stack([both[1], both[0], both[3]]), "space", 0)
-    near_c = swap(jnp.stack([both[0], both[1], both[2]]), "space", 1)
-
+    *pieces, near_c, far_c, here_c = call(
+        pack_body,
+        "pack",
+        [whole(12 * WIN, 128)] * 8 + [whole(3, TALL, 128)] * 2 + [whole(4, TALL, 128)],
+        5,
+        [pltpu.VMEM((8, 12 * WIN, 128), jnp.float32)],
+    )(pos, state_guess, adjoint_guess, target, diffusivity, initial_state)
+    far_c = swap(far_c, "space", 0)
+    near_c = swap(near_c, "space", 1)
     got = exchange(pieces)
-
-    kappa = jnp.stack([near_c[1], near_c[0], both[0], both[1], far_c[0], far_c[1]])[:, 1:23]
-    begin = jnp.stack([near_c[2], both[2], both[3], far_c[2]])[:, 2:22]
-    weights = face_weights(kappa, begin, t, s, flip)
-    inv = call(inverse_body, "inverse", [whole(68, 2, 8, 128)], 2, scalars=0)(weights, consts)[0]
+    weights, inv = call(
+        coefficient_body, "coefficients", [whole(4 * TALL * 8, 128), whole(68, 2, 8, 128)], 4
+    )(pos, here_c, near_c, far_c, consts)
+    weights = weights.reshape(4 * TALL, 8, 128)
 
     own, wish, near, far = call(
         spread_body,

time: 171 us -> 132 us (0.77)
  Pallas kernels: 48 us -> 13.2 us
  local copies, waits for them, and re-layouts: 8.81 us -> 4.59 us
  other arithmetic: 3.89 us -> 0.08 us
  waiting for transfers between devices: 57.5 us -> 61.3 us
    pallas_call x2, Pallas kernels: 26.1 us -> 4.68 us  [on_device(): call(residual_body, 'residual', [whole(68, 4, 8, 128), whole(2, 16, 4, 8,...]
    pallas_call x1, Pallas kernels: 8.51 us -> 2.15 us  [on_device(): call(last_body, 'last', [whole(8 * OWN, 128)] * 8, 9, sweep_scratch + [pl...]
    pallas_call x1, Pallas kernels: 8.27 us -> 1.97 us  [on_device(): call(middle_body, 'middle', [whole(2, OWN, 4, 8, 128), whole(2, HALO, 4,...]
    another operation x9 -> x0, local copies, waits for them, and re-layouts: 5.03 us -> none  [face_weights(): return jnp.stack(kinds, 2).reshape(4 * WIN, 8, 128)]
    ppermute x12, waiting for transfers between devices: 43.4 us -> 45.9 us  [swap(): return lax.ppermute(block, axis, route)]
    unnamed x15 -> x16, local copies, waits for them, and re-layouts: 2.17 us -> 4.59 us
  transfers between devices with their start and end apart: 26 -> 26, of which waited for: 14 -> 17; matrix products, arithmetic and copies ran while one was open for 5% -> 0% of each run, Pallas kernels for 1% -> 1%
where the time goes in v2:
time: 132 us; the launch traced here: 131 us
  waiting for transfers between devices  61.3 us (46%)
  starting transfers between devices  51.4 us (39%)
  Pallas kernels  13.2 us (10%)
  local copies, waits for them, and re-layouts  4.59 us (3%)
    ppermute x12, waiting for transfers between devices, swap(): return lax.ppermute(block, axis, route)  45.9 us
    ppermute x12, starting transfers between devices, swap(): return lax.ppermute(block, axis, route)  26.2 us
    ppermute x14, starting transfers between devices, exchange(): lax.ppermute(pieces[k], 'tm', [(i, i ^ k) for i in range(count)])  25.2 us
    ppermute x14, waiting for transfers between devices, exchange(): lax.ppermute(pieces[k], 'tm', [(i, i ^ k) for i in range(count)])  15.5 us
    pallas_call x2, Pallas kernels, on_device(): call(residual_body, 'residual', [whole(68, 4, 8, 128), whole(2, 16, 4, 8,...  4.68 us
    unnamed x16, local copies, waits for them, and re-layouts  4.59 us
  transfers between devices with their start and end apart: 26, of which 17 were waited for; matrix products, arithmetic and copies ran while one was open for 0% of the time, Pallas kernels for 1%

profile of v2, /device:TPU:6, one launch (start us, length us, event | category | flops | bytes accessed | tf_op | source)
XLA Modules:
  0.0 131.5 jit_solution(1250585013119602526)
XLA Ops:
  0.7 0.9 copy-done.3
  1.7 0.9 copy-done.4
  2.6 0.9 copy-done.5
  3.5 0.9 copy-done.6
  4.4 0.9 copy-done.7
  5.3 0.7 pack.1
  6.1 1.7 %collective-permute-start.1 = (f32[240,128]{1,0:T(8,128)S(1)}, f32[240,128]{1,0:T(8,128)S(1)}, u32[]{:S(2)}, u32[]{:S(2)}) collective-permute-start(f32[240,128]{1,0:T(8,128)S(1)} %get-tuple-element.43), channel_id=1, source_target_pairs={{0,64},{32,96},{64,0},{96,32},{128,192},{160,224},{192,128},{224,1... | collective-permute-start | bytes 368648 | tf_op jit(solution)/shard_map/ppermute | solution.py:398
  7.8 0.2 collective-permute-start.2
  8.0 3.2 %collective-permute-start.3 = (f32[240,128]{1,0:T(8,128)S(1)}, f32[240,128]{1,0:T(8,128)S(1)}, u32[]{:S(2)}, u32[]{:S(2)}) collective-permute-start(f32[240,128]{1,0:T(8,128)S(1)} %get-tuple-element.45), channel_id=1, source_target_pairs={{0,128},{32,160},{64,192},{96,224},{128,0},{160,32},{192,64},{224,... | collective-permute-start | bytes 368648 | tf_op jit(solution)/shard_map/ppermute | solution.py:398
  11.2 3.0 %collective-permute-start.5 = (f32[240,128]{1,0:T(8,128)S(1)}, f32[240,128]{1,0:T(8,128)S(1)}, u32[]{:S(2)}, u32[]{:S(2)}) collective-permute-start(f32[240,128]{1,0:T(8,128)S(1)} %get-tuple-element.47), channel_id=1, source_target_pairs={{0,192},{32,224},{64,128},{96,160},{128,64},{160,96},{192,0},{224,... | collective-permute-start | bytes 368648 | tf_op jit(solution)/shard_map/ppermute | solution.py:398
  14.2 0.1 collective-permute-start.6
  14.4 5.8 %collective-permute-done.3.rest_4_ = f32[240,128]{1,0:T(8,128)S(1)} collective-permute-done((f32[240,128]{1,0:T(8,128)S(1)}, f32[240,128]{1,0:T(8,128)S(1)}, u32[]{:S(2)}, u32[]{:S(2)}) %collective-permute-start.3) | collective-permute-done | bytes 122912 | tf_op jit(solution)/shard_map/ppermute | solution.py:398
  20.2 1.7 %collective-permute-done.4.rest_5_ = f32[240,128]{1,0:T(8,128)S(1)} collective-permute-done((f32[240,128]{1,0:T(8,128)S(1)}, f32[240,128]{1,0:T(8,128)S(1)}, u32[]{:S(2)}, u32[]{:S(2)}) %collective-permute-start.4) | collective-permute-done | bytes 122912 | tf_op jit(solution)/shard_map/ppermute | solution.py:398
  21.9 2.0 %collective-permute-done.5.rest_6_ = f32[240,128]{1,0:T(8,128)S(1)} collective-permute-done((f32[240,128]{1,0:T(8,128)S(1)}, f32[240,128]{1,0:T(8,128)S(1)}, u32[]{:S(2)}, u32[]{:S(2)}) %collective-permute-start.5) | collective-permute-done | bytes 122912 | tf_op jit(solution)/shard_map/ppermute | solution.py:398
  23.8 1.8 %collective-permute-done.6.rest_7_ = f32[240,128]{1,0:T(8,128)S(1)} collective-permute-done((f32[240,128]{1,0:T(8,128)S(1)}, f32[240,128]{1,0:T(8,128)S(1)}, u32[]{:S(2)}, u32[]{:S(2)}) %collective-permute-start.6) | collective-permute-done | bytes 122912 | tf_op jit(solution)/shard_map/ppermute | solution.py:398
  25.7 0.9 spread.1
  26.6 8.0 %collective-permute-start.7 = (f32[168,8,128]{2,1,0:T(8,128)S(1)}, f32[168,8,128]{2,1,0:T(8,128)S(1)}, u32[]{:S(2)}, u32[]{:S(2)}) collective-permute-start(f32[168,8,128]{2,1,0:T(8,128)S(1)} %get-tuple-element.51), channel_id=1, source_target_pairs={{1,2},{2,1},{3,4},{4,3},{5,6},{6,5},{7,8},{8,7},{9,10},{10,9},{11,... | collective-permute-start | bytes 2064392 | tf_op jit(solution)/shard_map/ppermute | solution.py:407
  34.7 3.9 %collective-permute-start.9 = (f32[3,24,128]{2,1,0:T(8,128)S(1)}, f32[3,24,128]{2,1,0:T(8,128)S(1)}, u32[]{:S(2)}, u32[]{:S(2)}) collective-permute-start(f32[3,24,128]{2,1,0:T(8,128)S(1)} %get-tuple-element.54), channel_id=1, source_target_pairs={{1,2},{2,1},{3,4},{4,3},{5,6},{6,5},{7,8},{8,7},{9,10},{10,9},{11,... | collective-permute-start | bytes 110600 | tf_op jit(solution)/shard_map/ppermute | solution.py:407
  38.6 0.8 collective-permute-start.10
  39.5 11.8 %collective-permute-done.9.near = f32[3,24,128]{2,1,0:T(8,128)S(1)} collective-permute-done((f32[3,24,128]{2,1,0:T(8,128)S(1)}, f32[3,24,128]{2,1,0:T(8,128)S(1)}, u32[]{:S(2)}, u32[]{:S(2)}) %collective-permute-start.9) | collective-permute-done | bytes 36896 | tf_op jit(solution)/shard_map/ppermute | solution.py:407
  51.2 1.6 %collective-permute-done.10.far = f32[3,24,128]{2,1,0:T(8,128)S(1)} collective-permute-done((f32[3,24,128]{2,1,0:T(8,128)S(1)}, f32[3,24,128]{2,1,0:T(8,128)S(1)}, u32[]{:S(2)}, u32[]{:S(2)}) %collective-permute-start.10) | collective-permute-done | bytes 36896 | tf_op jit(solution)/shard_map/ppermute | solution.py:407
  52.8 0.8 coefficients.1
  53.6 2.3 %residual.2 = (f32[68,4,8,128]{3,2,1,0:T(8,128)S(1)}, f32[2,16,4,8,128]{4,3,2,1,0:T(8,128)S(1)}, f32[26,4,8,128]{3,2,1,0:T(8,128)S(1)}, f32[26,4,8,128]{3,2,1,0:T(8,128)S(1)}) custom-call(f32[2,20,4,8,128]{4,3,2,1,0:T(8,128)S(1)} %get-tuple-element.49.own, f32[2,18,2,8,128]{4,3,2,1,0:T(8,128)S(1)} %get-tuple-element.50.wish, ...), custom_call_target="tpu_custom_call" | custom-call | tf_op jit(solution)/shard_map/residual/pallas_call | solution.py:447
  56.0 4.2 %collective-permute-start.11 = (f32[26,4,8,128]{3,2,1,0:T(8,128)S(1)}, f32[26,4,8,128]{3,2,1,0:T(8,128)S(1)}, u32[]{:S(2)}, u32[]{:S(2)}) collective-permute-start(f32[26,4,8,128]{3,2,1,0:T(8,128)S(1)} %get-tuple-element.59), channel_id=1, source_target_pairs={{1,2},{2,1},{3,4},{4,3},{5,6},{6,5},{7,8},{8,7},{9,10},{10,9},{11,... | collective-permute-start | bytes 1277960 | tf_op jit(solution)/shard_map/ppermute | solution.py:407
  60.3 10.5 %collective-permute-done.11.near = f32[26,4,8,128]{3,2,1,0:T(8,128)S(1)} collective-permute-done((f32[26,4,8,128]{3,2,1,0:T(8,128)S(1)}, f32[26,4,8,128]{3,2,1,0:T(8,128)S(1)}, u32[]{:S(2)}, u32[]{:S(2)}) %collective-permute-start.11) | collective-permute-done | bytes 426016 | tf_op jit(solution)/shard_map/ppermute | solution.py:407
  70.8 0.3 collective-permute-done.12.far
  71.1 2.0 %middle.1 = (f32[2,12,4,8,128]{4,3,2,1,0:T(8,128)S(1)}, f32[2,4,4,8,128]{4,3,2,1,0:T(8,128)S(1)}, f32[2,4,4,8,128]{4,3,2,1,0:T(8,128)S(1)}) custom-call(s32[3]{0:T(128)S(1)} %pad_add_fusion.pos, f32[2,16,4,8,128]{4,3,2,1,0:T(8,128)S(1)} %get-tuple-element.58.it, f32[26,4,8,128]{3,2,1,0:T(8,128)S(1)} %collective-permute-done.11.near, ...), custom_call_target="tpu_custom_call" | custom-call | tf_op jit(solution)/shard_map/middle/pallas_call | solution.py:458
  73.2 0.7 collective-permute-start.14
  73.9 0.7 collective-permute-done.13.got0
  74.5 0.7 widen.1
  75.2 4.2 %collective-permute-start.15 = (f32[136,8,128]{2,1,0:T(8,128)S(1)}, f32[136,8,128]{2,1,0:T(8,128)S(1)}, u32[]{:S(2)}, u32[]{:S(2)}) collective-permute-start(f32[136,8,128]{2,1,0:T(8,128)S(1)} %get-tuple-element.66), channel_id=1, source_target_pairs={{1,2},{2,1},{3,4},{4,3},{5,6},{6,5},{7,8},{8,7},{9,10},{10,9},{11,... | collective-permute-start | bytes 1671176 | tf_op jit(solution)/shard_map/ppermute | solution.py:407
  79.4 0.3 collective-permute-start.16
  79.7 10.5 %collective-permute-done.15.near = f32[136,8,128]{2,1,0:T(8,128)S(1)} collective-permute-done((f32[136,8,128]{2,1,0:T(8,128)S(1)}, f32[136,8,128]{2,1,0:T(8,128)S(1)}, u32[]{:S(2)}, u32[]{:S(2)}) %collective-permute-start.15) | collective-permute-done | bytes 557088 | tf_op jit(solution)/shard_map/ppermute | solution.py:407
  90.2 0.7 collective-permute-done.16.far
  90.9 2.3 %residual.3 = (f32[68,4,8,128]{3,2,1,0:T(8,128)S(1)}, f32[2,16,4,8,128]{4,3,2,1,0:T(8,128)S(1)}, f32[26,4,8,128]{3,2,1,0:T(8,128)S(1)}, f32[26,4,8,128]{3,2,1,0:T(8,128)S(1)}) custom-call(f32[2,20,4,8,128]{4,3,2,1,0:T(8,128)S(1)} %get-tuple-element.65.own, f32[2,18,2,8,128]{4,3,2,1,0:T(8,128)S(1)} %get-tuple-element.50.wish, ...), custom_call_target="tpu_custom_call" | custom-call | tf_op jit(solution)/shard_map/residual/pallas_call | solution.py:447
  93.3 3.8 %collective-permute-start.17 = (f32[26,4,8,128]{3,2,1,0:T(8,128)S(1)}, f32[26,4,8,128]{3,2,1,0:T(8,128)S(1)}, u32[]{:S(2)}, u32[]{:S(2)}) collective-permute-start(f32[26,4,8,128]{3,2,1,0:T(8,128)S(1)} %get-tuple-element.69), channel_id=1, source_target_pairs={{1,2},{2,1},{3,4},{4,3},{5,6},{6,5},{7,8},{8,7},{9,10},{10,9},{11,... | collective-permute-start | bytes 1277960 | tf_op jit(solution)/shard_map/ppermute | solution.py:407
  97.1 9.7 %collective-permute-done.17.near = f32[26,4,8,128]{3,2,1,0:T(8,128)S(1)} collective-permute-done((f32[26,4,8,128]{3,2,1,0:T(8,128)S(1)}, f32[26,4,8,128]{3,2,1,0:T(8,128)S(1)}, u32[]{:S(2)}, u32[]{:S(2)}) %collective-permute-start.17) | collective-permute-done | bytes 426016 | tf_op jit(solution)/shard_map/ppermute | solution.py:407
  106.8 0.1 collective-permute-done.18.far
  106.9 2.1 %last.1 = (f32[96,128]{1,0:T(8,128)S(1)}, f32[96,128]{1,0:T(8,128)S(1)}, f32[96,128]{1,0:T(8,128)S(1)}, f32[96,128]{1,0:T(8,128)S(1)}, f32[96,128]{1,0:T(8,128)S...) custom-call(s32[3]{0:T(128)S(1)} %pad_add_fusion.pos, ...), custom_call_target="tpu_custom_call" | custom-call | tf_op jit(solution)/shard_map/last/pallas_call | solution.py:470
  109.1 3.0 %collective-permute-start.19 = (f32[96,128]{1,0:T(8,128)S(1)}, f32[96,128]{1,0:T(8,128)S(1)}, u32[]{:S(2)}, u32[]{:S(2)}) collective-permute-start(f32[96,128]{1,0:T(8,128)S(1)} %get-tuple-element.73), channel_id=1, source_target_pairs={{0,32},{32,0},{64,96},{96,64},{128,160},{160,128},{192,224},{224,1... | collective-permute-start | bytes 147464 | tf_op jit(solution)/shard_map/ppermute | solution.py:398
  112.0 7.6 %collective-permute-start.20 = (f32[96,128]{1,0:T(8,128)S(1)}, f32[96,128]{1,0:T(8,128)S(1)}, u32[]{:S(2)}, u32[]{:S(2)}) collective-permute-start(f32[96,128]{1,0:T(8,128)S(1)} %get-tuple-element.74), channel_id=1, source_target_pairs={{0,64},{32,96},{64,0},{96,32},{128,192},{160,224},{192,128},{224,1... | collective-permute-start | bytes 147464 | tf_op jit(solution)/shard_map/ppermute | solution.py:398
  119.7 3.1 %collective-permute-start.22 = (f32[96,128]{1,0:T(8,128)S(1)}, f32[96,128]{1,0:T(8,128)S(1)}, u32[]{:S(2)}, u32[]{:S(2)}) collective-permute-start(f32[96,128]{1,0:T(8,128)S(1)} %get-tuple-element.76), channel_id=1, source_target_pairs={{0,128},{32,160},{64,192},{96,224},{128,0},{160,32},{192,64},{224,... | collective-permute-start | bytes 147464 | tf_op jit(solution)/shard_map/ppermute | solution.py:398
  122.8 1.8 %collective-permute-start.24 = (f32[96,128]{1,0:T(8,128)S(1)}, f32[96,128]{1,0:T(8,128)S(1)}, u32[]{:S(2)}, u32[]{:S(2)}) collective-permute-start(f32[96,128]{1,0:T(8,128)S(1)} %get-tuple-element.78), channel_id=1, source_target_pairs={{0,192},{32,224},{64,128},{96,160},{128,64},{160,96},{192,0},{224,... | collective-permute-start | bytes 147464 | tf_op jit(solution)/shard_map/ppermute | solution.py:398
  124.6 1.3 %collective-permute-start.25 = (f32[96,128]{1,0:T(8,128)S(1)}, f32[96,128]{1,0:T(8,128)S(1)}, u32[]{:S(2)}, u32[]{:S(2)}) collective-permute-start(f32[96,128]{1,0:T(8,128)S(1)} %get-tuple-element.79), channel_id=1, source_target_pairs={{0,224},{32,192},{64,160},{96,128},{128,96},{160,64},{192,32},{224... | collective-permute-start | bytes 147464 | tf_op jit(solution)/shard_map/ppermute | solution.py:398
  126.0 2.1 %collective-permute-done.23.rest_5_ = f32[96,128]{1,0:T(8,128)S(1)} collective-permute-done((f32[96,128]{1,0:T(8,128)S(1)}, f32[96,128]{1,0:T(8,128)S(1)}, u32[]{:S(2)}, u32[]{:S(2)}) %collective-permute-start.23) | collective-permute-done | bytes 49184 | tf_op jit(solution)/shard_map/ppermute | solution.py:398
  128.2 1.3 collective-permute-done.24.rest_6_
  129.4 0.7 collective-permute-done.25.rest_7_
  130.1 1.3 %unpack.1 = (f32[2,2,96,128]{3,2,1,0:T(8,128)}, f32[2,2,96,128]{3,2,1,0:T(8,128)}) custom-call(s32[3]{0:T(128)S(1)} %pad_add_fusion.pos, f32[96,128]{1,0:T(8,128)S(1)} %get-tuple-element.72.rest_0_, f32[96,128]{1,0:T(8,128)S(1)} %collective-permute-done.19.rest_1_, f32[96,128]{1,0:T(8,128)S(1)} %collective-permute-done.20.rest_2_, ...), custom_call_target="tpu_custom_call" | custom-call | tf_op jit(solution)/shard_map/unpack/pallas_call | solution.py:479
  (30 shorter events, 0.8 us)
Async XLA Ops:
  0.6 52.2 %copy-start = (f32[3,8,128]{2,1,0:T(8,128)S(1)}, f32[3,8,128]{2,1,0:T(8,128)}, u32[]{:S(2)}) copy-start(f32[3,8,128]{2,1,0:T(8,128)} %constant.19.clone.consts) | copy-start | bytes 36868
  0.6 53.0 %copy-start.2 = (f32[128,128]{1,0:T(8,128)S(1)}, f32[128,128]{1,0:T(8,128)}, u32[]{:S(2)}) copy-start(f32[128,128]{1,0:T(8,128)} %constant.17.clone.forward) | copy-start | bytes 196612
  0.7 0.9 copy-start.3
  1.7 0.9 copy-start.4
  2.6 0.9 copy-start.5
  3.5 0.9 copy-start.6
  4.4 0.9 copy-start.7
  6.0 5.2 %collective-permute-start = (f32[240,128]{1,0:T(8,128)S(1)}, f32[240,128]{1,0:T(8,128)S(1)}, u32[]{:S(2)}, u32[]{:S(2)}) collective-permute-start(f32[240,128]{1,0:T(8,128)S(1)} %get-tuple-element.42), channel_id=1, source_target_pairs={{0,32},{32,0},{64,96},{96,64},{128,160},{160,128},{192,224},{224,1... | collective-permute-start | bytes 368648 | tf_op jit(solution)/shard_map/ppermute | solution.py:398
  6.1 8.1 %collective-permute-start.1 = (f32[240,128]{1,0:T(8,128)S(1)}, f32[240,128]{1,0:T(8,128)S(1)}, u32[]{:S(2)}, u32[]{:S(2)}) collective-permute-start(f32[240,128]{1,0:T(8,128)S(1)} %get-tuple-element.43), channel_id=1, source_target_pairs={{0,64},{32,96},{64,0},{96,32},{128,192},{160,224},{192,128},{224,1... | collective-permute-start | bytes 368648 | tf_op jit(solution)/shard_map/ppermute | solution.py:398
  7.8 6.6 %collective-permute-start.2 = (f32[240,128]{1,0:T(8,128)S(1)}, f32[240,128]{1,0:T(8,128)S(1)}, u32[]{:S(2)}, u32[]{:S(2)}) collective-permute-start(f32[240,128]{1,0:T(8,128)S(1)} %get-tuple-element.44), channel_id=1, source_target_pairs={{0,96},{32,64},{64,32},{96,0},{128,224},{160,192},{192,160},{224,1... | collective-permute-start | bytes 368648 | tf_op jit(solution)/shard_map/ppermute | solution.py:398
  8.0 12.2 %collective-permute-start.3 = (f32[240,128]{1,0:T(8,128)S(1)}, f32[240,128]{1,0:T(8,128)S(1)}, u32[]{:S(2)}, u32[]{:S(2)}) collective-permute-start(f32[240,128]{1,0:T(8,128)S(1)} %get-tuple-element.45), channel_id=1, source_target_pairs={{0,128},{32,160},{64,192},{96,224},{128,0},{160,32},{192,64},{224,... | collective-permute-start | bytes 368648 | tf_op jit(solution)/shard_map/ppermute | solution.py:398
  11.2 10.6 %collective-permute-start.4 = (f32[240,128]{1,0:T(8,128)S(1)}, f32[240,128]{1,0:T(8,128)S(1)}, u32[]{:S(2)}, u32[]{:S(2)}) collective-permute-start(f32[240,128]{1,0:T(8,128)S(1)} %get-tuple-element.46), channel_id=1, source_target_pairs={{0,160},{32,128},{64,224},{96,192},{128,32},{160,0},{192,96},{224,... | collective-permute-start | bytes 368648 | tf_op jit(solution)/shard_map/ppermute | solution.py:398
  11.2 12.6 %collective-permute-start.5 = (f32[240,128]{1,0:T(8,128)S(1)}, f32[240,128]{1,0:T(8,128)S(1)}, u32[]{:S(2)}, u32[]{:S(2)}) collective-permute-start(f32[240,128]{1,0:T(8,128)S(1)} %get-tuple-element.47), channel_id=1, source_target_pairs={{0,192},{32,224},{64,128},{96,160},{128,64},{160,96},{192,0},{224,... | collective-permute-start | bytes 368648 | tf_op jit(solution)/shard_map/ppermute | solution.py:398
  14.2 11.4 %collective-permute-start.6 = (f32[240,128]{1,0:T(8,128)S(1)}, f32[240,128]{1,0:T(8,128)S(1)}, u32[]{:S(2)}, u32[]{:S(2)}) collective-permute-start(f32[240,128]{1,0:T(8,128)S(1)} %get-tuple-element.48), channel_id=1, source_target_pairs={{0,224},{32,192},{64,160},{96,128},{128,96},{160,64},{192,32},{224... | collective-permute-start | bytes 368648 | tf_op jit(solution)/shard_map/ppermute | solution.py:398
  26.6 27.0 %collective-permute-start.7 = (f32[168,8,128]{2,1,0:T(8,128)S(1)}, f32[168,8,128]{2,1,0:T(8,128)S(1)}, u32[]{:S(2)}, u32[]{:S(2)}) collective-permute-start(f32[168,8,128]{2,1,0:T(8,128)S(1)} %get-tuple-element.51), channel_id=1, source_target_pairs={{1,2},{2,1},{3,4},{4,3},{5,6},{6,5},{7,8},{8,7},{9,10},{10,9},{11,... | collective-permute-start | bytes 2064392 | tf_op jit(solution)/shard_map/ppermute | solution.py:407
  34.6 19.0 %collective-permute-start.8 = (f32[168,8,128]{2,1,0:T(8,128)S(1)}, f32[168,8,128]{2,1,0:T(8,128)S(1)}, u32[]{:S(2)}, u32[]{:S(2)}) collective-permute-start(f32[168,8,128]{2,1,0:T(8,128)S(1)} %get-tuple-element.52), channel_id=1, source_target_pairs={{0,1},{1,0},{2,3},{3,2},{4,5},{5,4},{6,7},{7,6},{8,9},{9,8},{10,11... | collective-permute-start | bytes 2064392 | tf_op jit(solution)/shard_map/ppermute | solution.py:407
  34.7 16.5 %collective-permute-start.9 = (f32[3,24,128]{2,1,0:T(8,128)S(1)}, f32[3,24,128]{2,1,0:T(8,128)S(1)}, u32[]{:S(2)}, u32[]{:S(2)}) collective-permute-start(f32[3,24,128]{2,1,0:T(8,128)S(1)} %get-tuple-element.54), channel_id=1, source_target_pairs={{1,2},{2,1},{3,4},{4,3},{5,6},{6,5},{7,8},{8,7},{9,10},{10,9},{11,... | collective-permute-start | bytes 110600 | tf_op jit(solution)/shard_map/ppermute | solution.py:407
  38.6 14.2 %collective-permute-start.10 = (f32[3,24,128]{2,1,0:T(8,128)S(1)}, f32[3,24,128]{2,1,0:T(8,128)S(1)}, u32[]{:S(2)}, u32[]{:S(2)}) collective-permute-start(f32[3,24,128]{2,1,0:T(8,128)S(1)} %get-tuple-element.55), channel_id=1, source_target_pairs={{0,1},{1,0},{2,3},{3,2},{4,5},{5,4},{6,7},{7,6},{8,9},{9,8},{10,11... | collective-permute-start | bytes 110600 | tf_op jit(solution)/shard_map/ppermute | solution.py:407
  53.6 17.5 %copy-start.1 = (f32[128,128]{1,0:T(8,128)S(1)}, f32[128,128]{1,0:T(8,128)}, u32[]{:S(2)}) copy-start(f32[128,128]{1,0:T(8,128)} %constant.18.clone.back) | copy-start | bytes 196612
  56.0 14.8 %collective-permute-start.11 = (f32[26,4,8,128]{3,2,1,0:T(8,128)S(1)}, f32[26,4,8,128]{3,2,1,0:T(8,128)S(1)}, u32[]{:S(2)}, u32[]{:S(2)}) collective-permute-start(f32[26,4,8,128]{3,2,1,0:T(8,128)S(1)} %get-tuple-element.59), channel_id=1, source_target_pairs={{1,2},{2,1},{3,4},{4,3},{5,6},{6,5},{7,8},{8,7},{9,10},{10,9},{11,... | collective-permute-start | bytes 1277960 | tf_op jit(solution)/shard_map/ppermute | solution.py:407
  60.2 10.9 %collective-permute-start.12 = (f32[26,4,8,128]{3,2,1,0:T(8,128)S(1)}, f32[26,4,8,128]{3,2,1,0:T(8,128)S(1)}, u32[]{:S(2)}, u32[]{:S(2)}) collective-permute-start(f32[26,4,8,128]{3,2,1,0:T(8,128)S(1)} %get-tuple-element.60), channel_id=1, source_target_pairs={{0,1},{1,0},{2,3},{3,2},{4,5},{5,4},{6,7},{7,6},{8,9},{9,8},{10,11... | collective-permute-start | bytes 1277960 | tf_op jit(solution)/shard_map/ppermute | solution.py:407
  73.1 1.4 %collective-permute-start.13 = (f32[2,4,4,8,128]{4,3,2,1,0:T(8,128)S(1)}, f32[2,4,4,8,128]{4,3,2,1,0:T(8,128)S(1)}, u32[]{:S(2)}, u32[]{:S(2)}) collective-permute-start(f32[2,4,4,8,128]{4,3,2,1,0:T(8,128)S(1)} %get-tuple-element.63), channel_id=1, source_target_pairs={{0,32},{32,0},{64,96},{96,64},{128,160},{160,128},{192,224},{224,1... | collective-permute-start | bytes 393224 | tf_op jit(solution)/shard_map/ppermute | solution.py:407
  73.2 1.3 %collective-permute-start.14 = (f32[2,4,4,8,128]{4,3,2,1,0:T(8,128)S(1)}, f32[2,4,4,8,128]{4,3,2,1,0:T(8,128)S(1)}, u32[]{:S(2)}, u32[]{:S(2)}) collective-permute-start(f32[2,4,4,8,128]{4,3,2,1,0:T(8,128)S(1)} %get-tuple-element.64), channel_id=1, source_target_pairs={{32,64},{64,32},{96,128},{128,96},{160,192},{192,160},{33,65},{65,... | collective-permute-start | bytes 393224 | tf_op jit(solution)/shard_map/ppermute | solution.py:407
  75.2 15.0 %collective-permute-start.15 = (f32[136,8,128]{2,1,0:T(8,128)S(1)}, f32[136,8,128]{2,1,0:T(8,128)S(1)}, u32[]{:S(2)}, u32[]{:S(2)}) collective-permute-start(f32[136,8,128]{2,1,0:T(8,128)S(1)} %get-tuple-element.66), channel_id=1, source_target_pairs={{1,2},{2,1},{3,4},{4,3},{5,6},{6,5},{7,8},{8,7},{9,10},{10,9},{11,... | collective-permute-start | bytes 1671176 | tf_op jit(solution)/shard_map/ppermute | solution.py:407
  79.4 11.5 %collective-permute-start.16 = (f32[136,8,128]{2,1,0:T(8,128)S(1)}, f32[136,8,128]{2,1,0:T(8,128)S(1)}, u32[]{:S(2)}, u32[]{:S(2)}) collective-permute-start(f32[136,8,128]{2,1,0:T(8,128)S(1)} %get-tuple-element.67), channel_id=1, source_target_pairs={{0,1},{1,0},{2,3},{3,2},{4,5},{5,4},{6,7},{7,6},{8,9},{9,8},{10,11... | collective-permute-start | bytes 1671176 | tf_op jit(solution)/shard_map/ppermute | solution.py:407
  93.3 13.5 %collective-permute-start.17 = (f32[26,4,8,128]{3,2,1,0:T(8,128)S(1)}, f32[26,4,8,128]{3,2,1,0:T(8,128)S(1)}, u32[]{:S(2)}, u32[]{:S(2)}) collective-permute-start(f32[26,4,8,128]{3,2,1,0:T(8,128)S(1)} %get-tuple-element.69), channel_id=1, source_target_pairs={{1,2},{2,1},{3,4},{4,3},{5,6},{6,5},{7,8},{8,7},{9,10},{10,9},{11,... | collective-permute-start | bytes 1277960 | tf_op jit(solution)/shard_map/ppermute | solution.py:407
  97.0 9.9 %collective-permute-start.18 = (f32[26,4,8,128]{3,2,1,0:T(8,128)S(1)}, f32[26,4,8,128]{3,2,1,0:T(8,128)S(1)}, u32[]{:S(2)}, u32[]{:S(2)}) collective-permute-start(f32[26,4,8,128]{3,2,1,0:T(8,128)S(1)} %get-tuple-element.70), channel_id=1, source_target_pairs={{0,1},{1,0},{2,3},{3,2},{4,5},{5,4},{6,7},{7,6},{8,9},{9,8},{10,11... | collective-permute-start | bytes 1277960 | tf_op jit(solution)/shard_map/ppermute | solution.py:407
  109.1 13.7 %collective-permute-start.19 = (f32[96,128]{1,0:T(8,128)S(1)}, f32[96,128]{1,0:T(8,128)S(1)}, u32[]{:S(2)}, u32[]{:S(2)}) collective-permute-start(f32[96,128]{1,0:T(8,128)S(1)} %get-tuple-element.73), channel_id=1, source_target_pairs={{0,32},{32,0},{64,96},{96,64},{128,160},{160,128},{192,224},{224,1... | collective-permute-start | bytes 147464 | tf_op jit(solution)/shard_map/ppermute | solution.py:398
  112.0 12.6 %collective-permute-start.20 = (f32[96,128]{1,0:T(8,128)S(1)}, f32[96,128]{1,0:T(8,128)S(1)}, u32[]{:S(2)}, u32[]{:S(2)}) collective-permute-start(f32[96,128]{1,0:T(8,128)S(1)} %get-tuple-element.74), channel_id=1, source_target_pairs={{0,64},{32,96},{64,0},{96,32},{128,192},{160,224},{192,128},{224,1... | collective-permute-start | bytes 147464 | tf_op jit(solution)/shard_map/ppermute | solution.py:398
  119.6 6.3 %collective-permute-start.21 = (f32[96,128]{1,0:T(8,128)S(1)}, f32[96,128]{1,0:T(8,128)S(1)}, u32[]{:S(2)}, u32[]{:S(2)}) collective-permute-start(f32[96,128]{1,0:T(8,128)S(1)} %get-tuple-element.75), channel_id=1, source_target_pairs={{0,96},{32,64},{64,32},{96,0},{128,224},{160,192},{192,160},{224,1... | collective-permute-start | bytes 147464 | tf_op jit(solution)/shard_map/ppermute | solution.py:398
  119.7 6.3 %collective-permute-start.22 = (f32[96,128]{1,0:T(8,128)S(1)}, f32[96,128]{1,0:T(8,128)S(1)}, u32[]{:S(2)}, u32[]{:S(2)}) collective-permute-start(f32[96,128]{1,0:T(8,128)S(1)} %get-tuple-element.76), channel_id=1, source_target_pairs={{0,128},{32,160},{64,192},{96,224},{128,0},{160,32},{192,64},{224,... | collective-permute-start | bytes 147464 | tf_op jit(solution)/shard_map/ppermute | solution.py:398
  122.8 5.4 %collective-permute-start.23 = (f32[96,128]{1,0:T(8,128)S(1)}, f32[96,128]{1,0:T(8,128)S(1)}, u32[]{:S(2)}, u32[]{:S(2)}) collective-permute-start(f32[96,128]{1,0:T(8,128)S(1)} %get-tuple-element.77), channel_id=1, source_target_pairs={{0,160},{32,128},{64,224},{96,192},{128,32},{160,0},{192,96},{224,... | collective-permute-start | bytes 147464 | tf_op jit(solution)/shard_map/ppermute | solution.py:398
  122.8 6.7 %collective-permute-start.24 = (f32[96,128]{1,0:T(8,128)S(1)}, f32[96,128]{1,0:T(8,128)S(1)}, u32[]{:S(2)}, u32[]{:S(2)}) collective-permute-start(f32[96,128]{1,0:T(8,128)S(1)} %get-tuple-element.78), channel_id=1, source_target_pairs={{0,192},{32,224},{64,128},{96,160},{128,64},{160,96},{192,0},{224,... | collective-permute-start | bytes 147464 | tf_op jit(solution)/shard_map/ppermute | solution.py:398
  124.6 5.5 %collective-permute-start.25 = (f32[96,128]{1,0:T(8,128)S(1)}, f32[96,128]{1,0:T(8,128)S(1)}, u32[]{:S(2)}, u32[]{:S(2)}) collective-permute-start(f32[96,128]{1,0:T(8,128)S(1)} %get-tuple-element.79), channel_id=1, source_target_pairs={{0,224},{32,192},{64,160},{96,128},{128,96},{160,64},{192,32},{224... | collective-permute-start | bytes 147464 | tf_op jit(solution)/shard_map/ppermute | solution.py:398

commit v3 on v2

--- a/solution.py
+++ b/solution.py
@@ -16,6 +16,7 @@
 OWN = 12
 HALO = 4
 WIN = OWN + 2 * HALO
+ORDER = (4, 2, 6, 5, 3, 7, 1)
 TALL = 24
 
 
@@ -47,14 +48,15 @@
     return jax.ShapeDtypeStruct(shape, jnp.float32)
 
 
-def call(body, name, outs, n_in, scratch=(), scalars=1):
+def call(body, name, outs, n_in, scratch=(), scalars=1, far_inputs=0):
     vmem = pl.BlockSpec(memory_space=pltpu.VMEM)
+    anywhere = pl.BlockSpec(memory_space=pltpu.HBM)
     smem = pl.BlockSpec(memory_space=pltpu.SMEM)
     return pl.pallas_call(
         body,
         name=name,
         out_shape=outs,
-        in_specs=[smem] * scalars + [vmem] * n_in,
+        in_specs=[smem] * scalars + [anywhere] * far_inputs + [vmem] * n_in,
         out_specs=[vmem] * len(outs),
         scratch_shapes=list(scratch),
         compiler_params=pltpu.CompilerParams(vmem_limit_bytes=16 * 1024 * 1024),
@@ -65,11 +67,16 @@
     lax.fori_loop(lo, hi, body, 0, unroll=True)
 
 
-def pack_body(pos, state, adjoint, target, kappa, begin, *rest):
-    outs, (near, far, here, stage) = rest[:8], rest[8:]
+def pack_body(pos, *rest):
+    sources, outs, (near, far, here, stage), held, sems = rest[:5], rest[5:13], rest[13:17], rest[17:22], rest[22]
+    copies = [pltpu.make_async_copy(sources[i], held[i], sems.at[i]) for i in range(5)]
+    for copy in copies:
+        copy.start()
+    state, adjoint, target, kappa, begin = held
     t = pos[0]
     flip = pos[1]
     for f, ref in enumerate((state, adjoint, target)):
+        copies[f].wait()
         for n in range(2):
             for x in range(2):
                 base = ((f * 2 + n) * 2 + x) * WIN
@@ -83,6 +90,8 @@
                         stage[d, base + last - low : base + WIN, :] = jnp.zeros((low + WIN - last, 128), jnp.float32)
     for k in range(8):
         outs[k][...] = stage[t ^ k]
+    copies[3].wait()
+    copies[4].wait()
     for d in range(8):
         @pl.when(t == d)
         def window(d=d):
@@ -106,6 +115,7 @@
 
 def coefficient_body(pos, here, near, far, consts, weights, inv):
     t, flip, s = pos[0], pos[1], pos[2]
+    near, far = ([side[168 + 3 * i : 171 + 3 * i].reshape(TALL, 128) for i in range(3)] for side in (near, far))
     kappa = [near[1], near[0], here[0], here[1], far[0], far[1]]
     begin = [near[2], here[2], here[3], far[2]]
     lane = lax.broadcasted_iota(jnp.int32, (TALL, 128), 1)
@@ -151,11 +161,14 @@
 
 
 def spread_body(pos, *rest):
-    pieces, (own, wish, near, far), stage = rest[:8], rest[8:12], rest[12]
+    pieces, (near_c, far_c), (own, wish, near, far), stage = rest[:8], rest[8:10], rest[10:14], rest[14]
+    for i in range(3):
+        near[168 + 3 * i : 171 + 3 * i] = near_c[i].reshape(3, 8, 128)
+        far[168 + 3 * i : 171 + 3 * i] = far_c[i].reshape(3, 8, 128)
     t = pos[0]
     rows = 12 * WIN
-    for k in range(8):
-        stage[pl.ds(pl.multiple_of((t ^ k) * rows, 8), rows), :] = pieces[k][...]
+    for k, piece in zip(ORDER + (0,), pieces):
+        stage[pl.ds(pl.multiple_of((t ^ k) * rows, 8), rows), :] = piece[...]
     for x in range(2):
         for j in range(WIN):
             for f in range(3):
@@ -339,31 +352,50 @@
     rows(0, 6, group)
 
 
-def middle_body(pos, it, near, far, rhs, weights, consts, inv, back, own, new, send0, send1, zed, fin):
+def middle_body(it, near, far, rhs, weights, consts, inv, back, own, new, out_near, out_far, zed, fin):
     sweep_body(it, near, far, rhs, weights, consts, inv, back, zed, fin)
+    for x in range(2):
+        first, second = (out_near, out_far) if x == 0 else (out_far, out_near)
+        for j in range(OWN):
+            for c in range(4):
+                v = own[x, j + HALO, c] + fin[x * OWN + j, c]
+                new[x, j, c] = v
+                first[j, c] = v
+                second[OWN + j, c] = v
+
+
+EDGE = ((0, 4), (4, 4), (8, 3), (11, 3), (14, 2), (16, 2))
+
+
+def edges_body(pos, new, near, far, send0, send1):
     odd = pos[0] & 1
-    for x in range(2):
-        for j in range(OWN):
-            for c in range(4):
-                new[x, j, c] = own[x, j + HALO, c] + fin[x * OWN + j, c]
-    top = pl.multiple_of(8 * (1 - odd), 4)
-    bottom = 8 * odd
-    for x in range(2):
-        for j in range(HALO):
-            send0[x, j] = new[x, top + j]
-            send1[x, j] = new[x, bottom + j]
-
-
-def widen_body(pos, new, got0, got1, own, near, far):
+    planes = (
+        lambda j, n: new[0, pl.ds(j, n)],
+        lambda j, n: new[1, pl.ds(j, n)],
+        lambda j, n: near[pl.ds(j, n)],
+        lambda j, n: far[pl.ds(j, n)],
+        lambda j, n: near[pl.ds(OWN + j, n)],
+        lambda j, n: far[pl.ds(OWN + j, n)],
+    )
+    for take, (at, n) in zip(planes, EDGE):
+        send0[at : at + n] = take((OWN - n) * (1 - odd), n)
+        send1[at : at + n] = take((OWN - n) * odd, n)
+
+
+def widen_body(pos, got1, got0, new, near_x, far_x, own, near, far):
     odd = pos[0] & 1
     for x in range(2):
         own[x, HALO : HALO + OWN] = new[x]
-        own[x, pl.ds(16 * (1 - odd), HALO)] = got0[x]
-        own[x, pl.ds(16 * odd, HALO)] = got1[x]
-    for x in range(2):
-        first, second = (near, far) if x == 0 else (far, near)
-        first[0:72] = own[x, 1:19].reshape(72, 8, 128)
-        second[72:136] = own[x, 2:18].reshape(64, 8, 128)
+    for out, got in ((near, near_x), (far, far_x)):
+        out[3 : 3 + OWN] = got[0:OWN]
+        out[20 : 20 + OWN] = got[OWN : 2 * OWN]
+    for got, high in ((got0, 1 - odd), (got1, odd)):
+        own[0, pl.ds(16 * high, 4)] = got[0:4]
+        own[1, pl.ds(16 * high, 4)] = got[4:8]
+        near[pl.ds(15 * high, 3)] = got[8:11]
+        far[pl.ds(15 * high, 3)] = got[11:14]
+        near[pl.ds(18 + 14 * high, 2)] = got[14:16]
+        far[pl.ds(18 + 14 * high, 2)] = got[16:18]
 
 
 def last_body(pos, it, near, far, rhs, weights, consts, inv, back, own, *rest):
@@ -382,8 +414,8 @@
     pieces, (state, adjoint), stage = rest[:8], rest[8:10], rest[10]
     t = pos[0]
     flip = pos[1]
-    for k in range(8):
-        stage[t ^ k] = pieces[k][...]
+    for k, piece in zip(ORDER + (0,), pieces):
+        stage[t ^ k] = piece[...]
     for f, ref in enumerate((state, adjoint)):
         for n in range(2):
             for x in range(2):
@@ -394,9 +426,7 @@
 
 def exchange(pieces):
     count = lax.axis_size("tm")
-    return [pieces[0]] + [
-        lax.ppermute(pieces[k], "tm", [(i, i ^ k) for i in range(count)]) for k in range(1, count)
-    ]
+    return [lax.ppermute(pieces[k], "tm", [(i, i ^ k) for i in range(count)]) for k in ORDER] + [pieces[0]]
 
 
 def swap(block, axis, start):
@@ -419,31 +449,30 @@
         pack_body,
         "pack",
         [whole(12 * WIN, 128)] * 8 + [whole(3, TALL, 128)] * 2 + [whole(4, TALL, 128)],
-        5,
-        [pltpu.VMEM((8, 12 * WIN, 128), jnp.float32)],
-    )(pos, state_guess, adjoint_guess, target, diffusivity, initial_state)
-    far_c = swap(far_c, "space", 0)
-    near_c = swap(near_c, "space", 1)
+        0,
+        [pltpu.VMEM((8, 12 * WIN, 128), jnp.float32)]
+        + [pltpu.VMEM((2, 2, 96, 128), jnp.float32)] * 3
+        + [pltpu.VMEM((2, 96, 128), jnp.float32)] * 2
+        + [pltpu.SemaphoreType.DMA((5,))],
+        far_inputs=5,
+    )(pos, *(pltpu.with_memory_space_constraint(a, pltpu.HBM) for a in (state_guess, adjoint_guess, target, diffusivity, initial_state)))
     got = exchange(pieces)
-    weights, inv = call(
-        coefficient_body, "coefficients", [whole(4 * TALL * 8, 128), whole(68, 2, 8, 128)], 4
-    )(pos, here_c, near_c, far_c, consts)
-    weights = weights.reshape(4 * TALL, 8, 128)
-
     own, wish, near, far = call(
         spread_body,
         "spread",
-        [whole(2, WIN, 4, 8, 128), whole(2, 18, 2, 8, 128), whole(168, 8, 128), whole(168, 8, 128)],
-        8,
+        [whole(2, WIN, 4, 8, 128), whole(2, 18, 2, 8, 128), whole(177, 8, 128), whole(177, 8, 128)],
+        10,
         [pltpu.VMEM((8 * 12 * WIN, 128), jnp.float32)],
-    )(pos, *got)
+    )(pos, *got, near_c, far_c)
+    far = far_first = swap(far, "space", 0)
+    near = near_first = swap(near, "space", 1)
+    weights, inv = call(
+        coefficient_body, "coefficients", [whole(4 * TALL * 8, 128), whole(68, 2, 8, 128)], 4
+    )(pos, here_c, near, far, consts)
+    weights = weights.reshape(4 * TALL, 8, 128)
 
     sweep_scratch = [pltpu.VMEM((52, 4, 8, 128), jnp.float32), pltpu.VMEM((24, 4, 8, 128), jnp.float32)]
     for outer in range(OUTER):
-        far_f = swap(far, "space", 0)
-        near_f = swap(near, "space", 1)
-        if outer == 0:
-            wish_near, wish_far = near_f, far_f
         rhs, it, near_z, far_z = call(
             residual_body,
             "residual",
@@ -451,22 +480,28 @@
             10,
             [pltpu.VMEM((68, 4, 8, 128), jnp.float32)] * 2,
             scalars=0,
-        )(own, wish, near_f, far_f, wish_near, wish_far, weights, consts, inv, forward)
+        )(own, wish, near, far, near_first, far_first, weights, consts, inv, forward)
         far_z = swap(far_z, "space", 0)
         near_z = swap(near_z, "space", 1)
         if outer < OUTER - 1:
-            new, send0, send1 = call(
+            new, near, far = call(
                 middle_body,
                 "middle",
-                [whole(2, OWN, 4, 8, 128), whole(2, HALO, 4, 8, 128), whole(2, HALO, 4, 8, 128)],
+                [whole(2, OWN, 4, 8, 128), whole(2 * OWN, 4, 8, 128), whole(2 * OWN, 4, 8, 128)],
                 9,
                 sweep_scratch,
-            )(pos, it, near_z, far_z, rhs, weights, consts, inv, back, own)
+                scalars=0,
+            )(it, near_z, far_z, rhs, weights, consts, inv, back, own)
+            far = swap(far, "space", 0)
+            near = swap(near, "space", 1)
+            send0, send1 = call(edges_body, "edges", [whole(18, 4, 8, 128)] * 2, 3)(pos, new, near, far)
+            got1 = swap(send1, "tm", 1)
             got0 = swap(send0, "tm", 0)
-            got1 = swap(send1, "tm", 1)
             own, near, far = call(
-                widen_body, "widen", [whole(2, WIN, 4, 8, 128), whole(136, 8, 128), whole(136, 8, 128)], 3
-            )(pos, new, got0, got1)
+                widen_body, "widen", [whole(2, WIN, 4, 8, 128), whole(34, 4, 8, 128), whole(34, 4, 8, 128)], 5
+            )(pos, got1, got0, new, near, far)
+            near = near.reshape(136, 8, 128)
+            far = far.reshape(136, 8, 128)
     pieces = call(
         last_body,
         "last",

time: 132 us -> 120 us (0.909)
  starting transfers between devices: 51.4 us -> 44.4 us
  local copies, waits for them, and re-layouts: 4.59 us -> 0.02 us
  waiting for transfers between devices: 61.3 us -> 59 us
    ppermute x14, waiting for transfers between devices: 15.5 us -> 8.62 us  [exchange(): lax.ppermute(pieces[k], 'tm', [(i, i ^ k) for i in range(count)])]
    ppermute x14, starting transfers between devices: 25.2 us -> 20.4 us  [exchange(): lax.ppermute(pieces[k], 'tm', [(i, i ^ k) for i in range(count)])]
    unnamed x16 -> x6, local copies, waits for them, and re-layouts: 4.59 us -> 0.02 us
    ppermute x12 -> x10, waiting for transfers between devices: 45.9 us -> 50.4 us  [swap(): return lax.ppermute(block, axis, route)]
    ppermute x12 -> x10, starting transfers between devices: 26.2 us -> 24.1 us  [swap(): return lax.ppermute(block, axis, route)]
    pallas_call x2 -> x3, Pallas kernels: 2.63 us -> 2.64 us  [the longest x1 1.4 us: on_device(): call(middle_body, 'middle', [whole(2, OWN, 4, 8, 128), whole(2 * OWN, 4,...]
  transfers between devices with their start and end apart: 26 -> 24, of which waited for: 17 -> 15; matrix products, arithmetic and copies ran while one was open for 0% -> 0% of each run, Pallas kernels for 1% -> 0%
where the time goes in v3:
time: 120 us; the launch traced here: 119 us
  waiting for transfers between devices  59 us (49%)
  starting transfers between devices  44.4 us (37%)
  Pallas kernels  14.4 us (12%)
    ppermute x10, waiting for transfers between devices, swap(): return lax.ppermute(block, axis, route)  50.4 us
    ppermute x10, starting transfers between devices, swap(): return lax.ppermute(block, axis, route)  24.1 us
    ppermute x14, starting transfers between devices, exchange(): lax.ppermute(pieces[k], 'tm', [(i, i ^ k) for i in range(count)])  20.4 us
    ppermute x14, waiting for transfers between devices, exchange(): lax.ppermute(pieces[k], 'tm', [(i, i ^ k) for i in range(count)])  8.62 us
    pallas_call x2, Pallas kernels, on_device(): call(residual_body, 'residual', [whole(68, 4, 8, 128), whole(2, 16, 4, 8,...  4.71 us
  transfers between devices with their start and end apart: 24, of which 15 were waited for; matrix products, arithmetic and copies ran while one was open for 0% of the time, Pallas kernels for 0%

profile of v3, /device:TPU:6, one launch (start us, length us, event | category | flops | bytes accessed | tf_op | source)
XLA Modules:
  0.0 118.8 jit_solution(1367275232292374756)
XLA Ops:
  0.6 0.1 pad_add_fusion.pos
  0.7 1.8 %pack.1 = (f32[240,128]{1,0:T(8,128)S(1)}, f32[240,128]{1,0:T(8,128)S(1)}, f32[240,128]{1,0:T(8,128)S(1)}, f32[240,128]{1,0:T(8,128)S(1)}, f32[240,128]{1,0:T(8,...) custom-call(s32[3]{0:T(128)S(1)} %pad_add_fusion.pos, ...), custom_call_target="tpu_custom_call" | custom-call | tf_op jit(solution)/shard_map/pack/pallas_call | solution.py:448
  2.6 3.3 %collective-permute-start = (f32[240,128]{1,0:T(8,128)S(1)}, f32[240,128]{1,0:T(8,128)S(1)}, u32[]{:S(2)}, u32[]{:S(2)}) collective-permute-start(f32[240,128]{1,0:T(8,128)S(1)} %get-tuple-element.43), channel_id=1, source_target_pairs={{0,128},{32,160},{64,192},{96,224},{128,0},{160,32},{192,64},{224,... | collective-permute-start | bytes 368648 | tf_op jit(solution)/shard_map/ppermute | solution.py:429
  5.8 0.7 collective-permute-start.1
  6.5 0.4 collective-permute-start.2
  6.9 1.6 %collective-permute-start.3 = (f32[240,128]{1,0:T(8,128)S(1)}, f32[240,128]{1,0:T(8,128)S(1)}, u32[]{:S(2)}, u32[]{:S(2)}) collective-permute-start(f32[240,128]{1,0:T(8,128)S(1)} %get-tuple-element.46), channel_id=1, source_target_pairs={{0,160},{32,128},{64,224},{96,192},{128,32},{160,0},{192,96},{224,... | collective-permute-start | bytes 368648 | tf_op jit(solution)/shard_map/ppermute | solution.py:429
  8.5 1.8 %collective-permute-start.4 = (f32[240,128]{1,0:T(8,128)S(1)}, f32[240,128]{1,0:T(8,128)S(1)}, u32[]{:S(2)}, u32[]{:S(2)}) collective-permute-start(f32[240,128]{1,0:T(8,128)S(1)} %get-tuple-element.47), channel_id=1, source_target_pairs={{0,96},{32,64},{64,32},{96,0},{128,224},{160,192},{192,160},{224,1... | collective-permute-start | bytes 368648 | tf_op jit(solution)/shard_map/ppermute | solution.py:429
  10.3 0.5 collective-permute-start.5
  10.8 1.9 %collective-permute-done.1.rest_1_ = f32[240,128]{1,0:T(8,128)S(1)} collective-permute-done((f32[240,128]{1,0:T(8,128)S(1)}, f32[240,128]{1,0:T(8,128)S(1)}, u32[]{:S(2)}, u32[]{:S(2)}) %collective-permute-start.1) | collective-permute-done | bytes 122912 | tf_op jit(solution)/shard_map/ppermute | solution.py:429
  12.7 0.8 collective-permute-start.6
  13.5 2.2 %collective-permute-done.2.rest_2_ = f32[240,128]{1,0:T(8,128)S(1)} collective-permute-done((f32[240,128]{1,0:T(8,128)S(1)}, f32[240,128]{1,0:T(8,128)S(1)}, u32[]{:S(2)}, u32[]{:S(2)}) %collective-permute-start.2) | collective-permute-done | bytes 122912 | tf_op jit(solution)/shard_map/ppermute | solution.py:429
  15.7 1.2 %collective-permute-done.4.rest_4_ = f32[240,128]{1,0:T(8,128)S(1)} collective-permute-done((f32[240,128]{1,0:T(8,128)S(1)}, f32[240,128]{1,0:T(8,128)S(1)}, u32[]{:S(2)}, u32[]{:S(2)}) %collective-permute-start.4) | collective-permute-done | bytes 122912 | tf_op jit(solution)/shard_map/ppermute | solution.py:429
  16.9 0.5 collective-permute-done.5.rest_5_
  17.4 0.9 spread.1
  18.4 8.0 %collective-permute-start.7 = (f32[177,8,128]{2,1,0:T(8,128)S(1)}, f32[177,8,128]{2,1,0:T(8,128)S(1)}, u32[]{:S(2)}, u32[]{:S(2)}) collective-permute-start(f32[177,8,128]{2,1,0:T(8,128)S(1)} %get-tuple-element.55), channel_id=1, source_target_pairs={{1,2},{2,1},{3,4},{4,3},{5,6},{6,5},{7,8},{8,7},{9,10},{10,9},{11,... | collective-permute-start | bytes 2174984 | tf_op jit(solution)/shard_map/ppermute | solution.py:437
  26.4 0.1 collective-permute-start.8
  26.5 16.5 %collective-permute-done.7.near.tnear = f32[177,8,128]{2,1,0:T(8,128)S(1)} collective-permute-done((f32[177,8,128]{2,1,0:T(8,128)S(1)}, f32[177,8,128]{2,1,0:T(8,128)S(1)}, u32[]{:S(2)}, u32[]{:S(2)}) %collective-permute-start.7) | collective-permute-done | bytes 725024 | tf_op jit(solution)/shard_map/ppermute | solution.py:437
  43.1 1.6 %collective-permute-done.8.far.tfar = f32[177,8,128]{2,1,0:T(8,128)S(1)} collective-permute-done((f32[177,8,128]{2,1,0:T(8,128)S(1)}, f32[177,8,128]{2,1,0:T(8,128)S(1)}, u32[]{:S(2)}, u32[]{:S(2)}) %collective-permute-start.8) | collective-permute-done | bytes 725024 | tf_op jit(solution)/shard_map/ppermute | solution.py:437
  44.6 0.8 coefficients.1
  45.4 2.4 %residual.2 = (f32[68,4,8,128]{3,2,1,0:T(8,128)S(1)}, f32[2,16,4,8,128]{4,3,2,1,0:T(8,128)S(1)}, f32[26,4,8,128]{3,2,1,0:T(8,128)S(1)}, f32[26,4,8,128]{3,2,1,0:T(8,128)S(1)}) custom-call(f32[2,20,4,8,128]{4,3,2,1,0:T(8,128)S(1)} %get-tuple-element.53.own, f32[2,18,2,8,128]{4,3,2,1,0:T(8,128)S(1)} %get-tuple-element.54.wish, ...), custom_call_target="tpu_custom_call" | custom-call | tf_op jit(solution)/shard_map/residual/pallas_call | solution.py:476
  47.8 4.2 %collective-permute-start.9 = (f32[26,4,8,128]{3,2,1,0:T(8,128)S(1)}, f32[26,4,8,128]{3,2,1,0:T(8,128)S(1)}, u32[]{:S(2)}, u32[]{:S(2)}) collective-permute-start(f32[26,4,8,128]{3,2,1,0:T(8,128)S(1)} %get-tuple-element.61), channel_id=1, source_target_pairs={{1,2},{2,1},{3,4},{4,3},{5,6},{6,5},{7,8},{8,7},{9,10},{10,9},{11,... | collective-permute-start | bytes 1277960 | tf_op jit(solution)/shard_map/ppermute | solution.py:437
  52.0 0.1 collective-permute-start.10
  52.1 10.6 %collective-permute-done.9.near = f32[26,4,8,128]{3,2,1,0:T(8,128)S(1)} collective-permute-done((f32[26,4,8,128]{3,2,1,0:T(8,128)S(1)}, f32[26,4,8,128]{3,2,1,0:T(8,128)S(1)}, u32[]{:S(2)}, u32[]{:S(2)}) %collective-permute-start.9) | collective-permute-done | bytes 426016 | tf_op jit(solution)/shard_map/ppermute | solution.py:437
  62.7 0.3 collective-permute-done.10.far
  63.0 1.4 %middle.1 = (f32[2,12,4,8,128]{4,3,2,1,0:T(8,128)S(1)}, f32[24,4,8,128]{3,2,1,0:T(8,128)S(1)}, f32[24,4,8,128]{3,2,1,0:T(8,128)S(1)}) custom-call(f32[2,16,4,8,128]{4,3,2,1,0:T(8,128)S(1)} %get-tuple-element.60.it, f32[26,4,8,128]{3,2,1,0:T(8,128)S(1)} %collective-permute-done.9.near, f32[26,4,8,128]{3,2,1,0:T(8,128)S(1)} %collective-permute-done.10.far, ...), custom_call_target="tpu_custom_call" | custom-call | tf_op jit(solution)/shard_map/middle/pallas_call | solution.py:487
  64.4 4.2 %collective-permute-start.11 = (f32[24,4,8,128]{3,2,1,0:T(8,128)S(1)}, f32[24,4,8,128]{3,2,1,0:T(8,128)S(1)}, u32[]{:S(2)}, u32[]{:S(2)}) collective-permute-start(f32[24,4,8,128]{3,2,1,0:T(8,128)S(1)} %get-tuple-element.65), channel_id=1, source_target_pairs={{1,2},{2,1},{3,4},{4,3},{5,6},{6,5},{7,8},{8,7},{9,10},{10,9},{11,... | collective-permute-start | bytes 1179656 | tf_op jit(solution)/shard_map/ppermute | solution.py:437
  68.6 0.1 collective-permute-start.12
  68.7 9.0 %collective-permute-done.11.near.near_x = f32[24,4,8,128]{3,2,1,0:T(8,128)S(1)} collective-permute-done((f32[24,4,8,128]{3,2,1,0:T(8,128)S(1)}, f32[24,4,8,128]{3,2,1,0:T(8,128)S(1)}, u32[]{:S(2)}, u32[]{:S(2)}) %collective-permute-start.11) | collective-permute-done | bytes 393248 | tf_op jit(solution)/shard_map/ppermute | solution.py:437
  77.7 0.3 collective-permute-done.12.far.far_x
  78.0 0.6 edges.1
  78.6 0.7 collective-permute-start.13
  79.2 2.4 %collective-permute-start.14 = (f32[18,4,8,128]{3,2,1,0:T(8,128)S(1)}, f32[18,4,8,128]{3,2,1,0:T(8,128)S(1)}, u32[]{:S(2)}, u32[]{:S(2)}) collective-permute-start(f32[18,4,8,128]{3,2,1,0:T(8,128)S(1)} %get-tuple-element.68), channel_id=1, source_target_pairs={{0,32},{32,0},{64,96},{96,64},{128,160},{160,128},{192,224},{224,1... | collective-permute-start | bytes 884744 | tf_op jit(solution)/shard_map/ppermute | solution.py:437
  81.7 1.2 %collective-permute-done.14.got0 = f32[18,4,8,128]{3,2,1,0:T(8,128)S(1)} collective-permute-done((f32[18,4,8,128]{3,2,1,0:T(8,128)S(1)}, f32[18,4,8,128]{3,2,1,0:T(8,128)S(1)}, u32[]{:S(2)}, u32[]{:S(2)}) %collective-permute-start.14) | collective-permute-done | bytes 294944 | tf_op jit(solution)/shard_map/ppermute | solution.py:437
  82.9 0.7 widen.1
  83.5 2.4 %residual.3 = (f32[68,4,8,128]{3,2,1,0:T(8,128)S(1)}, f32[2,16,4,8,128]{4,3,2,1,0:T(8,128)S(1)}, f32[26,4,8,128]{3,2,1,0:T(8,128)S(1)}, f32[26,4,8,128]{3,2,1,0:T(8,128)S(1)}) custom-call(f32[2,20,4,8,128]{4,3,2,1,0:T(8,128)S(1)} %get-tuple-element.69.own, f32[2,18,2,8,128]{4,3,2,1,0:T(8,128)S(1)} %get-tuple-element.54.wish, f32[136,8,128]{2,1,0:T(8,128)S(1)} %bitcast.10, ...), custom_call_target="tpu_custom_call" | custom-call | tf_op jit(solution)/shard_map/residual/pallas_call | solution.py:476
  85.9 4.2 %collective-permute-start.15 = (f32[26,4,8,128]{3,2,1,0:T(8,128)S(1)}, f32[26,4,8,128]{3,2,1,0:T(8,128)S(1)}, u32[]{:S(2)}, u32[]{:S(2)}) collective-permute-start(f32[26,4,8,128]{3,2,1,0:T(8,128)S(1)} %get-tuple-element.73), channel_id=1, source_target_pairs={{1,2},{2,1},{3,4},{4,3},{5,6},{6,5},{7,8},{8,7},{9,10},{10,9},{11,... | collective-permute-start | bytes 1277960 | tf_op jit(solution)/shard_map/ppermute | solution.py:437
  90.1 0.1 collective-permute-start.16
  90.2 10.4 %collective-permute-done.15.near = f32[26,4,8,128]{3,2,1,0:T(8,128)S(1)} collective-permute-done((f32[26,4,8,128]{3,2,1,0:T(8,128)S(1)}, f32[26,4,8,128]{3,2,1,0:T(8,128)S(1)}, u32[]{:S(2)}, u32[]{:S(2)}) %collective-permute-start.15) | collective-permute-done | bytes 426016 | tf_op jit(solution)/shard_map/ppermute | solution.py:437
  100.6 0.6 collective-permute-done.16.far
  101.1 2.2 %last.1 = (f32[96,128]{1,0:T(8,128)S(1)}, f32[96,128]{1,0:T(8,128)S(1)}, f32[96,128]{1,0:T(8,128)S(1)}, f32[96,128]{1,0:T(8,128)S(1)}, f32[96,128]{1,0:T(8,128)S...) custom-call(s32[3]{0:T(128)S(1)} %pad_add_fusion.pos, ...), custom_call_target="tpu_custom_call" | custom-call | tf_op jit(solution)/shard_map/last/pallas_call | solution.py:505
  103.3 5.6 %collective-permute-start.17 = (f32[96,128]{1,0:T(8,128)S(1)}, f32[96,128]{1,0:T(8,128)S(1)}, u32[]{:S(2)}, u32[]{:S(2)}) collective-permute-start(f32[96,128]{1,0:T(8,128)S(1)} %get-tuple-element.76), channel_id=1, source_target_pairs={{0,128},{32,160},{64,192},{96,224},{128,0},{160,32},{192,64},{224,... | collective-permute-start | bytes 147464 | tf_op jit(solution)/shard_map/ppermute | solution.py:429
  108.9 1.9 %collective-permute-start.19 = (f32[96,128]{1,0:T(8,128)S(1)}, f32[96,128]{1,0:T(8,128)S(1)}, u32[]{:S(2)}, u32[]{:S(2)}) collective-permute-start(f32[96,128]{1,0:T(8,128)S(1)} %get-tuple-element.78), channel_id=1, source_target_pairs={{0,192},{32,224},{64,128},{96,160},{128,64},{160,96},{192,0},{224,... | collective-permute-start | bytes 147464 | tf_op jit(solution)/shard_map/ppermute | solution.py:429
  110.7 2.0 %collective-permute-start.21 = (f32[96,128]{1,0:T(8,128)S(1)}, f32[96,128]{1,0:T(8,128)S(1)}, u32[]{:S(2)}, u32[]{:S(2)}) collective-permute-start(f32[96,128]{1,0:T(8,128)S(1)} %get-tuple-element.80), channel_id=1, source_target_pairs={{0,96},{32,64},{64,32},{96,0},{128,224},{160,192},{192,160},{224,1... | collective-permute-start | bytes 147464 | tf_op jit(solution)/shard_map/ppermute | solution.py:429
  112.7 1.9 %collective-permute-start.22 = (f32[96,128]{1,0:T(8,128)S(1)}, f32[96,128]{1,0:T(8,128)S(1)}, u32[]{:S(2)}, u32[]{:S(2)}) collective-permute-start(f32[96,128]{1,0:T(8,128)S(1)} %get-tuple-element.81), channel_id=1, source_target_pairs={{0,224},{32,192},{64,160},{96,128},{128,96},{160,64},{192,32},{224... | collective-permute-start | bytes 147464 | tf_op jit(solution)/shard_map/ppermute | solution.py:429
  114.6 0.1 collective-permute-start.23
  114.7 1.1 collective-permute-done.20.rest_3_
  115.8 1.7 %collective-permute-done.22.rest_5_ = f32[96,128]{1,0:T(8,128)S(1)} collective-permute-done((f32[96,128]{1,0:T(8,128)S(1)}, f32[96,128]{1,0:T(8,128)S(1)}, u32[]{:S(2)}, u32[]{:S(2)}) %collective-permute-start.22) | collective-permute-done | bytes 49184 | tf_op jit(solution)/shard_map/ppermute | solution.py:429
  117.4 1.3 %unpack.1 = (f32[2,2,96,128]{3,2,1,0:T(8,128)}, f32[2,2,96,128]{3,2,1,0:T(8,128)}) custom-call(s32[3]{0:T(128)S(1)} %pad_add_fusion.pos, f32[96,128]{1,0:T(8,128)S(1)} %collective-permute-done.17.rest_0_, f32[96,128]{1,0:T(8,128)S(1)} %collective-permute-done.18.rest_1_, f32[96,128]{1,0:T(8,128)S(1)} %collective-permute-done.19.rest_2_, ...), custom_call_target="tpu_custom_call" | custom-call | tf_op jit(solution)/shard_map/unpack/pallas_call | solution.py:514
  (17 shorter events, 0.0 us)
Async XLA Ops:
  0.6 44.0 %copy-start = (f32[3,8,128]{2,1,0:T(8,128)S(1)}, f32[3,8,128]{2,1,0:T(8,128)}, u32[]{:S(2)}) copy-start(f32[3,8,128]{2,1,0:T(8,128)} %constant.19.clone.consts) | copy-start | bytes 36868
  2.6 7.8 %collective-permute-start = (f32[240,128]{1,0:T(8,128)S(1)}, f32[240,128]{1,0:T(8,128)S(1)}, u32[]{:S(2)}, u32[]{:S(2)}) collective-permute-start(f32[240,128]{1,0:T(8,128)S(1)} %get-tuple-element.43), channel_id=1, source_target_pairs={{0,128},{32,160},{64,192},{96,224},{128,0},{160,32},{192,64},{224,... | collective-permute-start | bytes 368648 | tf_op jit(solution)/shard_map/ppermute | solution.py:429
  5.8 6.9 %collective-permute-start.1 = (f32[240,128]{1,0:T(8,128)S(1)}, f32[240,128]{1,0:T(8,128)S(1)}, u32[]{:S(2)}, u32[]{:S(2)}) collective-permute-start(f32[240,128]{1,0:T(8,128)S(1)} %get-tuple-element.44), channel_id=1, source_target_pairs={{0,64},{32,96},{64,0},{96,32},{128,192},{160,224},{192,128},{224,1... | collective-permute-start | bytes 368648 | tf_op jit(solution)/shard_map/ppermute | solution.py:429
  6.5 9.2 %collective-permute-start.2 = (f32[240,128]{1,0:T(8,128)S(1)}, f32[240,128]{1,0:T(8,128)S(1)}, u32[]{:S(2)}, u32[]{:S(2)}) collective-permute-start(f32[240,128]{1,0:T(8,128)S(1)} %get-tuple-element.45), channel_id=1, source_target_pairs={{0,192},{32,224},{64,128},{96,160},{128,64},{160,96},{192,0},{224,... | collective-permute-start | bytes 368648 | tf_op jit(solution)/shard_map/ppermute | solution.py:429
  6.9 8.8 %collective-permute-start.3 = (f32[240,128]{1,0:T(8,128)S(1)}, f32[240,128]{1,0:T(8,128)S(1)}, u32[]{:S(2)}, u32[]{:S(2)}) collective-permute-start(f32[240,128]{1,0:T(8,128)S(1)} %get-tuple-element.46), channel_id=1, source_target_pairs={{0,160},{32,128},{64,224},{96,192},{128,32},{160,0},{192,96},{224,... | collective-permute-start | bytes 368648 | tf_op jit(solution)/shard_map/ppermute | solution.py:429
  8.5 8.4 %collective-permute-start.4 = (f32[240,128]{1,0:T(8,128)S(1)}, f32[240,128]{1,0:T(8,128)S(1)}, u32[]{:S(2)}, u32[]{:S(2)}) collective-permute-start(f32[240,128]{1,0:T(8,128)S(1)} %get-tuple-element.47), channel_id=1, source_target_pairs={{0,96},{32,64},{64,32},{96,0},{128,224},{160,192},{192,160},{224,1... | collective-permute-start | bytes 368648 | tf_op jit(solution)/shard_map/ppermute | solution.py:429
  10.3 7.1 %collective-permute-start.5 = (f32[240,128]{1,0:T(8,128)S(1)}, f32[240,128]{1,0:T(8,128)S(1)}, u32[]{:S(2)}, u32[]{:S(2)}) collective-permute-start(f32[240,128]{1,0:T(8,128)S(1)} %get-tuple-element.48), channel_id=1, source_target_pairs={{0,224},{32,192},{64,160},{96,128},{128,96},{160,64},{192,32},{224... | collective-permute-start | bytes 368648 | tf_op jit(solution)/shard_map/ppermute | solution.py:429
  12.7 4.7 %collective-permute-start.6 = (f32[240,128]{1,0:T(8,128)S(1)}, f32[240,128]{1,0:T(8,128)S(1)}, u32[]{:S(2)}, u32[]{:S(2)}) collective-permute-start(f32[240,128]{1,0:T(8,128)S(1)} %get-tuple-element.49), channel_id=1, source_target_pairs={{0,32},{32,0},{64,96},{96,64},{128,160},{160,128},{192,224},{224,1... | collective-permute-start | bytes 368648 | tf_op jit(solution)/shard_map/ppermute | solution.py:429
  17.4 28.0 %copy-start.2 = (f32[128,128]{1,0:T(8,128)S(1)}, f32[128,128]{1,0:T(8,128)}, u32[]{:S(2)}) copy-start(f32[128,128]{1,0:T(8,128)} %constant.17.clone.forward) | copy-start | bytes 196612
  18.4 24.7 %collective-permute-start.7 = (f32[177,8,128]{2,1,0:T(8,128)S(1)}, f32[177,8,128]{2,1,0:T(8,128)S(1)}, u32[]{:S(2)}, u32[]{:S(2)}) collective-permute-start(f32[177,8,128]{2,1,0:T(8,128)S(1)} %get-tuple-element.55), channel_id=1, source_target_pairs={{1,2},{2,1},{3,4},{4,3},{5,6},{6,5},{7,8},{8,7},{9,10},{10,9},{11,... | collective-permute-start | bytes 2174984 | tf_op jit(solution)/shard_map/ppermute | solution.py:437
  26.4 18.2 %collective-permute-start.8 = (f32[177,8,128]{2,1,0:T(8,128)S(1)}, f32[177,8,128]{2,1,0:T(8,128)S(1)}, u32[]{:S(2)}, u32[]{:S(2)}) collective-permute-start(f32[177,8,128]{2,1,0:T(8,128)S(1)} %get-tuple-element.56), channel_id=1, source_target_pairs={{0,1},{1,0},{2,3},{3,2},{4,5},{5,4},{6,7},{7,6},{8,9},{9,8},{10,11... | collective-permute-start | bytes 2174984 | tf_op jit(solution)/shard_map/ppermute | solution.py:437
  45.4 17.6 %copy-start.1 = (f32[128,128]{1,0:T(8,128)S(1)}, f32[128,128]{1,0:T(8,128)}, u32[]{:S(2)}) copy-start(f32[128,128]{1,0:T(8,128)} %constant.18.clone.back) | copy-start | bytes 196612
  47.8 14.9 %collective-permute-start.9 = (f32[26,4,8,128]{3,2,1,0:T(8,128)S(1)}, f32[26,4,8,128]{3,2,1,0:T(8,128)S(1)}, u32[]{:S(2)}, u32[]{:S(2)}) collective-permute-start(f32[26,4,8,128]{3,2,1,0:T(8,128)S(1)} %get-tuple-element.61), channel_id=1, source_target_pairs={{1,2},{2,1},{3,4},{4,3},{5,6},{6,5},{7,8},{8,7},{9,10},{10,9},{11,... | collective-permute-start | bytes 1277960 | tf_op jit(solution)/shard_map/ppermute | solution.py:437
  52.0 11.0 %collective-permute-start.10 = (f32[26,4,8,128]{3,2,1,0:T(8,128)S(1)}, f32[26,4,8,128]{3,2,1,0:T(8,128)S(1)}, u32[]{:S(2)}, u32[]{:S(2)}) collective-permute-start(f32[26,4,8,128]{3,2,1,0:T(8,128)S(1)} %get-tuple-element.62), channel_id=1, source_target_pairs={{0,1},{1,0},{2,3},{3,2},{4,5},{5,4},{6,7},{7,6},{8,9},{9,8},{10,11... | collective-permute-start | bytes 1277960 | tf_op jit(solution)/shard_map/ppermute | solution.py:437
  64.4 13.3 %collective-permute-start.11 = (f32[24,4,8,128]{3,2,1,0:T(8,128)S(1)}, f32[24,4,8,128]{3,2,1,0:T(8,128)S(1)}, u32[]{:S(2)}, u32[]{:S(2)}) collective-permute-start(f32[24,4,8,128]{3,2,1,0:T(8,128)S(1)} %get-tuple-element.65), channel_id=1, source_target_pairs={{1,2},{2,1},{3,4},{4,3},{5,6},{6,5},{7,8},{8,7},{9,10},{10,9},{11,... | collective-permute-start | bytes 1179656 | tf_op jit(solution)/shard_map/ppermute | solution.py:437
  68.6 9.4 %collective-permute-start.12 = (f32[24,4,8,128]{3,2,1,0:T(8,128)S(1)}, f32[24,4,8,128]{3,2,1,0:T(8,128)S(1)}, u32[]{:S(2)}, u32[]{:S(2)}) collective-permute-start(f32[24,4,8,128]{3,2,1,0:T(8,128)S(1)} %get-tuple-element.66), channel_id=1, source_target_pairs={{0,1},{1,0},{2,3},{3,2},{4,5},{5,4},{6,7},{7,6},{8,9},{9,8},{10,11... | collective-permute-start | bytes 1179656 | tf_op jit(solution)/shard_map/ppermute | solution.py:437
  78.6 3.1 %collective-permute-start.13 = (f32[18,4,8,128]{3,2,1,0:T(8,128)S(1)}, f32[18,4,8,128]{3,2,1,0:T(8,128)S(1)}, u32[]{:S(2)}, u32[]{:S(2)}) collective-permute-start(f32[18,4,8,128]{3,2,1,0:T(8,128)S(1)} %get-tuple-element.67), channel_id=1, source_target_pairs={{32,64},{64,32},{96,128},{128,96},{160,192},{192,160},{33,65},{65,... | collective-permute-start | bytes 884744 | tf_op jit(solution)/shard_map/ppermute | solution.py:437
  79.2 3.6 %collective-permute-start.14 = (f32[18,4,8,128]{3,2,1,0:T(8,128)S(1)}, f32[18,4,8,128]{3,2,1,0:T(8,128)S(1)}, u32[]{:S(2)}, u32[]{:S(2)}) collective-permute-start(f32[18,4,8,128]{3,2,1,0:T(8,128)S(1)} %get-tuple-element.68), channel_id=1, source_target_pairs={{0,32},{32,0},{64,96},{96,64},{128,160},{160,128},{192,224},{224,1... | collective-permute-start | bytes 884744 | tf_op jit(solution)/shard_map/ppermute | solution.py:437
  85.9 14.7 %collective-permute-start.15 = (f32[26,4,8,128]{3,2,1,0:T(8,128)S(1)}, f32[26,4,8,128]{3,2,1,0:T(8,128)S(1)}, u32[]{:S(2)}, u32[]{:S(2)}) collective-permute-start(f32[26,4,8,128]{3,2,1,0:T(8,128)S(1)} %get-tuple-element.73), channel_id=1, source_target_pairs={{1,2},{2,1},{3,4},{4,3},{5,6},{6,5},{7,8},{8,7},{9,10},{10,9},{11,... | collective-permute-start | bytes 1277960 | tf_op jit(solution)/shard_map/ppermute | solution.py:437
  90.1 11.0 %collective-permute-start.16 = (f32[26,4,8,128]{3,2,1,0:T(8,128)S(1)}, f32[26,4,8,128]{3,2,1,0:T(8,128)S(1)}, u32[]{:S(2)}, u32[]{:S(2)}) collective-permute-start(f32[26,4,8,128]{3,2,1,0:T(8,128)S(1)} %get-tuple-element.74), channel_id=1, source_target_pairs={{0,1},{1,0},{2,3},{3,2},{4,5},{5,4},{6,7},{7,6},{8,9},{9,8},{10,11... | collective-permute-start | bytes 1277960 | tf_op jit(solution)/shard_map/ppermute | solution.py:437
  103.3 9.4 %collective-permute-start.17 = (f32[96,128]{1,0:T(8,128)S(1)}, f32[96,128]{1,0:T(8,128)S(1)}, u32[]{:S(2)}, u32[]{:S(2)}) collective-permute-start(f32[96,128]{1,0:T(8,128)S(1)} %get-tuple-element.76), channel_id=1, source_target_pairs={{0,128},{32,160},{64,192},{96,224},{128,0},{160,32},{192,64},{224,... | collective-permute-start | bytes 147464 | tf_op jit(solution)/shard_map/ppermute | solution.py:429
  108.9 5.7 %collective-permute-start.18 = (f32[96,128]{1,0:T(8,128)S(1)}, f32[96,128]{1,0:T(8,128)S(1)}, u32[]{:S(2)}, u32[]{:S(2)}) collective-permute-start(f32[96,128]{1,0:T(8,128)S(1)} %get-tuple-element.77), channel_id=1, source_target_pairs={{0,64},{32,96},{64,0},{96,32},{128,192},{160,224},{192,128},{224,1... | collective-permute-start | bytes 147464 | tf_op jit(solution)/shard_map/ppermute | solution.py:429
  108.9 5.8 %collective-permute-start.19 = (f32[96,128]{1,0:T(8,128)S(1)}, f32[96,128]{1,0:T(8,128)S(1)}, u32[]{:S(2)}, u32[]{:S(2)}) collective-permute-start(f32[96,128]{1,0:T(8,128)S(1)} %get-tuple-element.78), channel_id=1, source_target_pairs={{0,192},{32,224},{64,128},{96,160},{128,64},{160,96},{192,0},{224,... | collective-permute-start | bytes 147464 | tf_op jit(solution)/shard_map/ppermute | solution.py:429
  110.7 5.0 %collective-permute-start.20 = (f32[96,128]{1,0:T(8,128)S(1)}, f32[96,128]{1,0:T(8,128)S(1)}, u32[]{:S(2)}, u32[]{:S(2)}) collective-permute-start(f32[96,128]{1,0:T(8,128)S(1)} %get-tuple-element.79), channel_id=1, source_target_pairs={{0,160},{32,128},{64,224},{96,192},{128,32},{160,0},{192,96},{224,... | collective-permute-start | bytes 147464 | tf_op jit(solution)/shard_map/ppermute | solution.py:429
  110.7 5.0 %collective-permute-start.21 = (f32[96,128]{1,0:T(8,128)S(1)}, f32[96,128]{1,0:T(8,128)S(1)}, u32[]{:S(2)}, u32[]{:S(2)}) collective-permute-start(f32[96,128]{1,0:T(8,128)S(1)} %get-tuple-element.80), channel_id=1, source_target_pairs={{0,96},{32,64},{64,32},{96,0},{128,224},{160,192},{192,160},{224,1... | collective-permute-start | bytes 147464 | tf_op jit(solution)/shard_map/ppermute | solution.py:429
  112.7 4.7 %collective-permute-start.22 = (f32[96,128]{1,0:T(8,128)S(1)}, f32[96,128]{1,0:T(8,128)S(1)}, u32[]{:S(2)}, u32[]{:S(2)}) collective-permute-start(f32[96,128]{1,0:T(8,128)S(1)} %get-tuple-element.81), channel_id=1, source_target_pairs={{0,224},{32,192},{64,160},{96,128},{128,96},{160,64},{192,32},{224... | collective-permute-start | bytes 147464 | tf_op jit(solution)/shard_map/ppermute | solution.py:429
  114.6 2.8 %collective-permute-start.23 = (f32[96,128]{1,0:T(8,128)S(1)}, f32[96,128]{1,0:T(8,128)S(1)}, u32[]{:S(2)}, u32[]{:S(2)}) collective-permute-start(f32[96,128]{1,0:T(8,128)S(1)} %get-tuple-element.82), channel_id=1, source_target_pairs={{0,32},{32,0},{64,96},{96,64},{128,160},{160,128},{192,224},{224,1... | collective-permute-start | bytes 147464 | tf_op jit(solution)/shard_map/ppermute | solution.py:429

commit v4 on v3

--- a/solution.py
+++ b/solution.py
@@ -40,8 +40,15 @@
     shift_b = shift_a.copy()
     shift_b[0] = 2.0
     lag = np.sin(theta)
-    out = np.stack([shift_a, shift_b, lag])[:, :, None] * np.ones((1, 1, 128))
-    return out.astype(np.float32)
+    phase_a, phase_b = np.cos(theta), np.sin(theta)
+    phase_b[0] = -1.0
+    share = np.where(np.arange(8) == 0, 1.0, 2.0) / 16.0
+    last_a, last_b = share * np.cos(15.0 * theta), -share * np.sin(15.0 * theta)
+    last_b[0] = -1.0 / 16.0
+    first_a, first_b = share, np.where(np.arange(8) == 0, 1.0, 0.0) / 16.0
+    slot = np.where(np.arange(8) == 0, 1.0, 0.0)
+    kinds = [shift_a, shift_b, lag, phase_a, phase_b, last_a, last_b, first_a, first_b, slot]
+    return (np.stack(kinds)[:, :, None] * np.ones((1, 1, 128))).astype(np.float32)
 
 
 def whole(*shape):
@@ -68,8 +75,9 @@
 
 
 def pack_body(pos, *rest):
-    sources, outs, (near, far, here, stage), held, sems = rest[:5], rest[5:13], rest[13:17], rest[17:22], rest[22]
-    copies = [pltpu.make_async_copy(sources[i], held[i], sems.at[i]) for i in range(5)]
+    sources, outs, (near, far, here), tables = rest[:8], rest[8:16], rest[16:19], rest[19:22]
+    stage, held, sems = rest[22], rest[23:28], rest[28]
+    copies = [pltpu.make_async_copy(sources[i], ref, sems.at[i]) for i, ref in enumerate(held + tables)]
     for copy in copies:
         copy.start()
     state, adjoint, target, kappa, begin = held
@@ -90,8 +98,8 @@
                         stage[d, base + last - low : base + WIN, :] = jnp.zeros((low + WIN - last, 128), jnp.float32)
     for k in range(8):
         outs[k][...] = stage[t ^ k]
-    copies[3].wait()
-    copies[4].wait()
+    for copy in copies[3:]:
+        copy.wait()
     for d in range(8):
         @pl.when(t == d)
         def window(d=d):
@@ -161,7 +169,7 @@
 
 
 def spread_body(pos, *rest):
-    pieces, (near_c, far_c), (own, wish, near, far), stage = rest[:8], rest[8:10], rest[10:14], rest[14]
+    pieces, (near_c, far_c, forward), (own, wish, near, far), stage = rest[:8], rest[8:11], rest[11:15], rest[15]
     for i in range(3):
         near[168 + 3 * i : 171 + 3 * i] = near_c[i].reshape(3, 8, 128)
         far[168 + 3 * i : 171 + 3 * i] = far_c[i].reshape(3, 8, 128)
@@ -169,21 +177,36 @@
     rows = 12 * WIN
     for k, piece in zip(ORDER + (0,), pieces):
         stage[pl.ds(pl.multiple_of((t ^ k) * rows, 8), rows), :] = piece[...]
+
+    def steps(f, n, x, j):
+        return stage[pl.ds(((f * 2 + n) * 2 + x) * WIN + j, 8, stride=rows), :]
+
+    matrix = forward[...]
     for x in range(2):
-        for j in range(WIN):
-            for f in range(3):
-                for n in range(2):
-                    v = stage[pl.ds(((f * 2 + n) * 2 + x) * WIN + j, 8, stride=rows), :]
-                    if f < 2:
-                        c = f * 2 + n
-                        own[x, j, c] = v
-                        put_field(near, far, x, j, c, v)
-                    else:
-                        if 1 <= j <= 18:
-                            wish[x, j - 1, n] = v
-                        if 2 <= j <= 17:
-                            out = far if x == 1 else near
-                            out[136 + (j - 2) * 2 + n] = v
+        for low in range(0, WIN, 4):
+            block = [steps(f, n, x, low + i) for i in range(4) for f in range(2) for n in range(2)]
+            done = transform(matrix, jnp.concatenate(block, 0))
+            for i in range(4):
+                for c in range(4):
+                    v = done[(i * 4 + c) * 8 : (i * 4 + c + 1) * 8]
+                    own[x, low + i, c] = v
+                    put_field(near, far, x, low + i, c, v)
+    cells = [(x, j) for x in range(2) for j in range(WIN)]
+    for low in range(0, len(cells), 8):
+        block = [steps(2, n, x, j) for x, j in cells[low : low + 8] for n in range(2)]
+        done = transform(matrix, jnp.concatenate(block, 0))
+        for i, (x, j) in enumerate(cells[low : low + 8]):
+            for n in range(2):
+                v = done[(i * 2 + n) * 8 : (i * 2 + n + 1) * 8]
+                if 1 <= j <= 18:
+                    wish[x, j - 1, n] = v
+                if 2 <= j <= 17:
+                    out = far if x == 1 else near
+                    out[136 + (j - 2) * 2 + n] = v
+
+
+def transform(matrix, block):
+    return jnp.dot(matrix, block, precision=lax.Precision.HIGHEST, preferred_element_type=jnp.float32)
 
 
 def put_field(near, far, x, j, c, v):
@@ -226,7 +249,13 @@
     )
 
 
-def residual_body(own, wish, near, far, tnear, tfar, weights, consts, inv, forward, rhs, it, out_near, out_far, res, zed):
+def over_sublanes(v):
+    v = v + pltpu.roll(v, 4, 0)
+    v = v + pltpu.roll(v, 2, 0)
+    return v + pltpu.roll(v, 1, 0)
+
+
+def front_body(own, wish, near, far, tnear, tfar, weights, consts, inv, fixed, it, out_near, out_far, zed):
     def field(p, j, c):
         if p == 2 or p == 3:
             return own[p - 2, j, c]
@@ -240,43 +269,28 @@
             return wish[p - 2, j - 1, n]
         return (tnear if p == 1 else tfar)[136 + (j - 2) * 2 + n]
 
-    sub = lax.broadcasted_iota(jnp.int32, (8, 128), 0)
-    first = jnp.where(sub == 0, 1.0, 0.0)
-    not_first = jnp.where(sub == 0, 0.0, 1.0)
-    not_last = jnp.where(sub == 7, 0.0, 1.0)
+    cs = (consts[0], consts[1], consts[2])
+    phase_a, phase_b, last_a, last_b, first_a, first_b, slot = (consts[i] for i in range(3, 10))
     for p, lo, hi in ((2, 1, 19), (3, 1, 19), (1, 2, 18), (4, 2, 18)):
         def row(j, carry, p=p):
             w = row_weights(weights, p, j, 8)
-            td = w[6]
             v = [field(p, j, c) for c in range(4)]
-            n = [
-                spread_sum(v[c], (field(p + 1, j, c), field(p - 1, j, c), field(p, j + 1, c), field(p, j - 1, c)), w)
-                for c in range(4)
-            ]
+            last = over_sublanes(last_a * v[0] + last_b * v[1])
+            first = over_sublanes(first_a * v[2] + first_b * v[3])
+            begin = w[7] - last
+            kept = (
+                begin,
+                slot * begin,
+                -TAU * wanted(p, j, 0) - phase_a * first,
+                -TAU * wanted(p, j, 1) - phase_b * first,
+            )
             at = region(p, j)
-            ue, uo, pe, po = v
-            before = pltpu.roll(uo, 1, 0) * not_first
-            after = pltpu.roll(pe, 7, 0) * not_last
-            res[at, 0] = w[7] * first - (ue - before + (td * ue - n[0]) + COUPLING * pe)
-            res[at, 1] = -(uo - ue + (td * uo - n[1]) + COUPLING * po)
-            res[at, 2] = -TAU * wanted(p, j, 0) - (pe - po + (td * pe - n[2]) - TAU * ue)
-            res[at, 3] = -TAU * wanted(p, j, 1) - (po - after + (td * po - n[3]) - TAU * uo)
-            return carry
-        rows(lo, hi, row)
-
-    def group(g, carry):
-        block = res[pl.ds(g * 4, 4)].reshape(128, 128)
-        done = jnp.dot(forward[...], block, precision=lax.Precision.HIGHEST, preferred_element_type=jnp.float32)
-        rhs[pl.ds(g * 4, 4)] = done.reshape(4, 4, 8, 128)
-        return carry
-    rows(0, 17, group)
-
-    cs = (consts[0], consts[1], consts[2])
-    for p, lo, hi in ((2, 1, 19), (3, 1, 19), (1, 2, 18), (4, 2, 18)):
-        def row(j, carry, p=p):
-            td = row_weights(weights, p, j, 8)[6]
-            at = region(p, j)
-            z = solve([rhs[at, c] for c in range(4)], td, (inv[at, 0], inv[at, 1]), cs)
+            pushed = []
+            for c in range(4):
+                fixed[at, c] = kept[c]
+                around = (field(p + 1, j, c), field(p - 1, j, c), field(p, j + 1, c), field(p, j - 1, c))
+                pushed.append(kept[c] + spread_sum(v[c], around, w))
+            z = solve(pushed, w[6], (inv[at, 0], inv[at, 1]), cs)
             for c in range(4):
                 zed[at, c] = z[c]
             return carry
@@ -289,7 +303,7 @@
             pushed = []
             for c in range(4):
                 around = (zed[region(p + 1, j), c], zed[region(p - 1, j), c], zed[at + 1, c], zed[at - 1, c])
-                pushed.append(rhs[at, c] + spread_sum(zed[at, c], around, w))
+                pushed.append(fixed[at, c] + spread_sum(zed[at, c], around, w))
             z = solve(pushed, w[6], (inv[at, 0], inv[at, 1]), cs)
             for c in range(4):
                 it[p - 2, j - 2, c] = z[c]
@@ -301,7 +315,7 @@
     out_far[14:26] = it[0, 2:14]
 
 
-def sweep_body(it, near, far, rhs, weights, consts, inv, back, zed, fin):
+def sweep_body(it, near, far, fixed, weights, consts, inv, zed, put):
     def guess(p, j, c):
         if p == 2 or p == 3:
             return it[p - 2, j - 2, c]
@@ -323,7 +337,7 @@
             pushed = []
             for c in range(4):
                 around = (guess(p + 1, j, c), guess(p - 1, j, c), guess(p, j + 1, c), guess(p, j - 1, c))
-                pushed.append(rhs[at, c] + spread_sum(guess(p, j, c), around, w))
+                pushed.append(fixed[at, c] + spread_sum(guess(p, j, c), around, w))
             z = solve(pushed, w[6], (inv[at, 0], inv[at, 1]), cs)
             for c in range(4):
                 zed[at2(p, j), c] = z[c]
@@ -337,31 +351,21 @@
             pushed = []
             for c in range(4):
                 around = (zed[at2(p + 1, j), c], zed[at2(p - 1, j), c], zed[here + 1, c], zed[here - 1, c])
-                pushed.append(rhs[at, c] + spread_sum(zed[here, c], around, w))
+                pushed.append(fixed[at, c] + spread_sum(zed[here, c], around, w))
             z = solve(pushed, w[6], (inv[at, 0], inv[at, 1]), cs)
             for c in range(4):
-                fin[(p - 2) * OWN + j - 4, c] = z[c]
+                put(p - 2, j - 4, c, z[c])
             return carry
         rows(4, 16, row)
 
-    def group(g, carry):
-        block = fin[pl.ds(g * 4, 4)].reshape(128, 128)
-        done = jnp.dot(back[...], block, precision=lax.Precision.HIGHEST, preferred_element_type=jnp.float32)
-        fin[pl.ds(g * 4, 4)] = done.reshape(4, 4, 8, 128)
-        return carry
-    rows(0, 6, group)
-
-
-def middle_body(it, near, far, rhs, weights, consts, inv, back, own, new, out_near, out_far, zed, fin):
-    sweep_body(it, near, far, rhs, weights, consts, inv, back, zed, fin)
-    for x in range(2):
+
+def middle_body(it, near, far, fixed, weights, consts, inv, new, out_near, out_far, zed):
+    def put(x, j, c, v):
+        new[x, j, c] = v
         first, second = (out_near, out_far) if x == 0 else (out_far, out_near)
-        for j in range(OWN):
-            for c in range(4):
-                v = own[x, j + HALO, c] + fin[x * OWN + j, c]
-                new[x, j, c] = v
-                first[j, c] = v
-                second[OWN + j, c] = v
+        first[j, c] = v
+        second[OWN + j, c] = v
+    sweep_body(it, near, far, fixed, weights, consts, inv, zed, put)
 
 
 EDGE = ((0, 4), (4, 4), (8, 3), (11, 3), (14, 2), (16, 2))
@@ -398,14 +402,19 @@
         far[pl.ds(18 + 14 * high, 2)] = got[16:18]
 
 
-def last_body(pos, it, near, far, rhs, weights, consts, inv, back, own, *rest):
+def last_body(pos, it, near, far, fixed, weights, consts, inv, back, *rest):
     outs, (zed, fin, stage) = rest[:8], rest[8:]
-    sweep_body(it, near, far, rhs, weights, consts, inv, back, zed, fin)
+    def put(x, j, c, v):
+        fin[x * OWN + j, c] = v
+    sweep_body(it, near, far, fixed, weights, consts, inv, zed, put)
     t = pos[0]
-    for x in range(2):
-        for j in range(OWN):
-            for c in range(4):
-                stage[pl.ds((c * 2 + x) * OWN + j, 8, stride=8 * OWN), :] = own[x, j + HALO, c] + fin[x * OWN + j, c]
+    matrix = back[...]
+    for low in range(0, 2 * OWN, 4):
+        done = transform(matrix, fin[low : low + 4].reshape(128, 128))
+        for i in range(4):
+            x, j = divmod(low + i, OWN)
+            for c in range(4):
+                stage[pl.ds((c * 2 + x) * OWN + j, 8, stride=8 * OWN), :] = done[(i * 4 + c) * 8 : (i * 4 + c + 1) * 8]
     for k in range(8):
         outs[k][...] = stage[pl.ds(pl.multiple_of((t ^ k) * 8 * OWN, 8), 8 * OWN), :]
 
@@ -445,25 +454,27 @@
     forward, back = (jnp.asarray(m) for m in transform_matrices())
     consts = jnp.asarray(mode_constants())
 
-    *pieces, near_c, far_c, here_c = call(
+    arguments = (state_guess, adjoint_guess, target, diffusivity, initial_state, forward, back, consts)
+    *pieces, near_c, far_c, here_c, forward, back, consts = call(
         pack_body,
         "pack",
-        [whole(12 * WIN, 128)] * 8 + [whole(3, TALL, 128)] * 2 + [whole(4, TALL, 128)],
+        [whole(12 * WIN, 128)] * 8 + [whole(3, TALL, 128)] * 2 + [whole(4, TALL, 128)]
+        + [whole(128, 128)] * 2 + [whole(10, 8, 128)],
         0,
         [pltpu.VMEM((8, 12 * WIN, 128), jnp.float32)]
         + [pltpu.VMEM((2, 2, 96, 128), jnp.float32)] * 3
         + [pltpu.VMEM((2, 96, 128), jnp.float32)] * 2
-        + [pltpu.SemaphoreType.DMA((5,))],
-        far_inputs=5,
-    )(pos, *(pltpu.with_memory_space_constraint(a, pltpu.HBM) for a in (state_guess, adjoint_guess, target, diffusivity, initial_state)))
+        + [pltpu.SemaphoreType.DMA((8,))],
+        far_inputs=8,
+    )(pos, *(pltpu.with_memory_space_constraint(a, pltpu.HBM) for a in arguments))
     got = exchange(pieces)
     own, wish, near, far = call(
         spread_body,
         "spread",
         [whole(2, WIN, 4, 8, 128), whole(2, 18, 2, 8, 128), whole(177, 8, 128), whole(177, 8, 128)],
-        10,
+        11,
         [pltpu.VMEM((8 * 12 * WIN, 128), jnp.float32)],
-    )(pos, *got, near_c, far_c)
+    )(pos, *got, near_c, far_c, forward)
     far = far_first = swap(far, "space", 0)
     near = near_first = swap(near, "space", 1)
     weights, inv = call(
@@ -471,16 +482,16 @@
     )(pos, here_c, near, far, consts)
     weights = weights.reshape(4 * TALL, 8, 128)
 
-    sweep_scratch = [pltpu.VMEM((52, 4, 8, 128), jnp.float32), pltpu.VMEM((24, 4, 8, 128), jnp.float32)]
+    sweep_scratch = [pltpu.VMEM((52, 4, 8, 128), jnp.float32)]
     for outer in range(OUTER):
-        rhs, it, near_z, far_z = call(
-            residual_body,
-            "residual",
+        fixed, it, near_z, far_z = call(
+            front_body,
+            "front",
             [whole(68, 4, 8, 128), whole(2, 16, 4, 8, 128), whole(26, 4, 8, 128), whole(26, 4, 8, 128)],
-            10,
-            [pltpu.VMEM((68, 4, 8, 128), jnp.float32)] * 2,
+            9,
+            [pltpu.VMEM((68, 4, 8, 128), jnp.float32)],
             scalars=0,
-        )(own, wish, near, far, near_first, far_first, weights, consts, inv, forward)
+        )(own, wish, near, far, near_first, far_first, weights, consts, inv)
         far_z = swap(far_z, "space", 0)
         near_z = swap(near_z, "space", 1)
         if outer < OUTER - 1:
@@ -488,10 +499,10 @@
                 middle_body,
                 "middle",
                 [whole(2, OWN, 4, 8, 128), whole(2 * OWN, 4, 8, 128), whole(2 * OWN, 4, 8, 128)],
-                9,
+                7,
                 sweep_scratch,
                 scalars=0,
-            )(it, near_z, far_z, rhs, weights, consts, inv, back, own)
+            )(it, near_z, far_z, fixed, weights, consts, inv)
             far = swap(far, "space", 0)
             near = swap(near, "space", 1)
             send0, send1 = call(edges_body, "edges", [whole(18, 4, 8, 128)] * 2, 3)(pos, new, near, far)
@@ -506,9 +517,9 @@
         last_body,
         "last",
         [whole(8 * OWN, 128)] * 8,
-        9,
-        sweep_scratch + [pltpu.VMEM((64 * OWN, 128), jnp.float32)],
-    )(pos, it, near_z, far_z, rhs, weights, consts, inv, back, own)
+        8,
+        sweep_scratch + [pltpu.VMEM((2 * OWN, 4, 8, 128), jnp.float32), pltpu.VMEM((64 * OWN, 128), jnp.float32)],
+    )(pos, it, near_z, far_z, fixed, weights, consts, inv, back)
     got = exchange(pieces)
     return tuple(
         call(

time: 120 us -> 118 us (0.983)
  Pallas kernels: 14.4 us -> 12.8 us
    pallas_call x3, Pallas kernels: 6.87 us -> 5.05 us  [the longest x2 2.98 us: on_device(): call(front_body, 'front', [whole(68, 4, 8, 128), whole(2, 16, 4, 8, 128),...]
where the time goes in v4:
time: 118 us; the launch traced here: 117 us
  waiting for transfers between devices  58.9 us (50%)
  starting transfers between devices  44.8 us (38%)
  Pallas kernels  12.8 us (11%)
    ppermute x10, waiting for transfers between devices, swap(): return lax.ppermute(block, axis, route)  50.2 us
    ppermute x10, starting transfers between devices, swap(): return lax.ppermute(block, axis, route)  24.1 us
    ppermute x14, starting transfers between devices, exchange(): lax.ppermute(pieces[k], 'tm', [(i, i ^ k) for i in range(count)])  20.7 us
    ppermute x14, waiting for transfers between devices, exchange(): lax.ppermute(pieces[k], 'tm', [(i, i ^ k) for i in range(count)])  8.64 us
    pallas_call x2, Pallas kernels, on_device(): call(front_body, 'front', [whole(68, 4, 8, 128), whole(2, 16, 4, 8, 128),...  2.98 us
  transfers between devices with their start and end apart: 24, of which 15 were waited for; matrix products, arithmetic and copies ran while one was open for 0% of the time, Pallas kernels for 0%

profile of v4, /device:TPU:6, one launch (start us, length us, event | category | flops | bytes accessed | tf_op | source)
XLA Modules:
  0.0 117.3 jit_solution(13741097312262946978)
XLA Ops:
  0.6 0.1 pad_add_fusion.pos
  0.7 1.9 %pack.1 = (f32[240,128]{1,0:T(8,128)S(1)}, f32[240,128]{1,0:T(8,128)S(1)}, f32[240,128]{1,0:T(8,128)S(1)}, f32[240,128]{1,0:T(8,128)S(1)}, f32[240,128]{1,0:T(8,...) custom-call(s32[3]{0:T(128)S(1)} %pad_add_fusion.pos, ...), custom_call_target="tpu_custom_call" | custom-call | tf_op jit(solution)/shard_map/pack/pallas_call | solution.py:458
  2.6 3.3 %collective-permute-start = (f32[240,128]{1,0:T(8,128)S(1)}, f32[240,128]{1,0:T(8,128)S(1)}, u32[]{:S(2)}, u32[]{:S(2)}) collective-permute-start(f32[240,128]{1,0:T(8,128)S(1)} %get-tuple-element.46), channel_id=1, source_target_pairs={{0,128},{32,160},{64,192},{96,224},{128,0},{160,32},{192,64},{224,... | collective-permute-start | bytes 368648 | tf_op jit(solution)/shard_map/ppermute | solution.py:438
  5.9 0.7 collective-permute-start.1
  6.5 0.4 collective-permute-start.2
  6.9 1.6 %collective-permute-start.3 = (f32[240,128]{1,0:T(8,128)S(1)}, f32[240,128]{1,0:T(8,128)S(1)}, u32[]{:S(2)}, u32[]{:S(2)}) collective-permute-start(f32[240,128]{1,0:T(8,128)S(1)} %get-tuple-element.49), channel_id=1, source_target_pairs={{0,160},{32,128},{64,224},{96,192},{128,32},{160,0},{192,96},{224,... | collective-permute-start | bytes 368648 | tf_op jit(solution)/shard_map/ppermute | solution.py:438
  8.6 1.8 %collective-permute-start.4 = (f32[240,128]{1,0:T(8,128)S(1)}, f32[240,128]{1,0:T(8,128)S(1)}, u32[]{:S(2)}, u32[]{:S(2)}) collective-permute-start(f32[240,128]{1,0:T(8,128)S(1)} %get-tuple-element.50), channel_id=1, source_target_pairs={{0,96},{32,64},{64,32},{96,0},{128,224},{160,192},{192,160},{224,1... | collective-permute-start | bytes 368648 | tf_op jit(solution)/shard_map/ppermute | solution.py:438
  10.4 0.5 collective-permute-start.5
  10.8 1.9 %collective-permute-done.1.rest_1_ = f32[240,128]{1,0:T(8,128)S(1)} collective-permute-done((f32[240,128]{1,0:T(8,128)S(1)}, f32[240,128]{1,0:T(8,128)S(1)}, u32[]{:S(2)}, u32[]{:S(2)}) %collective-permute-start.1) | collective-permute-done | bytes 122912 | tf_op jit(solution)/shard_map/ppermute | solution.py:438
  12.8 0.8 collective-permute-start.6
  13.5 2.2 %collective-permute-done.2.rest_2_ = f32[240,128]{1,0:T(8,128)S(1)} collective-permute-done((f32[240,128]{1,0:T(8,128)S(1)}, f32[240,128]{1,0:T(8,128)S(1)}, u32[]{:S(2)}, u32[]{:S(2)}) %collective-permute-start.2) | collective-permute-done | bytes 122912 | tf_op jit(solution)/shard_map/ppermute | solution.py:438
  15.7 1.2 %collective-permute-done.4.rest_4_ = f32[240,128]{1,0:T(8,128)S(1)} collective-permute-done((f32[240,128]{1,0:T(8,128)S(1)}, f32[240,128]{1,0:T(8,128)S(1)}, u32[]{:S(2)}, u32[]{:S(2)}) %collective-permute-start.4) | collective-permute-done | bytes 122912 | tf_op jit(solution)/shard_map/ppermute | solution.py:438
  16.9 0.5 collective-permute-done.5.rest_5_
  17.5 1.6 %spread.1 = (f32[2,20,4,8,128]{4,3,2,1,0:T(8,128)S(1)}, f32[2,18,2,8,128]{4,3,2,1,0:T(8,128)S(1)}, f32[177,8,128]{2,1,0:T(8,128)S(1)}, f32[177,8,128]{2,1,0:T(8,128)S(1)}) custom-call(s32[3]{0:T(128)S(1)} %pad_add_fusion.pos, f32[240,128]{1,0:T(8,128)S(1)} %collective-permute-done.rest_0_, f32[240,128]{1,0:T(8,128)S(1)} %collective-permute-done.1.rest_1_, ...), custom_call_target="tpu_custom_call" | custom-call | tf_op jit(solution)/shard_map/spread/pallas_call | solution.py:471
  19.1 8.0 %collective-permute-start.7 = (f32[177,8,128]{2,1,0:T(8,128)S(1)}, f32[177,8,128]{2,1,0:T(8,128)S(1)}, u32[]{:S(2)}, u32[]{:S(2)}) collective-permute-start(f32[177,8,128]{2,1,0:T(8,128)S(1)} %get-tuple-element.59), channel_id=1, source_target_pairs={{1,2},{2,1},{3,4},{4,3},{5,6},{6,5},{7,8},{8,7},{9,10},{10,9},{11,... | collective-permute-start | bytes 2174984 | tf_op jit(solution)/shard_map/ppermute | solution.py:446
  27.1 0.1 collective-permute-start.8
  27.2 16.5 %collective-permute-done.7.near.tnear = f32[177,8,128]{2,1,0:T(8,128)S(1)} collective-permute-done((f32[177,8,128]{2,1,0:T(8,128)S(1)}, f32[177,8,128]{2,1,0:T(8,128)S(1)}, u32[]{:S(2)}, u32[]{:S(2)}) %collective-permute-start.7) | collective-permute-done | bytes 725024 | tf_op jit(solution)/shard_map/ppermute | solution.py:446
  43.7 1.6 %collective-permute-done.8.far.tfar = f32[177,8,128]{2,1,0:T(8,128)S(1)} collective-permute-done((f32[177,8,128]{2,1,0:T(8,128)S(1)}, f32[177,8,128]{2,1,0:T(8,128)S(1)}, u32[]{:S(2)}, u32[]{:S(2)}) %collective-permute-start.8) | collective-permute-done | bytes 725024 | tf_op jit(solution)/shard_map/ppermute | solution.py:446
  45.3 0.8 coefficients.1
  46.1 1.5 %front.2 = (f32[68,4,8,128]{3,2,1,0:T(8,128)S(1)}, f32[2,16,4,8,128]{4,3,2,1,0:T(8,128)S(1)}, f32[26,4,8,128]{3,2,1,0:T(8,128)S(1)}, f32[26,4,8,128]{3,2,1,0:T(8,128)S(1)}) custom-call(f32[2,20,4,8,128]{4,3,2,1,0:T(8,128)S(1)} %get-tuple-element.57.own, f32[2,18,2,8,128]{4,3,2,1,0:T(8,128)S(1)} %get-tuple-element.58.wish, ...), custom_call_target="tpu_custom_call" | custom-call | tf_op jit(solution)/shard_map/front/pallas_call | solution.py:487
  47.6 4.2 %collective-permute-start.9 = (f32[26,4,8,128]{3,2,1,0:T(8,128)S(1)}, f32[26,4,8,128]{3,2,1,0:T(8,128)S(1)}, u32[]{:S(2)}, u32[]{:S(2)}) collective-permute-start(f32[26,4,8,128]{3,2,1,0:T(8,128)S(1)} %get-tuple-element.66), channel_id=1, source_target_pairs={{1,2},{2,1},{3,4},{4,3},{5,6},{6,5},{7,8},{8,7},{9,10},{10,9},{11,... | collective-permute-start | bytes 1277960 | tf_op jit(solution)/shard_map/ppermute | solution.py:446
  51.8 0.1 collective-permute-start.10
  51.9 10.6 %collective-permute-done.9.near = f32[26,4,8,128]{3,2,1,0:T(8,128)S(1)} collective-permute-done((f32[26,4,8,128]{3,2,1,0:T(8,128)S(1)}, f32[26,4,8,128]{3,2,1,0:T(8,128)S(1)}, u32[]{:S(2)}, u32[]{:S(2)}) %collective-permute-start.9) | collective-permute-done | bytes 426016 | tf_op jit(solution)/shard_map/ppermute | solution.py:446
  62.4 0.3 collective-permute-done.10.far
  62.8 0.9 middle.1
  63.7 4.2 %collective-permute-start.11 = (f32[24,4,8,128]{3,2,1,0:T(8,128)S(1)}, f32[24,4,8,128]{3,2,1,0:T(8,128)S(1)}, u32[]{:S(2)}, u32[]{:S(2)}) collective-permute-start(f32[24,4,8,128]{3,2,1,0:T(8,128)S(1)} %get-tuple-element.70), channel_id=1, source_target_pairs={{1,2},{2,1},{3,4},{4,3},{5,6},{6,5},{7,8},{8,7},{9,10},{10,9},{11,... | collective-permute-start | bytes 1179656 | tf_op jit(solution)/shard_map/ppermute | solution.py:446
  67.9 0.1 collective-permute-start.12
  68.0 9.0 %collective-permute-done.11.near.near_x = f32[24,4,8,128]{3,2,1,0:T(8,128)S(1)} collective-permute-done((f32[24,4,8,128]{3,2,1,0:T(8,128)S(1)}, f32[24,4,8,128]{3,2,1,0:T(8,128)S(1)}, u32[]{:S(2)}, u32[]{:S(2)}) %collective-permute-start.11) | collective-permute-done | bytes 393248 | tf_op jit(solution)/shard_map/ppermute | solution.py:446
  77.0 0.3 collective-permute-done.12.far.far_x
  77.3 0.6 edges.1
  77.9 0.7 collective-permute-start.13
  78.5 2.2 %collective-permute-start.14 = (f32[18,4,8,128]{3,2,1,0:T(8,128)S(1)}, f32[18,4,8,128]{3,2,1,0:T(8,128)S(1)}, u32[]{:S(2)}, u32[]{:S(2)}) collective-permute-start(f32[18,4,8,128]{3,2,1,0:T(8,128)S(1)} %get-tuple-element.73), channel_id=1, source_target_pairs={{0,32},{32,0},{64,96},{96,64},{128,160},{160,128},{192,224},{224,1... | collective-permute-start | bytes 884744 | tf_op jit(solution)/shard_map/ppermute | solution.py:446
  80.8 1.2 %collective-permute-done.14.got0 = f32[18,4,8,128]{3,2,1,0:T(8,128)S(1)} collective-permute-done((f32[18,4,8,128]{3,2,1,0:T(8,128)S(1)}, f32[18,4,8,128]{3,2,1,0:T(8,128)S(1)}, u32[]{:S(2)}, u32[]{:S(2)}) %collective-permute-start.14) | collective-permute-done | bytes 294944 | tf_op jit(solution)/shard_map/ppermute | solution.py:446
  82.0 0.7 widen.1
  82.6 1.5 %front.3 = (f32[68,4,8,128]{3,2,1,0:T(8,128)S(1)}, f32[2,16,4,8,128]{4,3,2,1,0:T(8,128)S(1)}, f32[26,4,8,128]{3,2,1,0:T(8,128)S(1)}, f32[26,4,8,128]{3,2,1,0:T(8,128)S(1)}) custom-call(f32[2,20,4,8,128]{4,3,2,1,0:T(8,128)S(1)} %get-tuple-element.74.own, f32[2,18,2,8,128]{4,3,2,1,0:T(8,128)S(1)} %get-tuple-element.58.wish, f32[136,8,128]{2,1,0:T(8,128)S(1)} %bitcast.10, ...), custom_call_target="tpu_custom_call" | custom-call | tf_op jit(solution)/shard_map/front/pallas_call | solution.py:487
  84.1 4.2 %collective-permute-start.15 = (f32[26,4,8,128]{3,2,1,0:T(8,128)S(1)}, f32[26,4,8,128]{3,2,1,0:T(8,128)S(1)}, u32[]{:S(2)}, u32[]{:S(2)}) collective-permute-start(f32[26,4,8,128]{3,2,1,0:T(8,128)S(1)} %get-tuple-element.78), channel_id=1, source_target_pairs={{1,2},{2,1},{3,4},{4,3},{5,6},{6,5},{7,8},{8,7},{9,10},{10,9},{11,... | collective-permute-start | bytes 1277960 | tf_op jit(solution)/shard_map/ppermute | solution.py:446
  88.3 0.3 collective-permute-start.16
  88.6 10.0 %collective-permute-done.15.near = f32[26,4,8,128]{3,2,1,0:T(8,128)S(1)} collective-permute-done((f32[26,4,8,128]{3,2,1,0:T(8,128)S(1)}, f32[26,4,8,128]{3,2,1,0:T(8,128)S(1)}, u32[]{:S(2)}, u32[]{:S(2)}) %collective-permute-start.15) | collective-permute-done | bytes 426016 | tf_op jit(solution)/shard_map/ppermute | solution.py:446
  98.6 0.7 collective-permute-done.16.far
  99.4 2.1 %last.1 = (f32[96,128]{1,0:T(8,128)S(1)}, f32[96,128]{1,0:T(8,128)S(1)}, f32[96,128]{1,0:T(8,128)S(1)}, f32[96,128]{1,0:T(8,128)S(1)}, f32[96,128]{1,0:T(8,128)S...) custom-call(s32[3]{0:T(128)S(1)} %pad_add_fusion.pos, ...), custom_call_target="tpu_custom_call" | custom-call | tf_op jit(solution)/shard_map/last/pallas_call | solution.py:516
  101.4 6.0 %collective-permute-start.17 = (f32[96,128]{1,0:T(8,128)S(1)}, f32[96,128]{1,0:T(8,128)S(1)}, u32[]{:S(2)}, u32[]{:S(2)}) collective-permute-start(f32[96,128]{1,0:T(8,128)S(1)} %get-tuple-element.82), channel_id=1, source_target_pairs={{0,128},{32,160},{64,192},{96,224},{128,0},{160,32},{192,64},{224,... | collective-permute-start | bytes 147464 | tf_op jit(solution)/shard_map/ppermute | solution.py:438
  107.4 1.8 %collective-permute-start.19 = (f32[96,128]{1,0:T(8,128)S(1)}, f32[96,128]{1,0:T(8,128)S(1)}, u32[]{:S(2)}, u32[]{:S(2)}) collective-permute-start(f32[96,128]{1,0:T(8,128)S(1)} %get-tuple-element.84), channel_id=1, source_target_pairs={{0,192},{32,224},{64,128},{96,160},{128,64},{160,96},{192,0},{224,... | collective-permute-start | bytes 147464 | tf_op jit(solution)/shard_map/ppermute | solution.py:438
  109.3 2.0 %collective-permute-start.21 = (f32[96,128]{1,0:T(8,128)S(1)}, f32[96,128]{1,0:T(8,128)S(1)}, u32[]{:S(2)}, u32[]{:S(2)}) collective-permute-start(f32[96,128]{1,0:T(8,128)S(1)} %get-tuple-element.86), channel_id=1, source_target_pairs={{0,96},{32,64},{64,32},{96,0},{128,224},{160,192},{192,160},{224,1... | collective-permute-start | bytes 147464 | tf_op jit(solution)/shard_map/ppermute | solution.py:438
  111.3 1.9 %collective-permute-start.22 = (f32[96,128]{1,0:T(8,128)S(1)}, f32[96,128]{1,0:T(8,128)S(1)}, u32[]{:S(2)}, u32[]{:S(2)}) collective-permute-start(f32[96,128]{1,0:T(8,128)S(1)} %get-tuple-element.87), channel_id=1, source_target_pairs={{0,224},{32,192},{64,160},{96,128},{128,96},{160,64},{192,32},{224... | collective-permute-start | bytes 147464 | tf_op jit(solution)/shard_map/ppermute | solution.py:438
  113.1 0.1 collective-permute-start.23
  113.2 1.1 collective-permute-done.20.rest_3_
  114.3 1.7 %collective-permute-done.22.rest_5_ = f32[96,128]{1,0:T(8,128)S(1)} collective-permute-done((f32[96,128]{1,0:T(8,128)S(1)}, f32[96,128]{1,0:T(8,128)S(1)}, u32[]{:S(2)}, u32[]{:S(2)}) %collective-permute-start.22) | collective-permute-done | bytes 49184 | tf_op jit(solution)/shard_map/ppermute | solution.py:438
  116.0 1.3 %unpack.1 = (f32[2,2,96,128]{3,2,1,0:T(8,128)}, f32[2,2,96,128]{3,2,1,0:T(8,128)}) custom-call(s32[3]{0:T(128)S(1)} %pad_add_fusion.pos, f32[96,128]{1,0:T(8,128)S(1)} %collective-permute-done.17.rest_0_, f32[96,128]{1,0:T(8,128)S(1)} %collective-permute-done.18.rest_1_, f32[96,128]{1,0:T(8,128)S(1)} %collective-permute-done.19.rest_2_, ...), custom_call_target="tpu_custom_call" | custom-call | tf_op jit(solution)/shard_map/unpack/pallas_call | solution.py:525
  (11 shorter events, 0.0 us)
Async XLA Ops:
  2.6 7.8 %collective-permute-start = (f32[240,128]{1,0:T(8,128)S(1)}, f32[240,128]{1,0:T(8,128)S(1)}, u32[]{:S(2)}, u32[]{:S(2)}) collective-permute-start(f32[240,128]{1,0:T(8,128)S(1)} %get-tuple-element.46), channel_id=1, source_target_pairs={{0,128},{32,160},{64,192},{96,224},{128,0},{160,32},{192,64},{224,... | collective-permute-start | bytes 368648 | tf_op jit(solution)/shard_map/ppermute | solution.py:438
  5.9 6.9 %collective-permute-start.1 = (f32[240,128]{1,0:T(8,128)S(1)}, f32[240,128]{1,0:T(8,128)S(1)}, u32[]{:S(2)}, u32[]{:S(2)}) collective-permute-start(f32[240,128]{1,0:T(8,128)S(1)} %get-tuple-element.47), channel_id=1, source_target_pairs={{0,64},{32,96},{64,0},{96,32},{128,192},{160,224},{192,128},{224,1... | collective-permute-start | bytes 368648 | tf_op jit(solution)/shard_map/ppermute | solution.py:438
  6.5 9.2 %collective-permute-start.2 = (f32[240,128]{1,0:T(8,128)S(1)}, f32[240,128]{1,0:T(8,128)S(1)}, u32[]{:S(2)}, u32[]{:S(2)}) collective-permute-start(f32[240,128]{1,0:T(8,128)S(1)} %get-tuple-element.48), channel_id=1, source_target_pairs={{0,192},{32,224},{64,128},{96,160},{128,64},{160,96},{192,0},{224,... | collective-permute-start | bytes 368648 | tf_op jit(solution)/shard_map/ppermute | solution.py:438
  6.9 8.8 %collective-permute-start.3 = (f32[240,128]{1,0:T(8,128)S(1)}, f32[240,128]{1,0:T(8,128)S(1)}, u32[]{:S(2)}, u32[]{:S(2)}) collective-permute-start(f32[240,128]{1,0:T(8,128)S(1)} %get-tuple-element.49), channel_id=1, source_target_pairs={{0,160},{32,128},{64,224},{96,192},{128,32},{160,0},{192,96},{224,... | collective-permute-start | bytes 368648 | tf_op jit(solution)/shard_map/ppermute | solution.py:438
  8.6 8.4 %collective-permute-start.4 = (f32[240,128]{1,0:T(8,128)S(1)}, f32[240,128]{1,0:T(8,128)S(1)}, u32[]{:S(2)}, u32[]{:S(2)}) collective-permute-start(f32[240,128]{1,0:T(8,128)S(1)} %get-tuple-element.50), channel_id=1, source_target_pairs={{0,96},{32,64},{64,32},{96,0},{128,224},{160,192},{192,160},{224,1... | collective-permute-start | bytes 368648 | tf_op jit(solution)/shard_map/ppermute | solution.py:438
  10.4 7.1 %collective-permute-start.5 = (f32[240,128]{1,0:T(8,128)S(1)}, f32[240,128]{1,0:T(8,128)S(1)}, u32[]{:S(2)}, u32[]{:S(2)}) collective-permute-start(f32[240,128]{1,0:T(8,128)S(1)} %get-tuple-element.51), channel_id=1, source_target_pairs={{0,224},{32,192},{64,160},{96,128},{128,96},{160,64},{192,32},{224... | collective-permute-start | bytes 368648 | tf_op jit(solution)/shard_map/ppermute | solution.py:438
  12.8 4.7 %collective-permute-start.6 = (f32[240,128]{1,0:T(8,128)S(1)}, f32[240,128]{1,0:T(8,128)S(1)}, u32[]{:S(2)}, u32[]{:S(2)}) collective-permute-start(f32[240,128]{1,0:T(8,128)S(1)} %get-tuple-element.52), channel_id=1, source_target_pairs={{0,32},{32,0},{64,96},{96,64},{128,160},{160,128},{192,224},{224,1... | collective-permute-start | bytes 368648 | tf_op jit(solution)/shard_map/ppermute | solution.py:438
  19.1 24.7 %collective-permute-start.7 = (f32[177,8,128]{2,1,0:T(8,128)S(1)}, f32[177,8,128]{2,1,0:T(8,128)S(1)}, u32[]{:S(2)}, u32[]{:S(2)}) collective-permute-start(f32[177,8,128]{2,1,0:T(8,128)S(1)} %get-tuple-element.59), channel_id=1, source_target_pairs={{1,2},{2,1},{3,4},{4,3},{5,6},{6,5},{7,8},{8,7},{9,10},{10,9},{11,... | collective-permute-start | bytes 2174984 | tf_op jit(solution)/shard_map/ppermute | solution.py:446
  27.1 18.2 %collective-permute-start.8 = (f32[177,8,128]{2,1,0:T(8,128)S(1)}, f32[177,8,128]{2,1,0:T(8,128)S(1)}, u32[]{:S(2)}, u32[]{:S(2)}) collective-permute-start(f32[177,8,128]{2,1,0:T(8,128)S(1)} %get-tuple-element.60), channel_id=1, source_target_pairs={{0,1},{1,0},{2,3},{3,2},{4,5},{5,4},{6,7},{7,6},{8,9},{9,8},{10,11... | collective-permute-start | bytes 2174984 | tf_op jit(solution)/shard_map/ppermute | solution.py:446
  47.6 14.9 %collective-permute-start.9 = (f32[26,4,8,128]{3,2,1,0:T(8,128)S(1)}, f32[26,4,8,128]{3,2,1,0:T(8,128)S(1)}, u32[]{:S(2)}, u32[]{:S(2)}) collective-permute-start(f32[26,4,8,128]{3,2,1,0:T(8,128)S(1)} %get-tuple-element.66), channel_id=1, source_target_pairs={{1,2},{2,1},{3,4},{4,3},{5,6},{6,5},{7,8},{8,7},{9,10},{10,9},{11,... | collective-permute-start | bytes 1277960 | tf_op jit(solution)/shard_map/ppermute | solution.py:446
  51.8 11.0 %collective-permute-start.10 = (f32[26,4,8,128]{3,2,1,0:T(8,128)S(1)}, f32[26,4,8,128]{3,2,1,0:T(8,128)S(1)}, u32[]{:S(2)}, u32[]{:S(2)}) collective-permute-start(f32[26,4,8,128]{3,2,1,0:T(8,128)S(1)} %get-tuple-element.67), channel_id=1, source_target_pairs={{0,1},{1,0},{2,3},{3,2},{4,5},{5,4},{6,7},{7,6},{8,9},{9,8},{10,11... | collective-permute-start | bytes 1277960 | tf_op jit(solution)/shard_map/ppermute | solution.py:446
  63.7 13.3 %collective-permute-start.11 = (f32[24,4,8,128]{3,2,1,0:T(8,128)S(1)}, f32[24,4,8,128]{3,2,1,0:T(8,128)S(1)}, u32[]{:S(2)}, u32[]{:S(2)}) collective-permute-start(f32[24,4,8,128]{3,2,1,0:T(8,128)S(1)} %get-tuple-element.70), channel_id=1, source_target_pairs={{1,2},{2,1},{3,4},{4,3},{5,6},{6,5},{7,8},{8,7},{9,10},{10,9},{11,... | collective-permute-start | bytes 1179656 | tf_op jit(solution)/shard_map/ppermute | solution.py:446
  67.9 9.4 %collective-permute-start.12 = (f32[24,4,8,128]{3,2,1,0:T(8,128)S(1)}, f32[24,4,8,128]{3,2,1,0:T(8,128)S(1)}, u32[]{:S(2)}, u32[]{:S(2)}) collective-permute-start(f32[24,4,8,128]{3,2,1,0:T(8,128)S(1)} %get-tuple-element.71), channel_id=1, source_target_pairs={{0,1},{1,0},{2,3},{3,2},{4,5},{5,4},{6,7},{7,6},{8,9},{9,8},{10,11... | collective-permute-start | bytes 1179656 | tf_op jit(solution)/shard_map/ppermute | solution.py:446
  77.9 2.9 %collective-permute-start.13 = (f32[18,4,8,128]{3,2,1,0:T(8,128)S(1)}, f32[18,4,8,128]{3,2,1,0:T(8,128)S(1)}, u32[]{:S(2)}, u32[]{:S(2)}) collective-permute-start(f32[18,4,8,128]{3,2,1,0:T(8,128)S(1)} %get-tuple-element.72), channel_id=1, source_target_pairs={{32,64},{64,32},{96,128},{128,96},{160,192},{192,160},{33,65},{65,... | collective-permute-start | bytes 884744 | tf_op jit(solution)/shard_map/ppermute | solution.py:446
  78.5 3.4 %collective-permute-start.14 = (f32[18,4,8,128]{3,2,1,0:T(8,128)S(1)}, f32[18,4,8,128]{3,2,1,0:T(8,128)S(1)}, u32[]{:S(2)}, u32[]{:S(2)}) collective-permute-start(f32[18,4,8,128]{3,2,1,0:T(8,128)S(1)} %get-tuple-element.73), channel_id=1, source_target_pairs={{0,32},{32,0},{64,96},{96,64},{128,160},{160,128},{192,224},{224,1... | collective-permute-start | bytes 884744 | tf_op jit(solution)/shard_map/ppermute | solution.py:446
  84.1 14.5 %collective-permute-start.15 = (f32[26,4,8,128]{3,2,1,0:T(8,128)S(1)}, f32[26,4,8,128]{3,2,1,0:T(8,128)S(1)}, u32[]{:S(2)}, u32[]{:S(2)}) collective-permute-start(f32[26,4,8,128]{3,2,1,0:T(8,128)S(1)} %get-tuple-element.78), channel_id=1, source_target_pairs={{1,2},{2,1},{3,4},{4,3},{5,6},{6,5},{7,8},{8,7},{9,10},{10,9},{11,... | collective-permute-start | bytes 1277960 | tf_op jit(solution)/shard_map/ppermute | solution.py:446
  88.3 11.0 %collective-permute-start.16 = (f32[26,4,8,128]{3,2,1,0:T(8,128)S(1)}, f32[26,4,8,128]{3,2,1,0:T(8,128)S(1)}, u32[]{:S(2)}, u32[]{:S(2)}) collective-permute-start(f32[26,4,8,128]{3,2,1,0:T(8,128)S(1)} %get-tuple-element.79), channel_id=1, source_target_pairs={{0,1},{1,0},{2,3},{3,2},{4,5},{5,4},{6,7},{7,6},{8,9},{9,8},{10,11... | collective-permute-start | bytes 1277960 | tf_op jit(solution)/shard_map/ppermute | solution.py:446
  101.4 9.8 %collective-permute-start.17 = (f32[96,128]{1,0:T(8,128)S(1)}, f32[96,128]{1,0:T(8,128)S(1)}, u32[]{:S(2)}, u32[]{:S(2)}) collective-permute-start(f32[96,128]{1,0:T(8,128)S(1)} %get-tuple-element.82), channel_id=1, source_target_pairs={{0,128},{32,160},{64,192},{96,224},{128,0},{160,32},{192,64},{224,... | collective-permute-start | bytes 147464 | tf_op jit(solution)/shard_map/ppermute | solution.py:438
  107.4 5.7 %collective-permute-start.18 = (f32[96,128]{1,0:T(8,128)S(1)}, f32[96,128]{1,0:T(8,128)S(1)}, u32[]{:S(2)}, u32[]{:S(2)}) collective-permute-start(f32[96,128]{1,0:T(8,128)S(1)} %get-tuple-element.83), channel_id=1, source_target_pairs={{0,64},{32,96},{64,0},{96,32},{128,192},{160,224},{192,128},{224,1... | collective-permute-start | bytes 147464 | tf_op jit(solution)/shard_map/ppermute | solution.py:438
  107.4 5.8 %collective-permute-start.19 = (f32[96,128]{1,0:T(8,128)S(1)}, f32[96,128]{1,0:T(8,128)S(1)}, u32[]{:S(2)}, u32[]{:S(2)}) collective-permute-start(f32[96,128]{1,0:T(8,128)S(1)} %get-tuple-element.84), channel_id=1, source_target_pairs={{0,192},{32,224},{64,128},{96,160},{128,64},{160,96},{192,0},{224,... | collective-permute-start | bytes 147464 | tf_op jit(solution)/shard_map/ppermute | solution.py:438
  109.3 5.0 %collective-permute-start.20 = (f32[96,128]{1,0:T(8,128)S(1)}, f32[96,128]{1,0:T(8,128)S(1)}, u32[]{:S(2)}, u32[]{:S(2)}) collective-permute-start(f32[96,128]{1,0:T(8,128)S(1)} %get-tuple-element.85), channel_id=1, source_target_pairs={{0,160},{32,128},{64,224},{96,192},{128,32},{160,0},{192,96},{224,... | collective-permute-start | bytes 147464 | tf_op jit(solution)/shard_map/ppermute | solution.py:438
  109.3 5.0 %collective-permute-start.21 = (f32[96,128]{1,0:T(8,128)S(1)}, f32[96,128]{1,0:T(8,128)S(1)}, u32[]{:S(2)}, u32[]{:S(2)}) collective-permute-start(f32[96,128]{1,0:T(8,128)S(1)} %get-tuple-element.86), channel_id=1, source_target_pairs={{0,96},{32,64},{64,32},{96,0},{128,224},{160,192},{192,160},{224,1... | collective-permute-start | bytes 147464 | tf_op jit(solution)/shard_map/ppermute | solution.py:438
  111.3 4.7 %collective-permute-start.22 = (f32[96,128]{1,0:T(8,128)S(1)}, f32[96,128]{1,0:T(8,128)S(1)}, u32[]{:S(2)}, u32[]{:S(2)}) collective-permute-start(f32[96,128]{1,0:T(8,128)S(1)} %get-tuple-element.87), channel_id=1, source_target_pairs={{0,224},{32,192},{64,160},{96,128},{128,96},{160,64},{192,32},{224... | collective-permute-start | bytes 147464 | tf_op jit(solution)/shard_map/ppermute | solution.py:438
  113.1 2.9 %collective-permute-start.23 = (f32[96,128]{1,0:T(8,128)S(1)}, f32[96,128]{1,0:T(8,128)S(1)}, u32[]{:S(2)}, u32[]{:S(2)}) collective-permute-start(f32[96,128]{1,0:T(8,128)S(1)} %get-tuple-element.88), channel_id=1, source_target_pairs={{0,32},{32,0},{64,96},{96,64},{128,160},{160,128},{192,224},{224,1... | collective-permute-start | bytes 147464 | tf_op jit(solution)/shard_map/ppermute | solution.py:438

commit v5 on v4

--- a/solution.py
+++ b/solution.py
@@ -17,6 +17,7 @@
 HALO = 4
 WIN = OWN + 2 * HALO
 ORDER = (4, 2, 6, 5, 3, 7, 1)
+CHIPS = (2, 1, 3)
 TALL = 24
 
 
@@ -121,10 +122,13 @@
                 far[i] = parts[q]
 
 
-def coefficient_body(pos, here, near, far, consts, weights, inv):
+def coefficient_body(pos, far, near, here, consts, weights, inv):
     t, flip, s = pos[0], pos[1], pos[2]
     near, far = ([side[168 + 3 * i : 171 + 3 * i].reshape(TALL, 128) for i in range(3)] for side in (near, far))
     kappa = [near[1], near[0], here[0], here[1], far[0], far[1]]
+    for p in range(6):
+        plane = jnp.where(flip == 1, 2 * s + 3 - p, 2 * s - 2 + p)
+        kappa[p] = kappa[p] * jnp.where((plane >= 0) & (plane < 64), 1.0, 0.0)
     begin = [near[2], here[2], here[3], far[2]]
     lane = lax.broadcasted_iota(jnp.int32, (TALL, 128), 1)
     row = lax.broadcasted_iota(jnp.int32, (TALL, 128), 0) + (OWN * t - HALO)
@@ -255,7 +259,7 @@
     return v + pltpu.roll(v, 1, 0)
 
 
-def front_body(own, wish, near, far, tnear, tfar, weights, consts, inv, fixed, it, out_near, out_far, zed):
+def front_body(far, near, own, wish, tnear, tfar, weights, consts, inv, fixed, it, out_near, out_far, zed):
     def field(p, j, c):
         if p == 2 or p == 3:
             return own[p - 2, j, c]
@@ -359,7 +363,7 @@
         rows(4, 16, row)
 
 
-def middle_body(it, near, far, fixed, weights, consts, inv, new, out_near, out_far, zed):
+def middle_body(far, near, it, fixed, weights, consts, inv, new, out_near, out_far, zed):
     def put(x, j, c, v):
         new[x, j, c] = v
         first, second = (out_near, out_far) if x == 0 else (out_far, out_near)
@@ -371,7 +375,7 @@
 EDGE = ((0, 4), (4, 4), (8, 3), (11, 3), (14, 2), (16, 2))
 
 
-def edges_body(pos, new, near, far, send0, send1):
+def edges_body(pos, far, near, new, send0, send1):
     odd = pos[0] & 1
     planes = (
         lambda j, n: new[0, pl.ds(j, n)],
@@ -402,8 +406,8 @@
         far[pl.ds(18 + 14 * high, 2)] = got[16:18]
 
 
-def last_body(pos, it, near, far, fixed, weights, consts, inv, back, *rest):
-    outs, (zed, fin, stage) = rest[:8], rest[8:]
+def last_body(pos, far, near, it, fixed, weights, consts, inv, back, *rest):
+    outs, (zed, fin, stage) = rest[:2], rest[2:]
     def put(x, j, c, v):
         fin[x * OWN + j, c] = v
     sweep_body(it, near, far, fixed, weights, consts, inv, zed, put)
@@ -416,15 +420,23 @@
             for c in range(4):
                 stage[pl.ds((c * 2 + x) * OWN + j, 8, stride=8 * OWN), :] = done[(i * 4 + c) * 8 : (i * 4 + c + 1) * 8]
     for k in range(8):
-        outs[k][...] = stage[pl.ds(pl.multiple_of((t ^ k) * 8 * OWN, 8), 8 * OWN), :]
-
-
-def unpack_body(pos, *rest):
-    pieces, (state, adjoint), stage = rest[:8], rest[8:10], rest[10]
+        outs[k & 1][k >> 1] = stage[pl.ds(pl.multiple_of((t ^ k) * 8 * OWN, 8), 8 * OWN), :]
+
+
+def merge_body(other, mine, *outs):
+    for out, k in zip(outs, CHIPS):
+        out[0] = mine[k]
+        out[1] = other[k]
+
+
+def unpack_body(pos, a, b, c, other, mine, state, adjoint, stage):
     t = pos[0]
     flip = pos[1]
-    for k, piece in zip(ORDER + (0,), pieces):
-        stage[t ^ k] = piece[...]
+    for ref, k in zip((a, b, c), CHIPS):
+        stage[t ^ (2 * k)] = ref[0]
+        stage[t ^ (2 * k + 1)] = ref[1]
+    stage[t] = mine[0]
+    stage[t ^ 1] = other[0]
     for f, ref in enumerate((state, adjoint)):
         for n in range(2):
             for x in range(2):
@@ -441,8 +453,9 @@
 def swap(block, axis, start):
     count = lax.axis_size(axis)
     route = []
-    for i in range(start, count - 1, 2):
-        route += [(i, i + 1), (i + 1, i)]
+    for i in range(start, start + count, 2):
+        low, high = i % count, (i + 1) % count
+        route += [(low, high), (high, low)]
     return lax.ppermute(block, axis, route)
 
 
@@ -479,7 +492,7 @@
     near = near_first = swap(near, "space", 1)
     weights, inv = call(
         coefficient_body, "coefficients", [whole(4 * TALL * 8, 128), whole(68, 2, 8, 128)], 4
-    )(pos, here_c, near, far, consts)
+    )(pos, far, near, here_c, consts)
     weights = weights.reshape(4 * TALL, 8, 128)
 
     sweep_scratch = [pltpu.VMEM((52, 4, 8, 128), jnp.float32)]
@@ -491,7 +504,7 @@
             9,
             [pltpu.VMEM((68, 4, 8, 128), jnp.float32)],
             scalars=0,
-        )(own, wish, near, far, near_first, far_first, weights, consts, inv)
+        )(far, near, own, wish, near_first, far_first, weights, consts, inv)
         far_z = swap(far_z, "space", 0)
         near_z = swap(near_z, "space", 1)
         if outer < OUTER - 1:
@@ -502,10 +515,10 @@
                 7,
                 sweep_scratch,
                 scalars=0,
-            )(it, near_z, far_z, fixed, weights, consts, inv)
+            )(far_z, near_z, it, fixed, weights, consts, inv)
             far = swap(far, "space", 0)
             near = swap(near, "space", 1)
-            send0, send1 = call(edges_body, "edges", [whole(18, 4, 8, 128)] * 2, 3)(pos, new, near, far)
+            send0, send1 = call(edges_body, "edges", [whole(18, 4, 8, 128)] * 2, 3)(pos, far, near, new)
             got1 = swap(send1, "tm", 1)
             got0 = swap(send0, "tm", 0)
             own, near, far = call(
@@ -513,22 +526,27 @@
             )(pos, got1, got0, new, near, far)
             near = near.reshape(136, 8, 128)
             far = far.reshape(136, 8, 128)
-    pieces = call(
+    mine, other = call(
         last_body,
         "last",
-        [whole(8 * OWN, 128)] * 8,
+        [whole(4, 8 * OWN, 128)] * 2,
         8,
         sweep_scratch + [pltpu.VMEM((2 * OWN, 4, 8, 128), jnp.float32), pltpu.VMEM((64 * OWN, 128), jnp.float32)],
-    )(pos, it, near_z, far_z, fixed, weights, consts, inv, back)
-    got = exchange(pieces)
+    )(pos, far_z, near_z, it, fixed, weights, consts, inv, back)
+    other = swap(other, "tm", 0)
+    pairs = call(merge_body, "merge", [whole(2, 8 * OWN, 128)] * 3, 2, scalars=0)(other, mine)
+    count = lax.axis_size("tm")
+    got = [
+        lax.ppermute(pair, "tm", [(i, i ^ (2 * k)) for i in range(count)]) for pair, k in zip(pairs, CHIPS)
+    ]
     return tuple(
         call(
             unpack_body,
             "unpack",
             [whole(2, 2, 96, 128)] * 2,
-            8,
+            5,
             [pltpu.VMEM((8, 8 * OWN, 128), jnp.float32)],
-        )(pos, *got)
+        )(pos, *got, other, mine)
     )
 
 

time: 118 us -> 113 us (0.958)
  the two profiles are of different devices: /device:TPU:6 before, /device:TPU:1 now
where the time goes in v5:
time: 113 us
  waiting for transfers between devices  56.4 us (50%)
  starting transfers between devices  42.9 us (38%)
  Pallas kernels  12.8 us (11%)
    ppermute x11, waiting for transfers between devices, swap(): return lax.ppermute(block, axis, route)  47.1 us
    ppermute x11, starting transfers between devices, swap(): return lax.ppermute(block, axis, route)  27.7 us
    ppermute x7, starting transfers between devices, exchange(): lax.ppermute(pieces[k], 'tm', [(i, i ^ k) for i in range(count)])  11.9 us
    ppermute x7, waiting for transfers between devices, exchange(): lax.ppermute(pieces[k], 'tm', [(i, i ^ k) for i in range(count)])  5.07 us
    ppermute x3, waiting for transfers between devices, on_device(): lax.ppermute(pair, 'tm', [(i, i ^ 2 * k) for i in range(count)])  4.24 us
    ppermute x3, starting transfers between devices, on_device(): lax.ppermute(pair, 'tm', [(i, i ^ 2 * k) for i in range(count)])  3.34 us
    pallas_call x2, Pallas kernels, on_device(): call(front_body, 'front', [whole(68, 4, 8, 128), whole(2, 16, 4, 8, 128),...  2.94 us
  transfers between devices with their start and end apart: 21, of which 16 were waited for; matrix products, arithmetic and copies ran while one was open for 0% of the time, Pallas kernels for 0%

profile of v5, /device:TPU:1, one launch (start us, length us, event | category | flops | bytes accessed | tf_op | source)
XLA Modules:
  0.0 112.9 jit_solution(7973071067674234218)
XLA Ops:
  0.6 0.1 pad_add_fusion.pos
  0.7 1.9 %pack.1 = (f32[240,128]{1,0:T(8,128)S(1)}, f32[240,128]{1,0:T(8,128)S(1)}, f32[240,128]{1,0:T(8,128)S(1)}, f32[240,128]{1,0:T(8,128)S(1)}, f32[240,128]{1,0:T(8,...) custom-call(s32[3]{0:T(128)S(1)} %pad_add_fusion.pos, ...), custom_call_target="tpu_custom_call" | custom-call | tf_op jit(solution)/shard_map/pack/pallas_call | solution.py:471
  2.6 3.8 %collective-permute-start = (f32[240,128]{1,0:T(8,128)S(1)}, f32[240,128]{1,0:T(8,128)S(1)}, u32[]{:S(2)}, u32[]{:S(2)}) collective-permute-start(f32[240,128]{1,0:T(8,128)S(1)} %get-tuple-element.43), channel_id=1, source_target_pairs={{0,128},{32,160},{64,192},{96,224},{128,0},{160,32},{192,64},{224,... | collective-permute-start | bytes 368648 | tf_op jit(solution)/shard_map/ppermute | solution.py:450
  6.4 0.4 collective-permute-start.1
  6.8 0.4 collective-permute-start.2
  7.2 3.9 %collective-permute-start.3 = (f32[240,128]{1,0:T(8,128)S(1)}, f32[240,128]{1,0:T(8,128)S(1)}, u32[]{:S(2)}, u32[]{:S(2)}) collective-permute-start(f32[240,128]{1,0:T(8,128)S(1)} %get-tuple-element.46), channel_id=1, source_target_pairs={{0,160},{32,128},{64,224},{96,192},{128,32},{160,0},{192,96},{224,... | collective-permute-start | bytes 368648 | tf_op jit(solution)/shard_map/ppermute | solution.py:450
  11.1 0.0 collective-permute-start.4
  11.1 0.0 collective-permute-done.rest_0_
  11.1 3.4 %collective-permute-start.5 = (f32[240,128]{1,0:T(8,128)S(1)}, f32[240,128]{1,0:T(8,128)S(1)}, u32[]{:S(2)}, u32[]{:S(2)}) collective-permute-start(f32[240,128]{1,0:T(8,128)S(1)} %get-tuple-element.48), channel_id=1, source_target_pairs={{0,224},{32,192},{64,160},{96,128},{128,96},{160,64},{192,32},{224... | collective-permute-start | bytes 368648 | tf_op jit(solution)/shard_map/ppermute | solution.py:450
  14.5 2.1 %collective-permute-done.2.rest_2_ = f32[240,128]{1,0:T(8,128)S(1)} collective-permute-done((f32[240,128]{1,0:T(8,128)S(1)}, f32[240,128]{1,0:T(8,128)S(1)}, u32[]{:S(2)}, u32[]{:S(2)}) %collective-permute-start.2) | collective-permute-done | bytes 122912 | tf_op jit(solution)/shard_map/ppermute | solution.py:450
  16.6 2.0 %collective-permute-done.4.rest_4_ = f32[240,128]{1,0:T(8,128)S(1)} collective-permute-done((f32[240,128]{1,0:T(8,128)S(1)}, f32[240,128]{1,0:T(8,128)S(1)}, u32[]{:S(2)}, u32[]{:S(2)}) %collective-permute-start.4) | collective-permute-done | bytes 122912 | tf_op jit(solution)/shard_map/ppermute | solution.py:450
  18.6 1.0 collective-permute-done.5.rest_5_
  19.6 1.6 %spread.1 = (f32[2,20,4,8,128]{4,3,2,1,0:T(8,128)S(1)}, f32[2,18,2,8,128]{4,3,2,1,0:T(8,128)S(1)}, f32[177,8,128]{2,1,0:T(8,128)S(1)}, f32[177,8,128]{2,1,0:T(8,128)S(1)}) custom-call(s32[3]{0:T(128)S(1)} %pad_add_fusion.pos, f32[240,128]{1,0:T(8,128)S(1)} %collective-permute-done.rest_0_, f32[240,128]{1,0:T(8,128)S(1)} %collective-permute-done.1.rest_1_, ...), custom_call_target="tpu_custom_call" | custom-call | tf_op jit(solution)/shard_map/spread/pallas_call | solution.py:484
  21.2 0.9 collective-permute-start.7
  22.1 6.9 %collective-permute-start.8 = (f32[177,8,128]{2,1,0:T(8,128)S(1)}, f32[177,8,128]{2,1,0:T(8,128)S(1)}, u32[]{:S(2)}, u32[]{:S(2)}) collective-permute-start(f32[177,8,128]{2,1,0:T(8,128)S(1)} %get-tuple-element.55), channel_id=1, source_target_pairs={{1,2},{2,1},{3,4},{4,3},{5,6},{6,5},{7,8},{8,7},{9,10},{10,9},{11,... | collective-permute-start | bytes 2174984 | tf_op jit(solution)/shard_map/ppermute | solution.py:459
  28.9 10.0 %collective-permute-done.7.far.tfar = f32[177,8,128]{2,1,0:T(8,128)S(1)} collective-permute-done((f32[177,8,128]{2,1,0:T(8,128)S(1)}, f32[177,8,128]{2,1,0:T(8,128)S(1)}, u32[]{:S(2)}, u32[]{:S(2)}) %collective-permute-start.7) | collective-permute-done | bytes 725024 | tf_op jit(solution)/shard_map/ppermute | solution.py:459
  39.0 6.1 %collective-permute-done.8.near.tnear = f32[177,8,128]{2,1,0:T(8,128)S(1)} collective-permute-done((f32[177,8,128]{2,1,0:T(8,128)S(1)}, f32[177,8,128]{2,1,0:T(8,128)S(1)}, u32[]{:S(2)}, u32[]{:S(2)}) %collective-permute-start.8) | collective-permute-done | bytes 725024 | tf_op jit(solution)/shard_map/ppermute | solution.py:459
  45.0 0.8 coefficients.1
  45.8 1.5 %front.2 = (f32[68,4,8,128]{3,2,1,0:T(8,128)S(1)}, f32[2,16,4,8,128]{4,3,2,1,0:T(8,128)S(1)}, f32[26,4,8,128]{3,2,1,0:T(8,128)S(1)}, f32[26,4,8,128]{3,2,1,0:T(8,128)S(1)}) custom-call(f32[177,8,128]{2,1,0:T(8,128)S(1)} %collective-permute-done.7.far.tfar, f32[177,8,128]{2,1,0:T(8,128)S(1)} %collective-permute-done.8.near.tnear, ...), custom_call_target="tpu_custom_call" | custom-call | tf_op jit(solution)/shard_map/front/pallas_call | solution.py:500
  47.3 0.1 collective-permute-start.9
  47.4 4.6 %collective-permute-start.10 = (f32[26,4,8,128]{3,2,1,0:T(8,128)S(1)}, f32[26,4,8,128]{3,2,1,0:T(8,128)S(1)}, u32[]{:S(2)}, u32[]{:S(2)}) collective-permute-start(f32[26,4,8,128]{3,2,1,0:T(8,128)S(1)} %get-tuple-element.63), channel_id=1, source_target_pairs={{1,2},{2,1},{3,4},{4,3},{5,6},{6,5},{7,8},{8,7},{9,10},{10,9},{11,... | collective-permute-start | bytes 1277960 | tf_op jit(solution)/shard_map/ppermute | solution.py:459
  51.9 5.7 %collective-permute-done.9.far = f32[26,4,8,128]{3,2,1,0:T(8,128)S(1)} collective-permute-done((f32[26,4,8,128]{3,2,1,0:T(8,128)S(1)}, f32[26,4,8,128]{3,2,1,0:T(8,128)S(1)}, u32[]{:S(2)}, u32[]{:S(2)}) %collective-permute-start.9) | collective-permute-done | bytes 426016 | tf_op jit(solution)/shard_map/ppermute | solution.py:459
  57.6 3.4 %collective-permute-done.10.near = f32[26,4,8,128]{3,2,1,0:T(8,128)S(1)} collective-permute-done((f32[26,4,8,128]{3,2,1,0:T(8,128)S(1)}, f32[26,4,8,128]{3,2,1,0:T(8,128)S(1)}, u32[]{:S(2)}, u32[]{:S(2)}) %collective-permute-start.10) | collective-permute-done | bytes 426016 | tf_op jit(solution)/shard_map/ppermute | solution.py:459
  61.1 0.9 middle.1
  62.0 0.1 collective-permute-start.11
  62.1 4.2 %collective-permute-start.12 = (f32[24,4,8,128]{3,2,1,0:T(8,128)S(1)}, f32[24,4,8,128]{3,2,1,0:T(8,128)S(1)}, u32[]{:S(2)}, u32[]{:S(2)}) collective-permute-start(f32[24,4,8,128]{3,2,1,0:T(8,128)S(1)} %get-tuple-element.67), channel_id=1, source_target_pairs={{1,2},{2,1},{3,4},{4,3},{5,6},{6,5},{7,8},{8,7},{9,10},{10,9},{11,... | collective-permute-start | bytes 1179656 | tf_op jit(solution)/shard_map/ppermute | solution.py:459
  66.3 4.4 %collective-permute-done.11.far.far_x = f32[24,4,8,128]{3,2,1,0:T(8,128)S(1)} collective-permute-done((f32[24,4,8,128]{3,2,1,0:T(8,128)S(1)}, f32[24,4,8,128]{3,2,1,0:T(8,128)S(1)}, u32[]{:S(2)}, u32[]{:S(2)}) %collective-permute-start.11) | collective-permute-done | bytes 393248 | tf_op jit(solution)/shard_map/ppermute | solution.py:459
  70.7 3.4 %collective-permute-done.12.near.near_x = f32[24,4,8,128]{3,2,1,0:T(8,128)S(1)} collective-permute-done((f32[24,4,8,128]{3,2,1,0:T(8,128)S(1)}, f32[24,4,8,128]{3,2,1,0:T(8,128)S(1)}, u32[]{:S(2)}, u32[]{:S(2)}) %collective-permute-start.12) | collective-permute-done | bytes 393248 | tf_op jit(solution)/shard_map/ppermute | solution.py:459
  74.2 0.6 edges.1
  74.7 3.4 %collective-permute-start.13 = (f32[18,4,8,128]{3,2,1,0:T(8,128)S(1)}, f32[18,4,8,128]{3,2,1,0:T(8,128)S(1)}, u32[]{:S(2)}, u32[]{:S(2)}) collective-permute-start(f32[18,4,8,128]{3,2,1,0:T(8,128)S(1)} %get-tuple-element.69), channel_id=1, source_target_pairs={{32,64},{64,32},{96,128},{128,96},{160,192},{192,160},{224,0},{0,2... | collective-permute-start | bytes 884744 | tf_op jit(solution)/shard_map/ppermute | solution.py:459
  78.1 0.0 collective-permute-start.14
  78.1 4.7 %collective-permute-done.13.got1 = f32[18,4,8,128]{3,2,1,0:T(8,128)S(1)} collective-permute-done((f32[18,4,8,128]{3,2,1,0:T(8,128)S(1)}, f32[18,4,8,128]{3,2,1,0:T(8,128)S(1)}, u32[]{:S(2)}, u32[]{:S(2)}) %collective-permute-start.13) | collective-permute-done | bytes 294944 | tf_op jit(solution)/shard_map/ppermute | solution.py:459
  82.8 0.7 widen.1
  83.5 1.5 %front.3 = (f32[68,4,8,128]{3,2,1,0:T(8,128)S(1)}, f32[2,16,4,8,128]{4,3,2,1,0:T(8,128)S(1)}, f32[26,4,8,128]{3,2,1,0:T(8,128)S(1)}, f32[26,4,8,128]{3,2,1,0:T(8,128)S(1)}) custom-call(f32[136,8,128]{2,1,0:T(8,128)S(1)} %bitcast.11, f32[136,8,128]{2,1,0:T(8,128)S(1)} %bitcast.10, f32[2,20,4,8,128]{4,3,2,1,0:T(8,128)S(1)} %get-tuple-element.73.own, ...), custom_call_target="tpu_custom_call" | custom-call | tf_op jit(solution)/shard_map/front/pallas_call | solution.py:500
  85.0 0.1 collective-permute-start.15
  85.1 4.2 %collective-permute-start.16 = (f32[26,4,8,128]{3,2,1,0:T(8,128)S(1)}, f32[26,4,8,128]{3,2,1,0:T(8,128)S(1)}, u32[]{:S(2)}, u32[]{:S(2)}) collective-permute-start(f32[26,4,8,128]{3,2,1,0:T(8,128)S(1)} %get-tuple-element.75), channel_id=1, source_target_pairs={{1,2},{2,1},{3,4},{4,3},{5,6},{6,5},{7,8},{8,7},{9,10},{10,9},{11,... | collective-permute-start | bytes 1277960 | tf_op jit(solution)/shard_map/ppermute | solution.py:459
  89.3 4.8 %collective-permute-done.15.far = f32[26,4,8,128]{3,2,1,0:T(8,128)S(1)} collective-permute-done((f32[26,4,8,128]{3,2,1,0:T(8,128)S(1)}, f32[26,4,8,128]{3,2,1,0:T(8,128)S(1)}, u32[]{:S(2)}, u32[]{:S(2)}) %collective-permute-start.15) | collective-permute-done | bytes 426016 | tf_op jit(solution)/shard_map/ppermute | solution.py:459
  94.1 3.4 %collective-permute-done.16.near = f32[26,4,8,128]{3,2,1,0:T(8,128)S(1)} collective-permute-done((f32[26,4,8,128]{3,2,1,0:T(8,128)S(1)}, f32[26,4,8,128]{3,2,1,0:T(8,128)S(1)}, u32[]{:S(2)}, u32[]{:S(2)}) %collective-permute-start.16) | collective-permute-done | bytes 426016 | tf_op jit(solution)/shard_map/ppermute | solution.py:459
  97.5 2.1 %last.1 = (f32[4,96,128]{2,1,0:T(8,128)S(1)}, f32[4,96,128]{2,1,0:T(8,128)S(1)}) custom-call(s32[3]{0:T(128)S(1)} %pad_add_fusion.pos, f32[26,4,8,128]{3,2,1,0:T(8,128)S(1)} %collective-permute-done.15.far, f32[26,4,8,128]{3,2,1,0:T(8,128)S(1)} %collective-permute-done.16.near, f32[2,16,4,8,128]{4,3,2,1,0:T(8,128)S(1)} %get-tuple-element.76.it, ...), custom_call_target="tpu_custom_call" | custom-call | tf_op jit(solution)/shard_map/last/pallas_call | solution.py:529
  99.6 3.3 %collective-permute-start.17 = (f32[4,96,128]{2,1,0:T(8,128)S(1)}, f32[4,96,128]{2,1,0:T(8,128)S(1)}, u32[]{:S(2)}, u32[]{:S(2)}) collective-permute-start(f32[4,96,128]{2,1,0:T(8,128)S(1)} %get-tuple-element.79), channel_id=1, source_target_pairs={{0,32},{32,0},{64,96},{96,64},{128,160},{160,128},{192,224},{224,1... | collective-permute-start | bytes 589832 | tf_op jit(solution)/shard_map/ppermute | solution.py:459
  102.9 1.1 collective-permute-done.17.other
  104.0 1.6 %collective-permute-start.18 = (f32[2,96,128]{2,1,0:T(8,128)S(1)}, f32[2,96,128]{2,1,0:T(8,128)S(1)}, u32[]{:S(2)}, u32[]{:S(2)}) collective-permute-start(f32[2,96,128]{2,1,0:T(8,128)S(1)} %get-tuple-element.81), channel_id=1, source_target_pairs={{0,128},{32,160},{64,192},{96,224},{128,0},{160,32},{192,64},{224,... | collective-permute-start | bytes 294920 | tf_op jit(solution)/shard_map/ppermute | solution.py:540
  105.6 0.9 collective-permute-start.19
  106.5 0.8 collective-permute-start.20
  107.3 2.3 %collective-permute-done.18.a = f32[2,96,128]{2,1,0:T(8,128)S(1)} collective-permute-done((f32[2,96,128]{2,1,0:T(8,128)S(1)}, f32[2,96,128]{2,1,0:T(8,128)S(1)}, u32[]{:S(2)}, u32[]{:S(2)}) %collective-permute-start.18) | collective-permute-done | bytes 98336 | tf_op jit(solution)/shard_map/ppermute | solution.py:540
  109.6 1.6 %collective-permute-done.19.b = f32[2,96,128]{2,1,0:T(8,128)S(1)} collective-permute-done((f32[2,96,128]{2,1,0:T(8,128)S(1)}, f32[2,96,128]{2,1,0:T(8,128)S(1)}, u32[]{:S(2)}, u32[]{:S(2)}) %collective-permute-start.19) | collective-permute-done | bytes 98336 | tf_op jit(solution)/shard_map/ppermute | solution.py:540
  111.1 0.4 collective-permute-done.20.c
  111.6 1.3 %unpack.1 = (f32[2,2,96,128]{3,2,1,0:T(8,128)}, f32[2,2,96,128]{3,2,1,0:T(8,128)}) custom-call(s32[3]{0:T(128)S(1)} %pad_add_fusion.pos, f32[2,96,128]{2,1,0:T(8,128)S(1)} %collective-permute-done.18.a, f32[2,96,128]{2,1,0:T(8,128)S(1)} %collective-permute-done.19.b, f32[2,96,128]{2,1,0:T(8,128)S(1)} %collective-permute-done.20.c, ...), custom_call_target="tpu_custom_call" | custom-call | tf_op jit(solution)/shard_map/unpack/pallas_call | solution.py:543
  (6 shorter events, 0.0 us)
Async XLA Ops:
  2.6 8.5 %collective-permute-start = (f32[240,128]{1,0:T(8,128)S(1)}, f32[240,128]{1,0:T(8,128)S(1)}, u32[]{:S(2)}, u32[]{:S(2)}) collective-permute-start(f32[240,128]{1,0:T(8,128)S(1)} %get-tuple-element.43), channel_id=1, source_target_pairs={{0,128},{32,160},{64,192},{96,224},{128,0},{160,32},{192,64},{224,... | collective-permute-start | bytes 368648 | tf_op jit(solution)/shard_map/ppermute | solution.py:450
  6.4 8.1 %collective-permute-start.1 = (f32[240,128]{1,0:T(8,128)S(1)}, f32[240,128]{1,0:T(8,128)S(1)}, u32[]{:S(2)}, u32[]{:S(2)}) collective-permute-start(f32[240,128]{1,0:T(8,128)S(1)} %get-tuple-element.44), channel_id=1, source_target_pairs={{0,64},{32,96},{64,0},{96,32},{128,192},{160,224},{192,128},{224,1... | collective-permute-start | bytes 368648 | tf_op jit(solution)/shard_map/ppermute | solution.py:450
  6.8 9.8 %collective-permute-start.2 = (f32[240,128]{1,0:T(8,128)S(1)}, f32[240,128]{1,0:T(8,128)S(1)}, u32[]{:S(2)}, u32[]{:S(2)}) collective-permute-start(f32[240,128]{1,0:T(8,128)S(1)} %get-tuple-element.45), channel_id=1, source_target_pairs={{0,192},{32,224},{64,128},{96,160},{128,64},{160,96},{192,0},{224,... | collective-permute-start | bytes 368648 | tf_op jit(solution)/shard_map/ppermute | solution.py:450
  7.2 9.4 %collective-permute-start.3 = (f32[240,128]{1,0:T(8,128)S(1)}, f32[240,128]{1,0:T(8,128)S(1)}, u32[]{:S(2)}, u32[]{:S(2)}) collective-permute-start(f32[240,128]{1,0:T(8,128)S(1)} %get-tuple-element.46), channel_id=1, source_target_pairs={{0,160},{32,128},{64,224},{96,192},{128,32},{160,0},{192,96},{224,... | collective-permute-start | bytes 368648 | tf_op jit(solution)/shard_map/ppermute | solution.py:450
  11.1 7.5 %collective-permute-start.4 = (f32[240,128]{1,0:T(8,128)S(1)}, f32[240,128]{1,0:T(8,128)S(1)}, u32[]{:S(2)}, u32[]{:S(2)}) collective-permute-start(f32[240,128]{1,0:T(8,128)S(1)} %get-tuple-element.47), channel_id=1, source_target_pairs={{0,96},{32,64},{64,32},{96,0},{128,224},{160,192},{192,160},{224,1... | collective-permute-start | bytes 368648 | tf_op jit(solution)/shard_map/ppermute | solution.py:450
  11.1 8.5 %collective-permute-start.5 = (f32[240,128]{1,0:T(8,128)S(1)}, f32[240,128]{1,0:T(8,128)S(1)}, u32[]{:S(2)}, u32[]{:S(2)}) collective-permute-start(f32[240,128]{1,0:T(8,128)S(1)} %get-tuple-element.48), channel_id=1, source_target_pairs={{0,224},{32,192},{64,160},{96,128},{128,96},{160,64},{192,32},{224... | collective-permute-start | bytes 368648 | tf_op jit(solution)/shard_map/ppermute | solution.py:450
  14.5 5.1 %collective-permute-start.6 = (f32[240,128]{1,0:T(8,128)S(1)}, f32[240,128]{1,0:T(8,128)S(1)}, u32[]{:S(2)}, u32[]{:S(2)}) collective-permute-start(f32[240,128]{1,0:T(8,128)S(1)} %get-tuple-element.49), channel_id=1, source_target_pairs={{0,32},{32,0},{64,96},{96,64},{128,160},{160,128},{192,224},{224,1... | collective-permute-start | bytes 368648 | tf_op jit(solution)/shard_map/ppermute | solution.py:450
  21.2 17.8 %collective-permute-start.7 = (f32[177,8,128]{2,1,0:T(8,128)S(1)}, f32[177,8,128]{2,1,0:T(8,128)S(1)}, u32[]{:S(2)}, u32[]{:S(2)}) collective-permute-start(f32[177,8,128]{2,1,0:T(8,128)S(1)} %get-tuple-element.54), channel_id=1, source_target_pairs={{0,1},{1,0},{2,3},{3,2},{4,5},{5,4},{6,7},{7,6},{8,9},{9,8},{10,11... | collective-permute-start | bytes 2174984 | tf_op jit(solution)/shard_map/ppermute | solution.py:459
  22.1 23.0 %collective-permute-start.8 = (f32[177,8,128]{2,1,0:T(8,128)S(1)}, f32[177,8,128]{2,1,0:T(8,128)S(1)}, u32[]{:S(2)}, u32[]{:S(2)}) collective-permute-start(f32[177,8,128]{2,1,0:T(8,128)S(1)} %get-tuple-element.55), channel_id=1, source_target_pairs={{1,2},{2,1},{3,4},{4,3},{5,6},{6,5},{7,8},{8,7},{9,10},{10,9},{11,... | collective-permute-start | bytes 2174984 | tf_op jit(solution)/shard_map/ppermute | solution.py:459
  47.3 10.3 %collective-permute-start.9 = (f32[26,4,8,128]{3,2,1,0:T(8,128)S(1)}, f32[26,4,8,128]{3,2,1,0:T(8,128)S(1)}, u32[]{:S(2)}, u32[]{:S(2)}) collective-permute-start(f32[26,4,8,128]{3,2,1,0:T(8,128)S(1)} %get-tuple-element.62), channel_id=1, source_target_pairs={{0,1},{1,0},{2,3},{3,2},{4,5},{5,4},{6,7},{7,6},{8,9},{9,8},{10,11... | collective-permute-start | bytes 1277960 | tf_op jit(solution)/shard_map/ppermute | solution.py:459
  47.4 13.7 %collective-permute-start.10 = (f32[26,4,8,128]{3,2,1,0:T(8,128)S(1)}, f32[26,4,8,128]{3,2,1,0:T(8,128)S(1)}, u32[]{:S(2)}, u32[]{:S(2)}) collective-permute-start(f32[26,4,8,128]{3,2,1,0:T(8,128)S(1)} %get-tuple-element.63), channel_id=1, source_target_pairs={{1,2},{2,1},{3,4},{4,3},{5,6},{6,5},{7,8},{8,7},{9,10},{10,9},{11,... | collective-permute-start | bytes 1277960 | tf_op jit(solution)/shard_map/ppermute | solution.py:459
  62.0 8.7 %collective-permute-start.11 = (f32[24,4,8,128]{3,2,1,0:T(8,128)S(1)}, f32[24,4,8,128]{3,2,1,0:T(8,128)S(1)}, u32[]{:S(2)}, u32[]{:S(2)}) collective-permute-start(f32[24,4,8,128]{3,2,1,0:T(8,128)S(1)} %get-tuple-element.66), channel_id=1, source_target_pairs={{0,1},{1,0},{2,3},{3,2},{4,5},{5,4},{6,7},{7,6},{8,9},{9,8},{10,11... | collective-permute-start | bytes 1179656 | tf_op jit(solution)/shard_map/ppermute | solution.py:459
  62.1 12.0 %collective-permute-start.12 = (f32[24,4,8,128]{3,2,1,0:T(8,128)S(1)}, f32[24,4,8,128]{3,2,1,0:T(8,128)S(1)}, u32[]{:S(2)}, u32[]{:S(2)}) collective-permute-start(f32[24,4,8,128]{3,2,1,0:T(8,128)S(1)} %get-tuple-element.67), channel_id=1, source_target_pairs={{1,2},{2,1},{3,4},{4,3},{5,6},{6,5},{7,8},{8,7},{9,10},{10,9},{11,... | collective-permute-start | bytes 1179656 | tf_op jit(solution)/shard_map/ppermute | solution.py:459
  74.7 8.1 %collective-permute-start.13 = (f32[18,4,8,128]{3,2,1,0:T(8,128)S(1)}, f32[18,4,8,128]{3,2,1,0:T(8,128)S(1)}, u32[]{:S(2)}, u32[]{:S(2)}) collective-permute-start(f32[18,4,8,128]{3,2,1,0:T(8,128)S(1)} %get-tuple-element.69), channel_id=1, source_target_pairs={{32,64},{64,32},{96,128},{128,96},{160,192},{192,160},{224,0},{0,2... | collective-permute-start | bytes 884744 | tf_op jit(solution)/shard_map/ppermute | solution.py:459
  78.1 4.7 %collective-permute-start.14 = (f32[18,4,8,128]{3,2,1,0:T(8,128)S(1)}, f32[18,4,8,128]{3,2,1,0:T(8,128)S(1)}, u32[]{:S(2)}, u32[]{:S(2)}) collective-permute-start(f32[18,4,8,128]{3,2,1,0:T(8,128)S(1)} %get-tuple-element.70), channel_id=1, source_target_pairs={{0,32},{32,0},{64,96},{96,64},{128,160},{160,128},{192,224},{224,1... | collective-permute-start | bytes 884744 | tf_op jit(solution)/shard_map/ppermute | solution.py:459
  85.0 9.1 %collective-permute-start.15 = (f32[26,4,8,128]{3,2,1,0:T(8,128)S(1)}, f32[26,4,8,128]{3,2,1,0:T(8,128)S(1)}, u32[]{:S(2)}, u32[]{:S(2)}) collective-permute-start(f32[26,4,8,128]{3,2,1,0:T(8,128)S(1)} %get-tuple-element.74), channel_id=1, source_target_pairs={{0,1},{1,0},{2,3},{3,2},{4,5},{5,4},{6,7},{7,6},{8,9},{9,8},{10,11... | collective-permute-start | bytes 1277960 | tf_op jit(solution)/shard_map/ppermute | solution.py:459
  85.1 12.5 %collective-permute-start.16 = (f32[26,4,8,128]{3,2,1,0:T(8,128)S(1)}, f32[26,4,8,128]{3,2,1,0:T(8,128)S(1)}, u32[]{:S(2)}, u32[]{:S(2)}) collective-permute-start(f32[26,4,8,128]{3,2,1,0:T(8,128)S(1)} %get-tuple-element.75), channel_id=1, source_target_pairs={{1,2},{2,1},{3,4},{4,3},{5,6},{6,5},{7,8},{8,7},{9,10},{10,9},{11,... | collective-permute-start | bytes 1277960 | tf_op jit(solution)/shard_map/ppermute | solution.py:459
  99.6 4.3 %collective-permute-start.17 = (f32[4,96,128]{2,1,0:T(8,128)S(1)}, f32[4,96,128]{2,1,0:T(8,128)S(1)}, u32[]{:S(2)}, u32[]{:S(2)}) collective-permute-start(f32[4,96,128]{2,1,0:T(8,128)S(1)} %get-tuple-element.79), channel_id=1, source_target_pairs={{0,32},{32,0},{64,96},{96,64},{128,160},{160,128},{192,224},{224,1... | collective-permute-start | bytes 589832 | tf_op jit(solution)/shard_map/ppermute | solution.py:459
  104.0 5.6 %collective-permute-start.18 = (f32[2,96,128]{2,1,0:T(8,128)S(1)}, f32[2,96,128]{2,1,0:T(8,128)S(1)}, u32[]{:S(2)}, u32[]{:S(2)}) collective-permute-start(f32[2,96,128]{2,1,0:T(8,128)S(1)} %get-tuple-element.81), channel_id=1, source_target_pairs={{0,128},{32,160},{64,192},{96,224},{128,0},{160,32},{192,64},{224,... | collective-permute-start | bytes 294920 | tf_op jit(solution)/shard_map/ppermute | solution.py:540
  105.6 5.5 %collective-permute-start.19 = (f32[2,96,128]{2,1,0:T(8,128)S(1)}, f32[2,96,128]{2,1,0:T(8,128)S(1)}, u32[]{:S(2)}, u32[]{:S(2)}) collective-permute-start(f32[2,96,128]{2,1,0:T(8,128)S(1)} %get-tuple-element.82), channel_id=1, source_target_pairs={{0,64},{32,96},{64,0},{96,32},{128,192},{160,224},{192,128},{224,1... | collective-permute-start | bytes 294920 | tf_op jit(solution)/shard_map/ppermute | solution.py:540
  106.5 5.1 %collective-permute-start.20 = (f32[2,96,128]{2,1,0:T(8,128)S(1)}, f32[2,96,128]{2,1,0:T(8,128)S(1)}, u32[]{:S(2)}, u32[]{:S(2)}) collective-permute-start(f32[2,96,128]{2,1,0:T(8,128)S(1)} %get-tuple-element.83), channel_id=1, source_target_pairs={{0,192},{32,224},{64,128},{96,160},{128,64},{160,96},{192,0},{224,... | collective-permute-start | bytes 294920 | tf_op jit(solution)/shard_map/ppermute | solution.py:540

commit v6 on v5

--- a/solution.py
+++ b/solution.py
@@ -56,7 +56,7 @@
     return jax.ShapeDtypeStruct(shape, jnp.float32)
 
 
-def call(body, name, outs, n_in, scratch=(), scalars=1, far_inputs=0):
+def call(body, name, outs, n_in, scratch=(), scalars=1, far_inputs=0, far_outputs=False):
     vmem = pl.BlockSpec(memory_space=pltpu.VMEM)
     anywhere = pl.BlockSpec(memory_space=pltpu.HBM)
     smem = pl.BlockSpec(memory_space=pltpu.SMEM)
@@ -65,7 +65,7 @@
         name=name,
         out_shape=outs,
         in_specs=[smem] * scalars + [anywhere] * far_inputs + [vmem] * n_in,
-        out_specs=[vmem] * len(outs),
+        out_specs=[anywhere if far_outputs else vmem] * len(outs),
         scratch_shapes=list(scratch),
         compiler_params=pltpu.CompilerParams(vmem_limit_bytes=16 * 1024 * 1024),
     )
@@ -78,15 +78,18 @@
 def pack_body(pos, *rest):
     sources, outs, (near, far, here), tables = rest[:8], rest[8:16], rest[16:19], rest[19:22]
     stage, held, sems = rest[22], rest[23:28], rest[28]
-    copies = [pltpu.make_async_copy(sources[i], ref, sems.at[i]) for i, ref in enumerate(held + tables)]
-    for copy in copies:
+    slabs = [
+        pltpu.make_async_copy(sources[f].at[n], held[f].at[n], sems.at[2 * f + n]) for f in range(3) for n in range(2)
+    ]
+    copies = [pltpu.make_async_copy(sources[3 + i], ref, sems.at[6 + i]) for i, ref in enumerate(held[3:] + tables)]
+    for copy in slabs + copies:
         copy.start()
     state, adjoint, target, kappa, begin = held
     t = pos[0]
     flip = pos[1]
     for f, ref in enumerate((state, adjoint, target)):
-        copies[f].wait()
         for n in range(2):
+            slabs[2 * f + n].wait()
             for x in range(2):
                 base = ((f * 2 + n) * 2 + x) * WIN
                 for d in range(8):
@@ -99,7 +102,7 @@
                         stage[d, base + last - low : base + WIN, :] = jnp.zeros((low + WIN - last, 128), jnp.float32)
     for k in range(8):
         outs[k][...] = stage[t ^ k]
-    for copy in copies[3:]:
+    for copy in copies:
         copy.wait()
     for d in range(8):
         @pl.when(t == d)
@@ -429,7 +432,7 @@
         out[1] = other[k]
 
 
-def unpack_body(pos, a, b, c, other, mine, state, adjoint, stage):
+def unpack_body(pos, a, b, c, other, mine, state, adjoint, stage, held, sems):
     t = pos[0]
     flip = pos[1]
     for ref, k in zip((a, b, c), CHIPS):
@@ -437,12 +440,19 @@
         stage[t ^ (2 * k + 1)] = ref[1]
     stage[t] = mine[0]
     stage[t ^ 1] = other[0]
+    copies = []
     for f, ref in enumerate((state, adjoint)):
         for n in range(2):
             for x in range(2):
                 base = ((f * 2 + n) * 2 + x) * OWN
                 for d in range(8):
-                    ref[n, x ^ flip, OWN * d : OWN * (d + 1), :] = stage[d, base : base + OWN, :]
+                    held[f, n, x, OWN * d : OWN * (d + 1), :] = stage[d, base : base + OWN, :]
+                copies.append(
+                    pltpu.make_async_copy(held.at[f, n, x], ref.at[n, x ^ flip], sems.at[(f * 2 + n) * 2 + x])
+                )
+                copies[-1].start()
+    for copy in copies:
+        copy.wait()
 
 
 def exchange(pieces):
@@ -452,10 +462,10 @@
 
 def swap(block, axis, start):
     count = lax.axis_size(axis)
-    route = []
-    for i in range(start, start + count, 2):
-        low, high = i % count, (i + 1) % count
-        route += [(low, high), (high, low)]
+    route = [(i, i) for i in range(start)]
+    for i in range(start, count - 1, 2):
+        route += [(i, i + 1), (i + 1, i)]
+    route += [(i, i) for i in range(len(route), count)]
     return lax.ppermute(block, axis, route)
 
 
@@ -477,7 +487,7 @@
         [pltpu.VMEM((8, 12 * WIN, 128), jnp.float32)]
         + [pltpu.VMEM((2, 2, 96, 128), jnp.float32)] * 3
         + [pltpu.VMEM((2, 96, 128), jnp.float32)] * 2
-        + [pltpu.SemaphoreType.DMA((8,))],
+        + [pltpu.SemaphoreType.DMA((11,))],
         far_inputs=8,
     )(pos, *(pltpu.with_memory_space_constraint(a, pltpu.HBM) for a in arguments))
     got = exchange(pieces)
@@ -545,7 +555,12 @@
             "unpack",
             [whole(2, 2, 96, 128)] * 2,
             5,
-            [pltpu.VMEM((8, 8 * OWN, 128), jnp.float32)],
+            [
+                pltpu.VMEM((8, 8 * OWN, 128), jnp.float32),
+                pltpu.VMEM((2, 2, 2, 96, 128), jnp.float32),
+                pltpu.SemaphoreType.DMA((8,)),
+            ],
+            far_outputs=True,
         )(pos, *got, other, mine)
     )
 

time: 113 us -> 116 us (1.027)
  the two profiles are of different devices: /device:TPU:1 before, /device:TPU:6 now
where the time goes in v6:
time: 116 us
  waiting for transfers between devices  55.4 us (48%)
  starting transfers between devices  46.6 us (40%)
  Pallas kernels  12.9 us (11%)
    ppermute x11, waiting for transfers between devices, swap(): return lax.ppermute(block, axis, route)  45.6 us
    ppermute x11, starting transfers between devices, swap(): return lax.ppermute(block, axis, route)  30.9 us
    ppermute x7, starting transfers between devices, exchange(): lax.ppermute(pieces[k], 'tm', [(i, i ^ k) for i in range(count)])  8.99 us
    ppermute x3, starting transfers between devices, on_device(): lax.ppermute(pair, 'tm', [(i, i ^ 2 * k) for i in range(count)])  6.72 us
    ppermute x7, waiting for transfers between devices, exchange(): lax.ppermute(pieces[k], 'tm', [(i, i ^ k) for i in range(count)])  5.87 us
    ppermute x3, waiting for transfers between devices, on_device(): lax.ppermute(pair, 'tm', [(i, i ^ 2 * k) for i in range(count)])  3.99 us
    pallas_call x2, Pallas kernels, on_device(): call(front_body, 'front', [whole(68, 4, 8, 128), whole(2, 16, 4, 8, 128),...  2.94 us
  transfers between devices with their start and end apart: 21, of which 17 were waited for; matrix products, arithmetic and copies ran while one was open for 0% of the time, Pallas kernels for 0%

profile of v6, /device:TPU:6, one launch (start us, length us, event | category | flops | bytes accessed | tf_op | source)
XLA Modules:
  0.0 115.9 jit_solution(10484320323140414916)
XLA Ops:
  0.6 0.1 pad_add_fusion.pos
  0.7 1.9 %pack.1 = (f32[240,128]{1,0:T(8,128)S(1)}, f32[240,128]{1,0:T(8,128)S(1)}, f32[240,128]{1,0:T(8,128)S(1)}, f32[240,128]{1,0:T(8,128)S(1)}, f32[240,128]{1,0:T(8,...) custom-call(s32[3]{0:T(128)S(1)} %pad_add_fusion.pos, ...), custom_call_target="tpu_custom_call" | custom-call | tf_op jit(solution)/shard_map/pack/pallas_call | solution.py:481
  2.6 3.3 %collective-permute-start = (f32[240,128]{1,0:T(8,128)S(1)}, f32[240,128]{1,0:T(8,128)S(1)}, u32[]{:S(2)}, u32[]{:S(2)}) collective-permute-start(f32[240,128]{1,0:T(8,128)S(1)} %get-tuple-element.43), channel_id=1, source_target_pairs={{0,128},{32,160},{64,192},{96,224},{128,0},{160,32},{192,64},{224,... | collective-permute-start | bytes 368648 | tf_op jit(solution)/shard_map/ppermute | solution.py:460
  5.9 0.7 collective-permute-start.1
  6.6 0.4 collective-permute-start.2
  7.0 1.6 %collective-permute-start.3 = (f32[240,128]{1,0:T(8,128)S(1)}, f32[240,128]{1,0:T(8,128)S(1)}, u32[]{:S(2)}, u32[]{:S(2)}) collective-permute-start(f32[240,128]{1,0:T(8,128)S(1)} %get-tuple-element.46), channel_id=1, source_target_pairs={{0,160},{32,128},{64,224},{96,192},{128,32},{160,0},{192,96},{224,... | collective-permute-start | bytes 368648 | tf_op jit(solution)/shard_map/ppermute | solution.py:460
  8.6 1.8 %collective-permute-start.4 = (f32[240,128]{1,0:T(8,128)S(1)}, f32[240,128]{1,0:T(8,128)S(1)}, u32[]{:S(2)}, u32[]{:S(2)}) collective-permute-start(f32[240,128]{1,0:T(8,128)S(1)} %get-tuple-element.47), channel_id=1, source_target_pairs={{0,96},{32,64},{64,32},{96,0},{128,224},{160,192},{192,160},{224,1... | collective-permute-start | bytes 368648 | tf_op jit(solution)/shard_map/ppermute | solution.py:460
  10.4 0.5 collective-permute-start.5
  10.9 1.9 %collective-permute-done.1.rest_1_ = f32[240,128]{1,0:T(8,128)S(1)} collective-permute-done((f32[240,128]{1,0:T(8,128)S(1)}, f32[240,128]{1,0:T(8,128)S(1)}, u32[]{:S(2)}, u32[]{:S(2)}) %collective-permute-start.1) | collective-permute-done | bytes 122912 | tf_op jit(solution)/shard_map/ppermute | solution.py:460
  12.8 0.8 collective-permute-start.6
  13.5 2.2 %collective-permute-done.2.rest_2_ = f32[240,128]{1,0:T(8,128)S(1)} collective-permute-done((f32[240,128]{1,0:T(8,128)S(1)}, f32[240,128]{1,0:T(8,128)S(1)}, u32[]{:S(2)}, u32[]{:S(2)}) %collective-permute-start.2) | collective-permute-done | bytes 122912 | tf_op jit(solution)/shard_map/ppermute | solution.py:460
  15.8 1.2 %collective-permute-done.4.rest_4_ = f32[240,128]{1,0:T(8,128)S(1)} collective-permute-done((f32[240,128]{1,0:T(8,128)S(1)}, f32[240,128]{1,0:T(8,128)S(1)}, u32[]{:S(2)}, u32[]{:S(2)}) %collective-permute-start.4) | collective-permute-done | bytes 122912 | tf_op jit(solution)/shard_map/ppermute | solution.py:460
  17.0 0.5 collective-permute-done.5.rest_5_
  17.5 1.6 %spread.1 = (f32[2,20,4,8,128]{4,3,2,1,0:T(8,128)S(1)}, f32[2,18,2,8,128]{4,3,2,1,0:T(8,128)S(1)}, f32[177,8,128]{2,1,0:T(8,128)S(1)}, f32[177,8,128]{2,1,0:T(8,128)S(1)}) custom-call(s32[3]{0:T(128)S(1)} %pad_add_fusion.pos, f32[240,128]{1,0:T(8,128)S(1)} %collective-permute-done.rest_0_, f32[240,128]{1,0:T(8,128)S(1)} %collective-permute-done.1.rest_1_, ...), custom_call_target="tpu_custom_call" | custom-call | tf_op jit(solution)/shard_map/spread/pallas_call | solution.py:494
  19.1 2.0 %collective-permute-start.7 = (f32[177,8,128]{2,1,0:T(8,128)S(1)}, f32[177,8,128]{2,1,0:T(8,128)S(1)}, u32[]{:S(2)}, u32[]{:S(2)}) collective-permute-start(f32[177,8,128]{2,1,0:T(8,128)S(1)} %get-tuple-element.54), channel_id=1, source_target_pairs={{0,1},{1,0},{2,3},{3,2},{4,5},{5,4},{6,7},{7,6},{8,9},{9,8},{10,11... | collective-permute-start | bytes 2174984 | tf_op jit(solution)/shard_map/ppermute | solution.py:469
  21.1 7.1 %collective-permute-start.8 = (f32[177,8,128]{2,1,0:T(8,128)S(1)}, f32[177,8,128]{2,1,0:T(8,128)S(1)}, u32[]{:S(2)}, u32[]{:S(2)}) collective-permute-start(f32[177,8,128]{2,1,0:T(8,128)S(1)} %get-tuple-element.55), channel_id=1, source_target_pairs={{0,0},{1,2},{2,1},{3,4},{4,3},{5,6},{6,5},{7,8},{8,7},{9,10},{10,9... | collective-permute-start | bytes 2174984 | tf_op jit(solution)/shard_map/ppermute | solution.py:469
  28.2 9.6 %collective-permute-done.7.far.tfar = f32[177,8,128]{2,1,0:T(8,128)S(1)} collective-permute-done((f32[177,8,128]{2,1,0:T(8,128)S(1)}, f32[177,8,128]{2,1,0:T(8,128)S(1)}, u32[]{:S(2)}, u32[]{:S(2)}) %collective-permute-start.7) | collective-permute-done | bytes 725024 | tf_op jit(solution)/shard_map/ppermute | solution.py:469
  37.8 6.8 %collective-permute-done.8.near.tnear = f32[177,8,128]{2,1,0:T(8,128)S(1)} collective-permute-done((f32[177,8,128]{2,1,0:T(8,128)S(1)}, f32[177,8,128]{2,1,0:T(8,128)S(1)}, u32[]{:S(2)}, u32[]{:S(2)}) %collective-permute-start.8) | collective-permute-done | bytes 725024 | tf_op jit(solution)/shard_map/ppermute | solution.py:469
  44.6 0.8 coefficients.1
  45.4 1.5 %front.2 = (f32[68,4,8,128]{3,2,1,0:T(8,128)S(1)}, f32[2,16,4,8,128]{4,3,2,1,0:T(8,128)S(1)}, f32[26,4,8,128]{3,2,1,0:T(8,128)S(1)}, f32[26,4,8,128]{3,2,1,0:T(8,128)S(1)}) custom-call(f32[177,8,128]{2,1,0:T(8,128)S(1)} %collective-permute-done.7.far.tfar, f32[177,8,128]{2,1,0:T(8,128)S(1)} %collective-permute-done.8.near.tnear, ...), custom_call_target="tpu_custom_call" | custom-call | tf_op jit(solution)/shard_map/front/pallas_call | solution.py:510
  46.8 0.1 collective-permute-start.9
  46.9 5.8 %collective-permute-start.10 = (f32[26,4,8,128]{3,2,1,0:T(8,128)S(1)}, f32[26,4,8,128]{3,2,1,0:T(8,128)S(1)}, u32[]{:S(2)}, u32[]{:S(2)}) collective-permute-start(f32[26,4,8,128]{3,2,1,0:T(8,128)S(1)} %get-tuple-element.63), channel_id=1, source_target_pairs={{0,0},{1,2},{2,1},{3,4},{4,3},{5,6},{6,5},{7,8},{8,7},{9,10},{10,9... | collective-permute-start | bytes 1277960 | tf_op jit(solution)/shard_map/ppermute | solution.py:469
  52.7 5.4 %collective-permute-done.9.far = f32[26,4,8,128]{3,2,1,0:T(8,128)S(1)} collective-permute-done((f32[26,4,8,128]{3,2,1,0:T(8,128)S(1)}, f32[26,4,8,128]{3,2,1,0:T(8,128)S(1)}, u32[]{:S(2)}, u32[]{:S(2)}) %collective-permute-start.9) | collective-permute-done | bytes 426016 | tf_op jit(solution)/shard_map/ppermute | solution.py:469
  58.1 4.0 %collective-permute-done.10.near = f32[26,4,8,128]{3,2,1,0:T(8,128)S(1)} collective-permute-done((f32[26,4,8,128]{3,2,1,0:T(8,128)S(1)}, f32[26,4,8,128]{3,2,1,0:T(8,128)S(1)}, u32[]{:S(2)}, u32[]{:S(2)}) %collective-permute-start.10) | collective-permute-done | bytes 426016 | tf_op jit(solution)/shard_map/ppermute | solution.py:469
  62.1 0.9 middle.1
  63.1 0.1 collective-permute-start.11
  63.2 5.4 %collective-permute-start.12 = (f32[24,4,8,128]{3,2,1,0:T(8,128)S(1)}, f32[24,4,8,128]{3,2,1,0:T(8,128)S(1)}, u32[]{:S(2)}, u32[]{:S(2)}) collective-permute-start(f32[24,4,8,128]{3,2,1,0:T(8,128)S(1)} %get-tuple-element.67), channel_id=1, source_target_pairs={{0,0},{1,2},{2,1},{3,4},{4,3},{5,6},{6,5},{7,8},{8,7},{9,10},{10,9... | collective-permute-start | bytes 1179656 | tf_op jit(solution)/shard_map/ppermute | solution.py:469
  68.6 4.1 %collective-permute-done.11.far.far_x = f32[24,4,8,128]{3,2,1,0:T(8,128)S(1)} collective-permute-done((f32[24,4,8,128]{3,2,1,0:T(8,128)S(1)}, f32[24,4,8,128]{3,2,1,0:T(8,128)S(1)}, u32[]{:S(2)}, u32[]{:S(2)}) %collective-permute-start.11) | collective-permute-done | bytes 393248 | tf_op jit(solution)/shard_map/ppermute | solution.py:469
  72.7 4.0 %collective-permute-done.12.near.near_x = f32[24,4,8,128]{3,2,1,0:T(8,128)S(1)} collective-permute-done((f32[24,4,8,128]{3,2,1,0:T(8,128)S(1)}, f32[24,4,8,128]{3,2,1,0:T(8,128)S(1)}, u32[]{:S(2)}, u32[]{:S(2)}) %collective-permute-start.12) | collective-permute-done | bytes 393248 | tf_op jit(solution)/shard_map/ppermute | solution.py:469
  76.7 0.6 edges.1
  77.3 0.7 collective-permute-start.13
  78.0 2.2 %collective-permute-start.14 = (f32[18,4,8,128]{3,2,1,0:T(8,128)S(1)}, f32[18,4,8,128]{3,2,1,0:T(8,128)S(1)}, u32[]{:S(2)}, u32[]{:S(2)}) collective-permute-start(f32[18,4,8,128]{3,2,1,0:T(8,128)S(1)} %get-tuple-element.70), channel_id=1, source_target_pairs={{0,32},{32,0},{64,96},{96,64},{128,160},{160,128},{192,224},{224,1... | collective-permute-start | bytes 884744 | tf_op jit(solution)/shard_map/ppermute | solution.py:469
  80.2 1.2 %collective-permute-done.14.got0 = f32[18,4,8,128]{3,2,1,0:T(8,128)S(1)} collective-permute-done((f32[18,4,8,128]{3,2,1,0:T(8,128)S(1)}, f32[18,4,8,128]{3,2,1,0:T(8,128)S(1)}, u32[]{:S(2)}, u32[]{:S(2)}) %collective-permute-start.14) | collective-permute-done | bytes 294944 | tf_op jit(solution)/shard_map/ppermute | solution.py:469
  81.4 0.7 widen.1
  82.1 1.5 %front.3 = (f32[68,4,8,128]{3,2,1,0:T(8,128)S(1)}, f32[2,16,4,8,128]{4,3,2,1,0:T(8,128)S(1)}, f32[26,4,8,128]{3,2,1,0:T(8,128)S(1)}, f32[26,4,8,128]{3,2,1,0:T(8,128)S(1)}) custom-call(f32[136,8,128]{2,1,0:T(8,128)S(1)} %bitcast.11, f32[136,8,128]{2,1,0:T(8,128)S(1)} %bitcast.10, f32[2,20,4,8,128]{4,3,2,1,0:T(8,128)S(1)} %get-tuple-element.73.own, ...), custom_call_target="tpu_custom_call" | custom-call | tf_op jit(solution)/shard_map/front/pallas_call | solution.py:510
  83.6 0.3 collective-permute-start.15
  83.8 5.1 %collective-permute-start.16 = (f32[26,4,8,128]{3,2,1,0:T(8,128)S(1)}, f32[26,4,8,128]{3,2,1,0:T(8,128)S(1)}, u32[]{:S(2)}, u32[]{:S(2)}) collective-permute-start(f32[26,4,8,128]{3,2,1,0:T(8,128)S(1)} %get-tuple-element.75), channel_id=1, source_target_pairs={{0,0},{1,2},{2,1},{3,4},{4,3},{5,6},{6,5},{7,8},{8,7},{9,10},{10,9... | collective-permute-start | bytes 1277960 | tf_op jit(solution)/shard_map/ppermute | solution.py:469
  89.0 5.4 %collective-permute-done.15.far = f32[26,4,8,128]{3,2,1,0:T(8,128)S(1)} collective-permute-done((f32[26,4,8,128]{3,2,1,0:T(8,128)S(1)}, f32[26,4,8,128]{3,2,1,0:T(8,128)S(1)}, u32[]{:S(2)}, u32[]{:S(2)}) %collective-permute-start.15) | collective-permute-done | bytes 426016 | tf_op jit(solution)/shard_map/ppermute | solution.py:469
  94.3 4.0 %collective-permute-done.16.near = f32[26,4,8,128]{3,2,1,0:T(8,128)S(1)} collective-permute-done((f32[26,4,8,128]{3,2,1,0:T(8,128)S(1)}, f32[26,4,8,128]{3,2,1,0:T(8,128)S(1)}, u32[]{:S(2)}, u32[]{:S(2)}) %collective-permute-start.16) | collective-permute-done | bytes 426016 | tf_op jit(solution)/shard_map/ppermute | solution.py:469
  98.3 2.1 %last.1 = (f32[4,96,128]{2,1,0:T(8,128)S(1)}, f32[4,96,128]{2,1,0:T(8,128)S(1)}) custom-call(s32[3]{0:T(128)S(1)} %pad_add_fusion.pos, f32[26,4,8,128]{3,2,1,0:T(8,128)S(1)} %collective-permute-done.15.far, f32[26,4,8,128]{3,2,1,0:T(8,128)S(1)} %collective-permute-done.16.near, f32[2,16,4,8,128]{4,3,2,1,0:T(8,128)S(1)} %get-tuple-element.76.it, ...), custom_call_target="tpu_custom_call" | custom-call | tf_op jit(solution)/shard_map/last/pallas_call | solution.py:539
  100.4 2.1 %collective-permute-start.17 = (f32[4,96,128]{2,1,0:T(8,128)S(1)}, f32[4,96,128]{2,1,0:T(8,128)S(1)}, u32[]{:S(2)}, u32[]{:S(2)}) collective-permute-start(f32[4,96,128]{2,1,0:T(8,128)S(1)} %get-tuple-element.79), channel_id=1, source_target_pairs={{0,32},{32,0},{64,96},{96,64},{128,160},{160,128},{192,224},{224,1... | collective-permute-start | bytes 589832 | tf_op jit(solution)/shard_map/ppermute | solution.py:469
  102.5 1.1 collective-permute-done.17.other
  103.6 4.9 %collective-permute-start.18 = (f32[2,96,128]{2,1,0:T(8,128)S(1)}, f32[2,96,128]{2,1,0:T(8,128)S(1)}, u32[]{:S(2)}, u32[]{:S(2)}) collective-permute-start(f32[2,96,128]{2,1,0:T(8,128)S(1)} %get-tuple-element.81), channel_id=1, source_target_pairs={{0,128},{32,160},{64,192},{96,224},{128,0},{160,32},{192,64},{224,... | collective-permute-start | bytes 294920 | tf_op jit(solution)/shard_map/ppermute | solution.py:550
  108.5 1.8 %collective-permute-start.20 = (f32[2,96,128]{2,1,0:T(8,128)S(1)}, f32[2,96,128]{2,1,0:T(8,128)S(1)}, u32[]{:S(2)}, u32[]{:S(2)}) collective-permute-start(f32[2,96,128]{2,1,0:T(8,128)S(1)} %get-tuple-element.83), channel_id=1, source_target_pairs={{0,192},{32,224},{64,128},{96,160},{128,64},{160,96},{192,0},{224,... | collective-permute-start | bytes 294920 | tf_op jit(solution)/shard_map/ppermute | solution.py:550
  110.4 1.3 %collective-permute-done.18.a = f32[2,96,128]{2,1,0:T(8,128)S(1)} collective-permute-done((f32[2,96,128]{2,1,0:T(8,128)S(1)}, f32[2,96,128]{2,1,0:T(8,128)S(1)}, u32[]{:S(2)}, u32[]{:S(2)}) %collective-permute-start.18) | collective-permute-done | bytes 98336 | tf_op jit(solution)/shard_map/ppermute | solution.py:550
  111.7 1.5 %collective-permute-done.19.b = f32[2,96,128]{2,1,0:T(8,128)S(1)} collective-permute-done((f32[2,96,128]{2,1,0:T(8,128)S(1)}, f32[2,96,128]{2,1,0:T(8,128)S(1)}, u32[]{:S(2)}, u32[]{:S(2)}) %collective-permute-start.19) | collective-permute-done | bytes 98336 | tf_op jit(solution)/shard_map/ppermute | solution.py:550
  113.1 1.2 %collective-permute-done.20.c = f32[2,96,128]{2,1,0:T(8,128)S(1)} collective-permute-done((f32[2,96,128]{2,1,0:T(8,128)S(1)}, f32[2,96,128]{2,1,0:T(8,128)S(1)}, u32[]{:S(2)}, u32[]{:S(2)}) %collective-permute-start.20) | collective-permute-done | bytes 98336 | tf_op jit(solution)/shard_map/ppermute | solution.py:550
  114.3 1.4 %unpack.1 = (f32[2,2,96,128]{3,2,1,0:T(8,128)}, f32[2,2,96,128]{3,2,1,0:T(8,128)}) custom-call(s32[3]{0:T(128)S(1)} %pad_add_fusion.pos, f32[2,96,128]{2,1,0:T(8,128)S(1)} %collective-permute-done.18.a, f32[2,96,128]{2,1,0:T(8,128)S(1)} %collective-permute-done.19.b, f32[2,96,128]{2,1,0:T(8,128)S(1)} %collective-permute-done.20.c, ...), custom_call_target="tpu_custom_call" | custom-call | tf_op jit(solution)/shard_map/unpack/pallas_call | solution.py:553
  (6 shorter events, 0.0 us)
Async XLA Ops:
  2.6 7.8 %collective-permute-start = (f32[240,128]{1,0:T(8,128)S(1)}, f32[240,128]{1,0:T(8,128)S(1)}, u32[]{:S(2)}, u32[]{:S(2)}) collective-permute-start(f32[240,128]{1,0:T(8,128)S(1)} %get-tuple-element.43), channel_id=1, source_target_pairs={{0,128},{32,160},{64,192},{96,224},{128,0},{160,32},{192,64},{224,... | collective-permute-start | bytes 368648 | tf_op jit(solution)/shard_map/ppermute | solution.py:460
  5.9 6.9 %collective-permute-start.1 = (f32[240,128]{1,0:T(8,128)S(1)}, f32[240,128]{1,0:T(8,128)S(1)}, u32[]{:S(2)}, u32[]{:S(2)}) collective-permute-start(f32[240,128]{1,0:T(8,128)S(1)} %get-tuple-element.44), channel_id=1, source_target_pairs={{0,64},{32,96},{64,0},{96,32},{128,192},{160,224},{192,128},{224,1... | collective-permute-start | bytes 368648 | tf_op jit(solution)/shard_map/ppermute | solution.py:460
  6.6 9.2 %collective-permute-start.2 = (f32[240,128]{1,0:T(8,128)S(1)}, f32[240,128]{1,0:T(8,128)S(1)}, u32[]{:S(2)}, u32[]{:S(2)}) collective-permute-start(f32[240,128]{1,0:T(8,128)S(1)} %get-tuple-element.45), channel_id=1, source_target_pairs={{0,192},{32,224},{64,128},{96,160},{128,64},{160,96},{192,0},{224,... | collective-permute-start | bytes 368648 | tf_op jit(solution)/shard_map/ppermute | solution.py:460
  7.0 8.8 %collective-permute-start.3 = (f32[240,128]{1,0:T(8,128)S(1)}, f32[240,128]{1,0:T(8,128)S(1)}, u32[]{:S(2)}, u32[]{:S(2)}) collective-permute-start(f32[240,128]{1,0:T(8,128)S(1)} %get-tuple-element.46), channel_id=1, source_target_pairs={{0,160},{32,128},{64,224},{96,192},{128,32},{160,0},{192,96},{224,... | collective-permute-start | bytes 368648 | tf_op jit(solution)/shard_map/ppermute | solution.py:460
  8.6 8.4 %collective-permute-start.4 = (f32[240,128]{1,0:T(8,128)S(1)}, f32[240,128]{1,0:T(8,128)S(1)}, u32[]{:S(2)}, u32[]{:S(2)}) collective-permute-start(f32[240,128]{1,0:T(8,128)S(1)} %get-tuple-element.47), channel_id=1, source_target_pairs={{0,96},{32,64},{64,32},{96,0},{128,224},{160,192},{192,160},{224,1... | collective-permute-start | bytes 368648 | tf_op jit(solution)/shard_map/ppermute | solution.py:460
  10.4 7.1 %collective-permute-start.5 = (f32[240,128]{1,0:T(8,128)S(1)}, f32[240,128]{1,0:T(8,128)S(1)}, u32[]{:S(2)}, u32[]{:S(2)}) collective-permute-start(f32[240,128]{1,0:T(8,128)S(1)} %get-tuple-element.48), channel_id=1, source_target_pairs={{0,224},{32,192},{64,160},{96,128},{128,96},{160,64},{192,32},{224... | collective-permute-start | bytes 368648 | tf_op jit(solution)/shard_map/ppermute | solution.py:460
  12.8 4.7 %collective-permute-start.6 = (f32[240,128]{1,0:T(8,128)S(1)}, f32[240,128]{1,0:T(8,128)S(1)}, u32[]{:S(2)}, u32[]{:S(2)}) collective-permute-start(f32[240,128]{1,0:T(8,128)S(1)} %get-tuple-element.49), channel_id=1, source_target_pairs={{0,32},{32,0},{64,96},{96,64},{128,160},{160,128},{192,224},{224,1... | collective-permute-start | bytes 368648 | tf_op jit(solution)/shard_map/ppermute | solution.py:460
  19.1 18.7 %collective-permute-start.7 = (f32[177,8,128]{2,1,0:T(8,128)S(1)}, f32[177,8,128]{2,1,0:T(8,128)S(1)}, u32[]{:S(2)}, u32[]{:S(2)}) collective-permute-start(f32[177,8,128]{2,1,0:T(8,128)S(1)} %get-tuple-element.54), channel_id=1, source_target_pairs={{0,1},{1,0},{2,3},{3,2},{4,5},{5,4},{6,7},{7,6},{8,9},{9,8},{10,11... | collective-permute-start | bytes 2174984 | tf_op jit(solution)/shard_map/ppermute | solution.py:469
  21.1 23.5 %collective-permute-start.8 = (f32[177,8,128]{2,1,0:T(8,128)S(1)}, f32[177,8,128]{2,1,0:T(8,128)S(1)}, u32[]{:S(2)}, u32[]{:S(2)}) collective-permute-start(f32[177,8,128]{2,1,0:T(8,128)S(1)} %get-tuple-element.55), channel_id=1, source_target_pairs={{0,0},{1,2},{2,1},{3,4},{4,3},{5,6},{6,5},{7,8},{8,7},{9,10},{10,9... | collective-permute-start | bytes 2174984 | tf_op jit(solution)/shard_map/ppermute | solution.py:469
  46.8 11.3 %collective-permute-start.9 = (f32[26,4,8,128]{3,2,1,0:T(8,128)S(1)}, f32[26,4,8,128]{3,2,1,0:T(8,128)S(1)}, u32[]{:S(2)}, u32[]{:S(2)}) collective-permute-start(f32[26,4,8,128]{3,2,1,0:T(8,128)S(1)} %get-tuple-element.62), channel_id=1, source_target_pairs={{0,1},{1,0},{2,3},{3,2},{4,5},{5,4},{6,7},{7,6},{8,9},{9,8},{10,11... | collective-permute-start | bytes 1277960 | tf_op jit(solution)/shard_map/ppermute | solution.py:469
  46.9 15.2 %collective-permute-start.10 = (f32[26,4,8,128]{3,2,1,0:T(8,128)S(1)}, f32[26,4,8,128]{3,2,1,0:T(8,128)S(1)}, u32[]{:S(2)}, u32[]{:S(2)}) collective-permute-start(f32[26,4,8,128]{3,2,1,0:T(8,128)S(1)} %get-tuple-element.63), channel_id=1, source_target_pairs={{0,0},{1,2},{2,1},{3,4},{4,3},{5,6},{6,5},{7,8},{8,7},{9,10},{10,9... | collective-permute-start | bytes 1277960 | tf_op jit(solution)/shard_map/ppermute | solution.py:469
  63.1 9.6 %collective-permute-start.11 = (f32[24,4,8,128]{3,2,1,0:T(8,128)S(1)}, f32[24,4,8,128]{3,2,1,0:T(8,128)S(1)}, u32[]{:S(2)}, u32[]{:S(2)}) collective-permute-start(f32[24,4,8,128]{3,2,1,0:T(8,128)S(1)} %get-tuple-element.66), channel_id=1, source_target_pairs={{0,1},{1,0},{2,3},{3,2},{4,5},{5,4},{6,7},{7,6},{8,9},{9,8},{10,11... | collective-permute-start | bytes 1179656 | tf_op jit(solution)/shard_map/ppermute | solution.py:469
  63.2 13.6 %collective-permute-start.12 = (f32[24,4,8,128]{3,2,1,0:T(8,128)S(1)}, f32[24,4,8,128]{3,2,1,0:T(8,128)S(1)}, u32[]{:S(2)}, u32[]{:S(2)}) collective-permute-start(f32[24,4,8,128]{3,2,1,0:T(8,128)S(1)} %get-tuple-element.67), channel_id=1, source_target_pairs={{0,0},{1,2},{2,1},{3,4},{4,3},{5,6},{6,5},{7,8},{8,7},{9,10},{10,9... | collective-permute-start | bytes 1179656 | tf_op jit(solution)/shard_map/ppermute | solution.py:469
  77.3 2.9 %collective-permute-start.13 = (f32[18,4,8,128]{3,2,1,0:T(8,128)S(1)}, f32[18,4,8,128]{3,2,1,0:T(8,128)S(1)}, u32[]{:S(2)}, u32[]{:S(2)}) collective-permute-start(f32[18,4,8,128]{3,2,1,0:T(8,128)S(1)} %get-tuple-element.69), channel_id=1, source_target_pairs={{0,0},{32,64},{64,32},{96,128},{128,96},{160,192},{192,160},{224,2... | collective-permute-start | bytes 884744 | tf_op jit(solution)/shard_map/ppermute | solution.py:469
  78.0 3.4 %collective-permute-start.14 = (f32[18,4,8,128]{3,2,1,0:T(8,128)S(1)}, f32[18,4,8,128]{3,2,1,0:T(8,128)S(1)}, u32[]{:S(2)}, u32[]{:S(2)}) collective-permute-start(f32[18,4,8,128]{3,2,1,0:T(8,128)S(1)} %get-tuple-element.70), channel_id=1, source_target_pairs={{0,32},{32,0},{64,96},{96,64},{128,160},{160,128},{192,224},{224,1... | collective-permute-start | bytes 884744 | tf_op jit(solution)/shard_map/ppermute | solution.py:469
  83.6 10.8 %collective-permute-start.15 = (f32[26,4,8,128]{3,2,1,0:T(8,128)S(1)}, f32[26,4,8,128]{3,2,1,0:T(8,128)S(1)}, u32[]{:S(2)}, u32[]{:S(2)}) collective-permute-start(f32[26,4,8,128]{3,2,1,0:T(8,128)S(1)} %get-tuple-element.74), channel_id=1, source_target_pairs={{0,1},{1,0},{2,3},{3,2},{4,5},{5,4},{6,7},{7,6},{8,9},{9,8},{10,11... | collective-permute-start | bytes 1277960 | tf_op jit(solution)/shard_map/ppermute | solution.py:469
  83.8 14.5 %collective-permute-start.16 = (f32[26,4,8,128]{3,2,1,0:T(8,128)S(1)}, f32[26,4,8,128]{3,2,1,0:T(8,128)S(1)}, u32[]{:S(2)}, u32[]{:S(2)}) collective-permute-start(f32[26,4,8,128]{3,2,1,0:T(8,128)S(1)} %get-tuple-element.75), channel_id=1, source_target_pairs={{0,0},{1,2},{2,1},{3,4},{4,3},{5,6},{6,5},{7,8},{8,7},{9,10},{10,9... | collective-permute-start | bytes 1277960 | tf_op jit(solution)/shard_map/ppermute | solution.py:469
  100.4 3.2 %collective-permute-start.17 = (f32[4,96,128]{2,1,0:T(8,128)S(1)}, f32[4,96,128]{2,1,0:T(8,128)S(1)}, u32[]{:S(2)}, u32[]{:S(2)}) collective-permute-start(f32[4,96,128]{2,1,0:T(8,128)S(1)} %get-tuple-element.79), channel_id=1, source_target_pairs={{0,32},{32,0},{64,96},{96,64},{128,160},{160,128},{192,224},{224,1... | collective-permute-start | bytes 589832 | tf_op jit(solution)/shard_map/ppermute | solution.py:469
  103.6 8.0 %collective-permute-start.18 = (f32[2,96,128]{2,1,0:T(8,128)S(1)}, f32[2,96,128]{2,1,0:T(8,128)S(1)}, u32[]{:S(2)}, u32[]{:S(2)}) collective-permute-start(f32[2,96,128]{2,1,0:T(8,128)S(1)} %get-tuple-element.81), channel_id=1, source_target_pairs={{0,128},{32,160},{64,192},{96,224},{128,0},{160,32},{192,64},{224,... | collective-permute-start | bytes 294920 | tf_op jit(solution)/shard_map/ppermute | solution.py:550
  108.5 4.6 %collective-permute-start.19 = (f32[2,96,128]{2,1,0:T(8,128)S(1)}, f32[2,96,128]{2,1,0:T(8,128)S(1)}, u32[]{:S(2)}, u32[]{:S(2)}) collective-permute-start(f32[2,96,128]{2,1,0:T(8,128)S(1)} %get-tuple-element.82), channel_id=1, source_target_pairs={{0,64},{32,96},{64,0},{96,32},{128,192},{160,224},{192,128},{224,1... | collective-permute-start | bytes 294920 | tf_op jit(solution)/shard_map/ppermute | solution.py:550
  108.5 5.8 %collective-permute-start.20 = (f32[2,96,128]{2,1,0:T(8,128)S(1)}, f32[2,96,128]{2,1,0:T(8,128)S(1)}, u32[]{:S(2)}, u32[]{:S(2)}) collective-permute-start(f32[2,96,128]{2,1,0:T(8,128)S(1)} %get-tuple-element.83), channel_id=1, source_target_pairs={{0,192},{32,224},{64,128},{96,160},{128,64},{160,96},{192,0},{224,... | collective-permute-start | bytes 294920 | tf_op jit(solution)/shard_map/ppermute | solution.py:550

commit v7 on v6

--- a/solution.py
+++ b/solution.py
@@ -460,13 +460,24 @@
     return [lax.ppermute(pieces[k], "tm", [(i, i ^ k) for i in range(count)]) for k in ORDER] + [pieces[0]]
 
 
-def swap(block, axis, start):
-    count = lax.axis_size(axis)
-    route = [(i, i) for i in range(start)]
-    for i in range(start, count - 1, 2):
-        route += [(i, i + 1), (i + 1, i)]
-    route += [(i, i) for i in range(len(route), count)]
-    return lax.ppermute(block, axis, route)
+def swap_rows(block, start):
+    count = lax.axis_size("tm")
+    route = []
+    for i in range(start, start + count, 2):
+        low, high = i % count, (i + 1) % count
+        route += [(low, high), (high, low)]
+    return lax.ppermute(block, "tm", route)
+
+
+def swap_planes(block, start):
+    sections, slabs = lax.axis_size("tm"), lax.axis_size("space")
+    route = []
+    for t in range(sections):
+        for s in range(slabs):
+            pair = s + 1 if (s - start) % 2 == 0 else s - 1
+            to = t * slabs + pair if 0 <= pair < slabs else (t ^ 1) * slabs + s
+            route.append((t * slabs + s, to))
+    return lax.ppermute(block, ("tm", "space"), route)
 
 
 def on_device(state_guess, adjoint_guess, target, initial_state, diffusivity):
@@ -498,8 +509,8 @@
         11,
         [pltpu.VMEM((8 * 12 * WIN, 128), jnp.float32)],
     )(pos, *got, near_c, far_c, forward)
-    far = far_first = swap(far, "space", 0)
-    near = near_first = swap(near, "space", 1)
+    far = far_first = swap_planes(far, 0)
+    near = near_first = swap_planes(near, 1)
     weights, inv = call(
         coefficient_body, "coefficients", [whole(4 * TALL * 8, 128), whole(68, 2, 8, 128)], 4
     )(pos, far, near, here_c, consts)
@@ -515,8 +526,8 @@
             [pltpu.VMEM((68, 4, 8, 128), jnp.float32)],
             scalars=0,
         )(far, near, own, wish, near_first, far_first, weights, consts, inv)
-        far_z = swap(far_z, "space", 0)
-        near_z = swap(near_z, "space", 1)
+        far_z = swap_planes(far_z, 0)
+        near_z = swap_planes(near_z, 1)
         if outer < OUTER - 1:
             new, near, far = call(
                 middle_body,
@@ -526,11 +537,11 @@
                 sweep_scratch,
                 scalars=0,
             )(far_z, near_z, it, fixed, weights, consts, inv)
-            far = swap(far, "space", 0)
-            near = swap(near, "space", 1)
+            far = swap_planes(far, 0)
+            near = swap_planes(near, 1)
             send0, send1 = call(edges_body, "edges", [whole(18, 4, 8, 128)] * 2, 3)(pos, far, near, new)
-            got1 = swap(send1, "tm", 1)
-            got0 = swap(send0, "tm", 0)
+            got1 = swap_rows(send1, 1)
+            got0 = swap_rows(send0, 0)
             own, near, far = call(
                 widen_body, "widen", [whole(2, WIN, 4, 8, 128), whole(34, 4, 8, 128), whole(34, 4, 8, 128)], 5
             )(pos, got1, got0, new, near, far)
@@ -543,7 +554,7 @@
         8,
         sweep_scratch + [pltpu.VMEM((2 * OWN, 4, 8, 128), jnp.float32), pltpu.VMEM((64 * OWN, 128), jnp.float32)],
     )(pos, far_z, near_z, it, fixed, weights, consts, inv, back)
-    other = swap(other, "tm", 0)
+    other = swap_rows(other, 0)
     pairs = call(merge_body, "merge", [whole(2, 8 * OWN, 128)] * 3, 2, scalars=0)(other, mine)
     count = lax.axis_size("tm")
     got = [

time: 116 us -> 108 us (0.931)
  starting transfers between devices: 46.6 us -> 32.6 us
  waiting for transfers between devices: 55.4 us -> 61.4 us
    ppermute x11, starting transfers between devices: 30.9 us -> 19.4 us  [the longest x8 18.3 us: swap_planes(): return lax.ppermute(block, ('tm', 'space'), route)]
    ppermute x11, waiting for transfers between devices: 45.6 us -> 50.7 us  [the longest x8 42.8 us: swap_planes(): return lax.ppermute(block, ('tm', 'space'), route)]
    ppermute x3, starting transfers between devices: 6.72 us -> 4.18 us  [on_device(): lax.ppermute(pair, 'tm', [(i, i ^ 2 * k) for i in range(count)])]
where the time goes in v7:
time: 108 us
  waiting for transfers between devices  61.4 us (57%)
  starting transfers between devices  32.6 us (30%)
  Pallas kernels  12.9 us (12%)
    ppermute x8, waiting for transfers between devices, swap_planes(): return lax.ppermute(block, ('tm', 'space'), route)  42.8 us
    ppermute x8, starting transfers between devices, swap_planes(): return lax.ppermute(block, ('tm', 'space'), route)  18.3 us
    ppermute x7, starting transfers between devices, exchange(): lax.ppermute(pieces[k], 'tm', [(i, i ^ k) for i in range(count)])  8.99 us
    ppermute x3, waiting for transfers between devices, swap_rows(): return lax.ppermute(block, 'tm', route)  7.88 us
    ppermute x7, waiting for transfers between devices, exchange(): lax.ppermute(pieces[k], 'tm', [(i, i ^ k) for i in range(count)])  5.87 us
    ppermute x3, waiting for transfers between devices, on_device(): lax.ppermute(pair, 'tm', [(i, i ^ 2 * k) for i in range(count)])  4.77 us
    ppermute x3, starting transfers between devices, on_device(): lax.ppermute(pair, 'tm', [(i, i ^ 2 * k) for i in range(count)])  4.18 us
    pallas_call x2, Pallas kernels, on_device(): call(front_body, 'front', [whole(68, 4, 8, 128), whole(2, 16, 4, 8, 128),...  2.94 us
  transfers between devices with their start and end apart: 21, of which 17 were waited for; matrix products, arithmetic and copies ran while one was open for 0% of the time, Pallas kernels for 0%

profile of v7, /device:TPU:6, one launch (start us, length us, event | category | flops | bytes accessed | tf_op | source)
XLA Modules:
  0.0 107.8 jit_solution(4193089220553994757)
XLA Ops:
  0.7 1.9 %pack.1 = (f32[240,128]{1,0:T(8,128)S(1)}, f32[240,128]{1,0:T(8,128)S(1)}, f32[240,128]{1,0:T(8,128)S(1)}, f32[240,128]{1,0:T(8,128)S(1)}, f32[240,128]{1,0:T(8,...) custom-call(s32[3]{0:T(128)S(1)} %pad_add_fusion.pos, ...), custom_call_target="tpu_custom_call" | custom-call | tf_op jit(solution)/shard_map/pack/pallas_call | solution.py:492
  2.6 3.3 %collective-permute-start = (f32[240,128]{1,0:T(8,128)S(1)}, f32[240,128]{1,0:T(8,128)S(1)}, u32[]{:S(2)}, u32[]{:S(2)}) collective-permute-start(f32[240,128]{1,0:T(8,128)S(1)} %get-tuple-element.43), channel_id=1, source_target_pairs={{0,128},{32,160},{64,192},{96,224},{128,0},{160,32},{192,64},{224,... | collective-permute-start | bytes 368648 | tf_op jit(solution)/shard_map/ppermute | solution.py:460
  5.9 0.7 collective-permute-start.1
  6.6 0.4 collective-permute-start.2
  7.0 1.6 %collective-permute-start.3 = (f32[240,128]{1,0:T(8,128)S(1)}, f32[240,128]{1,0:T(8,128)S(1)}, u32[]{:S(2)}, u32[]{:S(2)}) collective-permute-start(f32[240,128]{1,0:T(8,128)S(1)} %get-tuple-element.46), channel_id=1, source_target_pairs={{0,160},{32,128},{64,224},{96,192},{128,32},{160,0},{192,96},{224,... | collective-permute-start | bytes 368648 | tf_op jit(solution)/shard_map/ppermute | solution.py:460
  8.6 1.8 %collective-permute-start.4 = (f32[240,128]{1,0:T(8,128)S(1)}, f32[240,128]{1,0:T(8,128)S(1)}, u32[]{:S(2)}, u32[]{:S(2)}) collective-permute-start(f32[240,128]{1,0:T(8,128)S(1)} %get-tuple-element.47), channel_id=1, source_target_pairs={{0,96},{32,64},{64,32},{96,0},{128,224},{160,192},{192,160},{224,1... | collective-permute-start | bytes 368648 | tf_op jit(solution)/shard_map/ppermute | solution.py:460
  10.4 0.5 collective-permute-start.5
  10.9 1.9 %collective-permute-done.1.rest_1_ = f32[240,128]{1,0:T(8,128)S(1)} collective-permute-done((f32[240,128]{1,0:T(8,128)S(1)}, f32[240,128]{1,0:T(8,128)S(1)}, u32[]{:S(2)}, u32[]{:S(2)}) %collective-permute-start.1) | collective-permute-done | bytes 122912 | tf_op jit(solution)/shard_map/ppermute | solution.py:460
  12.8 0.8 collective-permute-start.6
  13.5 2.2 %collective-permute-done.2.rest_2_ = f32[240,128]{1,0:T(8,128)S(1)} collective-permute-done((f32[240,128]{1,0:T(8,128)S(1)}, f32[240,128]{1,0:T(8,128)S(1)}, u32[]{:S(2)}, u32[]{:S(2)}) %collective-permute-start.2) | collective-permute-done | bytes 122912 | tf_op jit(solution)/shard_map/ppermute | solution.py:460
  15.8 1.2 %collective-permute-done.4.rest_4_ = f32[240,128]{1,0:T(8,128)S(1)} collective-permute-done((f32[240,128]{1,0:T(8,128)S(1)}, f32[240,128]{1,0:T(8,128)S(1)}, u32[]{:S(2)}, u32[]{:S(2)}) %collective-permute-start.4) | collective-permute-done | bytes 122912 | tf_op jit(solution)/shard_map/ppermute | solution.py:460
  17.0 0.5 collective-permute-done.5.rest_5_
  17.5 1.6 %spread.1 = (f32[2,20,4,8,128]{4,3,2,1,0:T(8,128)S(1)}, f32[2,18,2,8,128]{4,3,2,1,0:T(8,128)S(1)}, f32[177,8,128]{2,1,0:T(8,128)S(1)}, f32[177,8,128]{2,1,0:T(8,128)S(1)}) custom-call(s32[3]{0:T(128)S(1)} %pad_add_fusion.pos, f32[240,128]{1,0:T(8,128)S(1)} %collective-permute-done.rest_0_, f32[240,128]{1,0:T(8,128)S(1)} %collective-permute-done.1.rest_1_, ...), custom_call_target="tpu_custom_call" | custom-call | tf_op jit(solution)/shard_map/spread/pallas_call | solution.py:505
  19.1 2.0 %collective-permute-start.7 = (f32[177,8,128]{2,1,0:T(8,128)S(1)}, f32[177,8,128]{2,1,0:T(8,128)S(1)}, u32[]{:S(2)}, u32[]{:S(2)}) collective-permute-start(f32[177,8,128]{2,1,0:T(8,128)S(1)} %get-tuple-element.54), channel_id=1, source_target_pairs={{0,1},{1,0},{2,3},{3,2},{4,5},{5,4},{6,7},{7,6},{8,9},{9,8},{10,11... | collective-permute-start | bytes 2174984 | tf_op jit(solution)/shard_map/ppermute | solution.py:480
  21.1 5.2 %collective-permute-start.8 = (f32[177,8,128]{2,1,0:T(8,128)S(1)}, f32[177,8,128]{2,1,0:T(8,128)S(1)}, u32[]{:S(2)}, u32[]{:S(2)}) collective-permute-start(f32[177,8,128]{2,1,0:T(8,128)S(1)} %get-tuple-element.55), channel_id=1, source_target_pairs={{0,32},{1,2},{2,1},{3,4},{4,3},{5,6},{6,5},{7,8},{8,7},{9,10},{10,... | collective-permute-start | bytes 2174984 | tf_op jit(solution)/shard_map/ppermute | solution.py:480
  26.3 11.5 %collective-permute-done.7.far.tfar = f32[177,8,128]{2,1,0:T(8,128)S(1)} collective-permute-done((f32[177,8,128]{2,1,0:T(8,128)S(1)}, f32[177,8,128]{2,1,0:T(8,128)S(1)}, u32[]{:S(2)}, u32[]{:S(2)}) %collective-permute-start.7) | collective-permute-done | bytes 725024 | tf_op jit(solution)/shard_map/ppermute | solution.py:480
  37.8 4.9 %collective-permute-done.8.near.tnear = f32[177,8,128]{2,1,0:T(8,128)S(1)} collective-permute-done((f32[177,8,128]{2,1,0:T(8,128)S(1)}, f32[177,8,128]{2,1,0:T(8,128)S(1)}, u32[]{:S(2)}, u32[]{:S(2)}) %collective-permute-start.8) | collective-permute-done | bytes 725024 | tf_op jit(solution)/shard_map/ppermute | solution.py:480
  42.7 0.8 coefficients.1
  43.5 1.5 %front.2 = (f32[68,4,8,128]{3,2,1,0:T(8,128)S(1)}, f32[2,16,4,8,128]{4,3,2,1,0:T(8,128)S(1)}, f32[26,4,8,128]{3,2,1,0:T(8,128)S(1)}, f32[26,4,8,128]{3,2,1,0:T(8,128)S(1)}) custom-call(f32[177,8,128]{2,1,0:T(8,128)S(1)} %collective-permute-done.7.far.tfar, f32[177,8,128]{2,1,0:T(8,128)S(1)} %collective-permute-done.8.near.tnear, ...), custom_call_target="tpu_custom_call" | custom-call | tf_op jit(solution)/shard_map/front/pallas_call | solution.py:521
  44.9 0.1 collective-permute-start.9
  45.0 3.9 %collective-permute-start.10 = (f32[26,4,8,128]{3,2,1,0:T(8,128)S(1)}, f32[26,4,8,128]{3,2,1,0:T(8,128)S(1)}, u32[]{:S(2)}, u32[]{:S(2)}) collective-permute-start(f32[26,4,8,128]{3,2,1,0:T(8,128)S(1)} %get-tuple-element.63), channel_id=1, source_target_pairs={{0,32},{1,2},{2,1},{3,4},{4,3},{5,6},{6,5},{7,8},{8,7},{9,10},{10,... | collective-permute-start | bytes 1277960 | tf_op jit(solution)/shard_map/ppermute | solution.py:480
  49.0 7.2 %collective-permute-done.9.far = f32[26,4,8,128]{3,2,1,0:T(8,128)S(1)} collective-permute-done((f32[26,4,8,128]{3,2,1,0:T(8,128)S(1)}, f32[26,4,8,128]{3,2,1,0:T(8,128)S(1)}, u32[]{:S(2)}, u32[]{:S(2)}) %collective-permute-start.9) | collective-permute-done | bytes 426016 | tf_op jit(solution)/shard_map/ppermute | solution.py:480
  56.2 2.2 %collective-permute-done.10.near = f32[26,4,8,128]{3,2,1,0:T(8,128)S(1)} collective-permute-done((f32[26,4,8,128]{3,2,1,0:T(8,128)S(1)}, f32[26,4,8,128]{3,2,1,0:T(8,128)S(1)}, u32[]{:S(2)}, u32[]{:S(2)}) %collective-permute-start.10) | collective-permute-done | bytes 426016 | tf_op jit(solution)/shard_map/ppermute | solution.py:480
  58.4 0.9 middle.1
  59.4 0.1 collective-permute-start.11
  59.5 3.6 %collective-permute-start.12 = (f32[24,4,8,128]{3,2,1,0:T(8,128)S(1)}, f32[24,4,8,128]{3,2,1,0:T(8,128)S(1)}, u32[]{:S(2)}, u32[]{:S(2)}) collective-permute-start(f32[24,4,8,128]{3,2,1,0:T(8,128)S(1)} %get-tuple-element.67), channel_id=1, source_target_pairs={{0,32},{1,2},{2,1},{3,4},{4,3},{5,6},{6,5},{7,8},{8,7},{9,10},{10,... | collective-permute-start | bytes 1179656 | tf_op jit(solution)/shard_map/ppermute | solution.py:480
  63.1 5.9 %collective-permute-done.11.far.far_x = f32[24,4,8,128]{3,2,1,0:T(8,128)S(1)} collective-permute-done((f32[24,4,8,128]{3,2,1,0:T(8,128)S(1)}, f32[24,4,8,128]{3,2,1,0:T(8,128)S(1)}, u32[]{:S(2)}, u32[]{:S(2)}) %collective-permute-start.11) | collective-permute-done | bytes 393248 | tf_op jit(solution)/shard_map/ppermute | solution.py:480
  69.0 2.2 %collective-permute-done.12.near.near_x = f32[24,4,8,128]{3,2,1,0:T(8,128)S(1)} collective-permute-done((f32[24,4,8,128]{3,2,1,0:T(8,128)S(1)}, f32[24,4,8,128]{3,2,1,0:T(8,128)S(1)}, u32[]{:S(2)}, u32[]{:S(2)}) %collective-permute-start.12) | collective-permute-done | bytes 393248 | tf_op jit(solution)/shard_map/ppermute | solution.py:480
  71.2 0.6 edges.1
  71.8 0.1 collective-permute-start.13
  71.9 0.9 collective-permute-start.14
  72.8 6.4 %collective-permute-done.13.got1 = f32[18,4,8,128]{3,2,1,0:T(8,128)S(1)} collective-permute-done((f32[18,4,8,128]{3,2,1,0:T(8,128)S(1)}, f32[18,4,8,128]{3,2,1,0:T(8,128)S(1)}, u32[]{:S(2)}, u32[]{:S(2)}) %collective-permute-start.13) | collective-permute-done | bytes 294944 | tf_op jit(solution)/shard_map/ppermute | solution.py:469
  79.3 0.7 widen.1
  79.9 1.5 %front.3 = (f32[68,4,8,128]{3,2,1,0:T(8,128)S(1)}, f32[2,16,4,8,128]{4,3,2,1,0:T(8,128)S(1)}, f32[26,4,8,128]{3,2,1,0:T(8,128)S(1)}, f32[26,4,8,128]{3,2,1,0:T(8,128)S(1)}) custom-call(f32[136,8,128]{2,1,0:T(8,128)S(1)} %bitcast.11, f32[136,8,128]{2,1,0:T(8,128)S(1)} %bitcast.10, f32[2,20,4,8,128]{4,3,2,1,0:T(8,128)S(1)} %get-tuple-element.73.own, ...), custom_call_target="tpu_custom_call" | custom-call | tf_op jit(solution)/shard_map/front/pallas_call | solution.py:521
  81.4 0.1 collective-permute-start.15
  81.5 3.3 %collective-permute-start.16 = (f32[26,4,8,128]{3,2,1,0:T(8,128)S(1)}, f32[26,4,8,128]{3,2,1,0:T(8,128)S(1)}, u32[]{:S(2)}, u32[]{:S(2)}) collective-permute-start(f32[26,4,8,128]{3,2,1,0:T(8,128)S(1)} %get-tuple-element.75), channel_id=1, source_target_pairs={{0,32},{1,2},{2,1},{3,4},{4,3},{5,6},{6,5},{7,8},{8,7},{9,10},{10,... | collective-permute-start | bytes 1277960 | tf_op jit(solution)/shard_map/ppermute | solution.py:480
  84.8 6.7 %collective-permute-done.15.far = f32[26,4,8,128]{3,2,1,0:T(8,128)S(1)} collective-permute-done((f32[26,4,8,128]{3,2,1,0:T(8,128)S(1)}, f32[26,4,8,128]{3,2,1,0:T(8,128)S(1)}, u32[]{:S(2)}, u32[]{:S(2)}) %collective-permute-start.15) | collective-permute-done | bytes 426016 | tf_op jit(solution)/shard_map/ppermute | solution.py:480
  91.5 2.2 %collective-permute-done.16.near = f32[26,4,8,128]{3,2,1,0:T(8,128)S(1)} collective-permute-done((f32[26,4,8,128]{3,2,1,0:T(8,128)S(1)}, f32[26,4,8,128]{3,2,1,0:T(8,128)S(1)}, u32[]{:S(2)}, u32[]{:S(2)}) %collective-permute-start.16) | collective-permute-done | bytes 426016 | tf_op jit(solution)/shard_map/ppermute | solution.py:480
  93.7 2.1 %last.1 = (f32[4,96,128]{2,1,0:T(8,128)S(1)}, f32[4,96,128]{2,1,0:T(8,128)S(1)}) custom-call(s32[3]{0:T(128)S(1)} %pad_add_fusion.pos, f32[26,4,8,128]{3,2,1,0:T(8,128)S(1)} %collective-permute-done.15.far, f32[26,4,8,128]{3,2,1,0:T(8,128)S(1)} %collective-permute-done.16.near, f32[2,16,4,8,128]{4,3,2,1,0:T(8,128)S(1)} %get-tuple-element.76.it, ...), custom_call_target="tpu_custom_call" | custom-call | tf_op jit(solution)/shard_map/last/pallas_call | solution.py:550
  95.8 0.1 collective-permute-start.17
  95.9 1.4 %collective-permute-done.17.other = f32[4,96,128]{2,1,0:T(8,128)S(1)} collective-permute-done((f32[4,96,128]{2,1,0:T(8,128)S(1)}, f32[4,96,128]{2,1,0:T(8,128)S(1)}, u32[]{:S(2)}, u32[]{:S(2)}) %collective-permute-start.17) | collective-permute-done | bytes 196640 | tf_op jit(solution)/shard_map/ppermute | solution.py:469
  97.3 1.9 %collective-permute-start.18 = (f32[2,96,128]{2,1,0:T(8,128)S(1)}, f32[2,96,128]{2,1,0:T(8,128)S(1)}, u32[]{:S(2)}, u32[]{:S(2)}) collective-permute-start(f32[2,96,128]{2,1,0:T(8,128)S(1)} %get-tuple-element.81), channel_id=1, source_target_pairs={{0,128},{32,160},{64,192},{96,224},{128,0},{160,32},{192,64},{224,... | collective-permute-start | bytes 294920 | tf_op jit(solution)/shard_map/ppermute | solution.py:561
  99.2 1.2 %collective-permute-start.19 = (f32[2,96,128]{2,1,0:T(8,128)S(1)}, f32[2,96,128]{2,1,0:T(8,128)S(1)}, u32[]{:S(2)}, u32[]{:S(2)}) collective-permute-start(f32[2,96,128]{2,1,0:T(8,128)S(1)} %get-tuple-element.82), channel_id=1, source_target_pairs={{0,64},{32,96},{64,0},{96,32},{128,192},{160,224},{192,128},{224,1... | collective-permute-start | bytes 294920 | tf_op jit(solution)/shard_map/ppermute | solution.py:561
  100.4 1.1 %collective-permute-start.20 = (f32[2,96,128]{2,1,0:T(8,128)S(1)}, f32[2,96,128]{2,1,0:T(8,128)S(1)}, u32[]{:S(2)}, u32[]{:S(2)}) collective-permute-start(f32[2,96,128]{2,1,0:T(8,128)S(1)} %get-tuple-element.83), channel_id=1, source_target_pairs={{0,192},{32,224},{64,128},{96,160},{128,64},{160,96},{192,0},{224,... | collective-permute-start | bytes 294920 | tf_op jit(solution)/shard_map/ppermute | solution.py:561
  101.5 3.0 %collective-permute-done.18.a = f32[2,96,128]{2,1,0:T(8,128)S(1)} collective-permute-done((f32[2,96,128]{2,1,0:T(8,128)S(1)}, f32[2,96,128]{2,1,0:T(8,128)S(1)}, u32[]{:S(2)}, u32[]{:S(2)}) %collective-permute-start.18) | collective-permute-done | bytes 98336 | tf_op jit(solution)/shard_map/ppermute | solution.py:561
  104.5 0.8 collective-permute-done.19.b
  105.3 0.9 collective-permute-done.20.c
  106.3 1.4 %unpack.1 = (f32[2,2,96,128]{3,2,1,0:T(8,128)}, f32[2,2,96,128]{3,2,1,0:T(8,128)}) custom-call(s32[3]{0:T(128)S(1)} %pad_add_fusion.pos, f32[2,96,128]{2,1,0:T(8,128)S(1)} %collective-permute-done.18.a, f32[2,96,128]{2,1,0:T(8,128)S(1)} %collective-permute-done.19.b, f32[2,96,128]{2,1,0:T(8,128)S(1)} %collective-permute-done.20.c, ...), custom_call_target="tpu_custom_call" | custom-call | tf_op jit(solution)/shard_map/unpack/pallas_call | solution.py:564
  (6 shorter events, 0.1 us)
Async XLA Ops:
  2.6 7.8 %collective-permute-start = (f32[240,128]{1,0:T(8,128)S(1)}, f32[240,128]{1,0:T(8,128)S(1)}, u32[]{:S(2)}, u32[]{:S(2)}) collective-permute-start(f32[240,128]{1,0:T(8,128)S(1)} %get-tuple-element.43), channel_id=1, source_target_pairs={{0,128},{32,160},{64,192},{96,224},{128,0},{160,32},{192,64},{224,... | collective-permute-start | bytes 368648 | tf_op jit(solution)/shard_map/ppermute | solution.py:460
  5.9 6.9 %collective-permute-start.1 = (f32[240,128]{1,0:T(8,128)S(1)}, f32[240,128]{1,0:T(8,128)S(1)}, u32[]{:S(2)}, u32[]{:S(2)}) collective-permute-start(f32[240,128]{1,0:T(8,128)S(1)} %get-tuple-element.44), channel_id=1, source_target_pairs={{0,64},{32,96},{64,0},{96,32},{128,192},{160,224},{192,128},{224,1... | collective-permute-start | bytes 368648 | tf_op jit(solution)/shard_map/ppermute | solution.py:460
  6.6 9.2 %collective-permute-start.2 = (f32[240,128]{1,0:T(8,128)S(1)}, f32[240,128]{1,0:T(8,128)S(1)}, u32[]{:S(2)}, u32[]{:S(2)}) collective-permute-start(f32[240,128]{1,0:T(8,128)S(1)} %get-tuple-element.45), channel_id=1, source_target_pairs={{0,192},{32,224},{64,128},{96,160},{128,64},{160,96},{192,0},{224,... | collective-permute-start | bytes 368648 | tf_op jit(solution)/shard_map/ppermute | solution.py:460
  7.0 8.8 %collective-permute-start.3 = (f32[240,128]{1,0:T(8,128)S(1)}, f32[240,128]{1,0:T(8,128)S(1)}, u32[]{:S(2)}, u32[]{:S(2)}) collective-permute-start(f32[240,128]{1,0:T(8,128)S(1)} %get-tuple-element.46), channel_id=1, source_target_pairs={{0,160},{32,128},{64,224},{96,192},{128,32},{160,0},{192,96},{224,... | collective-permute-start | bytes 368648 | tf_op jit(solution)/shard_map/ppermute | solution.py:460
  8.6 8.4 %collective-permute-start.4 = (f32[240,128]{1,0:T(8,128)S(1)}, f32[240,128]{1,0:T(8,128)S(1)}, u32[]{:S(2)}, u32[]{:S(2)}) collective-permute-start(f32[240,128]{1,0:T(8,128)S(1)} %get-tuple-element.47), channel_id=1, source_target_pairs={{0,96},{32,64},{64,32},{96,0},{128,224},{160,192},{192,160},{224,1... | collective-permute-start | bytes 368648 | tf_op jit(solution)/shard_map/ppermute | solution.py:460
  10.4 7.1 %collective-permute-start.5 = (f32[240,128]{1,0:T(8,128)S(1)}, f32[240,128]{1,0:T(8,128)S(1)}, u32[]{:S(2)}, u32[]{:S(2)}) collective-permute-start(f32[240,128]{1,0:T(8,128)S(1)} %get-tuple-element.48), channel_id=1, source_target_pairs={{0,224},{32,192},{64,160},{96,128},{128,96},{160,64},{192,32},{224... | collective-permute-start | bytes 368648 | tf_op jit(solution)/shard_map/ppermute | solution.py:460
  12.8 4.7 %collective-permute-start.6 = (f32[240,128]{1,0:T(8,128)S(1)}, f32[240,128]{1,0:T(8,128)S(1)}, u32[]{:S(2)}, u32[]{:S(2)}) collective-permute-start(f32[240,128]{1,0:T(8,128)S(1)} %get-tuple-element.49), channel_id=1, source_target_pairs={{0,32},{32,0},{64,96},{96,64},{128,160},{160,128},{192,224},{224,1... | collective-permute-start | bytes 368648 | tf_op jit(solution)/shard_map/ppermute | solution.py:460
  19.1 18.7 %collective-permute-start.7 = (f32[177,8,128]{2,1,0:T(8,128)S(1)}, f32[177,8,128]{2,1,0:T(8,128)S(1)}, u32[]{:S(2)}, u32[]{:S(2)}) collective-permute-start(f32[177,8,128]{2,1,0:T(8,128)S(1)} %get-tuple-element.54), channel_id=1, source_target_pairs={{0,1},{1,0},{2,3},{3,2},{4,5},{5,4},{6,7},{7,6},{8,9},{9,8},{10,11... | collective-permute-start | bytes 2174984 | tf_op jit(solution)/shard_map/ppermute | solution.py:480
  21.1 21.6 %collective-permute-start.8 = (f32[177,8,128]{2,1,0:T(8,128)S(1)}, f32[177,8,128]{2,1,0:T(8,128)S(1)}, u32[]{:S(2)}, u32[]{:S(2)}) collective-permute-start(f32[177,8,128]{2,1,0:T(8,128)S(1)} %get-tuple-element.55), channel_id=1, source_target_pairs={{0,32},{1,2},{2,1},{3,4},{4,3},{5,6},{6,5},{7,8},{8,7},{9,10},{10,... | collective-permute-start | bytes 2174984 | tf_op jit(solution)/shard_map/ppermute | solution.py:480
  44.9 11.3 %collective-permute-start.9 = (f32[26,4,8,128]{3,2,1,0:T(8,128)S(1)}, f32[26,4,8,128]{3,2,1,0:T(8,128)S(1)}, u32[]{:S(2)}, u32[]{:S(2)}) collective-permute-start(f32[26,4,8,128]{3,2,1,0:T(8,128)S(1)} %get-tuple-element.62), channel_id=1, source_target_pairs={{0,1},{1,0},{2,3},{3,2},{4,5},{5,4},{6,7},{7,6},{8,9},{9,8},{10,11... | collective-permute-start | bytes 1277960 | tf_op jit(solution)/shard_map/ppermute | solution.py:480
  45.0 13.4 %collective-permute-start.10 = (f32[26,4,8,128]{3,2,1,0:T(8,128)S(1)}, f32[26,4,8,128]{3,2,1,0:T(8,128)S(1)}, u32[]{:S(2)}, u32[]{:S(2)}) collective-permute-start(f32[26,4,8,128]{3,2,1,0:T(8,128)S(1)} %get-tuple-element.63), channel_id=1, source_target_pairs={{0,32},{1,2},{2,1},{3,4},{4,3},{5,6},{6,5},{7,8},{8,7},{9,10},{10,... | collective-permute-start | bytes 1277960 | tf_op jit(solution)/shard_map/ppermute | solution.py:480
  59.4 9.6 %collective-permute-start.11 = (f32[24,4,8,128]{3,2,1,0:T(8,128)S(1)}, f32[24,4,8,128]{3,2,1,0:T(8,128)S(1)}, u32[]{:S(2)}, u32[]{:S(2)}) collective-permute-start(f32[24,4,8,128]{3,2,1,0:T(8,128)S(1)} %get-tuple-element.66), channel_id=1, source_target_pairs={{0,1},{1,0},{2,3},{3,2},{4,5},{5,4},{6,7},{7,6},{8,9},{9,8},{10,11... | collective-permute-start | bytes 1179656 | tf_op jit(solution)/shard_map/ppermute | solution.py:480
  59.5 11.8 %collective-permute-start.12 = (f32[24,4,8,128]{3,2,1,0:T(8,128)S(1)}, f32[24,4,8,128]{3,2,1,0:T(8,128)S(1)}, u32[]{:S(2)}, u32[]{:S(2)}) collective-permute-start(f32[24,4,8,128]{3,2,1,0:T(8,128)S(1)} %get-tuple-element.67), channel_id=1, source_target_pairs={{0,32},{1,2},{2,1},{3,4},{4,3},{5,6},{6,5},{7,8},{8,7},{9,10},{10,... | collective-permute-start | bytes 1179656 | tf_op jit(solution)/shard_map/ppermute | solution.py:480
  71.8 7.4 %collective-permute-start.13 = (f32[18,4,8,128]{3,2,1,0:T(8,128)S(1)}, f32[18,4,8,128]{3,2,1,0:T(8,128)S(1)}, u32[]{:S(2)}, u32[]{:S(2)}) collective-permute-start(f32[18,4,8,128]{3,2,1,0:T(8,128)S(1)} %get-tuple-element.69), channel_id=1, source_target_pairs={{32,64},{64,32},{96,128},{128,96},{160,192},{192,160},{224,0},{0,2... | collective-permute-start | bytes 884744 | tf_op jit(solution)/shard_map/ppermute | solution.py:469
  71.9 7.3 %collective-permute-start.14 = (f32[18,4,8,128]{3,2,1,0:T(8,128)S(1)}, f32[18,4,8,128]{3,2,1,0:T(8,128)S(1)}, u32[]{:S(2)}, u32[]{:S(2)}) collective-permute-start(f32[18,4,8,128]{3,2,1,0:T(8,128)S(1)} %get-tuple-element.70), channel_id=1, source_target_pairs={{0,32},{32,0},{64,96},{96,64},{128,160},{160,128},{192,224},{224,1... | collective-permute-start | bytes 884744 | tf_op jit(solution)/shard_map/ppermute | solution.py:469
  81.4 10.1 %collective-permute-start.15 = (f32[26,4,8,128]{3,2,1,0:T(8,128)S(1)}, f32[26,4,8,128]{3,2,1,0:T(8,128)S(1)}, u32[]{:S(2)}, u32[]{:S(2)}) collective-permute-start(f32[26,4,8,128]{3,2,1,0:T(8,128)S(1)} %get-tuple-element.74), channel_id=1, source_target_pairs={{0,1},{1,0},{2,3},{3,2},{4,5},{5,4},{6,7},{7,6},{8,9},{9,8},{10,11... | collective-permute-start | bytes 1277960 | tf_op jit(solution)/shard_map/ppermute | solution.py:480
  81.5 12.2 %collective-permute-start.16 = (f32[26,4,8,128]{3,2,1,0:T(8,128)S(1)}, f32[26,4,8,128]{3,2,1,0:T(8,128)S(1)}, u32[]{:S(2)}, u32[]{:S(2)}) collective-permute-start(f32[26,4,8,128]{3,2,1,0:T(8,128)S(1)} %get-tuple-element.75), channel_id=1, source_target_pairs={{0,32},{1,2},{2,1},{3,4},{4,3},{5,6},{6,5},{7,8},{8,7},{9,10},{10,... | collective-permute-start | bytes 1277960 | tf_op jit(solution)/shard_map/ppermute | solution.py:480
  95.8 1.5 %collective-permute-start.17 = (f32[4,96,128]{2,1,0:T(8,128)S(1)}, f32[4,96,128]{2,1,0:T(8,128)S(1)}, u32[]{:S(2)}, u32[]{:S(2)}) collective-permute-start(f32[4,96,128]{2,1,0:T(8,128)S(1)} %get-tuple-element.79), channel_id=1, source_target_pairs={{0,32},{32,0},{64,96},{96,64},{128,160},{160,128},{192,224},{224,1... | collective-permute-start | bytes 589832 | tf_op jit(solution)/shard_map/ppermute | solution.py:469
  97.3 7.2 %collective-permute-start.18 = (f32[2,96,128]{2,1,0:T(8,128)S(1)}, f32[2,96,128]{2,1,0:T(8,128)S(1)}, u32[]{:S(2)}, u32[]{:S(2)}) collective-permute-start(f32[2,96,128]{2,1,0:T(8,128)S(1)} %get-tuple-element.81), channel_id=1, source_target_pairs={{0,128},{32,160},{64,192},{96,224},{128,0},{160,32},{192,64},{224,... | collective-permute-start | bytes 294920 | tf_op jit(solution)/shard_map/ppermute | solution.py:561
  99.2 6.1 %collective-permute-start.19 = (f32[2,96,128]{2,1,0:T(8,128)S(1)}, f32[2,96,128]{2,1,0:T(8,128)S(1)}, u32[]{:S(2)}, u32[]{:S(2)}) collective-permute-start(f32[2,96,128]{2,1,0:T(8,128)S(1)} %get-tuple-element.82), channel_id=1, source_target_pairs={{0,64},{32,96},{64,0},{96,32},{128,192},{160,224},{192,128},{224,1... | collective-permute-start | bytes 294920 | tf_op jit(solution)/shard_map/ppermute | solution.py:561
  100.4 5.9 %collective-permute-start.20 = (f32[2,96,128]{2,1,0:T(8,128)S(1)}, f32[2,96,128]{2,1,0:T(8,128)S(1)}, u32[]{:S(2)}, u32[]{:S(2)}) collective-permute-start(f32[2,96,128]{2,1,0:T(8,128)S(1)} %get-tuple-element.83), channel_id=1, source_target_pairs={{0,192},{32,224},{64,128},{96,160},{128,64},{160,96},{192,0},{224,... | collective-permute-start | bytes 294920 | tf_op jit(solution)/shard_map/ppermute | solution.py:561

commit v8 on v7

--- a/solution.py
+++ b/solution.py
@@ -19,6 +19,10 @@
 ORDER = (4, 2, 6, 5, 3, 7, 1)
 CHIPS = (2, 1, 3)
 TALL = 24
+
+
+def place():
+    return lax.axis_index("tm"), lax.axis_index("space")
 
 
 def transform_matrices():
@@ -56,15 +60,14 @@
     return jax.ShapeDtypeStruct(shape, jnp.float32)
 
 
-def call(body, name, outs, n_in, scratch=(), scalars=1, far_inputs=0, far_outputs=False):
+def call(body, name, outs, n_in, scratch=(), far_inputs=0, far_outputs=False):
     vmem = pl.BlockSpec(memory_space=pltpu.VMEM)
     anywhere = pl.BlockSpec(memory_space=pltpu.HBM)
-    smem = pl.BlockSpec(memory_space=pltpu.SMEM)
     return pl.pallas_call(
         body,
         name=name,
         out_shape=outs,
-        in_specs=[smem] * scalars + [anywhere] * far_inputs + [vmem] * n_in,
+        in_specs=[anywhere] * far_inputs + [vmem] * n_in,
         out_specs=[anywhere if far_outputs else vmem] * len(outs),
         scratch_shapes=list(scratch),
         compiler_params=pltpu.CompilerParams(vmem_limit_bytes=16 * 1024 * 1024),
@@ -75,7 +78,7 @@
     lax.fori_loop(lo, hi, body, 0, unroll=True)
 
 
-def pack_body(pos, *rest):
+def pack_body(*rest):
     sources, outs, (near, far, here), tables = rest[:8], rest[8:16], rest[16:19], rest[19:22]
     stage, held, sems = rest[22], rest[23:28], rest[28]
     slabs = [
@@ -85,8 +88,8 @@
     for copy in slabs + copies:
         copy.start()
     state, adjoint, target, kappa, begin = held
-    t = pos[0]
-    flip = pos[1]
+    t, s = place()
+    flip = s & 1
     for f, ref in enumerate((state, adjoint, target)):
         for n in range(2):
             slabs[2 * f + n].wait()
@@ -125,8 +128,9 @@
                 far[i] = parts[q]
 
 
-def coefficient_body(pos, far, near, here, consts, weights, inv):
-    t, flip, s = pos[0], pos[1], pos[2]
+def coefficient_body(far, near, here, consts, weights, inv):
+    t, s = place()
+    flip = s & 1
     near, far = ([side[168 + 3 * i : 171 + 3 * i].reshape(TALL, 128) for i in range(3)] for side in (near, far))
     kappa = [near[1], near[0], here[0], here[1], far[0], far[1]]
     for p in range(6):
@@ -175,12 +179,12 @@
             inv[at, 1] = 1.0 / (b * b + base)
 
 
-def spread_body(pos, *rest):
+def spread_body(*rest):
     pieces, (near_c, far_c, forward), (own, wish, near, far), stage = rest[:8], rest[8:11], rest[11:15], rest[15]
     for i in range(3):
         near[168 + 3 * i : 171 + 3 * i] = near_c[i].reshape(3, 8, 128)
         far[168 + 3 * i : 171 + 3 * i] = far_c[i].reshape(3, 8, 128)
-    t = pos[0]
+    t, _ = place()
     rows = 12 * WIN
     for k, piece in zip(ORDER + (0,), pieces):
         stage[pl.ds(pl.multiple_of((t ^ k) * rows, 8), rows), :] = piece[...]
@@ -378,8 +382,8 @@
 EDGE = ((0, 4), (4, 4), (8, 3), (11, 3), (14, 2), (16, 2))
 
 
-def edges_body(pos, far, near, new, send0, send1):
-    odd = pos[0] & 1
+def edges_body(far, near, new, send0, send1):
+    odd = place()[0] & 1
     planes = (
         lambda j, n: new[0, pl.ds(j, n)],
         lambda j, n: new[1, pl.ds(j, n)],
@@ -393,8 +397,8 @@
         send1[at : at + n] = take((OWN - n) * odd, n)
 
 
-def widen_body(pos, got1, got0, new, near_x, far_x, own, near, far):
-    odd = pos[0] & 1
+def widen_body(got1, got0, new, near_x, far_x, own, near, far):
+    odd = place()[0] & 1
     for x in range(2):
         own[x, HALO : HALO + OWN] = new[x]
     for out, got in ((near, near_x), (far, far_x)):
@@ -409,12 +413,12 @@
         far[pl.ds(18 + 14 * high, 2)] = got[16:18]
 
 
-def last_body(pos, far, near, it, fixed, weights, consts, inv, back, *rest):
+def last_body(far, near, it, fixed, weights, consts, inv, back, *rest):
     outs, (zed, fin, stage) = rest[:2], rest[2:]
     def put(x, j, c, v):
         fin[x * OWN + j, c] = v
     sweep_body(it, near, far, fixed, weights, consts, inv, zed, put)
-    t = pos[0]
+    t, _ = place()
     matrix = back[...]
     for low in range(0, 2 * OWN, 4):
         done = transform(matrix, fin[low : low + 4].reshape(128, 128))
@@ -432,9 +436,9 @@
         out[1] = other[k]
 
 
-def unpack_body(pos, a, b, c, other, mine, state, adjoint, stage, held, sems):
-    t = pos[0]
-    flip = pos[1]
+def unpack_body(a, b, c, other, mine, state, adjoint, stage, held, sems):
+    t, s = place()
+    flip = s & 1
     for ref, k in zip((a, b, c), CHIPS):
         stage[t ^ (2 * k)] = ref[0]
         stage[t ^ (2 * k + 1)] = ref[1]
@@ -481,10 +485,6 @@
 
 
 def on_device(state_guess, adjoint_guess, target, initial_state, diffusivity):
-    t = lax.axis_index("tm").astype(jnp.int32)
-    s = lax.axis_index("space").astype(jnp.int32)
-    flip = s & 1
-    pos = jnp.stack([t, flip, s])
     forward, back = (jnp.asarray(m) for m in transform_matrices())
     consts = jnp.asarray(mode_constants())
 
@@ -500,7 +500,7 @@
         + [pltpu.VMEM((2, 96, 128), jnp.float32)] * 2
         + [pltpu.SemaphoreType.DMA((11,))],
         far_inputs=8,
-    )(pos, *(pltpu.with_memory_space_constraint(a, pltpu.HBM) for a in arguments))
+    )(*(pltpu.with_memory_space_constraint(a, pltpu.HBM) for a in arguments))
     got = exchange(pieces)
     own, wish, near, far = call(
         spread_body,
@@ -508,12 +508,12 @@
         [whole(2, WIN, 4, 8, 128), whole(2, 18, 2, 8, 128), whole(177, 8, 128), whole(177, 8, 128)],
         11,
         [pltpu.VMEM((8 * 12 * WIN, 128), jnp.float32)],
-    )(pos, *got, near_c, far_c, forward)
+    )(*got, near_c, far_c, forward)
     far = far_first = swap_planes(far, 0)
     near = near_first = swap_planes(near, 1)
     weights, inv = call(
         coefficient_body, "coefficients", [whole(4 * TALL * 8, 128), whole(68, 2, 8, 128)], 4
-    )(pos, far, near, here_c, consts)
+    )(far, near, here_c, consts)
     weights = weights.reshape(4 * TALL, 8, 128)
 
     sweep_scratch = [pltpu.VMEM((52, 4, 8, 128), jnp.float32)]
@@ -524,7 +524,6 @@
             [whole(68, 4, 8, 128), whole(2, 16, 4, 8, 128), whole(26, 4, 8, 128), whole(26, 4, 8, 128)],
             9,
             [pltpu.VMEM((68, 4, 8, 128), jnp.float32)],
-            scalars=0,
         )(far, near, own, wish, near_first, far_first, weights, consts, inv)
         far_z = swap_planes(far_z, 0)
         near_z = swap_planes(near_z, 1)
@@ -535,16 +534,15 @@
                 [whole(2, OWN, 4, 8, 128), whole(2 * OWN, 4, 8, 128), whole(2 * OWN, 4, 8, 128)],
                 7,
                 sweep_scratch,
-                scalars=0,
             )(far_z, near_z, it, fixed, weights, consts, inv)
             far = swap_planes(far, 0)
             near = swap_planes(near, 1)
-            send0, send1 = call(edges_body, "edges", [whole(18, 4, 8, 128)] * 2, 3)(pos, far, near, new)
+            send0, send1 = call(edges_body, "edges", [whole(18, 4, 8, 128)] * 2, 3)(far, near, new)
             got1 = swap_rows(send1, 1)
             got0 = swap_rows(send0, 0)
             own, near, far = call(
                 widen_body, "widen", [whole(2, WIN, 4, 8, 128), whole(34, 4, 8, 128), whole(34, 4, 8, 128)], 5
-            )(pos, got1, got0, new, near, far)
+            )(got1, got0, new, near, far)
             near = near.reshape(136, 8, 128)
             far = far.reshape(136, 8, 128)
     mine, other = call(
@@ -553,9 +551,9 @@
         [whole(4, 8 * OWN, 128)] * 2,
         8,
         sweep_scratch + [pltpu.VMEM((2 * OWN, 4, 8, 128), jnp.float32), pltpu.VMEM((64 * OWN, 128), jnp.float32)],
-    )(pos, far_z, near_z, it, fixed, weights, consts, inv, back)
+    )(far_z, near_z, it, fixed, weights, consts, inv, back)
     other = swap_rows(other, 0)
-    pairs = call(merge_body, "merge", [whole(2, 8 * OWN, 128)] * 3, 2, scalars=0)(other, mine)
+    pairs = call(merge_body, "merge", [whole(2, 8 * OWN, 128)] * 3, 2)(other, mine)
     count = lax.axis_size("tm")
     got = [
         lax.ppermute(pair, "tm", [(i, i ^ (2 * k)) for i in range(count)]) for pair, k in zip(pairs, CHIPS)
@@ -572,7 +570,7 @@
                 pltpu.SemaphoreType.DMA((8,)),
             ],
             far_outputs=True,
-        )(pos, *got, other, mine)
+        )(*got, other, mine)
     )
 
 

time: 108 us -> 104 us (0.963)
  Pallas kernels: 12.9 us -> 8.94 us
where the time goes in v8:
time: 104 us
  waiting for transfers between devices  61.4 us (59%)
  starting transfers between devices  32.6 us (31%)
  Pallas kernels  8.94 us (9%)
    ppermute x8, waiting for transfers between devices, swap_planes(): return lax.ppermute(block, ('tm', 'space'), route)  42.8 us
    ppermute x8, starting transfers between devices, swap_planes(): return lax.ppermute(block, ('tm', 'space'), route)  18.3 us
    ppermute x7, starting transfers between devices, exchange(): lax.ppermute(pieces[k], 'tm', [(i, i ^ k) for i in range(count)])  8.99 us
    ppermute x3, waiting for transfers between devices, swap_rows(): return lax.ppermute(block, 'tm', route)  7.88 us
    ppermute x7, waiting for transfers between devices, exchange(): lax.ppermute(pieces[k], 'tm', [(i, i ^ k) for i in range(count)])  5.87 us
    ppermute x3, waiting for transfers between devices, on_device(): lax.ppermute(pair, 'tm', [(i, i ^ 2 * k) for i in range(count)])  4.77 us
    ppermute x3, starting transfers between devices, on_device(): lax.ppermute(pair, 'tm', [(i, i ^ 2 * k) for i in range(count)])  4.18 us
    pallas_call x2, Pallas kernels, on_device(): call(front_body, 'front', [whole(68, 4, 8, 128), whole(2, 16, 4, 8, 128),...  2.86 us
  transfers between devices with their start and end apart: 21, of which 17 were waited for; matrix products, arithmetic and copies ran while one was open for 0% of the time, Pallas kernels for 0%

profile of v8, /device:TPU:6, one launch (start us, length us, event | category | flops | bytes accessed | tf_op | source)
XLA Modules:
  0.0 103.8 jit_solution(15805314731144799838)
XLA Ops:
  0.6 1.4 %pack.1 = (f32[240,128]{1,0:T(8,128)S(1)}, f32[240,128]{1,0:T(8,128)S(1)}, f32[240,128]{1,0:T(8,128)S(1)}, f32[240,128]{1,0:T(8,128)S(1)}, f32[240,128]{1,0:T(8,...) custom-call(f32[2,2,96,128]{3,2,1,0:T(8,128)} %rest_0_.1, ...), custom_call_target="tpu_custom_call" | custom-call | tf_op jit(solution)/shard_map/pack/pallas_call | solution.py:492
  2.0 3.3 %collective-permute-start = (f32[240,128]{1,0:T(8,128)S(1)}, f32[240,128]{1,0:T(8,128)S(1)}, u32[]{:S(2)}, u32[]{:S(2)}) collective-permute-start(f32[240,128]{1,0:T(8,128)S(1)} %get-tuple-element.43), channel_id=1, source_target_pairs={{0,128},{32,160},{64,192},{96,224},{128,0},{160,32},{192,64},{224,... | collective-permute-start | bytes 368648 | tf_op jit(solution)/shard_map/ppermute | solution.py:464
  5.3 0.7 collective-permute-start.1
  6.0 0.4 collective-permute-start.2
  6.3 1.6 %collective-permute-start.3 = (f32[240,128]{1,0:T(8,128)S(1)}, f32[240,128]{1,0:T(8,128)S(1)}, u32[]{:S(2)}, u32[]{:S(2)}) collective-permute-start(f32[240,128]{1,0:T(8,128)S(1)} %get-tuple-element.46), channel_id=1, source_target_pairs={{0,160},{32,128},{64,224},{96,192},{128,32},{160,0},{192,96},{224,... | collective-permute-start | bytes 368648 | tf_op jit(solution)/shard_map/ppermute | solution.py:464
  8.0 1.8 %collective-permute-start.4 = (f32[240,128]{1,0:T(8,128)S(1)}, f32[240,128]{1,0:T(8,128)S(1)}, u32[]{:S(2)}, u32[]{:S(2)}) collective-permute-start(f32[240,128]{1,0:T(8,128)S(1)} %get-tuple-element.47), channel_id=1, source_target_pairs={{0,96},{32,64},{64,32},{96,0},{128,224},{160,192},{192,160},{224,1... | collective-permute-start | bytes 368648 | tf_op jit(solution)/shard_map/ppermute | solution.py:464
  9.8 0.0 collective-permute-done.rest_0_
  9.8 0.5 collective-permute-start.5
  10.2 1.9 %collective-permute-done.1.rest_1_ = f32[240,128]{1,0:T(8,128)S(1)} collective-permute-done((f32[240,128]{1,0:T(8,128)S(1)}, f32[240,128]{1,0:T(8,128)S(1)}, u32[]{:S(2)}, u32[]{:S(2)}) %collective-permute-start.1) | collective-permute-done | bytes 122912 | tf_op jit(solution)/shard_map/ppermute | solution.py:464
  12.2 0.8 collective-permute-start.6
  12.9 2.2 %collective-permute-done.2.rest_2_ = f32[240,128]{1,0:T(8,128)S(1)} collective-permute-done((f32[240,128]{1,0:T(8,128)S(1)}, f32[240,128]{1,0:T(8,128)S(1)}, u32[]{:S(2)}, u32[]{:S(2)}) %collective-permute-start.2) | collective-permute-done | bytes 122912 | tf_op jit(solution)/shard_map/ppermute | solution.py:464
  15.1 1.2 %collective-permute-done.4.rest_4_ = f32[240,128]{1,0:T(8,128)S(1)} collective-permute-done((f32[240,128]{1,0:T(8,128)S(1)}, f32[240,128]{1,0:T(8,128)S(1)}, u32[]{:S(2)}, u32[]{:S(2)}) %collective-permute-start.4) | collective-permute-done | bytes 122912 | tf_op jit(solution)/shard_map/ppermute | solution.py:464
  16.3 0.5 collective-permute-done.5.rest_5_
  16.9 1.1 %spread.1 = (f32[2,20,4,8,128]{4,3,2,1,0:T(8,128)S(1)}, f32[2,18,2,8,128]{4,3,2,1,0:T(8,128)S(1)}, f32[177,8,128]{2,1,0:T(8,128)S(1)}, f32[177,8,128]{2,1,0:T(8,128)S(1)}) custom-call(f32[240,128]{1,0:T(8,128)S(1)} %collective-permute-done.rest_0_, f32[240,128]{1,0:T(8,128)S(1)} %collective-permute-done.1.rest_1_, ...), custom_call_target="tpu_custom_call" | custom-call | tf_op jit(solution)/shard_map/spread/pallas_call | solution.py:505
  17.9 2.0 %collective-permute-start.7 = (f32[177,8,128]{2,1,0:T(8,128)S(1)}, f32[177,8,128]{2,1,0:T(8,128)S(1)}, u32[]{:S(2)}, u32[]{:S(2)}) collective-permute-start(f32[177,8,128]{2,1,0:T(8,128)S(1)} %get-tuple-element.54), channel_id=1, source_target_pairs={{0,1},{1,0},{2,3},{3,2},{4,5},{5,4},{6,7},{7,6},{8,9},{9,8},{10,11... | collective-permute-start | bytes 2174984 | tf_op jit(solution)/shard_map/ppermute | solution.py:484
  19.9 5.2 %collective-permute-start.8 = (f32[177,8,128]{2,1,0:T(8,128)S(1)}, f32[177,8,128]{2,1,0:T(8,128)S(1)}, u32[]{:S(2)}, u32[]{:S(2)}) collective-permute-start(f32[177,8,128]{2,1,0:T(8,128)S(1)} %get-tuple-element.55), channel_id=1, source_target_pairs={{0,32},{1,2},{2,1},{3,4},{4,3},{5,6},{6,5},{7,8},{8,7},{9,10},{10,... | collective-permute-start | bytes 2174984 | tf_op jit(solution)/shard_map/ppermute | solution.py:484
  25.1 11.5 %collective-permute-done.7.far.tfar = f32[177,8,128]{2,1,0:T(8,128)S(1)} collective-permute-done((f32[177,8,128]{2,1,0:T(8,128)S(1)}, f32[177,8,128]{2,1,0:T(8,128)S(1)}, u32[]{:S(2)}, u32[]{:S(2)}) %collective-permute-start.7) | collective-permute-done | bytes 725024 | tf_op jit(solution)/shard_map/ppermute | solution.py:484
  36.6 4.9 %collective-permute-done.8.near.tnear = f32[177,8,128]{2,1,0:T(8,128)S(1)} collective-permute-done((f32[177,8,128]{2,1,0:T(8,128)S(1)}, f32[177,8,128]{2,1,0:T(8,128)S(1)}, u32[]{:S(2)}, u32[]{:S(2)}) %collective-permute-start.8) | collective-permute-done | bytes 725024 | tf_op jit(solution)/shard_map/ppermute | solution.py:484
  41.5 0.2 coefficients.1
  41.8 1.4 %front.2 = (f32[68,4,8,128]{3,2,1,0:T(8,128)S(1)}, f32[2,16,4,8,128]{4,3,2,1,0:T(8,128)S(1)}, f32[26,4,8,128]{3,2,1,0:T(8,128)S(1)}, f32[26,4,8,128]{3,2,1,0:T(8,128)S(1)}) custom-call(f32[177,8,128]{2,1,0:T(8,128)S(1)} %collective-permute-done.7.far.tfar, f32[177,8,128]{2,1,0:T(8,128)S(1)} %collective-permute-done.8.near.tnear, ...), custom_call_target="tpu_custom_call" | custom-call | tf_op jit(solution)/shard_map/front/pallas_call | solution.py:521
  43.2 0.1 collective-permute-start.9
  43.3 3.9 %collective-permute-start.10 = (f32[26,4,8,128]{3,2,1,0:T(8,128)S(1)}, f32[26,4,8,128]{3,2,1,0:T(8,128)S(1)}, u32[]{:S(2)}, u32[]{:S(2)}) collective-permute-start(f32[26,4,8,128]{3,2,1,0:T(8,128)S(1)} %get-tuple-element.63), channel_id=1, source_target_pairs={{0,32},{1,2},{2,1},{3,4},{4,3},{5,6},{6,5},{7,8},{8,7},{9,10},{10,... | collective-permute-start | bytes 1277960 | tf_op jit(solution)/shard_map/ppermute | solution.py:484
  47.2 7.2 %collective-permute-done.9.far = f32[26,4,8,128]{3,2,1,0:T(8,128)S(1)} collective-permute-done((f32[26,4,8,128]{3,2,1,0:T(8,128)S(1)}, f32[26,4,8,128]{3,2,1,0:T(8,128)S(1)}, u32[]{:S(2)}, u32[]{:S(2)}) %collective-permute-start.9) | collective-permute-done | bytes 426016 | tf_op jit(solution)/shard_map/ppermute | solution.py:484
  54.5 2.2 %collective-permute-done.10.near = f32[26,4,8,128]{3,2,1,0:T(8,128)S(1)} collective-permute-done((f32[26,4,8,128]{3,2,1,0:T(8,128)S(1)}, f32[26,4,8,128]{3,2,1,0:T(8,128)S(1)}, u32[]{:S(2)}, u32[]{:S(2)}) %collective-permute-start.10) | collective-permute-done | bytes 426016 | tf_op jit(solution)/shard_map/ppermute | solution.py:484
  56.7 0.9 middle.1
  57.6 0.1 collective-permute-start.11
  57.7 3.6 %collective-permute-start.12 = (f32[24,4,8,128]{3,2,1,0:T(8,128)S(1)}, f32[24,4,8,128]{3,2,1,0:T(8,128)S(1)}, u32[]{:S(2)}, u32[]{:S(2)}) collective-permute-start(f32[24,4,8,128]{3,2,1,0:T(8,128)S(1)} %get-tuple-element.67), channel_id=1, source_target_pairs={{0,32},{1,2},{2,1},{3,4},{4,3},{5,6},{6,5},{7,8},{8,7},{9,10},{10,... | collective-permute-start | bytes 1179656 | tf_op jit(solution)/shard_map/ppermute | solution.py:484
  61.3 5.9 %collective-permute-done.11.far.far_x = f32[24,4,8,128]{3,2,1,0:T(8,128)S(1)} collective-permute-done((f32[24,4,8,128]{3,2,1,0:T(8,128)S(1)}, f32[24,4,8,128]{3,2,1,0:T(8,128)S(1)}, u32[]{:S(2)}, u32[]{:S(2)}) %collective-permute-start.11) | collective-permute-done | bytes 393248 | tf_op jit(solution)/shard_map/ppermute | solution.py:484
  67.2 2.2 %collective-permute-done.12.near.near_x = f32[24,4,8,128]{3,2,1,0:T(8,128)S(1)} collective-permute-done((f32[24,4,8,128]{3,2,1,0:T(8,128)S(1)}, f32[24,4,8,128]{3,2,1,0:T(8,128)S(1)}, u32[]{:S(2)}, u32[]{:S(2)}) %collective-permute-start.12) | collective-permute-done | bytes 393248 | tf_op jit(solution)/shard_map/ppermute | solution.py:484
  69.5 0.1 collective-permute-start.13
  69.6 0.9 collective-permute-start.14
  70.5 6.4 %collective-permute-done.13.got1 = f32[18,4,8,128]{3,2,1,0:T(8,128)S(1)} collective-permute-done((f32[18,4,8,128]{3,2,1,0:T(8,128)S(1)}, f32[18,4,8,128]{3,2,1,0:T(8,128)S(1)}, u32[]{:S(2)}, u32[]{:S(2)}) %collective-permute-start.13) | collective-permute-done | bytes 294944 | tf_op jit(solution)/shard_map/ppermute | solution.py:473
  76.9 0.1 widen.1
  77.1 1.4 %front.3 = (f32[68,4,8,128]{3,2,1,0:T(8,128)S(1)}, f32[2,16,4,8,128]{4,3,2,1,0:T(8,128)S(1)}, f32[26,4,8,128]{3,2,1,0:T(8,128)S(1)}, f32[26,4,8,128]{3,2,1,0:T(8,128)S(1)}) custom-call(f32[136,8,128]{2,1,0:T(8,128)S(1)} %bitcast.8, f32[136,8,128]{2,1,0:T(8,128)S(1)} %bitcast.7, f32[2,20,4,8,128]{4,3,2,1,0:T(8,128)S(1)} %get-tuple-element.73.own, ...), custom_call_target="tpu_custom_call" | custom-call | tf_op jit(solution)/shard_map/front/pallas_call | solution.py:521
  78.5 0.1 collective-permute-start.15
  78.6 3.3 %collective-permute-start.16 = (f32[26,4,8,128]{3,2,1,0:T(8,128)S(1)}, f32[26,4,8,128]{3,2,1,0:T(8,128)S(1)}, u32[]{:S(2)}, u32[]{:S(2)}) collective-permute-start(f32[26,4,8,128]{3,2,1,0:T(8,128)S(1)} %get-tuple-element.75), channel_id=1, source_target_pairs={{0,32},{1,2},{2,1},{3,4},{4,3},{5,6},{6,5},{7,8},{8,7},{9,10},{10,... | collective-permute-start | bytes 1277960 | tf_op jit(solution)/shard_map/ppermute | solution.py:484
  81.9 6.7 %collective-permute-done.15.far = f32[26,4,8,128]{3,2,1,0:T(8,128)S(1)} collective-permute-done((f32[26,4,8,128]{3,2,1,0:T(8,128)S(1)}, f32[26,4,8,128]{3,2,1,0:T(8,128)S(1)}, u32[]{:S(2)}, u32[]{:S(2)}) %collective-permute-start.15) | collective-permute-done | bytes 426016 | tf_op jit(solution)/shard_map/ppermute | solution.py:484
  88.6 2.2 %collective-permute-done.16.near = f32[26,4,8,128]{3,2,1,0:T(8,128)S(1)} collective-permute-done((f32[26,4,8,128]{3,2,1,0:T(8,128)S(1)}, f32[26,4,8,128]{3,2,1,0:T(8,128)S(1)}, u32[]{:S(2)}, u32[]{:S(2)}) %collective-permute-start.16) | collective-permute-done | bytes 426016 | tf_op jit(solution)/shard_map/ppermute | solution.py:484
  90.8 1.5 %last.1 = (f32[4,96,128]{2,1,0:T(8,128)S(1)}, f32[4,96,128]{2,1,0:T(8,128)S(1)}) custom-call(f32[26,4,8,128]{3,2,1,0:T(8,128)S(1)} %collective-permute-done.15.far, f32[26,4,8,128]{3,2,1,0:T(8,128)S(1)} %collective-permute-done.16.near, f32[2,16,4,8,128]{4,3,2,1,0:T(8,128)S(1)} %get-tuple-element.76.it, f32[68,4,8,128]{3,2,1,0:T(8,128)S(1)} %get-tuple-element.77.fixed, ...), custom_call_target="tpu_custom_call" | custom-call | tf_op jit(solution)/shard_map/last/pallas_call | solution.py:548
  92.3 0.1 collective-permute-start.17
  92.4 1.4 %collective-permute-done.17.other = f32[4,96,128]{2,1,0:T(8,128)S(1)} collective-permute-done((f32[4,96,128]{2,1,0:T(8,128)S(1)}, f32[4,96,128]{2,1,0:T(8,128)S(1)}, u32[]{:S(2)}, u32[]{:S(2)}) %collective-permute-start.17) | collective-permute-done | bytes 196640 | tf_op jit(solution)/shard_map/ppermute | solution.py:473
  93.8 1.9 %collective-permute-start.18 = (f32[2,96,128]{2,1,0:T(8,128)S(1)}, f32[2,96,128]{2,1,0:T(8,128)S(1)}, u32[]{:S(2)}, u32[]{:S(2)}) collective-permute-start(f32[2,96,128]{2,1,0:T(8,128)S(1)} %get-tuple-element.81), channel_id=1, source_target_pairs={{0,128},{32,160},{64,192},{96,224},{128,0},{160,32},{192,64},{224,... | collective-permute-start | bytes 294920 | tf_op jit(solution)/shard_map/ppermute | solution.py:559
  95.7 1.2 %collective-permute-start.19 = (f32[2,96,128]{2,1,0:T(8,128)S(1)}, f32[2,96,128]{2,1,0:T(8,128)S(1)}, u32[]{:S(2)}, u32[]{:S(2)}) collective-permute-start(f32[2,96,128]{2,1,0:T(8,128)S(1)} %get-tuple-element.82), channel_id=1, source_target_pairs={{0,64},{32,96},{64,0},{96,32},{128,192},{160,224},{192,128},{224,1... | collective-permute-start | bytes 294920 | tf_op jit(solution)/shard_map/ppermute | solution.py:559
  96.9 1.1 %collective-permute-start.20 = (f32[2,96,128]{2,1,0:T(8,128)S(1)}, f32[2,96,128]{2,1,0:T(8,128)S(1)}, u32[]{:S(2)}, u32[]{:S(2)}) collective-permute-start(f32[2,96,128]{2,1,0:T(8,128)S(1)} %get-tuple-element.83), channel_id=1, source_target_pairs={{0,192},{32,224},{64,128},{96,160},{128,64},{160,96},{192,0},{224,... | collective-permute-start | bytes 294920 | tf_op jit(solution)/shard_map/ppermute | solution.py:559
  98.0 3.0 %collective-permute-done.18.a = f32[2,96,128]{2,1,0:T(8,128)S(1)} collective-permute-done((f32[2,96,128]{2,1,0:T(8,128)S(1)}, f32[2,96,128]{2,1,0:T(8,128)S(1)}, u32[]{:S(2)}, u32[]{:S(2)}) %collective-permute-start.18) | collective-permute-done | bytes 98336 | tf_op jit(solution)/shard_map/ppermute | solution.py:559
  101.1 0.8 collective-permute-done.19.b
  101.8 0.9 collective-permute-done.20.c
  102.8 0.8 unpack.1
  (5 shorter events, 0.1 us)
Async XLA Ops:
  2.0 7.8 %collective-permute-start = (f32[240,128]{1,0:T(8,128)S(1)}, f32[240,128]{1,0:T(8,128)S(1)}, u32[]{:S(2)}, u32[]{:S(2)}) collective-permute-start(f32[240,128]{1,0:T(8,128)S(1)} %get-tuple-element.43), channel_id=1, source_target_pairs={{0,128},{32,160},{64,192},{96,224},{128,0},{160,32},{192,64},{224,... | collective-permute-start | bytes 368648 | tf_op jit(solution)/shard_map/ppermute | solution.py:464
  5.3 6.9 %collective-permute-start.1 = (f32[240,128]{1,0:T(8,128)S(1)}, f32[240,128]{1,0:T(8,128)S(1)}, u32[]{:S(2)}, u32[]{:S(2)}) collective-permute-start(f32[240,128]{1,0:T(8,128)S(1)} %get-tuple-element.44), channel_id=1, source_target_pairs={{0,64},{32,96},{64,0},{96,32},{128,192},{160,224},{192,128},{224,1... | collective-permute-start | bytes 368648 | tf_op jit(solution)/shard_map/ppermute | solution.py:464
  6.0 9.2 %collective-permute-start.2 = (f32[240,128]{1,0:T(8,128)S(1)}, f32[240,128]{1,0:T(8,128)S(1)}, u32[]{:S(2)}, u32[]{:S(2)}) collective-permute-start(f32[240,128]{1,0:T(8,128)S(1)} %get-tuple-element.45), channel_id=1, source_target_pairs={{0,192},{32,224},{64,128},{96,160},{128,64},{160,96},{192,0},{224,... | collective-permute-start | bytes 368648 | tf_op jit(solution)/shard_map/ppermute | solution.py:464
  6.3 8.8 %collective-permute-start.3 = (f32[240,128]{1,0:T(8,128)S(1)}, f32[240,128]{1,0:T(8,128)S(1)}, u32[]{:S(2)}, u32[]{:S(2)}) collective-permute-start(f32[240,128]{1,0:T(8,128)S(1)} %get-tuple-element.46), channel_id=1, source_target_pairs={{0,160},{32,128},{64,224},{96,192},{128,32},{160,0},{192,96},{224,... | collective-permute-start | bytes 368648 | tf_op jit(solution)/shard_map/ppermute | solution.py:464
  8.0 8.4 %collective-permute-start.4 = (f32[240,128]{1,0:T(8,128)S(1)}, f32[240,128]{1,0:T(8,128)S(1)}, u32[]{:S(2)}, u32[]{:S(2)}) collective-permute-start(f32[240,128]{1,0:T(8,128)S(1)} %get-tuple-element.47), channel_id=1, source_target_pairs={{0,96},{32,64},{64,32},{96,0},{128,224},{160,192},{192,160},{224,1... | collective-permute-start | bytes 368648 | tf_op jit(solution)/shard_map/ppermute | solution.py:464
  9.8 7.1 %collective-permute-start.5 = (f32[240,128]{1,0:T(8,128)S(1)}, f32[240,128]{1,0:T(8,128)S(1)}, u32[]{:S(2)}, u32[]{:S(2)}) collective-permute-start(f32[240,128]{1,0:T(8,128)S(1)} %get-tuple-element.48), channel_id=1, source_target_pairs={{0,224},{32,192},{64,160},{96,128},{128,96},{160,64},{192,32},{224... | collective-permute-start | bytes 368648 | tf_op jit(solution)/shard_map/ppermute | solution.py:464
  12.2 4.7 %collective-permute-start.6 = (f32[240,128]{1,0:T(8,128)S(1)}, f32[240,128]{1,0:T(8,128)S(1)}, u32[]{:S(2)}, u32[]{:S(2)}) collective-permute-start(f32[240,128]{1,0:T(8,128)S(1)} %get-tuple-element.49), channel_id=1, source_target_pairs={{0,32},{32,0},{64,96},{96,64},{128,160},{160,128},{192,224},{224,1... | collective-permute-start | bytes 368648 | tf_op jit(solution)/shard_map/ppermute | solution.py:464
  17.9 18.7 %collective-permute-start.7 = (f32[177,8,128]{2,1,0:T(8,128)S(1)}, f32[177,8,128]{2,1,0:T(8,128)S(1)}, u32[]{:S(2)}, u32[]{:S(2)}) collective-permute-start(f32[177,8,128]{2,1,0:T(8,128)S(1)} %get-tuple-element.54), channel_id=1, source_target_pairs={{0,1},{1,0},{2,3},{3,2},{4,5},{5,4},{6,7},{7,6},{8,9},{9,8},{10,11... | collective-permute-start | bytes 2174984 | tf_op jit(solution)/shard_map/ppermute | solution.py:484
  19.9 21.6 %collective-permute-start.8 = (f32[177,8,128]{2,1,0:T(8,128)S(1)}, f32[177,8,128]{2,1,0:T(8,128)S(1)}, u32[]{:S(2)}, u32[]{:S(2)}) collective-permute-start(f32[177,8,128]{2,1,0:T(8,128)S(1)} %get-tuple-element.55), channel_id=1, source_target_pairs={{0,32},{1,2},{2,1},{3,4},{4,3},{5,6},{6,5},{7,8},{8,7},{9,10},{10,... | collective-permute-start | bytes 2174984 | tf_op jit(solution)/shard_map/ppermute | solution.py:484
  43.2 11.3 %collective-permute-start.9 = (f32[26,4,8,128]{3,2,1,0:T(8,128)S(1)}, f32[26,4,8,128]{3,2,1,0:T(8,128)S(1)}, u32[]{:S(2)}, u32[]{:S(2)}) collective-permute-start(f32[26,4,8,128]{3,2,1,0:T(8,128)S(1)} %get-tuple-element.62), channel_id=1, source_target_pairs={{0,1},{1,0},{2,3},{3,2},{4,5},{5,4},{6,7},{7,6},{8,9},{9,8},{10,11... | collective-permute-start | bytes 1277960 | tf_op jit(solution)/shard_map/ppermute | solution.py:484
  43.3 13.4 %collective-permute-start.10 = (f32[26,4,8,128]{3,2,1,0:T(8,128)S(1)}, f32[26,4,8,128]{3,2,1,0:T(8,128)S(1)}, u32[]{:S(2)}, u32[]{:S(2)}) collective-permute-start(f32[26,4,8,128]{3,2,1,0:T(8,128)S(1)} %get-tuple-element.63), channel_id=1, source_target_pairs={{0,32},{1,2},{2,1},{3,4},{4,3},{5,6},{6,5},{7,8},{8,7},{9,10},{10,... | collective-permute-start | bytes 1277960 | tf_op jit(solution)/shard_map/ppermute | solution.py:484
  57.6 9.6 %collective-permute-start.11 = (f32[24,4,8,128]{3,2,1,0:T(8,128)S(1)}, f32[24,4,8,128]{3,2,1,0:T(8,128)S(1)}, u32[]{:S(2)}, u32[]{:S(2)}) collective-permute-start(f32[24,4,8,128]{3,2,1,0:T(8,128)S(1)} %get-tuple-element.66), channel_id=1, source_target_pairs={{0,1},{1,0},{2,3},{3,2},{4,5},{5,4},{6,7},{7,6},{8,9},{9,8},{10,11... | collective-permute-start | bytes 1179656 | tf_op jit(solution)/shard_map/ppermute | solution.py:484
  57.7 11.8 %collective-permute-start.12 = (f32[24,4,8,128]{3,2,1,0:T(8,128)S(1)}, f32[24,4,8,128]{3,2,1,0:T(8,128)S(1)}, u32[]{:S(2)}, u32[]{:S(2)}) collective-permute-start(f32[24,4,8,128]{3,2,1,0:T(8,128)S(1)} %get-tuple-element.67), channel_id=1, source_target_pairs={{0,32},{1,2},{2,1},{3,4},{4,3},{5,6},{6,5},{7,8},{8,7},{9,10},{10,... | collective-permute-start | bytes 1179656 | tf_op jit(solution)/shard_map/ppermute | solution.py:484
  69.5 7.4 %collective-permute-start.13 = (f32[18,4,8,128]{3,2,1,0:T(8,128)S(1)}, f32[18,4,8,128]{3,2,1,0:T(8,128)S(1)}, u32[]{:S(2)}, u32[]{:S(2)}) collective-permute-start(f32[18,4,8,128]{3,2,1,0:T(8,128)S(1)} %get-tuple-element.69), channel_id=1, source_target_pairs={{32,64},{64,32},{96,128},{128,96},{160,192},{192,160},{224,0},{0,2... | collective-permute-start | bytes 884744 | tf_op jit(solution)/shard_map/ppermute | solution.py:473
  69.6 7.3 %collective-permute-start.14 = (f32[18,4,8,128]{3,2,1,0:T(8,128)S(1)}, f32[18,4,8,128]{3,2,1,0:T(8,128)S(1)}, u32[]{:S(2)}, u32[]{:S(2)}) collective-permute-start(f32[18,4,8,128]{3,2,1,0:T(8,128)S(1)} %get-tuple-element.70), channel_id=1, source_target_pairs={{0,32},{32,0},{64,96},{96,64},{128,160},{160,128},{192,224},{224,1... | collective-permute-start | bytes 884744 | tf_op jit(solution)/shard_map/ppermute | solution.py:473
  78.5 10.1 %collective-permute-start.15 = (f32[26,4,8,128]{3,2,1,0:T(8,128)S(1)}, f32[26,4,8,128]{3,2,1,0:T(8,128)S(1)}, u32[]{:S(2)}, u32[]{:S(2)}) collective-permute-start(f32[26,4,8,128]{3,2,1,0:T(8,128)S(1)} %get-tuple-element.74), channel_id=1, source_target_pairs={{0,1},{1,0},{2,3},{3,2},{4,5},{5,4},{6,7},{7,6},{8,9},{9,8},{10,11... | collective-permute-start | bytes 1277960 | tf_op jit(solution)/shard_map/ppermute | solution.py:484
  78.6 12.2 %collective-permute-start.16 = (f32[26,4,8,128]{3,2,1,0:T(8,128)S(1)}, f32[26,4,8,128]{3,2,1,0:T(8,128)S(1)}, u32[]{:S(2)}, u32[]{:S(2)}) collective-permute-start(f32[26,4,8,128]{3,2,1,0:T(8,128)S(1)} %get-tuple-element.75), channel_id=1, source_target_pairs={{0,32},{1,2},{2,1},{3,4},{4,3},{5,6},{6,5},{7,8},{8,7},{9,10},{10,... | collective-permute-start | bytes 1277960 | tf_op jit(solution)/shard_map/ppermute | solution.py:484
  92.3 1.5 %collective-permute-start.17 = (f32[4,96,128]{2,1,0:T(8,128)S(1)}, f32[4,96,128]{2,1,0:T(8,128)S(1)}, u32[]{:S(2)}, u32[]{:S(2)}) collective-permute-start(f32[4,96,128]{2,1,0:T(8,128)S(1)} %get-tuple-element.79), channel_id=1, source_target_pairs={{0,32},{32,0},{64,96},{96,64},{128,160},{160,128},{192,224},{224,1... | collective-permute-start | bytes 589832 | tf_op jit(solution)/shard_map/ppermute | solution.py:473
  93.8 7.2 %collective-permute-start.18 = (f32[2,96,128]{2,1,0:T(8,128)S(1)}, f32[2,96,128]{2,1,0:T(8,128)S(1)}, u32[]{:S(2)}, u32[]{:S(2)}) collective-permute-start(f32[2,96,128]{2,1,0:T(8,128)S(1)} %get-tuple-element.81), channel_id=1, source_target_pairs={{0,128},{32,160},{64,192},{96,224},{128,0},{160,32},{192,64},{224,... | collective-permute-start | bytes 294920 | tf_op jit(solution)/shard_map/ppermute | solution.py:559
  95.7 6.1 %collective-permute-start.19 = (f32[2,96,128]{2,1,0:T(8,128)S(1)}, f32[2,96,128]{2,1,0:T(8,128)S(1)}, u32[]{:S(2)}, u32[]{:S(2)}) collective-permute-start(f32[2,96,128]{2,1,0:T(8,128)S(1)} %get-tuple-element.82), channel_id=1, source_target_pairs={{0,64},{32,96},{64,0},{96,32},{128,192},{160,224},{192,128},{224,1... | collective-permute-start | bytes 294920 | tf_op jit(solution)/shard_map/ppermute | solution.py:559
  96.9 5.9 %collective-permute-start.20 = (f32[2,96,128]{2,1,0:T(8,128)S(1)}, f32[2,96,128]{2,1,0:T(8,128)S(1)}, u32[]{:S(2)}, u32[]{:S(2)}) collective-permute-start(f32[2,96,128]{2,1,0:T(8,128)S(1)} %get-tuple-element.83), channel_id=1, source_target_pairs={{0,192},{32,224},{64,128},{96,160},{128,64},{160,96},{192,0},{224,... | collective-permute-start | bytes 294920 | tf_op jit(solution)/shard_map/ppermute | solution.py:559

commit v9 on v8

--- a/solution.py
+++ b/solution.py
@@ -17,6 +17,7 @@
 HALO = 4
 WIN = OWN + 2 * HALO
 ORDER = (4, 2, 6, 5, 3, 7, 1)
+PIECE = 8 * WIN + 4 * (WIN - 2)
 CHIPS = (2, 1, 3)
 TALL = 24
 
@@ -76,6 +77,10 @@
 
 def rows(lo, hi, body):
     lax.fori_loop(lo, hi, body, 0, unroll=True)
+
+
+def piece_row(f, n, x):
+    return ((f * 2 + n) * 2 + x) * WIN if f < 2 else 8 * WIN + (n * 2 + x) * (WIN - 2)
 
 
 def pack_body(*rest):
@@ -94,15 +99,16 @@
         for n in range(2):
             slabs[2 * f + n].wait()
             for x in range(2):
-                base = ((f * 2 + n) * 2 + x) * WIN
+                base = piece_row(f, n, x)
+                size = WIN if f < 2 else WIN - 2
                 for d in range(8):
-                    low = OWN * d - HALO
-                    first, last = max(low, 0), min(low + WIN, 96)
+                    low = OWN * d - (HALO if f < 2 else HALO - 1)
+                    first, last = max(low, 0), min(low + size, 96)
                     stage[d, base + first - low : base + last - low, :] = ref[n, x ^ flip, first:last, :]
                     if first > low:
                         stage[d, base : base + first - low, :] = jnp.zeros((first - low, 128), jnp.float32)
-                    if last < low + WIN:
-                        stage[d, base + last - low : base + WIN, :] = jnp.zeros((low + WIN - last, 128), jnp.float32)
+                    if last < low + size:
+                        stage[d, base + last - low : base + size, :] = jnp.zeros((low + size - last, 128), jnp.float32)
     for k in range(8):
         outs[k][...] = stage[t ^ k]
     for copy in copies:
@@ -185,12 +191,12 @@
         near[168 + 3 * i : 171 + 3 * i] = near_c[i].reshape(3, 8, 128)
         far[168 + 3 * i : 171 + 3 * i] = far_c[i].reshape(3, 8, 128)
     t, _ = place()
-    rows = 12 * WIN
+    rows = PIECE
     for k, piece in zip(ORDER + (0,), pieces):
         stage[pl.ds(pl.multiple_of((t ^ k) * rows, 8), rows), :] = piece[...]
 
     def steps(f, n, x, j):
-        return stage[pl.ds(((f * 2 + n) * 2 + x) * WIN + j, 8, stride=rows), :]
+        return stage[pl.ds(piece_row(f, n, x) + j - (0 if f < 2 else 1), 8, stride=rows), :]
 
     matrix = forward[...]
     for x in range(2):
@@ -202,15 +208,14 @@
                     v = done[(i * 4 + c) * 8 : (i * 4 + c + 1) * 8]
                     own[x, low + i, c] = v
                     put_field(near, far, x, low + i, c, v)
-    cells = [(x, j) for x in range(2) for j in range(WIN)]
+    cells = [(x, j) for x in range(2) for j in range(1, WIN - 1)]
     for low in range(0, len(cells), 8):
-        block = [steps(2, n, x, j) for x, j in cells[low : low + 8] for n in range(2)]
-        done = transform(matrix, jnp.concatenate(block, 0))
+        block = jnp.concatenate([steps(2, n, x, j) for x, j in cells[low : low + 8] for n in range(2)], 0)
+        done = transform(matrix[: len(block), : len(block)], block)
         for i, (x, j) in enumerate(cells[low : low + 8]):
             for n in range(2):
                 v = done[(i * 2 + n) * 8 : (i * 2 + n + 1) * 8]
-                if 1 <= j <= 18:
-                    wish[x, j - 1, n] = v
+                wish[x, j - 1, n] = v
                 if 2 <= j <= 17:
                     out = far if x == 1 else near
                     out[136 + (j - 2) * 2 + n] = v
@@ -370,54 +375,47 @@
         rows(4, 16, row)
 
 
-def middle_body(far, near, it, fixed, weights, consts, inv, new, out_near, out_far, zed):
+def middle_body(far, near, it, fixed, weights, consts, inv, new, out_near, out_far, send0, send1, zed):
     def put(x, j, c, v):
         new[x, j, c] = v
         first, second = (out_near, out_far) if x == 0 else (out_far, out_near)
         first[j, c] = v
         second[OWN + j, c] = v
-    sweep_body(it, near, far, fixed, weights, consts, inv, zed, put)
-
-
-EDGE = ((0, 4), (4, 4), (8, 3), (11, 3), (14, 2), (16, 2))
-
-
-def edges_body(far, near, new, send0, send1):
+    sweep_body(far=far, near=near, it=it, fixed=fixed, weights=weights, consts=consts, inv=inv, zed=zed, put=put)
     odd = place()[0] & 1
-    planes = (
-        lambda j, n: new[0, pl.ds(j, n)],
-        lambda j, n: new[1, pl.ds(j, n)],
-        lambda j, n: near[pl.ds(j, n)],
-        lambda j, n: far[pl.ds(j, n)],
-        lambda j, n: near[pl.ds(OWN + j, n)],
-        lambda j, n: far[pl.ds(OWN + j, n)],
-    )
-    for take, (at, n) in zip(planes, EDGE):
-        send0[at : at + n] = take((OWN - n) * (1 - odd), n)
-        send1[at : at + n] = take((OWN - n) * odd, n)
-
-
-def widen_body(got1, got0, new, near_x, far_x, own, near, far):
+    for x in range(2):
+        send0[x] = new[x, pl.ds((OWN - HALO) * (1 - odd), HALO)]
+        send1[x] = new[x, pl.ds((OWN - HALO) * odd, HALO)]
+
+
+def edges_body(far, near, row1, row0, new, own, send0, send1):
     odd = place()[0] & 1
     for x in range(2):
         own[x, HALO : HALO + OWN] = new[x]
+    for row, send, high in ((row0, send0, 1 - odd), (row1, send1, odd)):
+        for x in range(2):
+            own[x, pl.ds(16 * high, HALO)] = row[x]
+        for i, side in enumerate((near, far)):
+            send[3 * i : 3 * i + 3] = side[pl.ds((OWN - 3) * high, 3)]
+            send[6 + 2 * i : 8 + 2 * i] = side[pl.ds(OWN + (OWN - 2) * high, 2)]
+
+
+def widen_body(edge1, edge0, near_x, far_x, near, far):
+    odd = place()[0] & 1
     for out, got in ((near, near_x), (far, far_x)):
         out[3 : 3 + OWN] = got[0:OWN]
         out[20 : 20 + OWN] = got[OWN : 2 * OWN]
-    for got, high in ((got0, 1 - odd), (got1, odd)):
-        own[0, pl.ds(16 * high, 4)] = got[0:4]
-        own[1, pl.ds(16 * high, 4)] = got[4:8]
-        near[pl.ds(15 * high, 3)] = got[8:11]
-        far[pl.ds(15 * high, 3)] = got[11:14]
-        near[pl.ds(18 + 14 * high, 2)] = got[14:16]
-        far[pl.ds(18 + 14 * high, 2)] = got[16:18]
+    for edge, high in ((edge0, 1 - odd), (edge1, odd)):
+        for i, side in enumerate((near, far)):
+            side[pl.ds(15 * high, 3)] = edge[3 * i : 3 * i + 3]
+            side[pl.ds(18 + 14 * high, 2)] = edge[6 + 2 * i : 8 + 2 * i]
 
 
 def last_body(far, near, it, fixed, weights, consts, inv, back, *rest):
     outs, (zed, fin, stage) = rest[:2], rest[2:]
     def put(x, j, c, v):
         fin[x * OWN + j, c] = v
-    sweep_body(it, near, far, fixed, weights, consts, inv, zed, put)
+    sweep_body(far=far, near=near, it=it, fixed=fixed, weights=weights, consts=consts, inv=inv, zed=zed, put=put)
     t, _ = place()
     matrix = back[...]
     for low in range(0, 2 * OWN, 4):
@@ -492,10 +490,10 @@
     *pieces, near_c, far_c, here_c, forward, back, consts = call(
         pack_body,
         "pack",
-        [whole(12 * WIN, 128)] * 8 + [whole(3, TALL, 128)] * 2 + [whole(4, TALL, 128)]
+        [whole(PIECE, 128)] * 8 + [whole(3, TALL, 128)] * 2 + [whole(4, TALL, 128)]
         + [whole(128, 128)] * 2 + [whole(10, 8, 128)],
         0,
-        [pltpu.VMEM((8, 12 * WIN, 128), jnp.float32)]
+        [pltpu.VMEM((8, PIECE, 128), jnp.float32)]
         + [pltpu.VMEM((2, 2, 96, 128), jnp.float32)] * 3
         + [pltpu.VMEM((2, 96, 128), jnp.float32)] * 2
         + [pltpu.SemaphoreType.DMA((11,))],
@@ -507,7 +505,7 @@
         "spread",
         [whole(2, WIN, 4, 8, 128), whole(2, 18, 2, 8, 128), whole(177, 8, 128), whole(177, 8, 128)],
         11,
-        [pltpu.VMEM((8 * 12 * WIN, 128), jnp.float32)],
+        [pltpu.VMEM((8 * PIECE, 128), jnp.float32)],
     )(*got, near_c, far_c, forward)
     far = far_first = swap_planes(far, 0)
     near = near_first = swap_planes(near, 1)
@@ -528,21 +526,23 @@
         far_z = swap_planes(far_z, 0)
         near_z = swap_planes(near_z, 1)
         if outer < OUTER - 1:
-            new, near, far = call(
+            new, near, far, row0, row1 = call(
                 middle_body,
                 "middle",
-                [whole(2, OWN, 4, 8, 128), whole(2 * OWN, 4, 8, 128), whole(2 * OWN, 4, 8, 128)],
+                [whole(2, OWN, 4, 8, 128)] + [whole(2 * OWN, 4, 8, 128)] * 2 + [whole(2, HALO, 4, 8, 128)] * 2,
                 7,
                 sweep_scratch,
             )(far_z, near_z, it, fixed, weights, consts, inv)
             far = swap_planes(far, 0)
             near = swap_planes(near, 1)
-            send0, send1 = call(edges_body, "edges", [whole(18, 4, 8, 128)] * 2, 3)(far, near, new)
-            got1 = swap_rows(send1, 1)
-            got0 = swap_rows(send0, 0)
-            own, near, far = call(
-                widen_body, "widen", [whole(2, WIN, 4, 8, 128), whole(34, 4, 8, 128), whole(34, 4, 8, 128)], 5
-            )(got1, got0, new, near, far)
+            row1 = swap_rows(row1, 1)
+            row0 = swap_rows(row0, 0)
+            own, edge0, edge1 = call(
+                edges_body, "edges", [whole(2, WIN, 4, 8, 128)] + [whole(10, 4, 8, 128)] * 2, 5
+            )(far, near, row1, row0, new)
+            edge1 = swap_rows(edge1, 1)
+            edge0 = swap_rows(edge0, 0)
+            near, far = call(widen_body, "widen", [whole(34, 4, 8, 128)] * 2, 4)(edge1, edge0, near, far)
             near = near.reshape(136, 8, 128)
             far = far.reshape(136, 8, 128)
     mine, other = call(

time: 104 us -> 103 us (level)
  waiting for transfers between devices: 61.4 us -> 58.9 us
  starting transfers between devices: 32.6 us -> 33.7 us
    ppermute x8, waiting for transfers between devices: 42.8 us -> 36.9 us  [swap_planes(): return lax.ppermute(block, ('tm', 'space'), route)]
    ppermute x3 -> x5, waiting for transfers between devices: 7.88 us -> 11.4 us  [swap_rows(): return lax.ppermute(block, 'tm', route)]
  transfers between devices with their start and end apart: 21 -> 23, of which waited for: 17 -> 18; matrix products, arithmetic and copies ran while one was open for 0% -> 0% of each run, Pallas kernels for 0% -> 0%
where the time goes in v9:
time: 103 us; the launch traced here: 102 us
  waiting for transfers between devices  58.9 us (57%)
  starting transfers between devices  33.7 us (33%)
  Pallas kernels  8.88 us (9%)
    ppermute x8, waiting for transfers between devices, swap_planes(): return lax.ppermute(block, ('tm', 'space'), route)  36.9 us
    ppermute x8, starting transfers between devices, swap_planes(): return lax.ppermute(block, ('tm', 'space'), route)  18.3 us
    ppermute x5, waiting for transfers between devices, swap_rows(): return lax.ppermute(block, 'tm', route)  11.4 us
    ppermute x7, starting transfers between devices, exchange(): lax.ppermute(pieces[k], 'tm', [(i, i ^ k) for i in range(count)])  9.17 us
    ppermute x7, waiting for transfers between devices, exchange(): lax.ppermute(pieces[k], 'tm', [(i, i ^ k) for i in range(count)])  5.4 us
    ppermute x3, waiting for transfers between devices, on_device(): lax.ppermute(pair, 'tm', [(i, i ^ 2 * k) for i in range(count)])  5.21 us
    ppermute x3, starting transfers between devices, on_device(): lax.ppermute(pair, 'tm', [(i, i ^ 2 * k) for i in range(count)])  4.23 us
    pallas_call x2, Pallas kernels, on_device(): call(front_body, 'front', [whole(68, 4, 8, 128), whole(2, 16, 4, 8, 128),...  2.86 us
  transfers between devices with their start and end apart: 23, of which 18 were waited for; matrix products, arithmetic and copies ran while one was open for 0% of the time, Pallas kernels for 0%

profile of v9, /device:TPU:6, one launch (start us, length us, event | category | flops | bytes accessed | tf_op | source)
XLA Modules:
  0.0 102.4 jit_solution(2121390766123052752)
XLA Ops:
  0.6 1.4 %pack.1 = (f32[232,128]{1,0:T(8,128)S(1)}, f32[232,128]{1,0:T(8,128)S(1)}, f32[232,128]{1,0:T(8,128)S(1)}, f32[232,128]{1,0:T(8,128)S(1)}, f32[232,128]{1,0:T(8,...) custom-call(f32[2,2,96,128]{3,2,1,0:T(8,128)} %rest_0_.1, ...), custom_call_target="tpu_custom_call" | custom-call | tf_op jit(solution)/shard_map/pack/pallas_call | solution.py:490
  2.0 3.3 %collective-permute-start = (f32[232,128]{1,0:T(8,128)S(1)}, f32[232,128]{1,0:T(8,128)S(1)}, u32[]{:S(2)}, u32[]{:S(2)}) collective-permute-start(f32[232,128]{1,0:T(8,128)S(1)} %get-tuple-element.45), channel_id=1, source_target_pairs={{0,128},{32,160},{64,192},{96,224},{128,0},{160,32},{192,64},{224,... | collective-permute-start | bytes 356360 | tf_op jit(solution)/shard_map/ppermute | solution.py:462
  5.3 0.7 collective-permute-start.1
  6.0 0.4 collective-permute-start.2
  6.3 1.6 %collective-permute-start.3 = (f32[232,128]{1,0:T(8,128)S(1)}, f32[232,128]{1,0:T(8,128)S(1)}, u32[]{:S(2)}, u32[]{:S(2)}) collective-permute-start(f32[232,128]{1,0:T(8,128)S(1)} %get-tuple-element.48), channel_id=1, source_target_pairs={{0,160},{32,128},{64,224},{96,192},{128,32},{160,0},{192,96},{224,... | collective-permute-start | bytes 356360 | tf_op jit(solution)/shard_map/ppermute | solution.py:462
  8.0 1.8 %collective-permute-start.4 = (f32[232,128]{1,0:T(8,128)S(1)}, f32[232,128]{1,0:T(8,128)S(1)}, u32[]{:S(2)}, u32[]{:S(2)}) collective-permute-start(f32[232,128]{1,0:T(8,128)S(1)} %get-tuple-element.49), channel_id=1, source_target_pairs={{0,96},{32,64},{64,32},{96,0},{128,224},{160,192},{192,160},{224,1... | collective-permute-start | bytes 356360 | tf_op jit(solution)/shard_map/ppermute | solution.py:462
  9.8 0.4 collective-permute-start.5
  10.2 1.7 %collective-permute-done.1.rest_1_ = f32[232,128]{1,0:T(8,128)S(1)} collective-permute-done((f32[232,128]{1,0:T(8,128)S(1)}, f32[232,128]{1,0:T(8,128)S(1)}, u32[]{:S(2)}, u32[]{:S(2)}) %collective-permute-start.1) | collective-permute-done | bytes 118816 | tf_op jit(solution)/shard_map/ppermute | solution.py:462
  11.8 1.0 %collective-permute-start.6 = (f32[232,128]{1,0:T(8,128)S(1)}, f32[232,128]{1,0:T(8,128)S(1)}, u32[]{:S(2)}, u32[]{:S(2)}) collective-permute-start(f32[232,128]{1,0:T(8,128)S(1)} %get-tuple-element.51), channel_id=1, source_target_pairs={{0,32},{32,0},{64,96},{96,64},{128,160},{160,128},{192,224},{224,1... | collective-permute-start | bytes 356360 | tf_op jit(solution)/shard_map/ppermute | solution.py:462
  12.8 2.2 %collective-permute-done.2.rest_2_ = f32[232,128]{1,0:T(8,128)S(1)} collective-permute-done((f32[232,128]{1,0:T(8,128)S(1)}, f32[232,128]{1,0:T(8,128)S(1)}, u32[]{:S(2)}, u32[]{:S(2)}) %collective-permute-start.2) | collective-permute-done | bytes 118816 | tf_op jit(solution)/shard_map/ppermute | solution.py:462
  15.1 1.1 %collective-permute-done.4.rest_4_ = f32[232,128]{1,0:T(8,128)S(1)} collective-permute-done((f32[232,128]{1,0:T(8,128)S(1)}, f32[232,128]{1,0:T(8,128)S(1)}, u32[]{:S(2)}, u32[]{:S(2)}) %collective-permute-start.4) | collective-permute-done | bytes 118816 | tf_op jit(solution)/shard_map/ppermute | solution.py:462
  16.2 0.4 collective-permute-done.5.rest_5_
  16.6 1.0 spread.1
  17.6 2.0 %collective-permute-start.7 = (f32[177,8,128]{2,1,0:T(8,128)S(1)}, f32[177,8,128]{2,1,0:T(8,128)S(1)}, u32[]{:S(2)}, u32[]{:S(2)}) collective-permute-start(f32[177,8,128]{2,1,0:T(8,128)S(1)} %get-tuple-element.56), channel_id=1, source_target_pairs={{0,1},{1,0},{2,3},{3,2},{4,5},{5,4},{6,7},{7,6},{8,9},{9,8},{10,11... | collective-permute-start | bytes 2174984 | tf_op jit(solution)/shard_map/ppermute | solution.py:482
  19.6 5.2 %collective-permute-start.8 = (f32[177,8,128]{2,1,0:T(8,128)S(1)}, f32[177,8,128]{2,1,0:T(8,128)S(1)}, u32[]{:S(2)}, u32[]{:S(2)}) collective-permute-start(f32[177,8,128]{2,1,0:T(8,128)S(1)} %get-tuple-element.57), channel_id=1, source_target_pairs={{0,32},{1,2},{2,1},{3,4},{4,3},{5,6},{6,5},{7,8},{8,7},{9,10},{10,... | collective-permute-start | bytes 2174984 | tf_op jit(solution)/shard_map/ppermute | solution.py:482
  24.8 11.5 %collective-permute-done.7.far.tfar = f32[177,8,128]{2,1,0:T(8,128)S(1)} collective-permute-done((f32[177,8,128]{2,1,0:T(8,128)S(1)}, f32[177,8,128]{2,1,0:T(8,128)S(1)}, u32[]{:S(2)}, u32[]{:S(2)}) %collective-permute-start.7) | collective-permute-done | bytes 725024 | tf_op jit(solution)/shard_map/ppermute | solution.py:482
  36.3 4.9 %collective-permute-done.8.near.tnear = f32[177,8,128]{2,1,0:T(8,128)S(1)} collective-permute-done((f32[177,8,128]{2,1,0:T(8,128)S(1)}, f32[177,8,128]{2,1,0:T(8,128)S(1)}, u32[]{:S(2)}, u32[]{:S(2)}) %collective-permute-start.8) | collective-permute-done | bytes 725024 | tf_op jit(solution)/shard_map/ppermute | solution.py:482
  41.2 0.2 coefficients.1
  41.5 1.4 %front.2 = (f32[68,4,8,128]{3,2,1,0:T(8,128)S(1)}, f32[2,16,4,8,128]{4,3,2,1,0:T(8,128)S(1)}, f32[26,4,8,128]{3,2,1,0:T(8,128)S(1)}, f32[26,4,8,128]{3,2,1,0:T(8,128)S(1)}) custom-call(f32[177,8,128]{2,1,0:T(8,128)S(1)} %collective-permute-done.7.far.tfar, f32[177,8,128]{2,1,0:T(8,128)S(1)} %collective-permute-done.8.near.tnear, ...), custom_call_target="tpu_custom_call" | custom-call | tf_op jit(solution)/shard_map/front/pallas_call | solution.py:519
  42.9 0.1 collective-permute-start.9
  43.0 3.9 %collective-permute-start.10 = (f32[26,4,8,128]{3,2,1,0:T(8,128)S(1)}, f32[26,4,8,128]{3,2,1,0:T(8,128)S(1)}, u32[]{:S(2)}, u32[]{:S(2)}) collective-permute-start(f32[26,4,8,128]{3,2,1,0:T(8,128)S(1)} %get-tuple-element.65), channel_id=1, source_target_pairs={{0,32},{1,2},{2,1},{3,4},{4,3},{5,6},{6,5},{7,8},{8,7},{9,10},{10,... | collective-permute-start | bytes 1277960 | tf_op jit(solution)/shard_map/ppermute | solution.py:482
  46.9 7.3 %collective-permute-done.9.far = f32[26,4,8,128]{3,2,1,0:T(8,128)S(1)} collective-permute-done((f32[26,4,8,128]{3,2,1,0:T(8,128)S(1)}, f32[26,4,8,128]{3,2,1,0:T(8,128)S(1)}, u32[]{:S(2)}, u32[]{:S(2)}) %collective-permute-start.9) | collective-permute-done | bytes 426016 | tf_op jit(solution)/shard_map/ppermute | solution.py:482
  54.2 2.2 %collective-permute-done.10.near = f32[26,4,8,128]{3,2,1,0:T(8,128)S(1)} collective-permute-done((f32[26,4,8,128]{3,2,1,0:T(8,128)S(1)}, f32[26,4,8,128]{3,2,1,0:T(8,128)S(1)}, u32[]{:S(2)}, u32[]{:S(2)}) %collective-permute-start.10) | collective-permute-done | bytes 426016 | tf_op jit(solution)/shard_map/ppermute | solution.py:482
  56.4 0.9 middle.1
  57.4 0.1 collective-permute-start.11
  57.5 3.6 %collective-permute-start.12 = (f32[24,4,8,128]{3,2,1,0:T(8,128)S(1)}, f32[24,4,8,128]{3,2,1,0:T(8,128)S(1)}, u32[]{:S(2)}, u32[]{:S(2)}) collective-permute-start(f32[24,4,8,128]{3,2,1,0:T(8,128)S(1)} %get-tuple-element.69), channel_id=1, source_target_pairs={{0,32},{1,2},{2,1},{3,4},{4,3},{5,6},{6,5},{7,8},{8,7},{9,10},{10,... | collective-permute-start | bytes 1179656 | tf_op jit(solution)/shard_map/ppermute | solution.py:482
  61.1 0.9 collective-permute-start.14
  62.1 4.7 %collective-permute-done.13.row1 = f32[2,4,4,8,128]{4,3,2,1,0:T(8,128)S(1)} collective-permute-done((f32[2,4,4,8,128]{4,3,2,1,0:T(8,128)S(1)}, f32[2,4,4,8,128]{4,3,2,1,0:T(8,128)S(1)}, u32[]{:S(2)}, u32[]{:S(2)}) %collective-permute-start.13) | collective-permute-done | bytes 131104 | tf_op jit(solution)/shard_map/ppermute | solution.py:471
  66.7 0.4 collective-permute-done.11.far.far_x
  67.1 2.2 %collective-permute-done.12.near.near_x = f32[24,4,8,128]{3,2,1,0:T(8,128)S(1)} collective-permute-done((f32[24,4,8,128]{3,2,1,0:T(8,128)S(1)}, f32[24,4,8,128]{3,2,1,0:T(8,128)S(1)}, u32[]{:S(2)}, u32[]{:S(2)}) %collective-permute-start.12) | collective-permute-done | bytes 393248 | tf_op jit(solution)/shard_map/ppermute | solution.py:482
  69.4 0.3 collective-permute-start.15
  69.7 0.7 collective-permute-start.16
  70.4 5.3 %collective-permute-done.15.edge1 = f32[10,4,8,128]{3,2,1,0:T(8,128)S(1)} collective-permute-done((f32[10,4,8,128]{3,2,1,0:T(8,128)S(1)}, f32[10,4,8,128]{3,2,1,0:T(8,128)S(1)}, u32[]{:S(2)}, u32[]{:S(2)}) %collective-permute-start.15) | collective-permute-done | bytes 163872 | tf_op jit(solution)/shard_map/ppermute | solution.py:471
  75.7 1.4 %front.3 = (f32[68,4,8,128]{3,2,1,0:T(8,128)S(1)}, f32[2,16,4,8,128]{4,3,2,1,0:T(8,128)S(1)}, f32[26,4,8,128]{3,2,1,0:T(8,128)S(1)}, f32[26,4,8,128]{3,2,1,0:T(8,128)S(1)}) custom-call(f32[136,8,128]{2,1,0:T(8,128)S(1)} %bitcast.8, f32[136,8,128]{2,1,0:T(8,128)S(1)} %bitcast.7, f32[2,20,4,8,128]{4,3,2,1,0:T(8,128)S(1)} %get-tuple-element.77.own, ...), custom_call_target="tpu_custom_call" | custom-call | tf_op jit(solution)/shard_map/front/pallas_call | solution.py:519
  77.1 0.1 collective-permute-start.17
  77.2 3.3 %collective-permute-start.18 = (f32[26,4,8,128]{3,2,1,0:T(8,128)S(1)}, f32[26,4,8,128]{3,2,1,0:T(8,128)S(1)}, u32[]{:S(2)}, u32[]{:S(2)}) collective-permute-start(f32[26,4,8,128]{3,2,1,0:T(8,128)S(1)} %get-tuple-element.79), channel_id=1, source_target_pairs={{0,32},{1,2},{2,1},{3,4},{4,3},{5,6},{6,5},{7,8},{8,7},{9,10},{10,... | collective-permute-start | bytes 1277960 | tf_op jit(solution)/shard_map/ppermute | solution.py:482
  80.5 6.2 %collective-permute-done.17.far = f32[26,4,8,128]{3,2,1,0:T(8,128)S(1)} collective-permute-done((f32[26,4,8,128]{3,2,1,0:T(8,128)S(1)}, f32[26,4,8,128]{3,2,1,0:T(8,128)S(1)}, u32[]{:S(2)}, u32[]{:S(2)}) %collective-permute-start.17) | collective-permute-done | bytes 426016 | tf_op jit(solution)/shard_map/ppermute | solution.py:482
  86.7 2.2 %collective-permute-done.18.near = f32[26,4,8,128]{3,2,1,0:T(8,128)S(1)} collective-permute-done((f32[26,4,8,128]{3,2,1,0:T(8,128)S(1)}, f32[26,4,8,128]{3,2,1,0:T(8,128)S(1)}, u32[]{:S(2)}, u32[]{:S(2)}) %collective-permute-start.18) | collective-permute-done | bytes 426016 | tf_op jit(solution)/shard_map/ppermute | solution.py:482
  88.9 1.5 %last.1 = (f32[4,96,128]{2,1,0:T(8,128)S(1)}, f32[4,96,128]{2,1,0:T(8,128)S(1)}) custom-call(f32[26,4,8,128]{3,2,1,0:T(8,128)S(1)} %collective-permute-done.17.far, f32[26,4,8,128]{3,2,1,0:T(8,128)S(1)} %collective-permute-done.18.near, f32[2,16,4,8,128]{4,3,2,1,0:T(8,128)S(1)} %get-tuple-element.80.it, f32[68,4,8,128]{3,2,1,0:T(8,128)S(1)} %get-tuple-element.81.fixed, ...), custom_call_target="tpu_custom_call" | custom-call | tf_op jit(solution)/shard_map/last/pallas_call | solution.py:548
  90.4 0.1 collective-permute-start.19
  90.5 1.4 %collective-permute-done.19.other = f32[4,96,128]{2,1,0:T(8,128)S(1)} collective-permute-done((f32[4,96,128]{2,1,0:T(8,128)S(1)}, f32[4,96,128]{2,1,0:T(8,128)S(1)}, u32[]{:S(2)}, u32[]{:S(2)}) %collective-permute-start.19) | collective-permute-done | bytes 196640 | tf_op jit(solution)/shard_map/ppermute | solution.py:471
  91.9 2.2 %collective-permute-start.20 = (f32[2,96,128]{2,1,0:T(8,128)S(1)}, f32[2,96,128]{2,1,0:T(8,128)S(1)}, u32[]{:S(2)}, u32[]{:S(2)}) collective-permute-start(f32[2,96,128]{2,1,0:T(8,128)S(1)} %get-tuple-element.85), channel_id=1, source_target_pairs={{0,128},{32,160},{64,192},{96,224},{128,0},{160,32},{192,64},{224,... | collective-permute-start | bytes 294920 | tf_op jit(solution)/shard_map/ppermute | solution.py:559
  94.1 1.4 %collective-permute-start.21 = (f32[2,96,128]{2,1,0:T(8,128)S(1)}, f32[2,96,128]{2,1,0:T(8,128)S(1)}, u32[]{:S(2)}, u32[]{:S(2)}) collective-permute-start(f32[2,96,128]{2,1,0:T(8,128)S(1)} %get-tuple-element.86), channel_id=1, source_target_pairs={{0,64},{32,96},{64,0},{96,32},{128,192},{160,224},{192,128},{224,1... | collective-permute-start | bytes 294920 | tf_op jit(solution)/shard_map/ppermute | solution.py:559
  95.6 0.6 collective-permute-start.22
  96.2 2.5 %collective-permute-done.20.a = f32[2,96,128]{2,1,0:T(8,128)S(1)} collective-permute-done((f32[2,96,128]{2,1,0:T(8,128)S(1)}, f32[2,96,128]{2,1,0:T(8,128)S(1)}, u32[]{:S(2)}, u32[]{:S(2)}) %collective-permute-start.20) | collective-permute-done | bytes 98336 | tf_op jit(solution)/shard_map/ppermute | solution.py:559
  98.7 1.8 %collective-permute-done.21.b = f32[2,96,128]{2,1,0:T(8,128)S(1)} collective-permute-done((f32[2,96,128]{2,1,0:T(8,128)S(1)}, f32[2,96,128]{2,1,0:T(8,128)S(1)}, u32[]{:S(2)}, u32[]{:S(2)}) %collective-permute-start.21) | collective-permute-done | bytes 98336 | tf_op jit(solution)/shard_map/ppermute | solution.py:559
  100.5 0.9 collective-permute-done.22.c
  101.4 0.8 unpack.1
  (9 shorter events, 0.2 us)
Async XLA Ops:
  2.0 7.8 %collective-permute-start = (f32[232,128]{1,0:T(8,128)S(1)}, f32[232,128]{1,0:T(8,128)S(1)}, u32[]{:S(2)}, u32[]{:S(2)}) collective-permute-start(f32[232,128]{1,0:T(8,128)S(1)} %get-tuple-element.45), channel_id=1, source_target_pairs={{0,128},{32,160},{64,192},{96,224},{128,0},{160,32},{192,64},{224,... | collective-permute-start | bytes 356360 | tf_op jit(solution)/shard_map/ppermute | solution.py:462
  5.3 6.5 %collective-permute-start.1 = (f32[232,128]{1,0:T(8,128)S(1)}, f32[232,128]{1,0:T(8,128)S(1)}, u32[]{:S(2)}, u32[]{:S(2)}) collective-permute-start(f32[232,128]{1,0:T(8,128)S(1)} %get-tuple-element.46), channel_id=1, source_target_pairs={{0,64},{32,96},{64,0},{96,32},{128,192},{160,224},{192,128},{224,1... | collective-permute-start | bytes 356360 | tf_op jit(solution)/shard_map/ppermute | solution.py:462
  6.0 9.1 %collective-permute-start.2 = (f32[232,128]{1,0:T(8,128)S(1)}, f32[232,128]{1,0:T(8,128)S(1)}, u32[]{:S(2)}, u32[]{:S(2)}) collective-permute-start(f32[232,128]{1,0:T(8,128)S(1)} %get-tuple-element.47), channel_id=1, source_target_pairs={{0,192},{32,224},{64,128},{96,160},{128,64},{160,96},{192,0},{224,... | collective-permute-start | bytes 356360 | tf_op jit(solution)/shard_map/ppermute | solution.py:462
  6.3 8.7 %collective-permute-start.3 = (f32[232,128]{1,0:T(8,128)S(1)}, f32[232,128]{1,0:T(8,128)S(1)}, u32[]{:S(2)}, u32[]{:S(2)}) collective-permute-start(f32[232,128]{1,0:T(8,128)S(1)} %get-tuple-element.48), channel_id=1, source_target_pairs={{0,160},{32,128},{64,224},{96,192},{128,32},{160,0},{192,96},{224,... | collective-permute-start | bytes 356360 | tf_op jit(solution)/shard_map/ppermute | solution.py:462
  8.0 8.2 %collective-permute-start.4 = (f32[232,128]{1,0:T(8,128)S(1)}, f32[232,128]{1,0:T(8,128)S(1)}, u32[]{:S(2)}, u32[]{:S(2)}) collective-permute-start(f32[232,128]{1,0:T(8,128)S(1)} %get-tuple-element.49), channel_id=1, source_target_pairs={{0,96},{32,64},{64,32},{96,0},{128,224},{160,192},{192,160},{224,1... | collective-permute-start | bytes 356360 | tf_op jit(solution)/shard_map/ppermute | solution.py:462
  9.8 6.8 %collective-permute-start.5 = (f32[232,128]{1,0:T(8,128)S(1)}, f32[232,128]{1,0:T(8,128)S(1)}, u32[]{:S(2)}, u32[]{:S(2)}) collective-permute-start(f32[232,128]{1,0:T(8,128)S(1)} %get-tuple-element.50), channel_id=1, source_target_pairs={{0,224},{32,192},{64,160},{96,128},{128,96},{160,64},{192,32},{224... | collective-permute-start | bytes 356360 | tf_op jit(solution)/shard_map/ppermute | solution.py:462
  11.8 4.8 %collective-permute-start.6 = (f32[232,128]{1,0:T(8,128)S(1)}, f32[232,128]{1,0:T(8,128)S(1)}, u32[]{:S(2)}, u32[]{:S(2)}) collective-permute-start(f32[232,128]{1,0:T(8,128)S(1)} %get-tuple-element.51), channel_id=1, source_target_pairs={{0,32},{32,0},{64,96},{96,64},{128,160},{160,128},{192,224},{224,1... | collective-permute-start | bytes 356360 | tf_op jit(solution)/shard_map/ppermute | solution.py:462
  17.6 18.7 %collective-permute-start.7 = (f32[177,8,128]{2,1,0:T(8,128)S(1)}, f32[177,8,128]{2,1,0:T(8,128)S(1)}, u32[]{:S(2)}, u32[]{:S(2)}) collective-permute-start(f32[177,8,128]{2,1,0:T(8,128)S(1)} %get-tuple-element.56), channel_id=1, source_target_pairs={{0,1},{1,0},{2,3},{3,2},{4,5},{5,4},{6,7},{7,6},{8,9},{9,8},{10,11... | collective-permute-start | bytes 2174984 | tf_op jit(solution)/shard_map/ppermute | solution.py:482
  19.6 21.6 %collective-permute-start.8 = (f32[177,8,128]{2,1,0:T(8,128)S(1)}, f32[177,8,128]{2,1,0:T(8,128)S(1)}, u32[]{:S(2)}, u32[]{:S(2)}) collective-permute-start(f32[177,8,128]{2,1,0:T(8,128)S(1)} %get-tuple-element.57), channel_id=1, source_target_pairs={{0,32},{1,2},{2,1},{3,4},{4,3},{5,6},{6,5},{7,8},{8,7},{9,10},{10,... | collective-permute-start | bytes 2174984 | tf_op jit(solution)/shard_map/ppermute | solution.py:482
  42.9 11.3 %collective-permute-start.9 = (f32[26,4,8,128]{3,2,1,0:T(8,128)S(1)}, f32[26,4,8,128]{3,2,1,0:T(8,128)S(1)}, u32[]{:S(2)}, u32[]{:S(2)}) collective-permute-start(f32[26,4,8,128]{3,2,1,0:T(8,128)S(1)} %get-tuple-element.64), channel_id=1, source_target_pairs={{0,1},{1,0},{2,3},{3,2},{4,5},{5,4},{6,7},{7,6},{8,9},{9,8},{10,11... | collective-permute-start | bytes 1277960 | tf_op jit(solution)/shard_map/ppermute | solution.py:482
  43.0 13.4 %collective-permute-start.10 = (f32[26,4,8,128]{3,2,1,0:T(8,128)S(1)}, f32[26,4,8,128]{3,2,1,0:T(8,128)S(1)}, u32[]{:S(2)}, u32[]{:S(2)}) collective-permute-start(f32[26,4,8,128]{3,2,1,0:T(8,128)S(1)} %get-tuple-element.65), channel_id=1, source_target_pairs={{0,32},{1,2},{2,1},{3,4},{4,3},{5,6},{6,5},{7,8},{8,7},{9,10},{10,... | collective-permute-start | bytes 1277960 | tf_op jit(solution)/shard_map/ppermute | solution.py:482
  57.4 9.7 %collective-permute-start.11 = (f32[24,4,8,128]{3,2,1,0:T(8,128)S(1)}, f32[24,4,8,128]{3,2,1,0:T(8,128)S(1)}, u32[]{:S(2)}, u32[]{:S(2)}) collective-permute-start(f32[24,4,8,128]{3,2,1,0:T(8,128)S(1)} %get-tuple-element.68), channel_id=1, source_target_pairs={{0,1},{1,0},{2,3},{3,2},{4,5},{5,4},{6,7},{7,6},{8,9},{9,8},{10,11... | collective-permute-start | bytes 1179656 | tf_op jit(solution)/shard_map/ppermute | solution.py:482
  57.5 11.8 %collective-permute-start.12 = (f32[24,4,8,128]{3,2,1,0:T(8,128)S(1)}, f32[24,4,8,128]{3,2,1,0:T(8,128)S(1)}, u32[]{:S(2)}, u32[]{:S(2)}) collective-permute-start(f32[24,4,8,128]{3,2,1,0:T(8,128)S(1)} %get-tuple-element.69), channel_id=1, source_target_pairs={{0,32},{1,2},{2,1},{3,4},{4,3},{5,6},{6,5},{7,8},{8,7},{9,10},{10,... | collective-permute-start | bytes 1179656 | tf_op jit(solution)/shard_map/ppermute | solution.py:482
  61.1 5.6 %collective-permute-start.13 = (f32[2,4,4,8,128]{4,3,2,1,0:T(8,128)S(1)}, f32[2,4,4,8,128]{4,3,2,1,0:T(8,128)S(1)}, u32[]{:S(2)}, u32[]{:S(2)}) collective-permute-start(f32[2,4,4,8,128]{4,3,2,1,0:T(8,128)S(1)} %get-tuple-element.70), channel_id=1, source_target_pairs={{32,64},{64,32},{96,128},{128,96},{160,192},{192,160},{224,0},{0,2... | collective-permute-start | bytes 393224 | tf_op jit(solution)/shard_map/ppermute | solution.py:471
  61.1 5.6 %collective-permute-start.14 = (f32[2,4,4,8,128]{4,3,2,1,0:T(8,128)S(1)}, f32[2,4,4,8,128]{4,3,2,1,0:T(8,128)S(1)}, u32[]{:S(2)}, u32[]{:S(2)}) collective-permute-start(f32[2,4,4,8,128]{4,3,2,1,0:T(8,128)S(1)} %get-tuple-element.71), channel_id=1, source_target_pairs={{0,32},{32,0},{64,96},{96,64},{128,160},{160,128},{192,224},{224,1... | collective-permute-start | bytes 393224 | tf_op jit(solution)/shard_map/ppermute | solution.py:471
  69.4 6.2 %collective-permute-start.15 = (f32[10,4,8,128]{3,2,1,0:T(8,128)S(1)}, f32[10,4,8,128]{3,2,1,0:T(8,128)S(1)}, u32[]{:S(2)}, u32[]{:S(2)}) collective-permute-start(f32[10,4,8,128]{3,2,1,0:T(8,128)S(1)} %get-tuple-element.73), channel_id=1, source_target_pairs={{32,64},{64,32},{96,128},{128,96},{160,192},{192,160},{224,0},{0,2... | collective-permute-start | bytes 491528 | tf_op jit(solution)/shard_map/ppermute | solution.py:471
  69.7 5.9 %collective-permute-start.16 = (f32[10,4,8,128]{3,2,1,0:T(8,128)S(1)}, f32[10,4,8,128]{3,2,1,0:T(8,128)S(1)}, u32[]{:S(2)}, u32[]{:S(2)}) collective-permute-start(f32[10,4,8,128]{3,2,1,0:T(8,128)S(1)} %get-tuple-element.74), channel_id=1, source_target_pairs={{0,32},{32,0},{64,96},{96,64},{128,160},{160,128},{192,224},{224,1... | collective-permute-start | bytes 491528 | tf_op jit(solution)/shard_map/ppermute | solution.py:471
  77.1 9.5 %collective-permute-start.17 = (f32[26,4,8,128]{3,2,1,0:T(8,128)S(1)}, f32[26,4,8,128]{3,2,1,0:T(8,128)S(1)}, u32[]{:S(2)}, u32[]{:S(2)}) collective-permute-start(f32[26,4,8,128]{3,2,1,0:T(8,128)S(1)} %get-tuple-element.78), channel_id=1, source_target_pairs={{0,1},{1,0},{2,3},{3,2},{4,5},{5,4},{6,7},{7,6},{8,9},{9,8},{10,11... | collective-permute-start | bytes 1277960 | tf_op jit(solution)/shard_map/ppermute | solution.py:482
  77.2 11.7 %collective-permute-start.18 = (f32[26,4,8,128]{3,2,1,0:T(8,128)S(1)}, f32[26,4,8,128]{3,2,1,0:T(8,128)S(1)}, u32[]{:S(2)}, u32[]{:S(2)}) collective-permute-start(f32[26,4,8,128]{3,2,1,0:T(8,128)S(1)} %get-tuple-element.79), channel_id=1, source_target_pairs={{0,32},{1,2},{2,1},{3,4},{4,3},{5,6},{6,5},{7,8},{8,7},{9,10},{10,... | collective-permute-start | bytes 1277960 | tf_op jit(solution)/shard_map/ppermute | solution.py:482
  90.4 1.5 %collective-permute-start.19 = (f32[4,96,128]{2,1,0:T(8,128)S(1)}, f32[4,96,128]{2,1,0:T(8,128)S(1)}, u32[]{:S(2)}, u32[]{:S(2)}) collective-permute-start(f32[4,96,128]{2,1,0:T(8,128)S(1)} %get-tuple-element.83), channel_id=1, source_target_pairs={{0,32},{32,0},{64,96},{96,64},{128,160},{160,128},{192,224},{224,1... | collective-permute-start | bytes 589832 | tf_op jit(solution)/shard_map/ppermute | solution.py:471
  91.9 6.7 %collective-permute-start.20 = (f32[2,96,128]{2,1,0:T(8,128)S(1)}, f32[2,96,128]{2,1,0:T(8,128)S(1)}, u32[]{:S(2)}, u32[]{:S(2)}) collective-permute-start(f32[2,96,128]{2,1,0:T(8,128)S(1)} %get-tuple-element.85), channel_id=1, source_target_pairs={{0,128},{32,160},{64,192},{96,224},{128,0},{160,32},{192,64},{224,... | collective-permute-start | bytes 294920 | tf_op jit(solution)/shard_map/ppermute | solution.py:559
  94.1 6.4 %collective-permute-start.21 = (f32[2,96,128]{2,1,0:T(8,128)S(1)}, f32[2,96,128]{2,1,0:T(8,128)S(1)}, u32[]{:S(2)}, u32[]{:S(2)}) collective-permute-start(f32[2,96,128]{2,1,0:T(8,128)S(1)} %get-tuple-element.86), channel_id=1, source_target_pairs={{0,64},{32,96},{64,0},{96,32},{128,192},{160,224},{192,128},{224,1... | collective-permute-start | bytes 294920 | tf_op jit(solution)/shard_map/ppermute | solution.py:559
  95.6 5.8 %collective-permute-start.22 = (f32[2,96,128]{2,1,0:T(8,128)S(1)}, f32[2,96,128]{2,1,0:T(8,128)S(1)}, u32[]{:S(2)}, u32[]{:S(2)}) collective-permute-start(f32[2,96,128]{2,1,0:T(8,128)S(1)} %get-tuple-element.87), channel_id=1, source_target_pairs={{0,192},{32,224},{64,128},{96,160},{128,64},{160,96},{192,0},{224,... | collective-permute-start | bytes 294920 | tf_op jit(solution)/shard_map/ppermute | solution.py:559

commit v10 on v9

--- a/solution.py
+++ b/solution.py
@@ -137,7 +137,6 @@
 def coefficient_body(far, near, here, consts, weights, inv):
     t, s = place()
     flip = s & 1
-    near, far = ([side[168 + 3 * i : 171 + 3 * i].reshape(TALL, 128) for i in range(3)] for side in (near, far))
     kappa = [near[1], near[0], here[0], here[1], far[0], far[1]]
     for p in range(6):
         plane = jnp.where(flip == 1, 2 * s + 3 - p, 2 * s - 2 + p)
@@ -186,10 +185,7 @@
 
 
 def spread_body(*rest):
-    pieces, (near_c, far_c, forward), (own, wish, near, far), stage = rest[:8], rest[8:11], rest[11:15], rest[15]
-    for i in range(3):
-        near[168 + 3 * i : 171 + 3 * i] = near_c[i].reshape(3, 8, 128)
-        far[168 + 3 * i : 171 + 3 * i] = far_c[i].reshape(3, 8, 128)
+    pieces, forward, (own, wish, near, far), stage = rest[:8], rest[10], rest[11:15], rest[15]
     t, _ = place()
     rows = PIECE
     for k, piece in zip(ORDER + (0,), pieces):
@@ -271,55 +267,92 @@
     return v + pltpu.roll(v, 1, 0)
 
 
-def front_body(far, near, own, wish, tnear, tfar, weights, consts, inv, fixed, it, out_near, out_far, zed):
+def own_sum(v, other, py, my, w, p):
+    up = pltpu.roll(v, 127, 1)
+    down = pltpu.roll(v, 1, 1)
+    return ((w[0] if p == 2 else w[1]) * other + (w[2] * py + w[3] * my)) + (w[4] * up + w[5] * down)
+
+
+def kept_parts(v, wanted, begin, consts):
+    phase_a, phase_b, last_a, last_b, first_a, first_b, slot = (consts[i] for i in range(3, 10))
+    begin = begin - over_sublanes(last_a * v[0] + last_b * v[1])
+    first = over_sublanes(first_a * v[2] + first_b * v[3])
+    return begin, slot * begin, -TAU * wanted[0] - phase_a * first, -TAU * wanted[1] - phase_b * first
+
+
+def prepare_body(own, wish, weights, consts, kept, part):
+    for p in (2, 3):
+        def row(j, carry, p=p):
+            x = p - 2
+            w = row_weights(weights, p, j, 8)
+            v = [own[x, j, c] for c in range(4)]
+            at = region(p, j)
+            for c, k in enumerate(kept_parts(v, (wish[x, j - 1, 0], wish[x, j - 1, 1]), w[7], consts)):
+                kept[at, c] = k
+                part[at, c] = k + own_sum(v[c], own[1 - x, j, c], own[x, j + 1, c], own[x, j - 1, c], w, p)
+            return carry
+        rows(1, 19, row)
+
+
+def ahead_body(it, kept, weights, part):
+    for p in (2, 3):
+        def row(j, carry, p=p):
+            x = p - 2
+            w = row_weights(weights, p, j, 6)
+            for c in range(4):
+                around = own_sum(it[x, j - 2, c], it[1 - x, j - 2, c], it[x, j - 1, c], it[x, j - 3, c], w, p)
+                part[x * 14 + j - 3, c] = kept[region(p, j), c] + around
+            return carry
+        rows(3, 17, row)
+
+
+def front_body(far, near, own, tnear, tfar, weights, consts, inv, kept, part, side, it, out_near, out_far, zed):
     def field(p, j, c):
         if p == 2 or p == 3:
             return own[p - 2, j, c]
-        side = near if p < 2 else far
+        got = near if p < 2 else far
         if p == 1 or p == 4:
-            return side[(j - 1) * 4 + c]
-        return side[72 + (j - 2) * 4 + c]
-
-    def wanted(p, j, n):
-        if p == 2 or p == 3:
-            return wish[p - 2, j - 1, n]
-        return (tnear if p == 1 else tfar)[136 + (j - 2) * 2 + n]
+            return got[(j - 1) * 4 + c]
+        return got[72 + (j - 2) * 4 + c]
 
     cs = (consts[0], consts[1], consts[2])
-    phase_a, phase_b, last_a, last_b, first_a, first_b, slot = (consts[i] for i in range(3, 10))
-    for p, lo, hi in ((2, 1, 19), (3, 1, 19), (1, 2, 18), (4, 2, 18)):
-        def row(j, carry, p=p):
-            w = row_weights(weights, p, j, 8)
-            v = [field(p, j, c) for c in range(4)]
-            last = over_sublanes(last_a * v[0] + last_b * v[1])
-            first = over_sublanes(first_a * v[2] + first_b * v[3])
-            begin = w[7] - last
-            kept = (
-                begin,
-                slot * begin,
-                -TAU * wanted(p, j, 0) - phase_a * first,
-                -TAU * wanted(p, j, 1) - phase_b * first,
-            )
-            at = region(p, j)
-            pushed = []
-            for c in range(4):
-                fixed[at, c] = kept[c]
-                around = (field(p + 1, j, c), field(p - 1, j, c), field(p, j + 1, c), field(p, j - 1, c))
-                pushed.append(kept[c] + spread_sum(v[c], around, w))
-            z = solve(pushed, w[6], (inv[at, 0], inv[at, 1]), cs)
-            for c in range(4):
-                zed[at, c] = z[c]
-            return carry
-        rows(lo, hi, row)
-
     for p in (2, 3):
         def row(j, carry, p=p):
             w = row_weights(weights, p, j, 8)
             at = region(p, j)
             pushed = []
             for c in range(4):
+                pushed.append(part[at, c] + (w[1] * field(1, j, c) if p == 2 else w[0] * field(4, j, c)))
+            z = solve(pushed, w[6], (inv[at, 0], inv[at, 1]), cs)
+            for c in range(4):
+                zed[at, c] = z[c]
+            return carry
+        rows(1, 19, row)
+    for p in (1, 4):
+        def row(j, carry, p=p):
+            w = row_weights(weights, p, j, 8)
+            v = [field(p, j, c) for c in range(4)]
+            wanted = [(tnear if p == 1 else tfar)[136 + (j - 2) * 2 + n] for n in range(2)]
+            at = region(p, j)
+            pushed = []
+            for c, k in enumerate(kept_parts(v, wanted, w[7], consts)):
+                side[at - 36, c] = k
+                around = (field(p + 1, j, c), field(p - 1, j, c), field(p, j + 1, c), field(p, j - 1, c))
+                pushed.append(k + spread_sum(v[c], around, w))
+            z = solve(pushed, w[6], (inv[at, 0], inv[at, 1]), cs)
+            for c in range(4):
+                zed[at, c] = z[c]
+            return carry
+        rows(2, 18, row)
+
+    for p in (2, 3):
+        def row(j, carry, p=p):
+            w = row_weights(weights, p, j, 8)
+            at = region(p, j)
+            pushed = []
+            for c in range(4):
                 around = (zed[region(p + 1, j), c], zed[region(p - 1, j), c], zed[at + 1, c], zed[at - 1, c])
-                pushed.append(fixed[at, c] + spread_sum(zed[at, c], around, w))
+                pushed.append(kept[at, c] + spread_sum(zed[at, c], around, w))
             z = solve(pushed, w[6], (inv[at, 0], inv[at, 1]), cs)
             for c in range(4):
                 it[p - 2, j - 2, c] = z[c]
@@ -331,7 +364,7 @@
     out_far[14:26] = it[0, 2:14]
 
 
-def sweep_body(it, near, far, fixed, weights, consts, inv, zed, put):
+def sweep_body(it, near, far, kept, side, part, weights, consts, inv, zed, put):
     def guess(p, j, c):
         if p == 2 or p == 3:
             return it[p - 2, j - 2, c]
@@ -352,8 +385,12 @@
             at = region(p, j)
             pushed = []
             for c in range(4):
+                if p == 2 or p == 3:
+                    beside = w[1] * guess(1, j, c) if p == 2 else w[0] * guess(4, j, c)
+                    pushed.append(part[at2(p, j), c] + beside)
+                    continue
                 around = (guess(p + 1, j, c), guess(p - 1, j, c), guess(p, j + 1, c), guess(p, j - 1, c))
-                pushed.append(fixed[at, c] + spread_sum(guess(p, j, c), around, w))
+                pushed.append(side[at - 36, c] + spread_sum(guess(p, j, c), around, w))
             z = solve(pushed, w[6], (inv[at, 0], inv[at, 1]), cs)
             for c in range(4):
                 zed[at2(p, j), c] = z[c]
@@ -367,7 +404,7 @@
             pushed = []
             for c in range(4):
                 around = (zed[at2(p + 1, j), c], zed[at2(p - 1, j), c], zed[here + 1, c], zed[here - 1, c])
-                pushed.append(fixed[at, c] + spread_sum(zed[here, c], around, w))
+                pushed.append(kept[at, c] + spread_sum(zed[here, c], around, w))
             z = solve(pushed, w[6], (inv[at, 0], inv[at, 1]), cs)
             for c in range(4):
                 put(p - 2, j - 4, c, z[c])
@@ -375,13 +412,13 @@
         rows(4, 16, row)
 
 
-def middle_body(far, near, it, fixed, weights, consts, inv, new, out_near, out_far, send0, send1, zed):
+def middle_body(far, near, it, kept, side, part, weights, consts, inv, new, out_near, out_far, send0, send1, zed):
     def put(x, j, c, v):
         new[x, j, c] = v
         first, second = (out_near, out_far) if x == 0 else (out_far, out_near)
         first[j, c] = v
         second[OWN + j, c] = v
-    sweep_body(far=far, near=near, it=it, fixed=fixed, weights=weights, consts=consts, inv=inv, zed=zed, put=put)
+    sweep_body(far=far, near=near, it=it, kept=kept, side=side, part=part, weights=weights, consts=consts, inv=inv, zed=zed, put=put)
     odd = place()[0] & 1
     for x in range(2):
         send0[x] = new[x, pl.ds((OWN - HALO) * (1 - odd), HALO)]
@@ -411,11 +448,11 @@
             side[pl.ds(18 + 14 * high, 2)] = edge[6 + 2 * i : 8 + 2 * i]
 
 
-def last_body(far, near, it, fixed, weights, consts, inv, back, *rest):
+def last_body(far, near, it, kept, side, part, weights, consts, inv, back, *rest):
     outs, (zed, fin, stage) = rest[:2], rest[2:]
     def put(x, j, c, v):
         fin[x * OWN + j, c] = v
-    sweep_body(far=far, near=near, it=it, fixed=fixed, weights=weights, consts=consts, inv=inv, zed=zed, put=put)
+    sweep_body(far=far, near=near, it=it, kept=kept, side=side, part=part, weights=weights, consts=consts, inv=inv, zed=zed, put=put)
     t, _ = place()
     matrix = back[...]
     for low in range(0, 2 * OWN, 4):
@@ -500,29 +537,33 @@
         far_inputs=8,
     )(*(pltpu.with_memory_space_constraint(a, pltpu.HBM) for a in arguments))
     got = exchange(pieces)
+    far_c = swap_planes(far_c, 0)
+    near_c = swap_planes(near_c, 1)
     own, wish, near, far = call(
         spread_body,
         "spread",
-        [whole(2, WIN, 4, 8, 128), whole(2, 18, 2, 8, 128), whole(177, 8, 128), whole(177, 8, 128)],
+        [whole(2, WIN, 4, 8, 128), whole(2, 18, 2, 8, 128), whole(168, 8, 128), whole(168, 8, 128)],
         11,
         [pltpu.VMEM((8 * PIECE, 128), jnp.float32)],
-    )(*got, near_c, far_c, forward)
+    )(*got, far_c, near_c, forward)
     far = far_first = swap_planes(far, 0)
     near = near_first = swap_planes(near, 1)
     weights, inv = call(
         coefficient_body, "coefficients", [whole(4 * TALL * 8, 128), whole(68, 2, 8, 128)], 4
-    )(far, near, here_c, consts)
+    )(far_c, near_c, here_c, consts)
     weights = weights.reshape(4 * TALL, 8, 128)
 
     sweep_scratch = [pltpu.VMEM((52, 4, 8, 128), jnp.float32)]
     for outer in range(OUTER):
-        fixed, it, near_z, far_z = call(
+        kept, part = call(prepare_body, "prepare", [whole(36, 4, 8, 128)] * 2, 4)(own, wish, weights, consts)
+        side, it, near_z, far_z = call(
             front_body,
             "front",
-            [whole(68, 4, 8, 128), whole(2, 16, 4, 8, 128), whole(26, 4, 8, 128), whole(26, 4, 8, 128)],
-            9,
+            [whole(32, 4, 8, 128), whole(2, 16, 4, 8, 128), whole(26, 4, 8, 128), whole(26, 4, 8, 128)],
+            10,
             [pltpu.VMEM((68, 4, 8, 128), jnp.float32)],
-        )(far, near, own, wish, near_first, far_first, weights, consts, inv)
+        )(far, near, own, near_first, far_first, weights, consts, inv, kept, part)
+        ahead = call(ahead_body, "ahead", [whole(28, 4, 8, 128)], 3)(it, kept, weights)[0]
         far_z = swap_planes(far_z, 0)
         near_z = swap_planes(near_z, 1)
         if outer < OUTER - 1:
@@ -530,9 +571,9 @@
                 middle_body,
                 "middle",
                 [whole(2, OWN, 4, 8, 128)] + [whole(2 * OWN, 4, 8, 128)] * 2 + [whole(2, HALO, 4, 8, 128)] * 2,
-                7,
+                9,
                 sweep_scratch,
-            )(far_z, near_z, it, fixed, weights, consts, inv)
+            )(far_z, near_z, it, kept, side, ahead, weights, consts, inv)
             far = swap_planes(far, 0)
             near = swap_planes(near, 1)
             row1 = swap_rows(row1, 1)
@@ -549,9 +590,9 @@
         last_body,
         "last",
         [whole(4, 8 * OWN, 128)] * 2,
-        8,
+        10,
         sweep_scratch + [pltpu.VMEM((2 * OWN, 4, 8, 128), jnp.float32), pltpu.VMEM((64 * OWN, 128), jnp.float32)],
-    )(far_z, near_z, it, fixed, weights, consts, inv, back)
+    )(far_z, near_z, it, kept, side, ahead, weights, consts, inv, back)
     other = swap_rows(other, 0)
     pairs = call(merge_body, "merge", [whole(2, 8 * OWN, 128)] * 3, 2)(other, mine)
     count = lax.axis_size("tm")

time: 103 us -> 104 us (level)
  waiting for transfers between devices: 58.9 us -> 64.7 us
  starting transfers between devices: 33.7 us -> 28.8 us
    ppermute x8 -> x10, waiting for transfers between devices: 36.9 us -> 40.7 us  [swap_planes(): return lax.ppermute(block, ('tm', 'space'), route)]
    ppermute x8 -> x10, starting transfers between devices: 18.3 us -> 16.6 us  [swap_planes(): return lax.ppermute(block, ('tm', 'space'), route)]
    ppermute x5, starting transfers between devices: 1.98 us -> 0.28 us  [swap_rows(): return lax.ppermute(block, 'tm', route)]
    ppermute x7, starting transfers between devices: 9.17 us -> 7.79 us  [exchange(): lax.ppermute(pieces[k], 'tm', [(i, i ^ k) for i in range(count)])]
    ppermute x5, waiting for transfers between devices: 11.4 us -> 12.5 us  [swap_rows(): return lax.ppermute(block, 'tm', route)]
    pallas_call x3 -> x7, Pallas kernels: 4.35 us -> 4.72 us  [the longest x2 2.06 us: on_device(): call(front_body, 'front', [whole(32, 4, 8, 128), whole(2, 16, 4, 8, 128),...]
  transfers between devices with their start and end apart: 23 -> 25, of which waited for: 18 -> 17; matrix products, arithmetic and copies ran while one was open for 0% -> 0% of each run, Pallas kernels for 0% -> 2%
where the time goes in v10:
time: 104 us; the launch traced here: 103 us
  waiting for transfers between devices  64.7 us (62%)
  starting transfers between devices  28.8 us (28%)
  Pallas kernels  9.03 us (9%)
    ppermute x10, waiting for transfers between devices, swap_planes(): return lax.ppermute(block, ('tm', 'space'), route)  40.7 us
    ppermute x10, starting transfers between devices, swap_planes(): return lax.ppermute(block, ('tm', 'space'), route)  16.6 us
    ppermute x5, waiting for transfers between devices, swap_rows(): return lax.ppermute(block, 'tm', route)  12.5 us
    ppermute x7, starting transfers between devices, exchange(): lax.ppermute(pieces[k], 'tm', [(i, i ^ k) for i in range(count)])  7.79 us
    ppermute x7, waiting for transfers between devices, exchange(): lax.ppermute(pieces[k], 'tm', [(i, i ^ k) for i in range(count)])  6.31 us
    ppermute x3, waiting for transfers between devices, on_device(): lax.ppermute(pair, 'tm', [(i, i ^ 2 * k) for i in range(count)])  5.17 us
    ppermute x3, starting transfers between devices, on_device(): lax.ppermute(pair, 'tm', [(i, i ^ 2 * k) for i in range(count)])  4.18 us
  transfers between devices with their start and end apart: 25, of which 17 were waited for; matrix products, arithmetic and copies ran while one was open for 0% of the time, Pallas kernels for 2%

profile of v10, /device:TPU:6, one launch (start us, length us, event | category | flops | bytes accessed | tf_op | source)
XLA Modules:
  0.0 103.4 jit_solution(6589165876802250830)
XLA Ops:
  0.6 1.4 %pack.1 = (f32[232,128]{1,0:T(8,128)S(1)}, f32[232,128]{1,0:T(8,128)S(1)}, f32[232,128]{1,0:T(8,128)S(1)}, f32[232,128]{1,0:T(8,128)S(1)}, f32[232,128]{1,0:T(8,...) custom-call(f32[2,2,96,128]{3,2,1,0:T(8,128)} %rest_0_.1, ...), custom_call_target="tpu_custom_call" | custom-call | tf_op jit(solution)/shard_map/pack/pallas_call | solution.py:527
  2.0 3.3 %collective-permute-start = (f32[232,128]{1,0:T(8,128)S(1)}, f32[232,128]{1,0:T(8,128)S(1)}, u32[]{:S(2)}, u32[]{:S(2)}) collective-permute-start(f32[232,128]{1,0:T(8,128)S(1)} %get-tuple-element.49), channel_id=1, source_target_pairs={{0,128},{32,160},{64,192},{96,224},{128,0},{160,32},{192,64},{224,... | collective-permute-start | bytes 356360 | tf_op jit(solution)/shard_map/ppermute | solution.py:499
  5.3 0.7 collective-permute-start.1
  6.0 1.9 %collective-permute-start.7 = (f32[3,24,128]{2,1,0:T(8,128)S(1)}, f32[3,24,128]{2,1,0:T(8,128)S(1)}, u32[]{:S(2)}, u32[]{:S(2)}) collective-permute-start(f32[3,24,128]{2,1,0:T(8,128)S(1)} %get-tuple-element.57), channel_id=1, source_target_pairs={{0,1},{1,0},{2,3},{3,2},{4,5},{5,4},{6,7},{7,6},{8,9},{9,8},{10,11... | collective-permute-start | bytes 110600 | tf_op jit(solution)/shard_map/ppermute | solution.py:519
  7.9 5.2 %collective-permute-start.8 = (f32[3,24,128]{2,1,0:T(8,128)S(1)}, f32[3,24,128]{2,1,0:T(8,128)S(1)}, u32[]{:S(2)}, u32[]{:S(2)}) collective-permute-start(f32[3,24,128]{2,1,0:T(8,128)S(1)} %get-tuple-element.58), channel_id=1, source_target_pairs={{0,32},{1,2},{2,1},{3,4},{4,3},{5,6},{6,5},{7,8},{8,7},{9,10},{10,... | collective-permute-start | bytes 110600 | tf_op jit(solution)/shard_map/ppermute | solution.py:519
  13.1 0.4 collective-permute-start.2
  13.5 1.1 %collective-permute-start.3 = (f32[232,128]{1,0:T(8,128)S(1)}, f32[232,128]{1,0:T(8,128)S(1)}, u32[]{:S(2)}, u32[]{:S(2)}) collective-permute-start(f32[232,128]{1,0:T(8,128)S(1)} %get-tuple-element.52), channel_id=1, source_target_pairs={{0,160},{32,128},{64,224},{96,192},{128,32},{160,0},{192,96},{224,... | collective-permute-start | bytes 356360 | tf_op jit(solution)/shard_map/ppermute | solution.py:499
  14.5 0.5 collective-permute-done.8.rest_9_.near
  15.0 1.9 %collective-permute-start.4 = (f32[232,128]{1,0:T(8,128)S(1)}, f32[232,128]{1,0:T(8,128)S(1)}, u32[]{:S(2)}, u32[]{:S(2)}) collective-permute-start(f32[232,128]{1,0:T(8,128)S(1)} %get-tuple-element.53), channel_id=1, source_target_pairs={{0,96},{32,64},{64,32},{96,0},{128,224},{160,192},{192,160},{224,1... | collective-permute-start | bytes 356360 | tf_op jit(solution)/shard_map/ppermute | solution.py:499
  16.9 0.5 collective-permute-start.5
  17.4 4.8 %collective-permute-done.2.rest_2_ = f32[232,128]{1,0:T(8,128)S(1)} collective-permute-done((f32[232,128]{1,0:T(8,128)S(1)}, f32[232,128]{1,0:T(8,128)S(1)}, u32[]{:S(2)}, u32[]{:S(2)}) %collective-permute-start.2) | collective-permute-done | bytes 118816 | tf_op jit(solution)/shard_map/ppermute | solution.py:499
  22.2 1.5 %collective-permute-done.5.rest_5_ = f32[232,128]{1,0:T(8,128)S(1)} collective-permute-done((f32[232,128]{1,0:T(8,128)S(1)}, f32[232,128]{1,0:T(8,128)S(1)}, u32[]{:S(2)}, u32[]{:S(2)}) %collective-permute-start.5) | collective-permute-done | bytes 118816 | tf_op jit(solution)/shard_map/ppermute | solution.py:499
  23.7 1.0 spread.1
  24.7 0.1 collective-permute-start.9
  24.8 2.0 %collective-permute-start.10 = (f32[168,8,128]{2,1,0:T(8,128)S(1)}, f32[168,8,128]{2,1,0:T(8,128)S(1)}, u32[]{:S(2)}, u32[]{:S(2)}) collective-permute-start(f32[168,8,128]{2,1,0:T(8,128)S(1)} %get-tuple-element.61), channel_id=1, source_target_pairs={{0,32},{1,2},{2,1},{3,4},{4,3},{5,6},{6,5},{7,8},{8,7},{9,10},{10,... | collective-permute-start | bytes 2064392 | tf_op jit(solution)/shard_map/ppermute | solution.py:519
  26.8 0.2 coefficients.1
  27.0 0.4 prepare.2
  27.4 15.0 %collective-permute-done.9.far.tfar = f32[168,8,128]{2,1,0:T(8,128)S(1)} collective-permute-done((f32[168,8,128]{2,1,0:T(8,128)S(1)}, f32[168,8,128]{2,1,0:T(8,128)S(1)}, u32[]{:S(2)}, u32[]{:S(2)}) %collective-permute-start.9) | collective-permute-done | bytes 688160 | tf_op jit(solution)/shard_map/ppermute | solution.py:519
  42.5 2.2 %collective-permute-done.10.near.tnear = f32[168,8,128]{2,1,0:T(8,128)S(1)} collective-permute-done((f32[168,8,128]{2,1,0:T(8,128)S(1)}, f32[168,8,128]{2,1,0:T(8,128)S(1)}, u32[]{:S(2)}, u32[]{:S(2)}) %collective-permute-start.10) | collective-permute-done | bytes 688160 | tf_op jit(solution)/shard_map/ppermute | solution.py:519
  44.7 1.0 front.2
  45.8 2.1 %collective-permute-start.12 = (f32[26,4,8,128]{3,2,1,0:T(8,128)S(1)}, f32[26,4,8,128]{3,2,1,0:T(8,128)S(1)}, u32[]{:S(2)}, u32[]{:S(2)}) collective-permute-start(f32[26,4,8,128]{3,2,1,0:T(8,128)S(1)} %get-tuple-element.71), channel_id=1, source_target_pairs={{0,32},{1,2},{2,1},{3,4},{4,3},{5,6},{6,5},{7,8},{8,7},{9,10},{10,... | collective-permute-start | bytes 1277960 | tf_op jit(solution)/shard_map/ppermute | solution.py:519
  47.9 0.3 ahead.2.part
  48.2 8.8 %collective-permute-done.11.far = f32[26,4,8,128]{3,2,1,0:T(8,128)S(1)} collective-permute-done((f32[26,4,8,128]{3,2,1,0:T(8,128)S(1)}, f32[26,4,8,128]{3,2,1,0:T(8,128)S(1)}, u32[]{:S(2)}, u32[]{:S(2)}) %collective-permute-start.11) | collective-permute-done | bytes 426016 | tf_op jit(solution)/shard_map/ppermute | solution.py:519
  57.0 2.2 %collective-permute-done.12.near = f32[26,4,8,128]{3,2,1,0:T(8,128)S(1)} collective-permute-done((f32[26,4,8,128]{3,2,1,0:T(8,128)S(1)}, f32[26,4,8,128]{3,2,1,0:T(8,128)S(1)}, u32[]{:S(2)}, u32[]{:S(2)}) %collective-permute-start.12) | collective-permute-done | bytes 426016 | tf_op jit(solution)/shard_map/ppermute | solution.py:519
  59.2 0.7 middle.1
  60.0 0.1 collective-permute-start.13
  60.1 2.5 %collective-permute-start.14 = (f32[24,4,8,128]{3,2,1,0:T(8,128)S(1)}, f32[24,4,8,128]{3,2,1,0:T(8,128)S(1)}, u32[]{:S(2)}, u32[]{:S(2)}) collective-permute-start(f32[24,4,8,128]{3,2,1,0:T(8,128)S(1)} %get-tuple-element.75), channel_id=1, source_target_pairs={{0,32},{1,2},{2,1},{3,4},{4,3},{5,6},{6,5},{7,8},{8,7},{9,10},{10,... | collective-permute-start | bytes 1179656 | tf_op jit(solution)/shard_map/ppermute | solution.py:519
  62.5 5.6 %collective-permute-done.15.row1 = f32[2,4,4,8,128]{4,3,2,1,0:T(8,128)S(1)} collective-permute-done((f32[2,4,4,8,128]{4,3,2,1,0:T(8,128)S(1)}, f32[2,4,4,8,128]{4,3,2,1,0:T(8,128)S(1)}, u32[]{:S(2)}, u32[]{:S(2)}) %collective-permute-start.15) | collective-permute-done | bytes 131104 | tf_op jit(solution)/shard_map/ppermute | solution.py:508
  68.1 1.5 %collective-permute-done.13.far.far_x = f32[24,4,8,128]{3,2,1,0:T(8,128)S(1)} collective-permute-done((f32[24,4,8,128]{3,2,1,0:T(8,128)S(1)}, f32[24,4,8,128]{3,2,1,0:T(8,128)S(1)}, u32[]{:S(2)}, u32[]{:S(2)}) %collective-permute-start.13) | collective-permute-done | bytes 393248 | tf_op jit(solution)/shard_map/ppermute | solution.py:519
  69.7 2.4 %collective-permute-done.14.near.near_x = f32[24,4,8,128]{3,2,1,0:T(8,128)S(1)} collective-permute-done((f32[24,4,8,128]{3,2,1,0:T(8,128)S(1)}, f32[24,4,8,128]{3,2,1,0:T(8,128)S(1)}, u32[]{:S(2)}, u32[]{:S(2)}) %collective-permute-start.14) | collective-permute-done | bytes 393248 | tf_op jit(solution)/shard_map/ppermute | solution.py:519
  72.1 0.1 collective-permute-start.17
  72.3 0.4 prepare.3
  72.7 5.4 %collective-permute-done.17.edge1 = f32[10,4,8,128]{3,2,1,0:T(8,128)S(1)} collective-permute-done((f32[10,4,8,128]{3,2,1,0:T(8,128)S(1)}, f32[10,4,8,128]{3,2,1,0:T(8,128)S(1)}, u32[]{:S(2)}, u32[]{:S(2)}) %collective-permute-start.17) | collective-permute-done | bytes 163872 | tf_op jit(solution)/shard_map/ppermute | solution.py:508
  78.3 1.0 %front.3 = (f32[32,4,8,128]{3,2,1,0:T(8,128)S(1)}, f32[2,16,4,8,128]{4,3,2,1,0:T(8,128)S(1)}, f32[26,4,8,128]{3,2,1,0:T(8,128)S(1)}, f32[26,4,8,128]{3,2,1,0:T(8,128)S(1)}) custom-call(f32[136,8,128]{2,1,0:T(8,128)S(1)} %bitcast.12, f32[136,8,128]{2,1,0:T(8,128)S(1)} %bitcast.11, f32[2,20,4,8,128]{4,3,2,1,0:T(8,128)S(1)} %get-tuple-element.83.own, ...), custom_call_target="tpu_custom_call" | custom-call | tf_op jit(solution)/shard_map/front/pallas_call | solution.py:559
  79.4 2.5 %collective-permute-start.20 = (f32[26,4,8,128]{3,2,1,0:T(8,128)S(1)}, f32[26,4,8,128]{3,2,1,0:T(8,128)S(1)}, u32[]{:S(2)}, u32[]{:S(2)}) collective-permute-start(f32[26,4,8,128]{3,2,1,0:T(8,128)S(1)} %get-tuple-element.87), channel_id=1, source_target_pairs={{0,32},{1,2},{2,1},{3,4},{4,3},{5,6},{6,5},{7,8},{8,7},{9,10},{10,... | collective-permute-start | bytes 1277960 | tf_op jit(solution)/shard_map/ppermute | solution.py:519
  81.9 0.3 ahead.3.part
  82.2 5.9 %collective-permute-done.19.far = f32[26,4,8,128]{3,2,1,0:T(8,128)S(1)} collective-permute-done((f32[26,4,8,128]{3,2,1,0:T(8,128)S(1)}, f32[26,4,8,128]{3,2,1,0:T(8,128)S(1)}, u32[]{:S(2)}, u32[]{:S(2)}) %collective-permute-start.19) | collective-permute-done | bytes 426016 | tf_op jit(solution)/shard_map/ppermute | solution.py:519
  88.1 2.2 %collective-permute-done.20.near = f32[26,4,8,128]{3,2,1,0:T(8,128)S(1)} collective-permute-done((f32[26,4,8,128]{3,2,1,0:T(8,128)S(1)}, f32[26,4,8,128]{3,2,1,0:T(8,128)S(1)}, u32[]{:S(2)}, u32[]{:S(2)}) %collective-permute-start.20) | collective-permute-done | bytes 426016 | tf_op jit(solution)/shard_map/ppermute | solution.py:519
  90.3 1.3 %last.1 = (f32[4,96,128]{2,1,0:T(8,128)S(1)}, f32[4,96,128]{2,1,0:T(8,128)S(1)}) custom-call(f32[26,4,8,128]{3,2,1,0:T(8,128)S(1)} %collective-permute-done.19.far, f32[26,4,8,128]{3,2,1,0:T(8,128)S(1)} %collective-permute-done.20.near, f32[2,16,4,8,128]{4,3,2,1,0:T(8,128)S(1)} %get-tuple-element.88.it, f32[36,4,8,128]{3,2,1,0:T(8,128)S(1)} %get-tuple-element.84.kept, ...), custom_call_target="tpu_custom_call" | custom-call | tf_op jit(solution)/shard_map/last/pallas_call | solution.py:589
  91.5 0.1 collective-permute-start.21
  91.6 1.4 %collective-permute-done.21.other = f32[4,96,128]{2,1,0:T(8,128)S(1)} collective-permute-done((f32[4,96,128]{2,1,0:T(8,128)S(1)}, f32[4,96,128]{2,1,0:T(8,128)S(1)}, u32[]{:S(2)}, u32[]{:S(2)}) %collective-permute-start.21) | collective-permute-done | bytes 196640 | tf_op jit(solution)/shard_map/ppermute | solution.py:508
  93.1 2.2 %collective-permute-start.22 = (f32[2,96,128]{2,1,0:T(8,128)S(1)}, f32[2,96,128]{2,1,0:T(8,128)S(1)}, u32[]{:S(2)}, u32[]{:S(2)}) collective-permute-start(f32[2,96,128]{2,1,0:T(8,128)S(1)} %get-tuple-element.93), channel_id=1, source_target_pairs={{0,128},{32,160},{64,192},{96,224},{128,0},{160,32},{192,64},{224,... | collective-permute-start | bytes 294920 | tf_op jit(solution)/shard_map/ppermute | solution.py:600
  95.3 1.3 %collective-permute-start.23 = (f32[2,96,128]{2,1,0:T(8,128)S(1)}, f32[2,96,128]{2,1,0:T(8,128)S(1)}, u32[]{:S(2)}, u32[]{:S(2)}) collective-permute-start(f32[2,96,128]{2,1,0:T(8,128)S(1)} %get-tuple-element.94), channel_id=1, source_target_pairs={{0,64},{32,96},{64,0},{96,32},{128,192},{160,224},{192,128},{224,1... | collective-permute-start | bytes 294920 | tf_op jit(solution)/shard_map/ppermute | solution.py:600
  96.6 0.7 collective-permute-start.24
  97.3 3.0 %collective-permute-done.22.a = f32[2,96,128]{2,1,0:T(8,128)S(1)} collective-permute-done((f32[2,96,128]{2,1,0:T(8,128)S(1)}, f32[2,96,128]{2,1,0:T(8,128)S(1)}, u32[]{:S(2)}, u32[]{:S(2)}) %collective-permute-start.22) | collective-permute-done | bytes 98336 | tf_op jit(solution)/shard_map/ppermute | solution.py:600
  100.3 1.3 %collective-permute-done.23.b = f32[2,96,128]{2,1,0:T(8,128)S(1)} collective-permute-done((f32[2,96,128]{2,1,0:T(8,128)S(1)}, f32[2,96,128]{2,1,0:T(8,128)S(1)}, u32[]{:S(2)}, u32[]{:S(2)}) %collective-permute-start.23) | collective-permute-done | bytes 98336 | tf_op jit(solution)/shard_map/ppermute | solution.py:600
  101.6 0.8 collective-permute-done.24.c
  102.4 0.8 unpack.1
  (17 shorter events, 0.5 us)
Async XLA Ops:
  2.0 14.9 %collective-permute-start = (f32[232,128]{1,0:T(8,128)S(1)}, f32[232,128]{1,0:T(8,128)S(1)}, u32[]{:S(2)}, u32[]{:S(2)}) collective-permute-start(f32[232,128]{1,0:T(8,128)S(1)} %get-tuple-element.49), channel_id=1, source_target_pairs={{0,128},{32,160},{64,192},{96,224},{128,0},{160,32},{192,64},{224,... | collective-permute-start | bytes 356360 | tf_op jit(solution)/shard_map/ppermute | solution.py:499
  5.3 12.1 %collective-permute-start.1 = (f32[232,128]{1,0:T(8,128)S(1)}, f32[232,128]{1,0:T(8,128)S(1)}, u32[]{:S(2)}, u32[]{:S(2)}) collective-permute-start(f32[232,128]{1,0:T(8,128)S(1)} %get-tuple-element.50), channel_id=1, source_target_pairs={{0,64},{32,96},{64,0},{96,32},{128,192},{160,224},{192,128},{224,1... | collective-permute-start | bytes 356360 | tf_op jit(solution)/shard_map/ppermute | solution.py:499
  6.0 7.5 %collective-permute-start.7 = (f32[3,24,128]{2,1,0:T(8,128)S(1)}, f32[3,24,128]{2,1,0:T(8,128)S(1)}, u32[]{:S(2)}, u32[]{:S(2)}) collective-permute-start(f32[3,24,128]{2,1,0:T(8,128)S(1)} %get-tuple-element.57), channel_id=1, source_target_pairs={{0,1},{1,0},{2,3},{3,2},{4,5},{5,4},{6,7},{7,6},{8,9},{9,8},{10,11... | collective-permute-start | bytes 110600 | tf_op jit(solution)/shard_map/ppermute | solution.py:519
  7.9 7.1 %collective-permute-start.8 = (f32[3,24,128]{2,1,0:T(8,128)S(1)}, f32[3,24,128]{2,1,0:T(8,128)S(1)}, u32[]{:S(2)}, u32[]{:S(2)}) collective-permute-start(f32[3,24,128]{2,1,0:T(8,128)S(1)} %get-tuple-element.58), channel_id=1, source_target_pairs={{0,32},{1,2},{2,1},{3,4},{4,3},{5,6},{6,5},{7,8},{8,7},{9,10},{10,... | collective-permute-start | bytes 110600 | tf_op jit(solution)/shard_map/ppermute | solution.py:519
  13.1 9.1 %collective-permute-start.2 = (f32[232,128]{1,0:T(8,128)S(1)}, f32[232,128]{1,0:T(8,128)S(1)}, u32[]{:S(2)}, u32[]{:S(2)}) collective-permute-start(f32[232,128]{1,0:T(8,128)S(1)} %get-tuple-element.51), channel_id=1, source_target_pairs={{0,192},{32,224},{64,128},{96,160},{128,64},{160,96},{192,0},{224,... | collective-permute-start | bytes 356360 | tf_op jit(solution)/shard_map/ppermute | solution.py:499
  13.5 8.7 %collective-permute-start.3 = (f32[232,128]{1,0:T(8,128)S(1)}, f32[232,128]{1,0:T(8,128)S(1)}, u32[]{:S(2)}, u32[]{:S(2)}) collective-permute-start(f32[232,128]{1,0:T(8,128)S(1)} %get-tuple-element.52), channel_id=1, source_target_pairs={{0,160},{32,128},{64,224},{96,192},{128,32},{160,0},{192,96},{224,... | collective-permute-start | bytes 356360 | tf_op jit(solution)/shard_map/ppermute | solution.py:499
  15.0 7.2 %collective-permute-start.4 = (f32[232,128]{1,0:T(8,128)S(1)}, f32[232,128]{1,0:T(8,128)S(1)}, u32[]{:S(2)}, u32[]{:S(2)}) collective-permute-start(f32[232,128]{1,0:T(8,128)S(1)} %get-tuple-element.53), channel_id=1, source_target_pairs={{0,96},{32,64},{64,32},{96,0},{128,224},{160,192},{192,160},{224,1... | collective-permute-start | bytes 356360 | tf_op jit(solution)/shard_map/ppermute | solution.py:499
  16.9 6.8 %collective-permute-start.5 = (f32[232,128]{1,0:T(8,128)S(1)}, f32[232,128]{1,0:T(8,128)S(1)}, u32[]{:S(2)}, u32[]{:S(2)}) collective-permute-start(f32[232,128]{1,0:T(8,128)S(1)} %get-tuple-element.54), channel_id=1, source_target_pairs={{0,224},{32,192},{64,160},{96,128},{128,96},{160,64},{192,32},{224... | collective-permute-start | bytes 356360 | tf_op jit(solution)/shard_map/ppermute | solution.py:499
  17.4 6.3 %collective-permute-start.6 = (f32[232,128]{1,0:T(8,128)S(1)}, f32[232,128]{1,0:T(8,128)S(1)}, u32[]{:S(2)}, u32[]{:S(2)}) collective-permute-start(f32[232,128]{1,0:T(8,128)S(1)} %get-tuple-element.55), channel_id=1, source_target_pairs={{0,32},{32,0},{64,96},{96,64},{128,160},{160,128},{192,224},{224,1... | collective-permute-start | bytes 356360 | tf_op jit(solution)/shard_map/ppermute | solution.py:499
  24.7 17.8 %collective-permute-start.9 = (f32[168,8,128]{2,1,0:T(8,128)S(1)}, f32[168,8,128]{2,1,0:T(8,128)S(1)}, u32[]{:S(2)}, u32[]{:S(2)}) collective-permute-start(f32[168,8,128]{2,1,0:T(8,128)S(1)} %get-tuple-element.60), channel_id=1, source_target_pairs={{0,1},{1,0},{2,3},{3,2},{4,5},{5,4},{6,7},{7,6},{8,9},{9,8},{10,11... | collective-permute-start | bytes 2064392 | tf_op jit(solution)/shard_map/ppermute | solution.py:519
  24.8 19.9 %collective-permute-start.10 = (f32[168,8,128]{2,1,0:T(8,128)S(1)}, f32[168,8,128]{2,1,0:T(8,128)S(1)}, u32[]{:S(2)}, u32[]{:S(2)}) collective-permute-start(f32[168,8,128]{2,1,0:T(8,128)S(1)} %get-tuple-element.61), channel_id=1, source_target_pairs={{0,32},{1,2},{2,1},{3,4},{4,3},{5,6},{6,5},{7,8},{8,7},{9,10},{10,... | collective-permute-start | bytes 2064392 | tf_op jit(solution)/shard_map/ppermute | solution.py:519
  45.7 11.3 %collective-permute-start.11 = (f32[26,4,8,128]{3,2,1,0:T(8,128)S(1)}, f32[26,4,8,128]{3,2,1,0:T(8,128)S(1)}, u32[]{:S(2)}, u32[]{:S(2)}) collective-permute-start(f32[26,4,8,128]{3,2,1,0:T(8,128)S(1)} %get-tuple-element.70), channel_id=1, source_target_pairs={{0,1},{1,0},{2,3},{3,2},{4,5},{5,4},{6,7},{7,6},{8,9},{9,8},{10,11... | collective-permute-start | bytes 1277960 | tf_op jit(solution)/shard_map/ppermute | solution.py:519
  45.8 13.4 %collective-permute-start.12 = (f32[26,4,8,128]{3,2,1,0:T(8,128)S(1)}, f32[26,4,8,128]{3,2,1,0:T(8,128)S(1)}, u32[]{:S(2)}, u32[]{:S(2)}) collective-permute-start(f32[26,4,8,128]{3,2,1,0:T(8,128)S(1)} %get-tuple-element.71), channel_id=1, source_target_pairs={{0,32},{1,2},{2,1},{3,4},{4,3},{5,6},{6,5},{7,8},{8,7},{9,10},{10,... | collective-permute-start | bytes 1277960 | tf_op jit(solution)/shard_map/ppermute | solution.py:519
  60.0 9.7 %collective-permute-start.13 = (f32[24,4,8,128]{3,2,1,0:T(8,128)S(1)}, f32[24,4,8,128]{3,2,1,0:T(8,128)S(1)}, u32[]{:S(2)}, u32[]{:S(2)}) collective-permute-start(f32[24,4,8,128]{3,2,1,0:T(8,128)S(1)} %get-tuple-element.74), channel_id=1, source_target_pairs={{0,1},{1,0},{2,3},{3,2},{4,5},{5,4},{6,7},{7,6},{8,9},{9,8},{10,11... | collective-permute-start | bytes 1179656 | tf_op jit(solution)/shard_map/ppermute | solution.py:519
  60.1 12.0 %collective-permute-start.14 = (f32[24,4,8,128]{3,2,1,0:T(8,128)S(1)}, f32[24,4,8,128]{3,2,1,0:T(8,128)S(1)}, u32[]{:S(2)}, u32[]{:S(2)}) collective-permute-start(f32[24,4,8,128]{3,2,1,0:T(8,128)S(1)} %get-tuple-element.75), channel_id=1, source_target_pairs={{0,32},{1,2},{2,1},{3,4},{4,3},{5,6},{6,5},{7,8},{8,7},{9,10},{10,... | collective-permute-start | bytes 1179656 | tf_op jit(solution)/shard_map/ppermute | solution.py:519
  62.5 5.6 %collective-permute-start.15 = (f32[2,4,4,8,128]{4,3,2,1,0:T(8,128)S(1)}, f32[2,4,4,8,128]{4,3,2,1,0:T(8,128)S(1)}, u32[]{:S(2)}, u32[]{:S(2)}) collective-permute-start(f32[2,4,4,8,128]{4,3,2,1,0:T(8,128)S(1)} %get-tuple-element.76), channel_id=1, source_target_pairs={{32,64},{64,32},{96,128},{128,96},{160,192},{192,160},{224,0},{0,2... | collective-permute-start | bytes 393224 | tf_op jit(solution)/shard_map/ppermute | solution.py:508
  62.5 5.6 %collective-permute-start.16 = (f32[2,4,4,8,128]{4,3,2,1,0:T(8,128)S(1)}, f32[2,4,4,8,128]{4,3,2,1,0:T(8,128)S(1)}, u32[]{:S(2)}, u32[]{:S(2)}) collective-permute-start(f32[2,4,4,8,128]{4,3,2,1,0:T(8,128)S(1)} %get-tuple-element.77), channel_id=1, source_target_pairs={{0,32},{32,0},{64,96},{96,64},{128,160},{160,128},{192,224},{224,1... | collective-permute-start | bytes 393224 | tf_op jit(solution)/shard_map/ppermute | solution.py:508
  72.1 6.0 %collective-permute-start.17 = (f32[10,4,8,128]{3,2,1,0:T(8,128)S(1)}, f32[10,4,8,128]{3,2,1,0:T(8,128)S(1)}, u32[]{:S(2)}, u32[]{:S(2)}) collective-permute-start(f32[10,4,8,128]{3,2,1,0:T(8,128)S(1)} %get-tuple-element.79), channel_id=1, source_target_pairs={{32,64},{64,32},{96,128},{128,96},{160,192},{192,160},{224,0},{0,2... | collective-permute-start | bytes 491528 | tf_op jit(solution)/shard_map/ppermute | solution.py:508
  72.2 5.9 %collective-permute-start.18 = (f32[10,4,8,128]{3,2,1,0:T(8,128)S(1)}, f32[10,4,8,128]{3,2,1,0:T(8,128)S(1)}, u32[]{:S(2)}, u32[]{:S(2)}) collective-permute-start(f32[10,4,8,128]{3,2,1,0:T(8,128)S(1)} %get-tuple-element.80), channel_id=1, source_target_pairs={{0,32},{32,0},{64,96},{96,64},{128,160},{160,128},{192,224},{224,1... | collective-permute-start | bytes 491528 | tf_op jit(solution)/shard_map/ppermute | solution.py:508
  79.3 8.8 %collective-permute-start.19 = (f32[26,4,8,128]{3,2,1,0:T(8,128)S(1)}, f32[26,4,8,128]{3,2,1,0:T(8,128)S(1)}, u32[]{:S(2)}, u32[]{:S(2)}) collective-permute-start(f32[26,4,8,128]{3,2,1,0:T(8,128)S(1)} %get-tuple-element.86), channel_id=1, source_target_pairs={{0,1},{1,0},{2,3},{3,2},{4,5},{5,4},{6,7},{7,6},{8,9},{9,8},{10,11... | collective-permute-start | bytes 1277960 | tf_op jit(solution)/shard_map/ppermute | solution.py:519
  79.4 10.9 %collective-permute-start.20 = (f32[26,4,8,128]{3,2,1,0:T(8,128)S(1)}, f32[26,4,8,128]{3,2,1,0:T(8,128)S(1)}, u32[]{:S(2)}, u32[]{:S(2)}) collective-permute-start(f32[26,4,8,128]{3,2,1,0:T(8,128)S(1)} %get-tuple-element.87), channel_id=1, source_target_pairs={{0,32},{1,2},{2,1},{3,4},{4,3},{5,6},{6,5},{7,8},{8,7},{9,10},{10,... | collective-permute-start | bytes 1277960 | tf_op jit(solution)/shard_map/ppermute | solution.py:519
  91.5 1.5 %collective-permute-start.21 = (f32[4,96,128]{2,1,0:T(8,128)S(1)}, f32[4,96,128]{2,1,0:T(8,128)S(1)}, u32[]{:S(2)}, u32[]{:S(2)}) collective-permute-start(f32[4,96,128]{2,1,0:T(8,128)S(1)} %get-tuple-element.91), channel_id=1, source_target_pairs={{0,32},{32,0},{64,96},{96,64},{128,160},{160,128},{192,224},{224,1... | collective-permute-start | bytes 589832 | tf_op jit(solution)/shard_map/ppermute | solution.py:508
  93.1 7.2 %collective-permute-start.22 = (f32[2,96,128]{2,1,0:T(8,128)S(1)}, f32[2,96,128]{2,1,0:T(8,128)S(1)}, u32[]{:S(2)}, u32[]{:S(2)}) collective-permute-start(f32[2,96,128]{2,1,0:T(8,128)S(1)} %get-tuple-element.93), channel_id=1, source_target_pairs={{0,128},{32,160},{64,192},{96,224},{128,0},{160,32},{192,64},{224,... | collective-permute-start | bytes 294920 | tf_op jit(solution)/shard_map/ppermute | solution.py:600
  95.3 6.3 %collective-permute-start.23 = (f32[2,96,128]{2,1,0:T(8,128)S(1)}, f32[2,96,128]{2,1,0:T(8,128)S(1)}, u32[]{:S(2)}, u32[]{:S(2)}) collective-permute-start(f32[2,96,128]{2,1,0:T(8,128)S(1)} %get-tuple-element.94), channel_id=1, source_target_pairs={{0,64},{32,96},{64,0},{96,32},{128,192},{160,224},{192,128},{224,1... | collective-permute-start | bytes 294920 | tf_op jit(solution)/shard_map/ppermute | solution.py:600
  96.6 5.8 %collective-permute-start.24 = (f32[2,96,128]{2,1,0:T(8,128)S(1)}, f32[2,96,128]{2,1,0:T(8,128)S(1)}, u32[]{:S(2)}, u32[]{:S(2)}) collective-permute-start(f32[2,96,128]{2,1,0:T(8,128)S(1)} %get-tuple-element.95), channel_id=1, source_target_pairs={{0,192},{32,224},{64,128},{96,160},{128,64},{160,96},{192,0},{224,... | collective-permute-start | bytes 294920 | tf_op jit(solution)/shard_map/ppermute | solution.py:600

commit v11 on v10

--- a/solution.py
+++ b/solution.py
@@ -137,6 +137,7 @@
 def coefficient_body(far, near, here, consts, weights, inv):
     t, s = place()
     flip = s & 1
+    near, far = ([side[168 + 3 * i : 171 + 3 * i].reshape(TALL, 128) for i in range(3)] for side in (near, far))
     kappa = [near[1], near[0], here[0], here[1], far[0], far[1]]
     for p in range(6):
         plane = jnp.where(flip == 1, 2 * s + 3 - p, 2 * s - 2 + p)
@@ -185,7 +186,10 @@
 
 
 def spread_body(*rest):
-    pieces, forward, (own, wish, near, far), stage = rest[:8], rest[10], rest[11:15], rest[15]
+    pieces, (near_c, far_c, forward), (own, wish, near, far), stage = rest[:8], rest[8:11], rest[11:15], rest[15]
+    for i in range(3):
+        near[168 + 3 * i : 171 + 3 * i] = near_c[i].reshape(3, 8, 128)
+        far[168 + 3 * i : 171 + 3 * i] = far_c[i].reshape(3, 8, 128)
     t, _ = place()
     rows = PIECE
     for k, piece in zip(ORDER + (0,), pieces):
@@ -537,25 +541,25 @@
         far_inputs=8,
     )(*(pltpu.with_memory_space_constraint(a, pltpu.HBM) for a in arguments))
     got = exchange(pieces)
-    far_c = swap_planes(far_c, 0)
-    near_c = swap_planes(near_c, 1)
     own, wish, near, far = call(
         spread_body,
         "spread",
-        [whole(2, WIN, 4, 8, 128), whole(2, 18, 2, 8, 128), whole(168, 8, 128), whole(168, 8, 128)],
+        [whole(2, WIN, 4, 8, 128), whole(2, 18, 2, 8, 128), whole(177, 8, 128), whole(177, 8, 128)],
         11,
         [pltpu.VMEM((8 * PIECE, 128), jnp.float32)],
-    )(*got, far_c, near_c, forward)
+    )(*got, near_c, far_c, forward)
+    coefficients = call(
+        coefficient_body, "coefficients", [whole(4 * TALL * 8, 128), whole(68, 2, 8, 128)], 4
+    )
+    slab_weights = coefficients(far, near, here_c, consts)[0].reshape(4 * TALL, 8, 128)
     far = far_first = swap_planes(far, 0)
     near = near_first = swap_planes(near, 1)
-    weights, inv = call(
-        coefficient_body, "coefficients", [whole(4 * TALL * 8, 128), whole(68, 2, 8, 128)], 4
-    )(far_c, near_c, here_c, consts)
+    weights, inv = coefficients(far, near, here_c, consts)
     weights = weights.reshape(4 * TALL, 8, 128)
 
     sweep_scratch = [pltpu.VMEM((52, 4, 8, 128), jnp.float32)]
     for outer in range(OUTER):
-        kept, part = call(prepare_body, "prepare", [whole(36, 4, 8, 128)] * 2, 4)(own, wish, weights, consts)
+        kept, part = call(prepare_body, "prepare", [whole(36, 4, 8, 128)] * 2, 4)(own, wish, slab_weights, consts)
         side, it, near_z, far_z = call(
             front_body,
             "front",

time: 104 us -> 101 us (0.971)
  waiting for transfers between devices: 64.7 us -> 56.5 us
  starting transfers between devices: 28.8 us -> 33.5 us
    ppermute x10 -> x8, waiting for transfers between devices: 40.7 us -> 34.9 us  [swap_planes(): return lax.ppermute(block, ('tm', 'space'), route)]
    ppermute x10 -> x8, starting transfers between devices: 16.6 us -> 18.3 us  [swap_planes(): return lax.ppermute(block, ('tm', 'space'), route)]
    ppermute x5, waiting for transfers between devices: 12.5 us -> 11 us  [swap_rows(): return lax.ppermute(block, 'tm', route)]
    ppermute x5, starting transfers between devices: 0.28 us -> 1.8 us  [swap_rows(): return lax.ppermute(block, 'tm', route)]
    ppermute x7, starting transfers between devices: 7.79 us -> 9.17 us  [exchange(): lax.ppermute(pieces[k], 'tm', [(i, i ^ k) for i in range(count)])]
  transfers between devices with their start and end apart: 25 -> 23, of which waited for: 17 -> 18; matrix products, arithmetic and copies ran while one was open for 0% -> 0% of each run, Pallas kernels for 2% -> 2%
where the time goes in v11:
time: 101 us
  waiting for transfers between devices  56.5 us (56%)
  starting transfers between devices  33.5 us (33%)
  Pallas kernels  9.95 us (10%)
    ppermute x8, waiting for transfers between devices, swap_planes(): return lax.ppermute(block, ('tm', 'space'), route)  34.9 us
    ppermute x8, starting transfers between devices, swap_planes(): return lax.ppermute(block, ('tm', 'space'), route)  18.3 us
    ppermute x5, waiting for transfers between devices, swap_rows(): return lax.ppermute(block, 'tm', route)  11 us
    ppermute x7, starting transfers between devices, exchange(): lax.ppermute(pieces[k], 'tm', [(i, i ^ k) for i in range(count)])  9.17 us
    ppermute x7, waiting for transfers between devices, exchange(): lax.ppermute(pieces[k], 'tm', [(i, i ^ k) for i in range(count)])  5.4 us
    ppermute x3, waiting for transfers between devices, on_device(): lax.ppermute(pair, 'tm', [(i, i ^ 2 * k) for i in range(count)])  5.21 us
    ppermute x3, starting transfers between devices, on_device(): lax.ppermute(pair, 'tm', [(i, i ^ 2 * k) for i in range(count)])  4.22 us
  transfers between devices with their start and end apart: 23, of which 18 were waited for; matrix products, arithmetic and copies ran while one was open for 0% of the time, Pallas kernels for 2%

profile of v11, /device:TPU:6, one launch (start us, length us, event | category | flops | bytes accessed | tf_op | source)
XLA Modules:
  0.0 100.8 jit_solution(16225753809255164921)
XLA Ops:
  0.6 1.4 %pack.1 = (f32[232,128]{1,0:T(8,128)S(1)}, f32[232,128]{1,0:T(8,128)S(1)}, f32[232,128]{1,0:T(8,128)S(1)}, f32[232,128]{1,0:T(8,128)S(1)}, f32[232,128]{1,0:T(8,...) custom-call(f32[2,2,96,128]{3,2,1,0:T(8,128)} %rest_0_.1, ...), custom_call_target="tpu_custom_call" | custom-call | tf_op jit(solution)/shard_map/pack/pallas_call | solution.py:531
  2.0 3.3 %collective-permute-start = (f32[232,128]{1,0:T(8,128)S(1)}, f32[232,128]{1,0:T(8,128)S(1)}, u32[]{:S(2)}, u32[]{:S(2)}) collective-permute-start(f32[232,128]{1,0:T(8,128)S(1)} %get-tuple-element.50), channel_id=1, source_target_pairs={{0,128},{32,160},{64,192},{96,224},{128,0},{160,32},{192,64},{224,... | collective-permute-start | bytes 356360 | tf_op jit(solution)/shard_map/ppermute | solution.py:503
  5.3 0.7 collective-permute-start.1
  6.0 0.4 collective-permute-start.2
  6.3 1.6 %collective-permute-start.3 = (f32[232,128]{1,0:T(8,128)S(1)}, f32[232,128]{1,0:T(8,128)S(1)}, u32[]{:S(2)}, u32[]{:S(2)}) collective-permute-start(f32[232,128]{1,0:T(8,128)S(1)} %get-tuple-element.53), channel_id=1, source_target_pairs={{0,160},{32,128},{64,224},{96,192},{128,32},{160,0},{192,96},{224,... | collective-permute-start | bytes 356360 | tf_op jit(solution)/shard_map/ppermute | solution.py:503
  8.0 1.8 %collective-permute-start.4 = (f32[232,128]{1,0:T(8,128)S(1)}, f32[232,128]{1,0:T(8,128)S(1)}, u32[]{:S(2)}, u32[]{:S(2)}) collective-permute-start(f32[232,128]{1,0:T(8,128)S(1)} %get-tuple-element.54), channel_id=1, source_target_pairs={{0,96},{32,64},{64,32},{96,0},{128,224},{160,192},{192,160},{224,1... | collective-permute-start | bytes 356360 | tf_op jit(solution)/shard_map/ppermute | solution.py:503
  9.8 0.4 collective-permute-start.5
  10.2 1.7 %collective-permute-done.1.rest_1_ = f32[232,128]{1,0:T(8,128)S(1)} collective-permute-done((f32[232,128]{1,0:T(8,128)S(1)}, f32[232,128]{1,0:T(8,128)S(1)}, u32[]{:S(2)}, u32[]{:S(2)}) %collective-permute-start.1) | collective-permute-done | bytes 118816 | tf_op jit(solution)/shard_map/ppermute | solution.py:503
  11.8 1.0 %collective-permute-start.6 = (f32[232,128]{1,0:T(8,128)S(1)}, f32[232,128]{1,0:T(8,128)S(1)}, u32[]{:S(2)}, u32[]{:S(2)}) collective-permute-start(f32[232,128]{1,0:T(8,128)S(1)} %get-tuple-element.56), channel_id=1, source_target_pairs={{0,32},{32,0},{64,96},{96,64},{128,160},{160,128},{192,224},{224,1... | collective-permute-start | bytes 356360 | tf_op jit(solution)/shard_map/ppermute | solution.py:503
  12.8 2.2 %collective-permute-done.2.rest_2_ = f32[232,128]{1,0:T(8,128)S(1)} collective-permute-done((f32[232,128]{1,0:T(8,128)S(1)}, f32[232,128]{1,0:T(8,128)S(1)}, u32[]{:S(2)}, u32[]{:S(2)}) %collective-permute-start.2) | collective-permute-done | bytes 118816 | tf_op jit(solution)/shard_map/ppermute | solution.py:503
  15.1 1.1 %collective-permute-done.4.rest_4_ = f32[232,128]{1,0:T(8,128)S(1)} collective-permute-done((f32[232,128]{1,0:T(8,128)S(1)}, f32[232,128]{1,0:T(8,128)S(1)}, u32[]{:S(2)}, u32[]{:S(2)}) %collective-permute-start.4) | collective-permute-done | bytes 118816 | tf_op jit(solution)/shard_map/ppermute | solution.py:503
  16.2 0.4 collective-permute-done.5.rest_5_
  16.6 1.0 spread.1
  17.6 2.0 %collective-permute-start.7 = (f32[177,8,128]{2,1,0:T(8,128)S(1)}, f32[177,8,128]{2,1,0:T(8,128)S(1)}, u32[]{:S(2)}, u32[]{:S(2)}) collective-permute-start(f32[177,8,128]{2,1,0:T(8,128)S(1)} %get-tuple-element.61.far), channel_id=1, source_target_pairs={{0,1},{1,0},{2,3},{3,2},{4,5},{5,4},{6,7},{7,6},{8,9},{9,8},{10,11... | collective-permute-start | bytes 2174984 | tf_op jit(solution)/shard_map/ppermute | solution.py:523
  19.6 5.2 %collective-permute-start.8 = (f32[177,8,128]{2,1,0:T(8,128)S(1)}, f32[177,8,128]{2,1,0:T(8,128)S(1)}, u32[]{:S(2)}, u32[]{:S(2)}) collective-permute-start(f32[177,8,128]{2,1,0:T(8,128)S(1)} %get-tuple-element.62.near), channel_id=1, source_target_pairs={{0,32},{1,2},{2,1},{3,4},{4,3},{5,6},{6,5},{7,8},{8,7},{9,10},{10,... | collective-permute-start | bytes 2174984 | tf_op jit(solution)/shard_map/ppermute | solution.py:523
  24.8 1.0 %coefficients.3 = (f32[768,128]{1,0:T(8,128)S(1)}, f32[68,2,8,128]{3,2,1,0:T(8,128)}) custom-call(f32[177,8,128]{2,1,0:T(8,128)S(1)} %get-tuple-element.61.far, f32[177,8,128]{2,1,0:T(8,128)S(1)} %get-tuple-element.62.near, f32[4,24,128]{2,1,0:T(8,128)S(1)} %get-tuple-element.64.here, f32[10,8,128]{2,1,0:T(8,128)S(1)} %get-tuple-element.65.consts), custom_call_target="tpu_custom_call" | custom-call | tf_op jit(solution)/shard_map/coefficients/pallas_call | solution.py:554
  25.8 0.4 prepare.2
  26.2 10.1 %collective-permute-done.7.far.tfar = f32[177,8,128]{2,1,0:T(8,128)S(1)} collective-permute-done((f32[177,8,128]{2,1,0:T(8,128)S(1)}, f32[177,8,128]{2,1,0:T(8,128)S(1)}, u32[]{:S(2)}, u32[]{:S(2)}) %collective-permute-start.7) | collective-permute-done | bytes 725024 | tf_op jit(solution)/shard_map/ppermute | solution.py:523
  36.3 4.9 %collective-permute-done.8.near.tnear = f32[177,8,128]{2,1,0:T(8,128)S(1)} collective-permute-done((f32[177,8,128]{2,1,0:T(8,128)S(1)}, f32[177,8,128]{2,1,0:T(8,128)S(1)}, u32[]{:S(2)}, u32[]{:S(2)}) %collective-permute-start.8) | collective-permute-done | bytes 725024 | tf_op jit(solution)/shard_map/ppermute | solution.py:523
  41.2 0.2 coefficients.2
  41.5 1.0 %front.2 = (f32[32,4,8,128]{3,2,1,0:T(8,128)S(1)}, f32[2,16,4,8,128]{4,3,2,1,0:T(8,128)S(1)}, f32[26,4,8,128]{3,2,1,0:T(8,128)S(1)}, f32[26,4,8,128]{3,2,1,0:T(8,128)S(1)}) custom-call(f32[177,8,128]{2,1,0:T(8,128)S(1)} %collective-permute-done.7.far.tfar, f32[177,8,128]{2,1,0:T(8,128)S(1)} %collective-permute-done.8.near.tnear, ...), custom_call_target="tpu_custom_call" | custom-call | tf_op jit(solution)/shard_map/front/pallas_call | solution.py:563
  42.6 3.9 %collective-permute-start.10 = (f32[26,4,8,128]{3,2,1,0:T(8,128)S(1)}, f32[26,4,8,128]{3,2,1,0:T(8,128)S(1)}, u32[]{:S(2)}, u32[]{:S(2)}) collective-permute-start(f32[26,4,8,128]{3,2,1,0:T(8,128)S(1)} %get-tuple-element.73), channel_id=1, source_target_pairs={{0,32},{1,2},{2,1},{3,4},{4,3},{5,6},{6,5},{7,8},{8,7},{9,10},{10,... | collective-permute-start | bytes 1277960 | tf_op jit(solution)/shard_map/ppermute | solution.py:523
  46.5 0.3 ahead.2.part
  46.8 7.0 %collective-permute-done.9.far = f32[26,4,8,128]{3,2,1,0:T(8,128)S(1)} collective-permute-done((f32[26,4,8,128]{3,2,1,0:T(8,128)S(1)}, f32[26,4,8,128]{3,2,1,0:T(8,128)S(1)}, u32[]{:S(2)}, u32[]{:S(2)}) %collective-permute-start.9) | collective-permute-done | bytes 426016 | tf_op jit(solution)/shard_map/ppermute | solution.py:523
  53.8 2.2 %collective-permute-done.10.near = f32[26,4,8,128]{3,2,1,0:T(8,128)S(1)} collective-permute-done((f32[26,4,8,128]{3,2,1,0:T(8,128)S(1)}, f32[26,4,8,128]{3,2,1,0:T(8,128)S(1)}, u32[]{:S(2)}, u32[]{:S(2)}) %collective-permute-start.10) | collective-permute-done | bytes 426016 | tf_op jit(solution)/shard_map/ppermute | solution.py:523
  56.0 0.7 middle.1
  56.8 3.6 %collective-permute-start.12 = (f32[24,4,8,128]{3,2,1,0:T(8,128)S(1)}, f32[24,4,8,128]{3,2,1,0:T(8,128)S(1)}, u32[]{:S(2)}, u32[]{:S(2)}) collective-permute-start(f32[24,4,8,128]{3,2,1,0:T(8,128)S(1)} %get-tuple-element.77), channel_id=1, source_target_pairs={{0,32},{1,2},{2,1},{3,4},{4,3},{5,6},{6,5},{7,8},{8,7},{9,10},{10,... | collective-permute-start | bytes 1179656 | tf_op jit(solution)/shard_map/ppermute | solution.py:523
  60.4 0.9 collective-permute-start.14
  61.4 4.7 %collective-permute-done.13.row1 = f32[2,4,4,8,128]{4,3,2,1,0:T(8,128)S(1)} collective-permute-done((f32[2,4,4,8,128]{4,3,2,1,0:T(8,128)S(1)}, f32[2,4,4,8,128]{4,3,2,1,0:T(8,128)S(1)}, u32[]{:S(2)}, u32[]{:S(2)}) %collective-permute-start.13) | collective-permute-done | bytes 131104 | tf_op jit(solution)/shard_map/ppermute | solution.py:512
  66.0 0.4 collective-permute-done.11.far.far_x
  66.4 2.2 %collective-permute-done.12.near.near_x = f32[24,4,8,128]{3,2,1,0:T(8,128)S(1)} collective-permute-done((f32[24,4,8,128]{3,2,1,0:T(8,128)S(1)}, f32[24,4,8,128]{3,2,1,0:T(8,128)S(1)}, u32[]{:S(2)}, u32[]{:S(2)}) %collective-permute-start.12) | collective-permute-done | bytes 393248 | tf_op jit(solution)/shard_map/ppermute | solution.py:523
  68.8 0.7 collective-permute-start.16
  69.5 0.4 prepare.3
  69.9 4.9 %collective-permute-done.15.edge1 = f32[10,4,8,128]{3,2,1,0:T(8,128)S(1)} collective-permute-done((f32[10,4,8,128]{3,2,1,0:T(8,128)S(1)}, f32[10,4,8,128]{3,2,1,0:T(8,128)S(1)}, u32[]{:S(2)}, u32[]{:S(2)}) %collective-permute-start.15) | collective-permute-done | bytes 163872 | tf_op jit(solution)/shard_map/ppermute | solution.py:512
  74.8 1.0 front.3
  76.0 3.3 %collective-permute-start.18 = (f32[26,4,8,128]{3,2,1,0:T(8,128)S(1)}, f32[26,4,8,128]{3,2,1,0:T(8,128)S(1)}, u32[]{:S(2)}, u32[]{:S(2)}) collective-permute-start(f32[26,4,8,128]{3,2,1,0:T(8,128)S(1)} %get-tuple-element.89), channel_id=1, source_target_pairs={{0,32},{1,2},{2,1},{3,4},{4,3},{5,6},{6,5},{7,8},{8,7},{9,10},{10,... | collective-permute-start | bytes 1277960 | tf_op jit(solution)/shard_map/ppermute | solution.py:523
  79.2 0.3 ahead.3.part
  79.6 5.8 %collective-permute-done.17.far = f32[26,4,8,128]{3,2,1,0:T(8,128)S(1)} collective-permute-done((f32[26,4,8,128]{3,2,1,0:T(8,128)S(1)}, f32[26,4,8,128]{3,2,1,0:T(8,128)S(1)}, u32[]{:S(2)}, u32[]{:S(2)}) %collective-permute-start.17) | collective-permute-done | bytes 426016 | tf_op jit(solution)/shard_map/ppermute | solution.py:523
  85.4 2.2 %collective-permute-done.18.near = f32[26,4,8,128]{3,2,1,0:T(8,128)S(1)} collective-permute-done((f32[26,4,8,128]{3,2,1,0:T(8,128)S(1)}, f32[26,4,8,128]{3,2,1,0:T(8,128)S(1)}, u32[]{:S(2)}, u32[]{:S(2)}) %collective-permute-start.18) | collective-permute-done | bytes 426016 | tf_op jit(solution)/shard_map/ppermute | solution.py:523
  87.6 1.2 %last.1 = (f32[4,96,128]{2,1,0:T(8,128)S(1)}, f32[4,96,128]{2,1,0:T(8,128)S(1)}) custom-call(f32[26,4,8,128]{3,2,1,0:T(8,128)S(1)} %collective-permute-done.17.far, f32[26,4,8,128]{3,2,1,0:T(8,128)S(1)} %collective-permute-done.18.near, f32[2,16,4,8,128]{4,3,2,1,0:T(8,128)S(1)} %get-tuple-element.90.it, f32[36,4,8,128]{3,2,1,0:T(8,128)S(1)} %get-tuple-element.86.kept, ...), custom_call_target="tpu_custom_call" | custom-call | tf_op jit(solution)/shard_map/last/pallas_call | solution.py:593
  88.9 1.4 %collective-permute-done.19.other = f32[4,96,128]{2,1,0:T(8,128)S(1)} collective-permute-done((f32[4,96,128]{2,1,0:T(8,128)S(1)}, f32[4,96,128]{2,1,0:T(8,128)S(1)}, u32[]{:S(2)}, u32[]{:S(2)}) %collective-permute-start.19) | collective-permute-done | bytes 196640 | tf_op jit(solution)/shard_map/ppermute | solution.py:512
  90.4 2.2 %collective-permute-start.20 = (f32[2,96,128]{2,1,0:T(8,128)S(1)}, f32[2,96,128]{2,1,0:T(8,128)S(1)}, u32[]{:S(2)}, u32[]{:S(2)}) collective-permute-start(f32[2,96,128]{2,1,0:T(8,128)S(1)} %get-tuple-element.95), channel_id=1, source_target_pairs={{0,128},{32,160},{64,192},{96,224},{128,0},{160,32},{192,64},{224,... | collective-permute-start | bytes 294920 | tf_op jit(solution)/shard_map/ppermute | solution.py:604
  92.6 1.4 %collective-permute-start.21 = (f32[2,96,128]{2,1,0:T(8,128)S(1)}, f32[2,96,128]{2,1,0:T(8,128)S(1)}, u32[]{:S(2)}, u32[]{:S(2)}) collective-permute-start(f32[2,96,128]{2,1,0:T(8,128)S(1)} %get-tuple-element.96), channel_id=1, source_target_pairs={{0,64},{32,96},{64,0},{96,32},{128,192},{160,224},{192,128},{224,1... | collective-permute-start | bytes 294920 | tf_op jit(solution)/shard_map/ppermute | solution.py:604
  94.0 0.6 collective-permute-start.22
  94.6 2.5 %collective-permute-done.20.a = f32[2,96,128]{2,1,0:T(8,128)S(1)} collective-permute-done((f32[2,96,128]{2,1,0:T(8,128)S(1)}, f32[2,96,128]{2,1,0:T(8,128)S(1)}, u32[]{:S(2)}, u32[]{:S(2)}) %collective-permute-start.20) | collective-permute-done | bytes 98336 | tf_op jit(solution)/shard_map/ppermute | solution.py:604
  97.2 1.8 %collective-permute-done.21.b = f32[2,96,128]{2,1,0:T(8,128)S(1)} collective-permute-done((f32[2,96,128]{2,1,0:T(8,128)S(1)}, f32[2,96,128]{2,1,0:T(8,128)S(1)}, u32[]{:S(2)}, u32[]{:S(2)}) %collective-permute-start.21) | collective-permute-done | bytes 98336 | tf_op jit(solution)/shard_map/ppermute | solution.py:604
  98.9 0.9 collective-permute-done.22.c
  99.8 0.8 unpack.1
  (14 shorter events, 0.6 us)
Async XLA Ops:
  2.0 7.8 %collective-permute-start = (f32[232,128]{1,0:T(8,128)S(1)}, f32[232,128]{1,0:T(8,128)S(1)}, u32[]{:S(2)}, u32[]{:S(2)}) collective-permute-start(f32[232,128]{1,0:T(8,128)S(1)} %get-tuple-element.50), channel_id=1, source_target_pairs={{0,128},{32,160},{64,192},{96,224},{128,0},{160,32},{192,64},{224,... | collective-permute-start | bytes 356360 | tf_op jit(solution)/shard_map/ppermute | solution.py:503
  5.3 6.5 %collective-permute-start.1 = (f32[232,128]{1,0:T(8,128)S(1)}, f32[232,128]{1,0:T(8,128)S(1)}, u32[]{:S(2)}, u32[]{:S(2)}) collective-permute-start(f32[232,128]{1,0:T(8,128)S(1)} %get-tuple-element.51), channel_id=1, source_target_pairs={{0,64},{32,96},{64,0},{96,32},{128,192},{160,224},{192,128},{224,1... | collective-permute-start | bytes 356360 | tf_op jit(solution)/shard_map/ppermute | solution.py:503
  6.0 9.1 %collective-permute-start.2 = (f32[232,128]{1,0:T(8,128)S(1)}, f32[232,128]{1,0:T(8,128)S(1)}, u32[]{:S(2)}, u32[]{:S(2)}) collective-permute-start(f32[232,128]{1,0:T(8,128)S(1)} %get-tuple-element.52), channel_id=1, source_target_pairs={{0,192},{32,224},{64,128},{96,160},{128,64},{160,96},{192,0},{224,... | collective-permute-start | bytes 356360 | tf_op jit(solution)/shard_map/ppermute | solution.py:503
  6.3 8.7 %collective-permute-start.3 = (f32[232,128]{1,0:T(8,128)S(1)}, f32[232,128]{1,0:T(8,128)S(1)}, u32[]{:S(2)}, u32[]{:S(2)}) collective-permute-start(f32[232,128]{1,0:T(8,128)S(1)} %get-tuple-element.53), channel_id=1, source_target_pairs={{0,160},{32,128},{64,224},{96,192},{128,32},{160,0},{192,96},{224,... | collective-permute-start | bytes 356360 | tf_op jit(solution)/shard_map/ppermute | solution.py:503
  8.0 8.2 %collective-permute-start.4 = (f32[232,128]{1,0:T(8,128)S(1)}, f32[232,128]{1,0:T(8,128)S(1)}, u32[]{:S(2)}, u32[]{:S(2)}) collective-permute-start(f32[232,128]{1,0:T(8,128)S(1)} %get-tuple-element.54), channel_id=1, source_target_pairs={{0,96},{32,64},{64,32},{96,0},{128,224},{160,192},{192,160},{224,1... | collective-permute-start | bytes 356360 | tf_op jit(solution)/shard_map/ppermute | solution.py:503
  9.8 6.8 %collective-permute-start.5 = (f32[232,128]{1,0:T(8,128)S(1)}, f32[232,128]{1,0:T(8,128)S(1)}, u32[]{:S(2)}, u32[]{:S(2)}) collective-permute-start(f32[232,128]{1,0:T(8,128)S(1)} %get-tuple-element.55), channel_id=1, source_target_pairs={{0,224},{32,192},{64,160},{96,128},{128,96},{160,64},{192,32},{224... | collective-permute-start | bytes 356360 | tf_op jit(solution)/shard_map/ppermute | solution.py:503
  11.8 4.8 %collective-permute-start.6 = (f32[232,128]{1,0:T(8,128)S(1)}, f32[232,128]{1,0:T(8,128)S(1)}, u32[]{:S(2)}, u32[]{:S(2)}) collective-permute-start(f32[232,128]{1,0:T(8,128)S(1)} %get-tuple-element.56), channel_id=1, source_target_pairs={{0,32},{32,0},{64,96},{96,64},{128,160},{160,128},{192,224},{224,1... | collective-permute-start | bytes 356360 | tf_op jit(solution)/shard_map/ppermute | solution.py:503
  17.6 18.7 %collective-permute-start.7 = (f32[177,8,128]{2,1,0:T(8,128)S(1)}, f32[177,8,128]{2,1,0:T(8,128)S(1)}, u32[]{:S(2)}, u32[]{:S(2)}) collective-permute-start(f32[177,8,128]{2,1,0:T(8,128)S(1)} %get-tuple-element.61.far), channel_id=1, source_target_pairs={{0,1},{1,0},{2,3},{3,2},{4,5},{5,4},{6,7},{7,6},{8,9},{9,8},{10,11... | collective-permute-start | bytes 2174984 | tf_op jit(solution)/shard_map/ppermute | solution.py:523
  19.6 21.6 %collective-permute-start.8 = (f32[177,8,128]{2,1,0:T(8,128)S(1)}, f32[177,8,128]{2,1,0:T(8,128)S(1)}, u32[]{:S(2)}, u32[]{:S(2)}) collective-permute-start(f32[177,8,128]{2,1,0:T(8,128)S(1)} %get-tuple-element.62.near), channel_id=1, source_target_pairs={{0,32},{1,2},{2,1},{3,4},{4,3},{5,6},{6,5},{7,8},{8,7},{9,10},{10,... | collective-permute-start | bytes 2174984 | tf_op jit(solution)/shard_map/ppermute | solution.py:523
  42.5 11.3 %collective-permute-start.9 = (f32[26,4,8,128]{3,2,1,0:T(8,128)S(1)}, f32[26,4,8,128]{3,2,1,0:T(8,128)S(1)}, u32[]{:S(2)}, u32[]{:S(2)}) collective-permute-start(f32[26,4,8,128]{3,2,1,0:T(8,128)S(1)} %get-tuple-element.72), channel_id=1, source_target_pairs={{0,1},{1,0},{2,3},{3,2},{4,5},{5,4},{6,7},{7,6},{8,9},{9,8},{10,11... | collective-permute-start | bytes 1277960 | tf_op jit(solution)/shard_map/ppermute | solution.py:523
  42.6 13.4 %collective-permute-start.10 = (f32[26,4,8,128]{3,2,1,0:T(8,128)S(1)}, f32[26,4,8,128]{3,2,1,0:T(8,128)S(1)}, u32[]{:S(2)}, u32[]{:S(2)}) collective-permute-start(f32[26,4,8,128]{3,2,1,0:T(8,128)S(1)} %get-tuple-element.73), channel_id=1, source_target_pairs={{0,32},{1,2},{2,1},{3,4},{4,3},{5,6},{6,5},{7,8},{8,7},{9,10},{10,... | collective-permute-start | bytes 1277960 | tf_op jit(solution)/shard_map/ppermute | solution.py:523
  56.7 9.7 %collective-permute-start.11 = (f32[24,4,8,128]{3,2,1,0:T(8,128)S(1)}, f32[24,4,8,128]{3,2,1,0:T(8,128)S(1)}, u32[]{:S(2)}, u32[]{:S(2)}) collective-permute-start(f32[24,4,8,128]{3,2,1,0:T(8,128)S(1)} %get-tuple-element.76), channel_id=1, source_target_pairs={{0,1},{1,0},{2,3},{3,2},{4,5},{5,4},{6,7},{7,6},{8,9},{9,8},{10,11... | collective-permute-start | bytes 1179656 | tf_op jit(solution)/shard_map/ppermute | solution.py:523
  56.8 11.8 %collective-permute-start.12 = (f32[24,4,8,128]{3,2,1,0:T(8,128)S(1)}, f32[24,4,8,128]{3,2,1,0:T(8,128)S(1)}, u32[]{:S(2)}, u32[]{:S(2)}) collective-permute-start(f32[24,4,8,128]{3,2,1,0:T(8,128)S(1)} %get-tuple-element.77), channel_id=1, source_target_pairs={{0,32},{1,2},{2,1},{3,4},{4,3},{5,6},{6,5},{7,8},{8,7},{9,10},{10,... | collective-permute-start | bytes 1179656 | tf_op jit(solution)/shard_map/ppermute | solution.py:523
  60.4 5.6 %collective-permute-start.13 = (f32[2,4,4,8,128]{4,3,2,1,0:T(8,128)S(1)}, f32[2,4,4,8,128]{4,3,2,1,0:T(8,128)S(1)}, u32[]{:S(2)}, u32[]{:S(2)}) collective-permute-start(f32[2,4,4,8,128]{4,3,2,1,0:T(8,128)S(1)} %get-tuple-element.78), channel_id=1, source_target_pairs={{32,64},{64,32},{96,128},{128,96},{160,192},{192,160},{224,0},{0,2... | collective-permute-start | bytes 393224 | tf_op jit(solution)/shard_map/ppermute | solution.py:512
  60.4 5.6 %collective-permute-start.14 = (f32[2,4,4,8,128]{4,3,2,1,0:T(8,128)S(1)}, f32[2,4,4,8,128]{4,3,2,1,0:T(8,128)S(1)}, u32[]{:S(2)}, u32[]{:S(2)}) collective-permute-start(f32[2,4,4,8,128]{4,3,2,1,0:T(8,128)S(1)} %get-tuple-element.79), channel_id=1, source_target_pairs={{0,32},{32,0},{64,96},{96,64},{128,160},{160,128},{192,224},{224,1... | collective-permute-start | bytes 393224 | tf_op jit(solution)/shard_map/ppermute | solution.py:512
  68.7 6.0 %collective-permute-start.15 = (f32[10,4,8,128]{3,2,1,0:T(8,128)S(1)}, f32[10,4,8,128]{3,2,1,0:T(8,128)S(1)}, u32[]{:S(2)}, u32[]{:S(2)}) collective-permute-start(f32[10,4,8,128]{3,2,1,0:T(8,128)S(1)} %get-tuple-element.81), channel_id=1, source_target_pairs={{32,64},{64,32},{96,128},{128,96},{160,192},{192,160},{224,0},{0,2... | collective-permute-start | bytes 491528 | tf_op jit(solution)/shard_map/ppermute | solution.py:512
  68.8 5.9 %collective-permute-start.16 = (f32[10,4,8,128]{3,2,1,0:T(8,128)S(1)}, f32[10,4,8,128]{3,2,1,0:T(8,128)S(1)}, u32[]{:S(2)}, u32[]{:S(2)}) collective-permute-start(f32[10,4,8,128]{3,2,1,0:T(8,128)S(1)} %get-tuple-element.82), channel_id=1, source_target_pairs={{0,32},{32,0},{64,96},{96,64},{128,160},{160,128},{192,224},{224,1... | collective-permute-start | bytes 491528 | tf_op jit(solution)/shard_map/ppermute | solution.py:512
  75.9 9.5 %collective-permute-start.17 = (f32[26,4,8,128]{3,2,1,0:T(8,128)S(1)}, f32[26,4,8,128]{3,2,1,0:T(8,128)S(1)}, u32[]{:S(2)}, u32[]{:S(2)}) collective-permute-start(f32[26,4,8,128]{3,2,1,0:T(8,128)S(1)} %get-tuple-element.88), channel_id=1, source_target_pairs={{0,1},{1,0},{2,3},{3,2},{4,5},{5,4},{6,7},{7,6},{8,9},{9,8},{10,11... | collective-permute-start | bytes 1277960 | tf_op jit(solution)/shard_map/ppermute | solution.py:523
  76.0 11.7 %collective-permute-start.18 = (f32[26,4,8,128]{3,2,1,0:T(8,128)S(1)}, f32[26,4,8,128]{3,2,1,0:T(8,128)S(1)}, u32[]{:S(2)}, u32[]{:S(2)}) collective-permute-start(f32[26,4,8,128]{3,2,1,0:T(8,128)S(1)} %get-tuple-element.89), channel_id=1, source_target_pairs={{0,32},{1,2},{2,1},{3,4},{4,3},{5,6},{6,5},{7,8},{8,7},{9,10},{10,... | collective-permute-start | bytes 1277960 | tf_op jit(solution)/shard_map/ppermute | solution.py:523
  88.8 1.5 %collective-permute-start.19 = (f32[4,96,128]{2,1,0:T(8,128)S(1)}, f32[4,96,128]{2,1,0:T(8,128)S(1)}, u32[]{:S(2)}, u32[]{:S(2)}) collective-permute-start(f32[4,96,128]{2,1,0:T(8,128)S(1)} %get-tuple-element.93), channel_id=1, source_target_pairs={{0,32},{32,0},{64,96},{96,64},{128,160},{160,128},{192,224},{224,1... | collective-permute-start | bytes 589832 | tf_op jit(solution)/shard_map/ppermute | solution.py:512
  90.4 6.8 %collective-permute-start.20 = (f32[2,96,128]{2,1,0:T(8,128)S(1)}, f32[2,96,128]{2,1,0:T(8,128)S(1)}, u32[]{:S(2)}, u32[]{:S(2)}) collective-permute-start(f32[2,96,128]{2,1,0:T(8,128)S(1)} %get-tuple-element.95), channel_id=1, source_target_pairs={{0,128},{32,160},{64,192},{96,224},{128,0},{160,32},{192,64},{224,... | collective-permute-start | bytes 294920 | tf_op jit(solution)/shard_map/ppermute | solution.py:604
  92.6 6.4 %collective-permute-start.21 = (f32[2,96,128]{2,1,0:T(8,128)S(1)}, f32[2,96,128]{2,1,0:T(8,128)S(1)}, u32[]{:S(2)}, u32[]{:S(2)}) collective-permute-start(f32[2,96,128]{2,1,0:T(8,128)S(1)} %get-tuple-element.96), channel_id=1, source_target_pairs={{0,64},{32,96},{64,0},{96,32},{128,192},{160,224},{192,128},{224,1... | collective-permute-start | bytes 294920 | tf_op jit(solution)/shard_map/ppermute | solution.py:604
  94.0 5.8 %collective-permute-start.22 = (f32[2,96,128]{2,1,0:T(8,128)S(1)}, f32[2,96,128]{2,1,0:T(8,128)S(1)}, u32[]{:S(2)}, u32[]{:S(2)}) collective-permute-start(f32[2,96,128]{2,1,0:T(8,128)S(1)} %get-tuple-element.97), channel_id=1, source_target_pairs={{0,192},{32,224},{64,128},{96,160},{128,64},{160,96},{192,0},{224,... | collective-permute-start | bytes 294920 | tf_op jit(solution)/shard_map/ppermute | solution.py:604

commit v12 on v10

--- a/solution.py
+++ b/solution.py
@@ -537,6 +537,7 @@
         far_inputs=8,
     )(*(pltpu.with_memory_space_constraint(a, pltpu.HBM) for a in arguments))
     got = exchange(pieces)
+    got[1], far_c, near_c = lax.optimization_barrier((got[1], far_c, near_c))
     far_c = swap_planes(far_c, 0)
     near_c = swap_planes(near_c, 1)
     own, wish, near, far = call(

time: 104 us -> 102 us (0.981)
  waiting for transfers between devices: 64.7 us -> 43.2 us
  starting transfers between devices: 28.8 us -> 48.4 us
    ppermute x5, starting transfers between devices: 0.28 us -> 11.1 us  [swap_rows(): return lax.ppermute(block, 'tm', route)]
    ppermute x10, waiting for transfers between devices: 40.7 us -> 31.2 us  [swap_planes(): return lax.ppermute(block, ('tm', 'space'), route)]
    ppermute x5, waiting for transfers between devices: 12.5 us -> 3.55 us  [swap_rows(): return lax.ppermute(block, 'tm', route)]
    ppermute x10, starting transfers between devices: 16.6 us -> 22.2 us  [swap_planes(): return lax.ppermute(block, ('tm', 'space'), route)]
    ppermute x7, waiting for transfers between devices: 6.31 us -> 3.88 us  [exchange(): lax.ppermute(pieces[k], 'tm', [(i, i ^ k) for i in range(count)])]
    ppermute x3, starting transfers between devices: 4.18 us -> 5.96 us  [on_device(): lax.ppermute(pair, 'tm', [(i, i ^ 2 * k) for i in range(count)])]
    ppermute x7, starting transfers between devices: 7.79 us -> 9.17 us  [exchange(): lax.ppermute(pieces[k], 'tm', [(i, i ^ k) for i in range(count)])]
  transfers between devices with their start and end apart: 25 -> 25, of which waited for: 17 -> 16; matrix products, arithmetic and copies ran while one was open for 0% -> 0% of each run, Pallas kernels for 2% -> 2%
where the time goes in v12:
time: 102 us
  starting transfers between devices  48.4 us (47%)
  waiting for transfers between devices  43.2 us (42%)
  Pallas kernels  9.02 us (9%)
    ppermute x10, waiting for transfers between devices, swap_planes(): return lax.ppermute(block, ('tm', 'space'), route)  31.2 us
    ppermute x10, starting transfers between devices, swap_planes(): return lax.ppermute(block, ('tm', 'space'), route)  22.2 us
    ppermute x5, starting transfers between devices, swap_rows(): return lax.ppermute(block, 'tm', route)  11.1 us
    ppermute x7, starting transfers between devices, exchange(): lax.ppermute(pieces[k], 'tm', [(i, i ^ k) for i in range(count)])  9.17 us
    ppermute x3, starting transfers between devices, on_device(): lax.ppermute(pair, 'tm', [(i, i ^ 2 * k) for i in range(count)])  5.96 us
    ppermute x3, waiting for transfers between devices, on_device(): lax.ppermute(pair, 'tm', [(i, i ^ 2 * k) for i in range(count)])  4.59 us
    ppermute x7, waiting for transfers between devices, exchange(): lax.ppermute(pieces[k], 'tm', [(i, i ^ k) for i in range(count)])  3.88 us
    ppermute x5, waiting for transfers between devices, swap_rows(): return lax.ppermute(block, 'tm', route)  3.55 us
  transfers between devices with their start and end apart: 25, of which 16 were waited for; matrix products, arithmetic and copies ran while one was open for 0% of the time, Pallas kernels for 2%

profile of v12, /device:TPU:6, one launch (start us, length us, event | category | flops | bytes accessed | tf_op | source)
XLA Modules:
  0.0 101.6 jit_solution(17856727445536798761)
XLA Ops:
  0.6 1.4 %pack.1 = (f32[232,128]{1,0:T(8,128)S(1)}, f32[232,128]{1,0:T(8,128)S(1)}, f32[232,128]{1,0:T(8,128)S(1)}, f32[232,128]{1,0:T(8,128)S(1)}, f32[232,128]{1,0:T(8,...) custom-call(f32[2,2,96,128]{3,2,1,0:T(8,128)} %rest_0_.1, ...), custom_call_target="tpu_custom_call" | custom-call | tf_op jit(solution)/shard_map/pack/pallas_call | solution.py:527
  2.0 3.3 %collective-permute-start = (f32[232,128]{1,0:T(8,128)S(1)}, f32[232,128]{1,0:T(8,128)S(1)}, u32[]{:S(2)}, u32[]{:S(2)}) collective-permute-start(f32[232,128]{1,0:T(8,128)S(1)} %get-tuple-element.52), channel_id=1, source_target_pairs={{0,128},{32,160},{64,192},{96,224},{128,0},{160,32},{192,64},{224,... | collective-permute-start | bytes 356360 | tf_op jit(solution)/shard_map/ppermute | solution.py:499
  5.3 0.7 collective-permute-start.1
  6.0 0.4 collective-permute-start.2
  6.3 1.6 %collective-permute-start.3 = (f32[232,128]{1,0:T(8,128)S(1)}, f32[232,128]{1,0:T(8,128)S(1)}, u32[]{:S(2)}, u32[]{:S(2)}) collective-permute-start(f32[232,128]{1,0:T(8,128)S(1)} %get-tuple-element.58), channel_id=1, source_target_pairs={{0,160},{32,128},{64,224},{96,192},{128,32},{160,0},{192,96},{224,... | collective-permute-start | bytes 356360 | tf_op jit(solution)/shard_map/ppermute | solution.py:499
  8.0 1.8 %collective-permute-start.4 = (f32[232,128]{1,0:T(8,128)S(1)}, f32[232,128]{1,0:T(8,128)S(1)}, u32[]{:S(2)}, u32[]{:S(2)}) collective-permute-start(f32[232,128]{1,0:T(8,128)S(1)} %get-tuple-element.59), channel_id=1, source_target_pairs={{0,96},{32,64},{64,32},{96,0},{128,224},{160,192},{192,160},{224,1... | collective-permute-start | bytes 356360 | tf_op jit(solution)/shard_map/ppermute | solution.py:499
  9.8 0.4 collective-permute-start.5
  10.2 1.7 %collective-permute-done.1.rest_1_ = f32[232,128]{1,0:T(8,128)S(1)} collective-permute-done((f32[232,128]{1,0:T(8,128)S(1)}, f32[232,128]{1,0:T(8,128)S(1)}, u32[]{:S(2)}, u32[]{:S(2)}) %collective-permute-start.1) | collective-permute-done | bytes 118816 | tf_op jit(solution)/shard_map/ppermute | solution.py:499
  11.8 1.0 %collective-permute-start.6 = (f32[232,128]{1,0:T(8,128)S(1)}, f32[232,128]{1,0:T(8,128)S(1)}, u32[]{:S(2)}, u32[]{:S(2)}) collective-permute-start(f32[232,128]{1,0:T(8,128)S(1)} %get-tuple-element.61), channel_id=1, source_target_pairs={{0,32},{32,0},{64,96},{96,64},{128,160},{160,128},{192,224},{224,1... | collective-permute-start | bytes 356360 | tf_op jit(solution)/shard_map/ppermute | solution.py:499
  12.8 2.2 %collective-permute-done.2.rest_2_ = f32[232,128]{1,0:T(8,128)S(1)} collective-permute-done((f32[232,128]{1,0:T(8,128)S(1)}, f32[232,128]{1,0:T(8,128)S(1)}, u32[]{:S(2)}, u32[]{:S(2)}) %collective-permute-start.2) | collective-permute-done | bytes 118816 | tf_op jit(solution)/shard_map/ppermute | solution.py:499
  15.1 1.9 %collective-permute-start.7 = (f32[3,24,128]{2,1,0:T(8,128)S(1)}, f32[3,24,128]{2,1,0:T(8,128)S(1)}, u32[]{:S(2)}, u32[]{:S(2)}) collective-permute-start(f32[3,24,128]{2,1,0:T(8,128)S(1)} %get-tuple-element.63), channel_id=1, source_target_pairs={{0,1},{1,0},{2,3},{3,2},{4,5},{5,4},{6,7},{7,6},{8,9},{9,8},{10,11... | collective-permute-start | bytes 110600 | tf_op jit(solution)/shard_map/ppermute | solution.py:519
  17.0 5.2 %collective-permute-start.8 = (f32[3,24,128]{2,1,0:T(8,128)S(1)}, f32[3,24,128]{2,1,0:T(8,128)S(1)}, u32[]{:S(2)}, u32[]{:S(2)}) collective-permute-start(f32[3,24,128]{2,1,0:T(8,128)S(1)} %get-tuple-element.64), channel_id=1, source_target_pairs={{0,32},{1,2},{2,1},{3,4},{4,3},{5,6},{6,5},{7,8},{8,7},{9,10},{10,... | collective-permute-start | bytes 110600 | tf_op jit(solution)/shard_map/ppermute | solution.py:519
  22.2 1.9 %collective-permute-done.8.rest_9_.near = f32[3,24,128]{2,1,0:T(8,128)S(1)} collective-permute-done((f32[3,24,128]{2,1,0:T(8,128)S(1)}, f32[3,24,128]{2,1,0:T(8,128)S(1)}, u32[]{:S(2)}, u32[]{:S(2)}) %collective-permute-start.8) | collective-permute-done | bytes 36896 | tf_op jit(solution)/shard_map/ppermute | solution.py:519
  24.1 1.0 spread.1
  25.2 4.2 %collective-permute-start.10 = (f32[168,8,128]{2,1,0:T(8,128)S(1)}, f32[168,8,128]{2,1,0:T(8,128)S(1)}, u32[]{:S(2)}, u32[]{:S(2)}) collective-permute-start(f32[168,8,128]{2,1,0:T(8,128)S(1)} %get-tuple-element.67), channel_id=1, source_target_pairs={{0,32},{1,2},{2,1},{3,4},{4,3},{5,6},{6,5},{7,8},{8,7},{9,10},{10,... | collective-permute-start | bytes 2064392 | tf_op jit(solution)/shard_map/ppermute | solution.py:519
  29.4 0.2 coefficients.1
  29.7 0.4 prepare.2
  30.1 9.3 %collective-permute-done.9.far.tfar = f32[168,8,128]{2,1,0:T(8,128)S(1)} collective-permute-done((f32[168,8,128]{2,1,0:T(8,128)S(1)}, f32[168,8,128]{2,1,0:T(8,128)S(1)}, u32[]{:S(2)}, u32[]{:S(2)}) %collective-permute-start.9) | collective-permute-done | bytes 688160 | tf_op jit(solution)/shard_map/ppermute | solution.py:519
  39.3 2.2 %collective-permute-done.10.near.tnear = f32[168,8,128]{2,1,0:T(8,128)S(1)} collective-permute-done((f32[168,8,128]{2,1,0:T(8,128)S(1)}, f32[168,8,128]{2,1,0:T(8,128)S(1)}, u32[]{:S(2)}, u32[]{:S(2)}) %collective-permute-start.10) | collective-permute-done | bytes 688160 | tf_op jit(solution)/shard_map/ppermute | solution.py:519
  41.5 1.0 front.2
  42.7 3.9 %collective-permute-start.12 = (f32[26,4,8,128]{3,2,1,0:T(8,128)S(1)}, f32[26,4,8,128]{3,2,1,0:T(8,128)S(1)}, u32[]{:S(2)}, u32[]{:S(2)}) collective-permute-start(f32[26,4,8,128]{3,2,1,0:T(8,128)S(1)} %get-tuple-element.77), channel_id=1, source_target_pairs={{0,32},{1,2},{2,1},{3,4},{4,3},{5,6},{6,5},{7,8},{8,7},{9,10},{10,... | collective-permute-start | bytes 1277960 | tf_op jit(solution)/shard_map/ppermute | solution.py:519
  46.6 0.3 ahead.2.part
  46.9 3.9 %collective-permute-done.11.far = f32[26,4,8,128]{3,2,1,0:T(8,128)S(1)} collective-permute-done((f32[26,4,8,128]{3,2,1,0:T(8,128)S(1)}, f32[26,4,8,128]{3,2,1,0:T(8,128)S(1)}, u32[]{:S(2)}, u32[]{:S(2)}) %collective-permute-start.11) | collective-permute-done | bytes 426016 | tf_op jit(solution)/shard_map/ppermute | solution.py:519
  50.8 2.2 %collective-permute-done.12.near = f32[26,4,8,128]{3,2,1,0:T(8,128)S(1)} collective-permute-done((f32[26,4,8,128]{3,2,1,0:T(8,128)S(1)}, f32[26,4,8,128]{3,2,1,0:T(8,128)S(1)}, u32[]{:S(2)}, u32[]{:S(2)}) %collective-permute-start.12) | collective-permute-done | bytes 426016 | tf_op jit(solution)/shard_map/ppermute | solution.py:519
  53.0 0.7 middle.1
  53.8 4.1 %collective-permute-start.14 = (f32[24,4,8,128]{3,2,1,0:T(8,128)S(1)}, f32[24,4,8,128]{3,2,1,0:T(8,128)S(1)}, u32[]{:S(2)}, u32[]{:S(2)}) collective-permute-start(f32[24,4,8,128]{3,2,1,0:T(8,128)S(1)} %get-tuple-element.81), channel_id=1, source_target_pairs={{0,32},{1,2},{2,1},{3,4},{4,3},{5,6},{6,5},{7,8},{8,7},{9,10},{10,... | collective-permute-start | bytes 1179656 | tf_op jit(solution)/shard_map/ppermute | solution.py:519
  57.9 2.0 %collective-permute-start.15 = (f32[2,4,4,8,128]{4,3,2,1,0:T(8,128)S(1)}, f32[2,4,4,8,128]{4,3,2,1,0:T(8,128)S(1)}, u32[]{:S(2)}, u32[]{:S(2)}) collective-permute-start(f32[2,4,4,8,128]{4,3,2,1,0:T(8,128)S(1)} %get-tuple-element.82), channel_id=1, source_target_pairs={{32,64},{64,32},{96,128},{128,96},{160,192},{192,160},{224,0},{0,2... | collective-permute-start | bytes 393224 | tf_op jit(solution)/shard_map/ppermute | solution.py:508
  59.9 1.9 %collective-permute-start.16 = (f32[2,4,4,8,128]{4,3,2,1,0:T(8,128)S(1)}, f32[2,4,4,8,128]{4,3,2,1,0:T(8,128)S(1)}, u32[]{:S(2)}, u32[]{:S(2)}) collective-permute-start(f32[2,4,4,8,128]{4,3,2,1,0:T(8,128)S(1)} %get-tuple-element.83), channel_id=1, source_target_pairs={{0,32},{32,0},{64,96},{96,64},{128,160},{160,128},{192,224},{224,1... | collective-permute-start | bytes 393224 | tf_op jit(solution)/shard_map/ppermute | solution.py:508
  61.8 1.7 %collective-permute-done.15.row1 = f32[2,4,4,8,128]{4,3,2,1,0:T(8,128)S(1)} collective-permute-done((f32[2,4,4,8,128]{4,3,2,1,0:T(8,128)S(1)}, f32[2,4,4,8,128]{4,3,2,1,0:T(8,128)S(1)}, u32[]{:S(2)}, u32[]{:S(2)}) %collective-permute-start.15) | collective-permute-done | bytes 131104 | tf_op jit(solution)/shard_map/ppermute | solution.py:508
  63.5 0.4 collective-permute-done.14.near.near_x
  64.0 4.6 %collective-permute-start.17 = (f32[10,4,8,128]{3,2,1,0:T(8,128)S(1)}, f32[10,4,8,128]{3,2,1,0:T(8,128)S(1)}, u32[]{:S(2)}, u32[]{:S(2)}) collective-permute-start(f32[10,4,8,128]{3,2,1,0:T(8,128)S(1)} %get-tuple-element.85), channel_id=1, source_target_pairs={{32,64},{64,32},{96,128},{128,96},{160,192},{192,160},{224,0},{0,2... | collective-permute-start | bytes 491528 | tf_op jit(solution)/shard_map/ppermute | solution.py:508
  68.6 1.9 %collective-permute-start.18 = (f32[10,4,8,128]{3,2,1,0:T(8,128)S(1)}, f32[10,4,8,128]{3,2,1,0:T(8,128)S(1)}, u32[]{:S(2)}, u32[]{:S(2)}) collective-permute-start(f32[10,4,8,128]{3,2,1,0:T(8,128)S(1)} %get-tuple-element.86), channel_id=1, source_target_pairs={{0,32},{32,0},{64,96},{96,64},{128,160},{160,128},{192,224},{224,1... | collective-permute-start | bytes 491528 | tf_op jit(solution)/shard_map/ppermute | solution.py:508
  70.5 0.4 prepare.3
  70.9 0.7 collective-permute-done.17.edge1
  71.7 1.0 %front.3 = (f32[32,4,8,128]{3,2,1,0:T(8,128)S(1)}, f32[2,16,4,8,128]{4,3,2,1,0:T(8,128)S(1)}, f32[26,4,8,128]{3,2,1,0:T(8,128)S(1)}, f32[26,4,8,128]{3,2,1,0:T(8,128)S(1)}) custom-call(f32[136,8,128]{2,1,0:T(8,128)S(1)} %bitcast.12, f32[136,8,128]{2,1,0:T(8,128)S(1)} %bitcast.11, f32[2,20,4,8,128]{4,3,2,1,0:T(8,128)S(1)} %get-tuple-element.89.own, ...), custom_call_target="tpu_custom_call" | custom-call | tf_op jit(solution)/shard_map/front/pallas_call | solution.py:560
  72.9 2.4 %collective-permute-start.20 = (f32[26,4,8,128]{3,2,1,0:T(8,128)S(1)}, f32[26,4,8,128]{3,2,1,0:T(8,128)S(1)}, u32[]{:S(2)}, u32[]{:S(2)}) collective-permute-start(f32[26,4,8,128]{3,2,1,0:T(8,128)S(1)} %get-tuple-element.93), channel_id=1, source_target_pairs={{0,32},{1,2},{2,1},{3,4},{4,3},{5,6},{6,5},{7,8},{8,7},{9,10},{10,... | collective-permute-start | bytes 1277960 | tf_op jit(solution)/shard_map/ppermute | solution.py:519
  75.2 0.3 ahead.3.part
  75.6 9.1 %collective-permute-done.19.far = f32[26,4,8,128]{3,2,1,0:T(8,128)S(1)} collective-permute-done((f32[26,4,8,128]{3,2,1,0:T(8,128)S(1)}, f32[26,4,8,128]{3,2,1,0:T(8,128)S(1)}, u32[]{:S(2)}, u32[]{:S(2)}) %collective-permute-start.19) | collective-permute-done | bytes 426016 | tf_op jit(solution)/shard_map/ppermute | solution.py:519
  84.6 2.2 %collective-permute-done.20.near = f32[26,4,8,128]{3,2,1,0:T(8,128)S(1)} collective-permute-done((f32[26,4,8,128]{3,2,1,0:T(8,128)S(1)}, f32[26,4,8,128]{3,2,1,0:T(8,128)S(1)}, u32[]{:S(2)}, u32[]{:S(2)}) %collective-permute-start.20) | collective-permute-done | bytes 426016 | tf_op jit(solution)/shard_map/ppermute | solution.py:519
  86.9 1.3 %last.1 = (f32[4,96,128]{2,1,0:T(8,128)S(1)}, f32[4,96,128]{2,1,0:T(8,128)S(1)}) custom-call(f32[26,4,8,128]{3,2,1,0:T(8,128)S(1)} %collective-permute-done.19.far, f32[26,4,8,128]{3,2,1,0:T(8,128)S(1)} %collective-permute-done.20.near, f32[2,16,4,8,128]{4,3,2,1,0:T(8,128)S(1)} %get-tuple-element.94.it, f32[36,4,8,128]{3,2,1,0:T(8,128)S(1)} %get-tuple-element.90.kept, ...), custom_call_target="tpu_custom_call" | custom-call | tf_op jit(solution)/shard_map/last/pallas_call | solution.py:590
  88.1 0.8 collective-permute-start.21
  88.9 1.1 %collective-permute-done.21.other = f32[4,96,128]{2,1,0:T(8,128)S(1)} collective-permute-done((f32[4,96,128]{2,1,0:T(8,128)S(1)}, f32[4,96,128]{2,1,0:T(8,128)S(1)}, u32[]{:S(2)}, u32[]{:S(2)}) %collective-permute-start.21) | collective-permute-done | bytes 196640 | tf_op jit(solution)/shard_map/ppermute | solution.py:508
  90.0 4.7 %collective-permute-start.22 = (f32[2,96,128]{2,1,0:T(8,128)S(1)}, f32[2,96,128]{2,1,0:T(8,128)S(1)}, u32[]{:S(2)}, u32[]{:S(2)}) collective-permute-start(f32[2,96,128]{2,1,0:T(8,128)S(1)} %get-tuple-element.99), channel_id=1, source_target_pairs={{0,128},{32,160},{64,192},{96,224},{128,0},{160,32},{192,64},{224,... | collective-permute-start | bytes 294920 | tf_op jit(solution)/shard_map/ppermute | solution.py:601
  94.7 1.2 %collective-permute-start.24 = (f32[2,96,128]{2,1,0:T(8,128)S(1)}, f32[2,96,128]{2,1,0:T(8,128)S(1)}, u32[]{:S(2)}, u32[]{:S(2)}) collective-permute-start(f32[2,96,128]{2,1,0:T(8,128)S(1)} %get-tuple-element.101), channel_id=1, source_target_pairs={{0,192},{32,224},{64,128},{96,160},{128,64},{160,96},{192,0},{224,... | collective-permute-start | bytes 294920 | tf_op jit(solution)/shard_map/ppermute | solution.py:601
  96.0 1.9 %collective-permute-done.22.a = f32[2,96,128]{2,1,0:T(8,128)S(1)} collective-permute-done((f32[2,96,128]{2,1,0:T(8,128)S(1)}, f32[2,96,128]{2,1,0:T(8,128)S(1)}, u32[]{:S(2)}, u32[]{:S(2)}) %collective-permute-start.22) | collective-permute-done | bytes 98336 | tf_op jit(solution)/shard_map/ppermute | solution.py:601
  97.9 1.5 %collective-permute-done.23.b = f32[2,96,128]{2,1,0:T(8,128)S(1)} collective-permute-done((f32[2,96,128]{2,1,0:T(8,128)S(1)}, f32[2,96,128]{2,1,0:T(8,128)S(1)}, u32[]{:S(2)}, u32[]{:S(2)}) %collective-permute-start.23) | collective-permute-done | bytes 98336 | tf_op jit(solution)/shard_map/ppermute | solution.py:601
  99.4 1.2 %collective-permute-done.24.c = f32[2,96,128]{2,1,0:T(8,128)S(1)} collective-permute-done((f32[2,96,128]{2,1,0:T(8,128)S(1)}, f32[2,96,128]{2,1,0:T(8,128)S(1)}, u32[]{:S(2)}, u32[]{:S(2)}) %collective-permute-start.24) | collective-permute-done | bytes 98336 | tf_op jit(solution)/shard_map/ppermute | solution.py:601
  100.6 0.8 unpack.1
  (17 shorter events, 0.6 us)
Async XLA Ops:
  2.0 7.8 %collective-permute-start = (f32[232,128]{1,0:T(8,128)S(1)}, f32[232,128]{1,0:T(8,128)S(1)}, u32[]{:S(2)}, u32[]{:S(2)}) collective-permute-start(f32[232,128]{1,0:T(8,128)S(1)} %get-tuple-element.52), channel_id=1, source_target_pairs={{0,128},{32,160},{64,192},{96,224},{128,0},{160,32},{192,64},{224,... | collective-permute-start | bytes 356360 | tf_op jit(solution)/shard_map/ppermute | solution.py:499
  5.3 6.5 %collective-permute-start.1 = (f32[232,128]{1,0:T(8,128)S(1)}, f32[232,128]{1,0:T(8,128)S(1)}, u32[]{:S(2)}, u32[]{:S(2)}) collective-permute-start(f32[232,128]{1,0:T(8,128)S(1)} %get-tuple-element.53), channel_id=1, source_target_pairs={{0,64},{32,96},{64,0},{96,32},{128,192},{160,224},{192,128},{224,1... | collective-permute-start | bytes 356360 | tf_op jit(solution)/shard_map/ppermute | solution.py:499
  6.0 9.1 %collective-permute-start.2 = (f32[232,128]{1,0:T(8,128)S(1)}, f32[232,128]{1,0:T(8,128)S(1)}, u32[]{:S(2)}, u32[]{:S(2)}) collective-permute-start(f32[232,128]{1,0:T(8,128)S(1)} %get-tuple-element.57), channel_id=1, source_target_pairs={{0,192},{32,224},{64,128},{96,160},{128,64},{160,96},{192,0},{224,... | collective-permute-start | bytes 356360 | tf_op jit(solution)/shard_map/ppermute | solution.py:499
  6.3 10.6 %collective-permute-start.3 = (f32[232,128]{1,0:T(8,128)S(1)}, f32[232,128]{1,0:T(8,128)S(1)}, u32[]{:S(2)}, u32[]{:S(2)}) collective-permute-start(f32[232,128]{1,0:T(8,128)S(1)} %get-tuple-element.58), channel_id=1, source_target_pairs={{0,160},{32,128},{64,224},{96,192},{128,32},{160,0},{192,96},{224,... | collective-permute-start | bytes 356360 | tf_op jit(solution)/shard_map/ppermute | solution.py:499
  8.0 14.2 %collective-permute-start.4 = (f32[232,128]{1,0:T(8,128)S(1)}, f32[232,128]{1,0:T(8,128)S(1)}, u32[]{:S(2)}, u32[]{:S(2)}) collective-permute-start(f32[232,128]{1,0:T(8,128)S(1)} %get-tuple-element.59), channel_id=1, source_target_pairs={{0,96},{32,64},{64,32},{96,0},{128,224},{160,192},{192,160},{224,1... | collective-permute-start | bytes 356360 | tf_op jit(solution)/shard_map/ppermute | solution.py:499
  9.8 12.4 %collective-permute-start.5 = (f32[232,128]{1,0:T(8,128)S(1)}, f32[232,128]{1,0:T(8,128)S(1)}, u32[]{:S(2)}, u32[]{:S(2)}) collective-permute-start(f32[232,128]{1,0:T(8,128)S(1)} %get-tuple-element.60), channel_id=1, source_target_pairs={{0,224},{32,192},{64,160},{96,128},{128,96},{160,64},{192,32},{224... | collective-permute-start | bytes 356360 | tf_op jit(solution)/shard_map/ppermute | solution.py:499
  11.8 10.4 %collective-permute-start.6 = (f32[232,128]{1,0:T(8,128)S(1)}, f32[232,128]{1,0:T(8,128)S(1)}, u32[]{:S(2)}, u32[]{:S(2)}) collective-permute-start(f32[232,128]{1,0:T(8,128)S(1)} %get-tuple-element.61), channel_id=1, source_target_pairs={{0,32},{32,0},{64,96},{96,64},{128,160},{160,128},{192,224},{224,1... | collective-permute-start | bytes 356360 | tf_op jit(solution)/shard_map/ppermute | solution.py:499
  15.1 7.1 %collective-permute-start.7 = (f32[3,24,128]{2,1,0:T(8,128)S(1)}, f32[3,24,128]{2,1,0:T(8,128)S(1)}, u32[]{:S(2)}, u32[]{:S(2)}) collective-permute-start(f32[3,24,128]{2,1,0:T(8,128)S(1)} %get-tuple-element.63), channel_id=1, source_target_pairs={{0,1},{1,0},{2,3},{3,2},{4,5},{5,4},{6,7},{7,6},{8,9},{9,8},{10,11... | collective-permute-start | bytes 110600 | tf_op jit(solution)/shard_map/ppermute | solution.py:519
  17.0 7.1 %collective-permute-start.8 = (f32[3,24,128]{2,1,0:T(8,128)S(1)}, f32[3,24,128]{2,1,0:T(8,128)S(1)}, u32[]{:S(2)}, u32[]{:S(2)}) collective-permute-start(f32[3,24,128]{2,1,0:T(8,128)S(1)} %get-tuple-element.64), channel_id=1, source_target_pairs={{0,32},{1,2},{2,1},{3,4},{4,3},{5,6},{6,5},{7,8},{8,7},{9,10},{10,... | collective-permute-start | bytes 110600 | tf_op jit(solution)/shard_map/ppermute | solution.py:519
  25.1 14.2 %collective-permute-start.9 = (f32[168,8,128]{2,1,0:T(8,128)S(1)}, f32[168,8,128]{2,1,0:T(8,128)S(1)}, u32[]{:S(2)}, u32[]{:S(2)}) collective-permute-start(f32[168,8,128]{2,1,0:T(8,128)S(1)} %get-tuple-element.66), channel_id=1, source_target_pairs={{0,1},{1,0},{2,3},{3,2},{4,5},{5,4},{6,7},{7,6},{8,9},{9,8},{10,11... | collective-permute-start | bytes 2064392 | tf_op jit(solution)/shard_map/ppermute | solution.py:519
  25.2 16.3 %collective-permute-start.10 = (f32[168,8,128]{2,1,0:T(8,128)S(1)}, f32[168,8,128]{2,1,0:T(8,128)S(1)}, u32[]{:S(2)}, u32[]{:S(2)}) collective-permute-start(f32[168,8,128]{2,1,0:T(8,128)S(1)} %get-tuple-element.67), channel_id=1, source_target_pairs={{0,32},{1,2},{2,1},{3,4},{4,3},{5,6},{6,5},{7,8},{8,7},{9,10},{10,... | collective-permute-start | bytes 2064392 | tf_op jit(solution)/shard_map/ppermute | solution.py:519
  42.6 8.2 %collective-permute-start.11 = (f32[26,4,8,128]{3,2,1,0:T(8,128)S(1)}, f32[26,4,8,128]{3,2,1,0:T(8,128)S(1)}, u32[]{:S(2)}, u32[]{:S(2)}) collective-permute-start(f32[26,4,8,128]{3,2,1,0:T(8,128)S(1)} %get-tuple-element.76), channel_id=1, source_target_pairs={{0,1},{1,0},{2,3},{3,2},{4,5},{5,4},{6,7},{7,6},{8,9},{9,8},{10,11... | collective-permute-start | bytes 1277960 | tf_op jit(solution)/shard_map/ppermute | solution.py:519
  42.7 10.3 %collective-permute-start.12 = (f32[26,4,8,128]{3,2,1,0:T(8,128)S(1)}, f32[26,4,8,128]{3,2,1,0:T(8,128)S(1)}, u32[]{:S(2)}, u32[]{:S(2)}) collective-permute-start(f32[26,4,8,128]{3,2,1,0:T(8,128)S(1)} %get-tuple-element.77), channel_id=1, source_target_pairs={{0,32},{1,2},{2,1},{3,4},{4,3},{5,6},{6,5},{7,8},{8,7},{9,10},{10,... | collective-permute-start | bytes 1277960 | tf_op jit(solution)/shard_map/ppermute | solution.py:519
  53.7 9.8 %collective-permute-start.13 = (f32[24,4,8,128]{3,2,1,0:T(8,128)S(1)}, f32[24,4,8,128]{3,2,1,0:T(8,128)S(1)}, u32[]{:S(2)}, u32[]{:S(2)}) collective-permute-start(f32[24,4,8,128]{3,2,1,0:T(8,128)S(1)} %get-tuple-element.80), channel_id=1, source_target_pairs={{0,1},{1,0},{2,3},{3,2},{4,5},{5,4},{6,7},{7,6},{8,9},{9,8},{10,11... | collective-permute-start | bytes 1179656 | tf_op jit(solution)/shard_map/ppermute | solution.py:519
  53.8 10.2 %collective-permute-start.14 = (f32[24,4,8,128]{3,2,1,0:T(8,128)S(1)}, f32[24,4,8,128]{3,2,1,0:T(8,128)S(1)}, u32[]{:S(2)}, u32[]{:S(2)}) collective-permute-start(f32[24,4,8,128]{3,2,1,0:T(8,128)S(1)} %get-tuple-element.81), channel_id=1, source_target_pairs={{0,32},{1,2},{2,1},{3,4},{4,3},{5,6},{6,5},{7,8},{8,7},{9,10},{10,... | collective-permute-start | bytes 1179656 | tf_op jit(solution)/shard_map/ppermute | solution.py:519
  57.9 5.6 %collective-permute-start.15 = (f32[2,4,4,8,128]{4,3,2,1,0:T(8,128)S(1)}, f32[2,4,4,8,128]{4,3,2,1,0:T(8,128)S(1)}, u32[]{:S(2)}, u32[]{:S(2)}) collective-permute-start(f32[2,4,4,8,128]{4,3,2,1,0:T(8,128)S(1)} %get-tuple-element.82), channel_id=1, source_target_pairs={{32,64},{64,32},{96,128},{128,96},{160,192},{192,160},{224,0},{0,2... | collective-permute-start | bytes 393224 | tf_op jit(solution)/shard_map/ppermute | solution.py:508
  59.9 3.6 %collective-permute-start.16 = (f32[2,4,4,8,128]{4,3,2,1,0:T(8,128)S(1)}, f32[2,4,4,8,128]{4,3,2,1,0:T(8,128)S(1)}, u32[]{:S(2)}, u32[]{:S(2)}) collective-permute-start(f32[2,4,4,8,128]{4,3,2,1,0:T(8,128)S(1)} %get-tuple-element.83), channel_id=1, source_target_pairs={{0,32},{32,0},{64,96},{96,64},{128,160},{160,128},{192,224},{224,1... | collective-permute-start | bytes 393224 | tf_op jit(solution)/shard_map/ppermute | solution.py:508
  64.0 7.6 %collective-permute-start.17 = (f32[10,4,8,128]{3,2,1,0:T(8,128)S(1)}, f32[10,4,8,128]{3,2,1,0:T(8,128)S(1)}, u32[]{:S(2)}, u32[]{:S(2)}) collective-permute-start(f32[10,4,8,128]{3,2,1,0:T(8,128)S(1)} %get-tuple-element.85), channel_id=1, source_target_pairs={{32,64},{64,32},{96,128},{128,96},{160,192},{192,160},{224,0},{0,2... | collective-permute-start | bytes 491528 | tf_op jit(solution)/shard_map/ppermute | solution.py:508
  68.6 3.0 %collective-permute-start.18 = (f32[10,4,8,128]{3,2,1,0:T(8,128)S(1)}, f32[10,4,8,128]{3,2,1,0:T(8,128)S(1)}, u32[]{:S(2)}, u32[]{:S(2)}) collective-permute-start(f32[10,4,8,128]{3,2,1,0:T(8,128)S(1)} %get-tuple-element.86), channel_id=1, source_target_pairs={{0,32},{32,0},{64,96},{96,64},{128,160},{160,128},{192,224},{224,1... | collective-permute-start | bytes 491528 | tf_op jit(solution)/shard_map/ppermute | solution.py:508
  72.8 11.9 %collective-permute-start.19 = (f32[26,4,8,128]{3,2,1,0:T(8,128)S(1)}, f32[26,4,8,128]{3,2,1,0:T(8,128)S(1)}, u32[]{:S(2)}, u32[]{:S(2)}) collective-permute-start(f32[26,4,8,128]{3,2,1,0:T(8,128)S(1)} %get-tuple-element.92), channel_id=1, source_target_pairs={{0,1},{1,0},{2,3},{3,2},{4,5},{5,4},{6,7},{7,6},{8,9},{9,8},{10,11... | collective-permute-start | bytes 1277960 | tf_op jit(solution)/shard_map/ppermute | solution.py:519
  72.9 14.0 %collective-permute-start.20 = (f32[26,4,8,128]{3,2,1,0:T(8,128)S(1)}, f32[26,4,8,128]{3,2,1,0:T(8,128)S(1)}, u32[]{:S(2)}, u32[]{:S(2)}) collective-permute-start(f32[26,4,8,128]{3,2,1,0:T(8,128)S(1)} %get-tuple-element.93), channel_id=1, source_target_pairs={{0,32},{1,2},{2,1},{3,4},{4,3},{5,6},{6,5},{7,8},{8,7},{9,10},{10,... | collective-permute-start | bytes 1277960 | tf_op jit(solution)/shard_map/ppermute | solution.py:519
  88.1 1.9 %collective-permute-start.21 = (f32[4,96,128]{2,1,0:T(8,128)S(1)}, f32[4,96,128]{2,1,0:T(8,128)S(1)}, u32[]{:S(2)}, u32[]{:S(2)}) collective-permute-start(f32[4,96,128]{2,1,0:T(8,128)S(1)} %get-tuple-element.97), channel_id=1, source_target_pairs={{0,32},{32,0},{64,96},{96,64},{128,160},{160,128},{192,224},{224,1... | collective-permute-start | bytes 589832 | tf_op jit(solution)/shard_map/ppermute | solution.py:508
  90.0 7.9 %collective-permute-start.22 = (f32[2,96,128]{2,1,0:T(8,128)S(1)}, f32[2,96,128]{2,1,0:T(8,128)S(1)}, u32[]{:S(2)}, u32[]{:S(2)}) collective-permute-start(f32[2,96,128]{2,1,0:T(8,128)S(1)} %get-tuple-element.99), channel_id=1, source_target_pairs={{0,128},{32,160},{64,192},{96,224},{128,0},{160,32},{192,64},{224,... | collective-permute-start | bytes 294920 | tf_op jit(solution)/shard_map/ppermute | solution.py:601
  94.7 4.6 %collective-permute-start.23 = (f32[2,96,128]{2,1,0:T(8,128)S(1)}, f32[2,96,128]{2,1,0:T(8,128)S(1)}, u32[]{:S(2)}, u32[]{:S(2)}) collective-permute-start(f32[2,96,128]{2,1,0:T(8,128)S(1)} %get-tuple-element.100), channel_id=1, source_target_pairs={{0,64},{32,96},{64,0},{96,32},{128,192},{160,224},{192,128},{224,1... | collective-permute-start | bytes 294920 | tf_op jit(solution)/shard_map/ppermute | solution.py:601
  94.7 5.8 %collective-permute-start.24 = (f32[2,96,128]{2,1,0:T(8,128)S(1)}, f32[2,96,128]{2,1,0:T(8,128)S(1)}, u32[]{:S(2)}, u32[]{:S(2)}) collective-permute-start(f32[2,96,128]{2,1,0:T(8,128)S(1)} %get-tuple-element.101), channel_id=1, source_target_pairs={{0,192},{32,224},{64,128},{96,160},{128,64},{160,96},{192,0},{224,... | collective-permute-start | bytes 294920 | tf_op jit(solution)/shard_map/ppermute | solution.py:601

commit v13 on v11

--- a/solution.py
+++ b/solution.py
@@ -221,8 +221,15 @@
                     out[136 + (j - 2) * 2 + n] = v
 
 
+def halves(v):
+    high = v.astype(jnp.bfloat16)
+    return high, (v - high.astype(jnp.float32)).astype(jnp.bfloat16)
+
+
 def transform(matrix, block):
-    return jnp.dot(matrix, block, precision=lax.Precision.HIGHEST, preferred_element_type=jnp.float32)
+    (mh, ml), (bh, bl) = halves(matrix), halves(block)
+    dot = lambda p, q: jnp.dot(p, q, preferred_element_type=jnp.float32)
+    return dot(mh, bh) + (dot(mh, bl) + dot(ml, bh))
 
 
 def put_field(near, far, x, j, c, v):

time: 101 us -> 101 us (level)
  no operation moved by 1% of the time
where the time goes in v13:
time: 101 us
  waiting for transfers between devices  56.4 us (56%)
  starting transfers between devices  33.7 us (33%)
  Pallas kernels  9.48 us (9%)
    ppermute x8, waiting for transfers between devices, swap_planes(): return lax.ppermute(block, ('tm', 'space'), route)  34.9 us
    ppermute x8, starting transfers between devices, swap_planes(): return lax.ppermute(block, ('tm', 'space'), route)  18.3 us
    ppermute x5, waiting for transfers between devices, swap_rows(): return lax.ppermute(block, 'tm', route)  10.9 us
    ppermute x7, starting transfers between devices, exchange(): lax.ppermute(pieces[k], 'tm', [(i, i ^ k) for i in range(count)])  9.17 us
    ppermute x7, waiting for transfers between devices, exchange(): lax.ppermute(pieces[k], 'tm', [(i, i ^ k) for i in range(count)])  5.4 us
    ppermute x3, waiting for transfers between devices, on_device(): lax.ppermute(pair, 'tm', [(i, i ^ 2 * k) for i in range(count)])  5.21 us
    ppermute x3, starting transfers between devices, on_device(): lax.ppermute(pair, 'tm', [(i, i ^ 2 * k) for i in range(count)])  4.21 us
  transfers between devices with their start and end apart: 23, of which 18 were waited for; matrix products, arithmetic and copies ran while one was open for 0% of the time, Pallas kernels for 2%

profile of v13, /device:TPU:6, one launch (start us, length us, event | category | flops | bytes accessed | tf_op | source)
XLA Modules:
  0.0 100.5 jit_solution(14399329495524643332)
XLA Ops:
  0.6 1.4 %pack.1 = (f32[232,128]{1,0:T(8,128)S(1)}, f32[232,128]{1,0:T(8,128)S(1)}, f32[232,128]{1,0:T(8,128)S(1)}, f32[232,128]{1,0:T(8,128)S(1)}, f32[232,128]{1,0:T(8,...) custom-call(f32[2,2,96,128]{3,2,1,0:T(8,128)} %rest_0_.1, ...), custom_call_target="tpu_custom_call" | custom-call | tf_op jit(solution)/shard_map/pack/pallas_call | solution.py:538
  2.0 3.3 %collective-permute-start = (f32[232,128]{1,0:T(8,128)S(1)}, f32[232,128]{1,0:T(8,128)S(1)}, u32[]{:S(2)}, u32[]{:S(2)}) collective-permute-start(f32[232,128]{1,0:T(8,128)S(1)} %get-tuple-element.50), channel_id=1, source_target_pairs={{0,128},{32,160},{64,192},{96,224},{128,0},{160,32},{192,64},{224,... | collective-permute-start | bytes 356360 | tf_op jit(solution)/shard_map/ppermute | solution.py:510
  5.3 0.7 collective-permute-start.1
  6.0 0.4 collective-permute-start.2
  6.3 1.6 %collective-permute-start.3 = (f32[232,128]{1,0:T(8,128)S(1)}, f32[232,128]{1,0:T(8,128)S(1)}, u32[]{:S(2)}, u32[]{:S(2)}) collective-permute-start(f32[232,128]{1,0:T(8,128)S(1)} %get-tuple-element.53), channel_id=1, source_target_pairs={{0,160},{32,128},{64,224},{96,192},{128,32},{160,0},{192,96},{224,... | collective-permute-start | bytes 356360 | tf_op jit(solution)/shard_map/ppermute | solution.py:510
  8.0 1.8 %collective-permute-start.4 = (f32[232,128]{1,0:T(8,128)S(1)}, f32[232,128]{1,0:T(8,128)S(1)}, u32[]{:S(2)}, u32[]{:S(2)}) collective-permute-start(f32[232,128]{1,0:T(8,128)S(1)} %get-tuple-element.54), channel_id=1, source_target_pairs={{0,96},{32,64},{64,32},{96,0},{128,224},{160,192},{192,160},{224,1... | collective-permute-start | bytes 356360 | tf_op jit(solution)/shard_map/ppermute | solution.py:510
  9.8 0.4 collective-permute-start.5
  10.2 1.7 %collective-permute-done.1.rest_1_ = f32[232,128]{1,0:T(8,128)S(1)} collective-permute-done((f32[232,128]{1,0:T(8,128)S(1)}, f32[232,128]{1,0:T(8,128)S(1)}, u32[]{:S(2)}, u32[]{:S(2)}) %collective-permute-start.1) | collective-permute-done | bytes 118816 | tf_op jit(solution)/shard_map/ppermute | solution.py:510
  11.8 1.0 %collective-permute-start.6 = (f32[232,128]{1,0:T(8,128)S(1)}, f32[232,128]{1,0:T(8,128)S(1)}, u32[]{:S(2)}, u32[]{:S(2)}) collective-permute-start(f32[232,128]{1,0:T(8,128)S(1)} %get-tuple-element.56), channel_id=1, source_target_pairs={{0,32},{32,0},{64,96},{96,64},{128,160},{160,128},{192,224},{224,1... | collective-permute-start | bytes 356360 | tf_op jit(solution)/shard_map/ppermute | solution.py:510
  12.8 2.2 %collective-permute-done.2.rest_2_ = f32[232,128]{1,0:T(8,128)S(1)} collective-permute-done((f32[232,128]{1,0:T(8,128)S(1)}, f32[232,128]{1,0:T(8,128)S(1)}, u32[]{:S(2)}, u32[]{:S(2)}) %collective-permute-start.2) | collective-permute-done | bytes 118816 | tf_op jit(solution)/shard_map/ppermute | solution.py:510
  15.1 1.1 %collective-permute-done.4.rest_4_ = f32[232,128]{1,0:T(8,128)S(1)} collective-permute-done((f32[232,128]{1,0:T(8,128)S(1)}, f32[232,128]{1,0:T(8,128)S(1)}, u32[]{:S(2)}, u32[]{:S(2)}) %collective-permute-start.4) | collective-permute-done | bytes 118816 | tf_op jit(solution)/shard_map/ppermute | solution.py:510
  16.2 0.4 collective-permute-done.5.rest_5_
  16.6 0.6 spread.1
  17.2 2.0 %collective-permute-start.7 = (f32[177,8,128]{2,1,0:T(8,128)S(1)}, f32[177,8,128]{2,1,0:T(8,128)S(1)}, u32[]{:S(2)}, u32[]{:S(2)}) collective-permute-start(f32[177,8,128]{2,1,0:T(8,128)S(1)} %get-tuple-element.61.far), channel_id=1, source_target_pairs={{0,1},{1,0},{2,3},{3,2},{4,5},{5,4},{6,7},{7,6},{8,9},{9,8},{10,11... | collective-permute-start | bytes 2174984 | tf_op jit(solution)/shard_map/ppermute | solution.py:530
  19.2 5.2 %collective-permute-start.8 = (f32[177,8,128]{2,1,0:T(8,128)S(1)}, f32[177,8,128]{2,1,0:T(8,128)S(1)}, u32[]{:S(2)}, u32[]{:S(2)}) collective-permute-start(f32[177,8,128]{2,1,0:T(8,128)S(1)} %get-tuple-element.62.near), channel_id=1, source_target_pairs={{0,32},{1,2},{2,1},{3,4},{4,3},{5,6},{6,5},{7,8},{8,7},{9,10},{10,... | collective-permute-start | bytes 2174984 | tf_op jit(solution)/shard_map/ppermute | solution.py:530
  24.4 1.0 %coefficients.3 = (f32[768,128]{1,0:T(8,128)S(1)}, f32[68,2,8,128]{3,2,1,0:T(8,128)}) custom-call(f32[177,8,128]{2,1,0:T(8,128)S(1)} %get-tuple-element.61.far, f32[177,8,128]{2,1,0:T(8,128)S(1)} %get-tuple-element.62.near, f32[4,24,128]{2,1,0:T(8,128)S(1)} %get-tuple-element.64.here, f32[10,8,128]{2,1,0:T(8,128)S(1)} %get-tuple-element.65.consts), custom_call_target="tpu_custom_call" | custom-call | tf_op jit(solution)/shard_map/coefficients/pallas_call | solution.py:561
  25.4 0.4 prepare.2
  25.8 10.1 %collective-permute-done.7.far.tfar = f32[177,8,128]{2,1,0:T(8,128)S(1)} collective-permute-done((f32[177,8,128]{2,1,0:T(8,128)S(1)}, f32[177,8,128]{2,1,0:T(8,128)S(1)}, u32[]{:S(2)}, u32[]{:S(2)}) %collective-permute-start.7) | collective-permute-done | bytes 725024 | tf_op jit(solution)/shard_map/ppermute | solution.py:530
  35.9 4.9 %collective-permute-done.8.near.tnear = f32[177,8,128]{2,1,0:T(8,128)S(1)} collective-permute-done((f32[177,8,128]{2,1,0:T(8,128)S(1)}, f32[177,8,128]{2,1,0:T(8,128)S(1)}, u32[]{:S(2)}, u32[]{:S(2)}) %collective-permute-start.8) | collective-permute-done | bytes 725024 | tf_op jit(solution)/shard_map/ppermute | solution.py:530
  41.1 1.0 %front.2 = (f32[32,4,8,128]{3,2,1,0:T(8,128)S(1)}, f32[2,16,4,8,128]{4,3,2,1,0:T(8,128)S(1)}, f32[26,4,8,128]{3,2,1,0:T(8,128)S(1)}, f32[26,4,8,128]{3,2,1,0:T(8,128)S(1)}) custom-call(f32[177,8,128]{2,1,0:T(8,128)S(1)} %collective-permute-done.7.far.tfar, f32[177,8,128]{2,1,0:T(8,128)S(1)} %collective-permute-done.8.near.tnear, ...), custom_call_target="tpu_custom_call" | custom-call | tf_op jit(solution)/shard_map/front/pallas_call | solution.py:570
  42.2 3.9 %collective-permute-start.10 = (f32[26,4,8,128]{3,2,1,0:T(8,128)S(1)}, f32[26,4,8,128]{3,2,1,0:T(8,128)S(1)}, u32[]{:S(2)}, u32[]{:S(2)}) collective-permute-start(f32[26,4,8,128]{3,2,1,0:T(8,128)S(1)} %get-tuple-element.73), channel_id=1, source_target_pairs={{0,32},{1,2},{2,1},{3,4},{4,3},{5,6},{6,5},{7,8},{8,7},{9,10},{10,... | collective-permute-start | bytes 1277960 | tf_op jit(solution)/shard_map/ppermute | solution.py:530
  46.1 0.3 ahead.2.part
  46.4 7.0 %collective-permute-done.9.far = f32[26,4,8,128]{3,2,1,0:T(8,128)S(1)} collective-permute-done((f32[26,4,8,128]{3,2,1,0:T(8,128)S(1)}, f32[26,4,8,128]{3,2,1,0:T(8,128)S(1)}, u32[]{:S(2)}, u32[]{:S(2)}) %collective-permute-start.9) | collective-permute-done | bytes 426016 | tf_op jit(solution)/shard_map/ppermute | solution.py:530
  53.4 2.2 %collective-permute-done.10.near = f32[26,4,8,128]{3,2,1,0:T(8,128)S(1)} collective-permute-done((f32[26,4,8,128]{3,2,1,0:T(8,128)S(1)}, f32[26,4,8,128]{3,2,1,0:T(8,128)S(1)}, u32[]{:S(2)}, u32[]{:S(2)}) %collective-permute-start.10) | collective-permute-done | bytes 426016 | tf_op jit(solution)/shard_map/ppermute | solution.py:530
  55.6 0.7 middle.1
  56.4 3.6 %collective-permute-start.12 = (f32[24,4,8,128]{3,2,1,0:T(8,128)S(1)}, f32[24,4,8,128]{3,2,1,0:T(8,128)S(1)}, u32[]{:S(2)}, u32[]{:S(2)}) collective-permute-start(f32[24,4,8,128]{3,2,1,0:T(8,128)S(1)} %get-tuple-element.77), channel_id=1, source_target_pairs={{0,32},{1,2},{2,1},{3,4},{4,3},{5,6},{6,5},{7,8},{8,7},{9,10},{10,... | collective-permute-start | bytes 1179656 | tf_op jit(solution)/shard_map/ppermute | solution.py:530
  60.1 0.9 collective-permute-start.14
  61.0 4.7 %collective-permute-done.13.row1 = f32[2,4,4,8,128]{4,3,2,1,0:T(8,128)S(1)} collective-permute-done((f32[2,4,4,8,128]{4,3,2,1,0:T(8,128)S(1)}, f32[2,4,4,8,128]{4,3,2,1,0:T(8,128)S(1)}, u32[]{:S(2)}, u32[]{:S(2)}) %collective-permute-start.13) | collective-permute-done | bytes 131104 | tf_op jit(solution)/shard_map/ppermute | solution.py:519
  65.7 0.4 collective-permute-done.11.far.far_x
  66.1 2.2 %collective-permute-done.12.near.near_x = f32[24,4,8,128]{3,2,1,0:T(8,128)S(1)} collective-permute-done((f32[24,4,8,128]{3,2,1,0:T(8,128)S(1)}, f32[24,4,8,128]{3,2,1,0:T(8,128)S(1)}, u32[]{:S(2)}, u32[]{:S(2)}) %collective-permute-start.12) | collective-permute-done | bytes 393248 | tf_op jit(solution)/shard_map/ppermute | solution.py:530
  68.3 0.3 collective-permute-start.15
  68.6 0.7 collective-permute-start.16
  69.3 0.4 prepare.3
  69.7 4.8 %collective-permute-done.15.edge1 = f32[10,4,8,128]{3,2,1,0:T(8,128)S(1)} collective-permute-done((f32[10,4,8,128]{3,2,1,0:T(8,128)S(1)}, f32[10,4,8,128]{3,2,1,0:T(8,128)S(1)}, u32[]{:S(2)}, u32[]{:S(2)}) %collective-permute-start.15) | collective-permute-done | bytes 163872 | tf_op jit(solution)/shard_map/ppermute | solution.py:519
  74.7 1.0 front.3
  75.8 3.3 %collective-permute-start.18 = (f32[26,4,8,128]{3,2,1,0:T(8,128)S(1)}, f32[26,4,8,128]{3,2,1,0:T(8,128)S(1)}, u32[]{:S(2)}, u32[]{:S(2)}) collective-permute-start(f32[26,4,8,128]{3,2,1,0:T(8,128)S(1)} %get-tuple-element.89), channel_id=1, source_target_pairs={{0,32},{1,2},{2,1},{3,4},{4,3},{5,6},{6,5},{7,8},{8,7},{9,10},{10,... | collective-permute-start | bytes 1277960 | tf_op jit(solution)/shard_map/ppermute | solution.py:530
  79.0 0.3 ahead.3.part
  79.4 5.9 %collective-permute-done.17.far = f32[26,4,8,128]{3,2,1,0:T(8,128)S(1)} collective-permute-done((f32[26,4,8,128]{3,2,1,0:T(8,128)S(1)}, f32[26,4,8,128]{3,2,1,0:T(8,128)S(1)}, u32[]{:S(2)}, u32[]{:S(2)}) %collective-permute-start.17) | collective-permute-done | bytes 426016 | tf_op jit(solution)/shard_map/ppermute | solution.py:530
  85.2 2.2 %collective-permute-done.18.near = f32[26,4,8,128]{3,2,1,0:T(8,128)S(1)} collective-permute-done((f32[26,4,8,128]{3,2,1,0:T(8,128)S(1)}, f32[26,4,8,128]{3,2,1,0:T(8,128)S(1)}, u32[]{:S(2)}, u32[]{:S(2)}) %collective-permute-start.18) | collective-permute-done | bytes 426016 | tf_op jit(solution)/shard_map/ppermute | solution.py:530
  87.4 1.1 %last.1 = (f32[4,96,128]{2,1,0:T(8,128)S(1)}, f32[4,96,128]{2,1,0:T(8,128)S(1)}) custom-call(f32[26,4,8,128]{3,2,1,0:T(8,128)S(1)} %collective-permute-done.17.far, f32[26,4,8,128]{3,2,1,0:T(8,128)S(1)} %collective-permute-done.18.near, f32[2,16,4,8,128]{4,3,2,1,0:T(8,128)S(1)} %get-tuple-element.90.it, f32[36,4,8,128]{3,2,1,0:T(8,128)S(1)} %get-tuple-element.86.kept, ...), custom_call_target="tpu_custom_call" | custom-call | tf_op jit(solution)/shard_map/last/pallas_call | solution.py:600
  88.7 1.4 %collective-permute-done.19.other = f32[4,96,128]{2,1,0:T(8,128)S(1)} collective-permute-done((f32[4,96,128]{2,1,0:T(8,128)S(1)}, f32[4,96,128]{2,1,0:T(8,128)S(1)}, u32[]{:S(2)}, u32[]{:S(2)}) %collective-permute-start.19) | collective-permute-done | bytes 196640 | tf_op jit(solution)/shard_map/ppermute | solution.py:519
  90.1 2.2 %collective-permute-start.20 = (f32[2,96,128]{2,1,0:T(8,128)S(1)}, f32[2,96,128]{2,1,0:T(8,128)S(1)}, u32[]{:S(2)}, u32[]{:S(2)}) collective-permute-start(f32[2,96,128]{2,1,0:T(8,128)S(1)} %get-tuple-element.95), channel_id=1, source_target_pairs={{0,128},{32,160},{64,192},{96,224},{128,0},{160,32},{192,64},{224,... | collective-permute-start | bytes 294920 | tf_op jit(solution)/shard_map/ppermute | solution.py:611
  92.3 1.4 %collective-permute-start.21 = (f32[2,96,128]{2,1,0:T(8,128)S(1)}, f32[2,96,128]{2,1,0:T(8,128)S(1)}, u32[]{:S(2)}, u32[]{:S(2)}) collective-permute-start(f32[2,96,128]{2,1,0:T(8,128)S(1)} %get-tuple-element.96), channel_id=1, source_target_pairs={{0,64},{32,96},{64,0},{96,32},{128,192},{160,224},{192,128},{224,1... | collective-permute-start | bytes 294920 | tf_op jit(solution)/shard_map/ppermute | solution.py:611
  93.7 0.6 collective-permute-start.22
  94.3 2.6 %collective-permute-done.20.a = f32[2,96,128]{2,1,0:T(8,128)S(1)} collective-permute-done((f32[2,96,128]{2,1,0:T(8,128)S(1)}, f32[2,96,128]{2,1,0:T(8,128)S(1)}, u32[]{:S(2)}, u32[]{:S(2)}) %collective-permute-start.20) | collective-permute-done | bytes 98336 | tf_op jit(solution)/shard_map/ppermute | solution.py:611
  96.9 1.7 %collective-permute-done.21.b = f32[2,96,128]{2,1,0:T(8,128)S(1)} collective-permute-done((f32[2,96,128]{2,1,0:T(8,128)S(1)}, f32[2,96,128]{2,1,0:T(8,128)S(1)}, u32[]{:S(2)}, u32[]{:S(2)}) %collective-permute-start.21) | collective-permute-done | bytes 98336 | tf_op jit(solution)/shard_map/ppermute | solution.py:611
  98.6 0.9 collective-permute-done.22.c
  99.5 0.8 unpack.1
  (14 shorter events, 0.8 us)
Async XLA Ops:
  2.0 7.8 %collective-permute-start = (f32[232,128]{1,0:T(8,128)S(1)}, f32[232,128]{1,0:T(8,128)S(1)}, u32[]{:S(2)}, u32[]{:S(2)}) collective-permute-start(f32[232,128]{1,0:T(8,128)S(1)} %get-tuple-element.50), channel_id=1, source_target_pairs={{0,128},{32,160},{64,192},{96,224},{128,0},{160,32},{192,64},{224,... | collective-permute-start | bytes 356360 | tf_op jit(solution)/shard_map/ppermute | solution.py:510
  5.3 6.5 %collective-permute-start.1 = (f32[232,128]{1,0:T(8,128)S(1)}, f32[232,128]{1,0:T(8,128)S(1)}, u32[]{:S(2)}, u32[]{:S(2)}) collective-permute-start(f32[232,128]{1,0:T(8,128)S(1)} %get-tuple-element.51), channel_id=1, source_target_pairs={{0,64},{32,96},{64,0},{96,32},{128,192},{160,224},{192,128},{224,1... | collective-permute-start | bytes 356360 | tf_op jit(solution)/shard_map/ppermute | solution.py:510
  6.0 9.1 %collective-permute-start.2 = (f32[232,128]{1,0:T(8,128)S(1)}, f32[232,128]{1,0:T(8,128)S(1)}, u32[]{:S(2)}, u32[]{:S(2)}) collective-permute-start(f32[232,128]{1,0:T(8,128)S(1)} %get-tuple-element.52), channel_id=1, source_target_pairs={{0,192},{32,224},{64,128},{96,160},{128,64},{160,96},{192,0},{224,... | collective-permute-start | bytes 356360 | tf_op jit(solution)/shard_map/ppermute | solution.py:510
  6.3 8.7 %collective-permute-start.3 = (f32[232,128]{1,0:T(8,128)S(1)}, f32[232,128]{1,0:T(8,128)S(1)}, u32[]{:S(2)}, u32[]{:S(2)}) collective-permute-start(f32[232,128]{1,0:T(8,128)S(1)} %get-tuple-element.53), channel_id=1, source_target_pairs={{0,160},{32,128},{64,224},{96,192},{128,32},{160,0},{192,96},{224,... | collective-permute-start | bytes 356360 | tf_op jit(solution)/shard_map/ppermute | solution.py:510
  8.0 8.2 %collective-permute-start.4 = (f32[232,128]{1,0:T(8,128)S(1)}, f32[232,128]{1,0:T(8,128)S(1)}, u32[]{:S(2)}, u32[]{:S(2)}) collective-permute-start(f32[232,128]{1,0:T(8,128)S(1)} %get-tuple-element.54), channel_id=1, source_target_pairs={{0,96},{32,64},{64,32},{96,0},{128,224},{160,192},{192,160},{224,1... | collective-permute-start | bytes 356360 | tf_op jit(solution)/shard_map/ppermute | solution.py:510
  9.8 6.8 %collective-permute-start.5 = (f32[232,128]{1,0:T(8,128)S(1)}, f32[232,128]{1,0:T(8,128)S(1)}, u32[]{:S(2)}, u32[]{:S(2)}) collective-permute-start(f32[232,128]{1,0:T(8,128)S(1)} %get-tuple-element.55), channel_id=1, source_target_pairs={{0,224},{32,192},{64,160},{96,128},{128,96},{160,64},{192,32},{224... | collective-permute-start | bytes 356360 | tf_op jit(solution)/shard_map/ppermute | solution.py:510
  11.8 4.8 %collective-permute-start.6 = (f32[232,128]{1,0:T(8,128)S(1)}, f32[232,128]{1,0:T(8,128)S(1)}, u32[]{:S(2)}, u32[]{:S(2)}) collective-permute-start(f32[232,128]{1,0:T(8,128)S(1)} %get-tuple-element.56), channel_id=1, source_target_pairs={{0,32},{32,0},{64,96},{96,64},{128,160},{160,128},{192,224},{224,1... | collective-permute-start | bytes 356360 | tf_op jit(solution)/shard_map/ppermute | solution.py:510
  17.2 18.7 %collective-permute-start.7 = (f32[177,8,128]{2,1,0:T(8,128)S(1)}, f32[177,8,128]{2,1,0:T(8,128)S(1)}, u32[]{:S(2)}, u32[]{:S(2)}) collective-permute-start(f32[177,8,128]{2,1,0:T(8,128)S(1)} %get-tuple-element.61.far), channel_id=1, source_target_pairs={{0,1},{1,0},{2,3},{3,2},{4,5},{5,4},{6,7},{7,6},{8,9},{9,8},{10,11... | collective-permute-start | bytes 2174984 | tf_op jit(solution)/shard_map/ppermute | solution.py:530
  19.2 21.6 %collective-permute-start.8 = (f32[177,8,128]{2,1,0:T(8,128)S(1)}, f32[177,8,128]{2,1,0:T(8,128)S(1)}, u32[]{:S(2)}, u32[]{:S(2)}) collective-permute-start(f32[177,8,128]{2,1,0:T(8,128)S(1)} %get-tuple-element.62.near), channel_id=1, source_target_pairs={{0,32},{1,2},{2,1},{3,4},{4,3},{5,6},{6,5},{7,8},{8,7},{9,10},{10,... | collective-permute-start | bytes 2174984 | tf_op jit(solution)/shard_map/ppermute | solution.py:530
  42.1 11.3 %collective-permute-start.9 = (f32[26,4,8,128]{3,2,1,0:T(8,128)S(1)}, f32[26,4,8,128]{3,2,1,0:T(8,128)S(1)}, u32[]{:S(2)}, u32[]{:S(2)}) collective-permute-start(f32[26,4,8,128]{3,2,1,0:T(8,128)S(1)} %get-tuple-element.72), channel_id=1, source_target_pairs={{0,1},{1,0},{2,3},{3,2},{4,5},{5,4},{6,7},{7,6},{8,9},{9,8},{10,11... | collective-permute-start | bytes 1277960 | tf_op jit(solution)/shard_map/ppermute | solution.py:530
  42.2 13.4 %collective-permute-start.10 = (f32[26,4,8,128]{3,2,1,0:T(8,128)S(1)}, f32[26,4,8,128]{3,2,1,0:T(8,128)S(1)}, u32[]{:S(2)}, u32[]{:S(2)}) collective-permute-start(f32[26,4,8,128]{3,2,1,0:T(8,128)S(1)} %get-tuple-element.73), channel_id=1, source_target_pairs={{0,32},{1,2},{2,1},{3,4},{4,3},{5,6},{6,5},{7,8},{8,7},{9,10},{10,... | collective-permute-start | bytes 1277960 | tf_op jit(solution)/shard_map/ppermute | solution.py:530
  56.3 9.7 %collective-permute-start.11 = (f32[24,4,8,128]{3,2,1,0:T(8,128)S(1)}, f32[24,4,8,128]{3,2,1,0:T(8,128)S(1)}, u32[]{:S(2)}, u32[]{:S(2)}) collective-permute-start(f32[24,4,8,128]{3,2,1,0:T(8,128)S(1)} %get-tuple-element.76), channel_id=1, source_target_pairs={{0,1},{1,0},{2,3},{3,2},{4,5},{5,4},{6,7},{7,6},{8,9},{9,8},{10,11... | collective-permute-start | bytes 1179656 | tf_op jit(solution)/shard_map/ppermute | solution.py:530
  56.4 11.8 %collective-permute-start.12 = (f32[24,4,8,128]{3,2,1,0:T(8,128)S(1)}, f32[24,4,8,128]{3,2,1,0:T(8,128)S(1)}, u32[]{:S(2)}, u32[]{:S(2)}) collective-permute-start(f32[24,4,8,128]{3,2,1,0:T(8,128)S(1)} %get-tuple-element.77), channel_id=1, source_target_pairs={{0,32},{1,2},{2,1},{3,4},{4,3},{5,6},{6,5},{7,8},{8,7},{9,10},{10,... | collective-permute-start | bytes 1179656 | tf_op jit(solution)/shard_map/ppermute | solution.py:530
  60.1 5.6 %collective-permute-start.13 = (f32[2,4,4,8,128]{4,3,2,1,0:T(8,128)S(1)}, f32[2,4,4,8,128]{4,3,2,1,0:T(8,128)S(1)}, u32[]{:S(2)}, u32[]{:S(2)}) collective-permute-start(f32[2,4,4,8,128]{4,3,2,1,0:T(8,128)S(1)} %get-tuple-element.78), channel_id=1, source_target_pairs={{32,64},{64,32},{96,128},{128,96},{160,192},{192,160},{224,0},{0,2... | collective-permute-start | bytes 393224 | tf_op jit(solution)/shard_map/ppermute | solution.py:519
  60.1 5.6 %collective-permute-start.14 = (f32[2,4,4,8,128]{4,3,2,1,0:T(8,128)S(1)}, f32[2,4,4,8,128]{4,3,2,1,0:T(8,128)S(1)}, u32[]{:S(2)}, u32[]{:S(2)}) collective-permute-start(f32[2,4,4,8,128]{4,3,2,1,0:T(8,128)S(1)} %get-tuple-element.79), channel_id=1, source_target_pairs={{0,32},{32,0},{64,96},{96,64},{128,160},{160,128},{192,224},{224,1... | collective-permute-start | bytes 393224 | tf_op jit(solution)/shard_map/ppermute | solution.py:519
  68.3 6.2 %collective-permute-start.15 = (f32[10,4,8,128]{3,2,1,0:T(8,128)S(1)}, f32[10,4,8,128]{3,2,1,0:T(8,128)S(1)}, u32[]{:S(2)}, u32[]{:S(2)}) collective-permute-start(f32[10,4,8,128]{3,2,1,0:T(8,128)S(1)} %get-tuple-element.81), channel_id=1, source_target_pairs={{32,64},{64,32},{96,128},{128,96},{160,192},{192,160},{224,0},{0,2... | collective-permute-start | bytes 491528 | tf_op jit(solution)/shard_map/ppermute | solution.py:519
  68.6 5.9 %collective-permute-start.16 = (f32[10,4,8,128]{3,2,1,0:T(8,128)S(1)}, f32[10,4,8,128]{3,2,1,0:T(8,128)S(1)}, u32[]{:S(2)}, u32[]{:S(2)}) collective-permute-start(f32[10,4,8,128]{3,2,1,0:T(8,128)S(1)} %get-tuple-element.82), channel_id=1, source_target_pairs={{0,32},{32,0},{64,96},{96,64},{128,160},{160,128},{192,224},{224,1... | collective-permute-start | bytes 491528 | tf_op jit(solution)/shard_map/ppermute | solution.py:519
  75.7 9.6 %collective-permute-start.17 = (f32[26,4,8,128]{3,2,1,0:T(8,128)S(1)}, f32[26,4,8,128]{3,2,1,0:T(8,128)S(1)}, u32[]{:S(2)}, u32[]{:S(2)}) collective-permute-start(f32[26,4,8,128]{3,2,1,0:T(8,128)S(1)} %get-tuple-element.88), channel_id=1, source_target_pairs={{0,1},{1,0},{2,3},{3,2},{4,5},{5,4},{6,7},{7,6},{8,9},{9,8},{10,11... | collective-permute-start | bytes 1277960 | tf_op jit(solution)/shard_map/ppermute | solution.py:530
  75.8 11.7 %collective-permute-start.18 = (f32[26,4,8,128]{3,2,1,0:T(8,128)S(1)}, f32[26,4,8,128]{3,2,1,0:T(8,128)S(1)}, u32[]{:S(2)}, u32[]{:S(2)}) collective-permute-start(f32[26,4,8,128]{3,2,1,0:T(8,128)S(1)} %get-tuple-element.89), channel_id=1, source_target_pairs={{0,32},{1,2},{2,1},{3,4},{4,3},{5,6},{6,5},{7,8},{8,7},{9,10},{10,... | collective-permute-start | bytes 1277960 | tf_op jit(solution)/shard_map/ppermute | solution.py:530
  88.6 1.5 %collective-permute-start.19 = (f32[4,96,128]{2,1,0:T(8,128)S(1)}, f32[4,96,128]{2,1,0:T(8,128)S(1)}, u32[]{:S(2)}, u32[]{:S(2)}) collective-permute-start(f32[4,96,128]{2,1,0:T(8,128)S(1)} %get-tuple-element.93), channel_id=1, source_target_pairs={{0,32},{32,0},{64,96},{96,64},{128,160},{160,128},{192,224},{224,1... | collective-permute-start | bytes 589832 | tf_op jit(solution)/shard_map/ppermute | solution.py:519
  90.1 6.8 %collective-permute-start.20 = (f32[2,96,128]{2,1,0:T(8,128)S(1)}, f32[2,96,128]{2,1,0:T(8,128)S(1)}, u32[]{:S(2)}, u32[]{:S(2)}) collective-permute-start(f32[2,96,128]{2,1,0:T(8,128)S(1)} %get-tuple-element.95), channel_id=1, source_target_pairs={{0,128},{32,160},{64,192},{96,224},{128,0},{160,32},{192,64},{224,... | collective-permute-start | bytes 294920 | tf_op jit(solution)/shard_map/ppermute | solution.py:611
  92.3 6.4 %collective-permute-start.21 = (f32[2,96,128]{2,1,0:T(8,128)S(1)}, f32[2,96,128]{2,1,0:T(8,128)S(1)}, u32[]{:S(2)}, u32[]{:S(2)}) collective-permute-start(f32[2,96,128]{2,1,0:T(8,128)S(1)} %get-tuple-element.96), channel_id=1, source_target_pairs={{0,64},{32,96},{64,0},{96,32},{128,192},{160,224},{192,128},{224,1... | collective-permute-start | bytes 294920 | tf_op jit(solution)/shard_map/ppermute | solution.py:611
  93.7 5.8 %collective-permute-start.22 = (f32[2,96,128]{2,1,0:T(8,128)S(1)}, f32[2,96,128]{2,1,0:T(8,128)S(1)}, u32[]{:S(2)}, u32[]{:S(2)}) collective-permute-start(f32[2,96,128]{2,1,0:T(8,128)S(1)} %get-tuple-element.97), channel_id=1, source_target_pairs={{0,192},{32,224},{64,128},{96,160},{128,64},{160,96},{192,0},{224,... | collective-permute-start | bytes 294920 | tf_op jit(solution)/shard_map/ppermute | solution.py:611
